TPU v7x, 256 devices: a whole 4x4x8 slice. The times are simulated.
256 devices in a mesh: group: 2 (over core), ctx: 32 (over x, z_hi, y), tp: 4 (over z_lo).
Axes of the slice: x: 4, y: 4, z: 8 (z_hi: 2, z_lo: 4; z = z_hi * 4 + z_lo), core: 2. Of those that a mesh axis runs over, the one named last changes fastest.
Arguments:
- activations: bfloat16 [8192, 8192], P(('group', 'ctx')), may hold values from -6 to 6
- queries: bfloat16 [8192, 4096], P(('group', 'ctx'), 'tp'), may hold values from -400 to 400
- out_grad: bfloat16 [8192, 4096], P(('group', 'ctx'), 'tp'), may hold values from -6 to 6
- key_weight: bfloat16 [8192, 512], P('ctx', 'tp'), may hold values from -0.0625 to 0.0625
- value_weight: bfloat16 [8192, 512], P('ctx', 'tp'), may hold values from -0.0625 to 0.0625
- sessions: int32 [32, 128], P('ctx'), may hold values from 0 to 3, never falling along the last dimension, each value on 1 to 64 neighbouring positions
Outputs:
- attention: bfloat16 [8192, 4096], P(('group', 'ctx'), 'tp')
- query_grad: bfloat16 [8192, 4096], P(('group', 'ctx'), 'tp')
- key_weight_grad: float32 [8192, 512], P(('group', 'ctx'), 'tp')
- value_weight_grad: float32 [8192, 512], P(('group', 'ctx'), 'tp')
- input_grad: bfloat16 [8192, 8192], P(('group', 'ctx'), 'tp')
Inputs may be any that keep to these rules, and one draw needn't show every extreme that they name: `sessions`: each row never falls; every session in a row has 1 to 64 tokens, and one session of each row has exactly that many.
All inputs are finite; a program needn't handle non-finite values.
Results may differ from a plain program's by a relative error of at most 0.025.
The roundings to bfloat16 on the way count: a program that leaves them out, or rounds other values in their place, can miss the bound.
Values may be sent and summed in bfloat16 or wider, within the bound.
No kernel may reach another device: no remote copies, remote signals or barrier semaphores. Data moves between devices by JAX's collectives and lax.ppermute only.
A program may use at most 64 MiB of HBM per device.

v0:
```python
import math

import jax
import jax.numpy as jnp
from jax import lax
from jax.experimental import pallas as pl
from jax.experimental.pallas import tpu as pltpu
from jax.sharding import PartitionSpec as P


HD = 128
HALF = HD // 2
THETA = 500000.0
TOK = 128
NX, NZ, NY, NT = 4, 2, 4, 4
SCALE = 1.0 / math.sqrt(HD)
F32 = jnp.float32
BF16 = jnp.bfloat16


def ctx_of(x, z, y):
    return (x * NZ + z) * NY + y


PLANES = [[ctx_of(x, z, y) for x in range(NX) for y in range(NY)] for z in range(NZ)]
TURN = [
    (ctx_of(x, z, y) * NT + t, ctx_of(t, z, y) * NT + x)
    for x in range(NX)
    for z in range(NZ)
    for y in range(NY)
    for t in range(NT)
]
FAR_TURN = [(source, (target // NT ^ NY) * NT + target % NT) for source, target in TURN]
ACROSS = [
    (ctx_of(x, z, y), ctx_of(x, 1 - z, y)) for x in range(NX) for z in range(NZ) for y in range(NY)
]


def partner(array):
    return lax.ppermute(array, "group", [(0, 1), (1, 0)])


def across(array):
    return lax.ppermute(array, "ctx", ACROSS)


def along(array, step):
    return lax.ppermute(array, "tp", [(t, (t + step) % NT) for t in range(NT)])


def after(first, second):
    return lax.optimization_barrier((first, second))


def plane_exchange(blocks):
    return lax.all_to_all(
        blocks, "ctx", split_axis=0, concat_axis=0, tiled=True, axis_index_groups=PLANES
    )


def plane_gather(block):
    return plane_exchange(jnp.broadcast_to(block[None], (NX * NY, *block.shape)))


def turn(rows, cosine, sine):
    shaped = rows.reshape(rows.shape[0], -1, HD)
    first, second = shaped[..., :HALF], shaped[..., HALF:]
    cosine, sine = cosine[:, None, :], sine[:, None, :]
    turned = jnp.concatenate(
        [first * cosine - second * sine, second * cosine + first * sine], -1
    )
    return turned.reshape(rows.shape)


def product(left, right, left_dim, right_dim):
    return lax.dot_general(
        left, right, (((left_dim,), (right_dim,)), ((), ())), preferred_element_type=F32
    )


GH = 4
ROWS = GH * TOK
CHUNK = NY * TOK


def attention_kernel(
    place_ref,
    q_keep, q_got, do_keep, do_got, ctx_mine, ctx_other, short_mine, short_other,
    allowed_ref, table_ref,
    out_mine, out_other, qgrad_mine, qgrad_other, kv_keep, kv_send, short_keep, short_send,
    scores, tops, acc, qacc,
):
    core = place_ref[0]
    rank = place_ref[1]
    long_core = core == 0
    last = rank >> 2
    count = last + 1

    def heads_down(ref_a, ref_b, take_a):
        picked = jnp.where(take_a, ref_a[...], ref_b[...])
        return jnp.concatenate([picked[:, h * HD : (h + 1) * HD] for h in range(GH)], 0)

    def store_out(mine, other, long_part, short_part):
        for h in range(GH):
            long_head = long_part[:, h * TOK : (h + 1) * TOK]
            short_head = short_part[:, h * TOK : (h + 1) * TOK]
            here = (slice(None), slice(h * HD, (h + 1) * HD))
            mine[here] = jnp.transpose(jnp.where(long_core, long_head, short_head)).astype(BF16)
            other[here] = jnp.transpose(jnp.where(long_core, short_head, long_head)).astype(BF16)

    def unturn(transposed, which):
        cosine = jnp.concatenate([table_ref[which, 0]] * GH, 1)
        sine = jnp.concatenate([table_ref[which, 1]] * GH, 1)
        first, second = transposed[:HALF], transposed[HALF:]
        return jnp.concatenate(
            [first * cosine + second * sine, second * cosine - first * sine], 0
        )

    def dots(grads_t, attended_t):
        return jnp.sum(grads_t * attended_t.astype(BF16).astype(F32), 0, keepdims=True)

    q_long = heads_down(q_keep, q_got, long_core)
    do_long = heads_down(do_keep, do_got, long_core)
    q_short = heads_down(q_got, q_keep, long_core)
    do_short = heads_down(do_got, do_keep, long_core)

    def blocks_of(j, take_mine):
        base = (j >> 1) * (NY * NZ) + (j & 1)
        return jnp.concatenate(
            [
                jnp.where(take_mine, ctx_mine[base + y * NZ], ctx_other[base + y * NZ])
                for y in range(NY)
            ],
            0,
        )

    key_at = lax.broadcasted_iota(jnp.int32, (CHUNK, ROWS), 0)
    row_at = lax.broadcasted_iota(jnp.int32, (CHUNK, ROWS), 1) & (TOK - 1)
    ahead = key_at - row_at

    def score_chunk(j, top, total, masked):
        scored = product(blocks_of(j, long_core), q_long, 1, 1) * SCALE
        if masked:
            scored = jnp.where(ahead <= rank * TOK - j * CHUNK, scored, -jnp.inf)
        new_top = jnp.maximum(top, jnp.max(scored, 0, keepdims=True))
        powers = jnp.exp(scored - new_top)
        scores[j] = powers
        tops[j] = new_top
        return new_top, total * jnp.exp(top - new_top) + jnp.sum(powers, 0, keepdims=True)

    start = (jnp.full((1, ROWS), -jnp.inf, F32), jnp.zeros((1, ROWS), F32))
    top, total = lax.fori_loop(
        0, last, lambda j, state: score_chunk(j, state[0], state[1], False), start
    )
    top, total = score_chunk(last, top, total, True)
    inverse = 1.0 / total

    acc[...] = jnp.zeros_like(acc)
    qacc[...] = jnp.zeros_like(qacc)

    def out_pass(j, carry):
        values = blocks_of(j, core == 1)
        weights = scores[j] * (jnp.exp(tops[j] - top) * inverse)
        scores[j] = weights
        acc[...] += product(values, weights.astype(BF16), 0, 0)
        return carry

    lax.fori_loop(0, count, out_pass, 0)
    attended = acc[...]
    do_long_t = jnp.transpose(do_long.astype(F32))
    out_dot = dots(do_long_t, attended)

    def grad_pass(j, carry):
        keys = blocks_of(j, long_core)
        values = blocks_of(j, core == 1)
        weights = scores[j]
        prob_grad = product(values, do_long, 1, 1)
        score_grad = (weights * (prob_grad - out_dot)).astype(BF16)
        qacc[...] += product(keys, score_grad, 0, 0)
        key_part = product(score_grad, q_long, 1, 0) * SCALE
        value_part = product(weights.astype(BF16), do_long, 1, 0)
        base = (j >> 1) * (NY * NZ) + (j & 1)
        keep = jnp.where(long_core, key_part, value_part)
        send = jnp.where(long_core, value_part, key_part)
        for y in range(NY):
            kv_keep[base + y * NZ] = keep[y * TOK : (y + 1) * TOK]
            kv_send[base + y * NZ] = send[y * TOK : (y + 1) * TOK]
        return carry

    lax.fori_loop(0, count, grad_pass, 0)

    def clear_pass(j, carry):
        base = (j >> 1) * (NY * NZ) + (j & 1)
        for y in range(NY):
            kv_keep[base + y * NZ] = jnp.zeros((TOK, HD), F32)
            kv_send[base + y * NZ] = jnp.zeros((TOK, HD), F32)
        return carry

    lax.fori_loop(count, NX * NZ, clear_pass, 0)

    keys = jnp.where(long_core, short_mine[...], short_other[...])
    values = jnp.where(long_core, short_other[...], short_mine[...])
    allowed = jnp.concatenate([allowed_ref[...]] * GH, 1) > 0
    scored = jnp.where(allowed, product(keys, q_short, 1, 1) * SCALE, -jnp.inf)
    powers = jnp.exp(scored - jnp.max(scored, 0, keepdims=True))
    weights = powers * (1.0 / jnp.sum(powers, 0, keepdims=True))
    rounded = weights.astype(BF16)
    short_attended = product(values, rounded, 0, 0)
    store_out(out_mine, out_other, attended, short_attended)
    short_dot = dots(jnp.transpose(do_short.astype(F32)), short_attended)
    prob_grad = product(values, do_short, 1, 1)
    score_grad = (weights * (prob_grad - short_dot)).astype(BF16)
    short_qgrad = product(keys, score_grad, 0, 0)
    store_out(
        qgrad_mine, qgrad_other, unturn(qacc[...] * SCALE, 0), unturn(short_qgrad * SCALE, 1)
    )
    key_part = product(score_grad, q_short, 1, 0) * SCALE
    value_part = product(rounded, do_short, 1, 0)
    short_keep[...] = jnp.where(long_core, key_part, value_part)
    short_send[...] = jnp.where(long_core, value_part, key_part)


def attention_call(place, *arrays):
    rows = jax.ShapeDtypeStruct((TOK, GH * HD), BF16)
    blocks = jax.ShapeDtypeStruct((NX * NZ * NY, TOK, HD), F32)
    block = jax.ShapeDtypeStruct((TOK, HD), F32)
    vmem = pl.BlockSpec(memory_space=pltpu.VMEM)
    return pl.pallas_call(
        attention_kernel,
        out_shape=(rows, rows, rows, rows, blocks, blocks, block, block),
        in_specs=[pl.BlockSpec(memory_space=pltpu.SMEM)] + [vmem] * len(arrays),
        out_specs=(vmem,) * 8,
        scratch_shapes=[
            pltpu.VMEM((NX * NZ, CHUNK, ROWS), F32),
            pltpu.VMEM((NX * NZ, 1, ROWS), F32),
            pltpu.VMEM((HD, ROWS), F32),
            pltpu.VMEM((HD, ROWS), F32),
        ],
        compiler_params=pltpu.CompilerParams(vmem_limit_bytes=48 << 20),
        name="attention",
    )(place, *arrays)


def pack_kernel(source, target):
    for x in range(NX):
        for y in range(NY):
            for part in range(2 * NZ):
                column = (part // NZ) * (NX * NZ * NY) + ctx_of(x, part % NZ, y)
                target[x * NY + y, :, part * TOK : (part + 1) * TOK] = source[
                    :, column * TOK : (column + 1) * TOK
                ]


def pack_columns(activations):
    vmem = pl.BlockSpec(memory_space=pltpu.VMEM)
    return pl.pallas_call(
        pack_kernel,
        out_shape=jax.ShapeDtypeStruct((NX * NY, TOK, 2 * NZ * TOK), activations.dtype),
        in_specs=[vmem],
        out_specs=vmem,
        name="pack",
    )(activations)


def body(activations, queries, out_grad, key_weight, value_weight, sessions):
    core = lax.axis_index("group").astype(jnp.int32)
    rank = lax.axis_index("ctx").astype(jnp.int32)
    tp = lax.axis_index("tp").astype(jnp.int32)
    is_long = core == 0
    upper = ((rank >> 2) & 1) == 1
    features = activations.shape[1]
    slice_cols = features // NT
    plane = NX * NY

    local = jnp.arange(TOK, dtype=jnp.int32)
    frequency = THETA ** (-2.0 * jnp.arange(HALF, dtype=F32) / HD)
    positions = jnp.concatenate([rank * TOK + local, local])
    angles = positions.astype(F32)[:, None] * frequency[None, :]
    cosine, sine = jnp.cos(angles), jnp.sin(angles)
    own_cos = jnp.where(is_long, cosine[:TOK], cosine[TOK:])
    own_sin = jnp.where(is_long, sine[:TOK], sine[TOK:])

    def halves_by_zone(mine, other):
        return jnp.where(upper, jnp.stack([other, mine]), jnp.stack([mine, other]))

    def role(first, second):
        return jnp.where(is_long, first, second)

    weight = role(key_weight, value_weight)
    near = lax.ppermute(weight, ("ctx", "tp"), TURN)
    far = lax.ppermute(weight, ("ctx", "tp"), FAR_TURN)
    weight = plane_gather(halves_by_zone(near, far))
    weight = weight.reshape(NX, NY * NZ * weight.shape[-2], HD)

    own_slice = lax.dynamic_slice_in_dim(activations, tp * slice_cols, slice_cols, 1)
    step = slice_cols // (NZ * NY)

    def columns_at(array, block):
        return array[:, block * step : (block + 1) * step]

    own_slice = jnp.concatenate(
        [columns_at(own_slice, z * NY + y) for y in range(NY) for z in range(NZ)], 1
    )
    other_slice = partner(own_slice)
    both_slices = jnp.concatenate(
        [role(own_slice, other_slice), role(other_slice, own_slice)], 0
    )

    rotated = turn(queries.astype(F32), own_cos, own_sin).astype(BF16)
    width = GH * HD
    q_keep = role(rotated[:, :width], rotated[:, width:])
    q_got = partner(role(rotated[:, width:], rotated[:, :width]))
    do_keep = role(out_grad[:, :width], out_grad[:, width:])
    do_got = partner(role(out_grad[:, width:], out_grad[:, :width]))

    partial = jnp.einsum("tk,hkn->htn", both_slices, weight, preferred_element_type=F32)
    parts = [lax.dynamic_index_in_dim(partial, (tp + d) & (NT - 1), 0, False) for d in range(NT)]
    long_sum = parts[0][:TOK] + sum(along(parts[d][:TOK], d) for d in range(1, NT))
    long_rows = role(turn(long_sum, cosine[:TOK], sine[:TOK]), long_sum).astype(BF16)
    parts, long_rows = after(parts, long_rows)
    arrivals = [along(parts[d][TOK:], d) for d in range(1, NT)]
    short_sum = parts[0][TOK:] + sum(arrivals)
    short_rows = role(turn(short_sum, cosine[TOK:], sine[TOK:]), short_sum).astype(BF16)
    other_short = partner(short_rows)
    context = halves_by_zone(long_rows, across(long_rows))
    context = plane_gather(context)

    packed, context = after(pack_columns(activations), context)
    columns = plane_exchange(packed)
    context = context.reshape(plane * NZ, TOK, HD)
    other_context = partner(context)

    own_sessions = sessions[0]
    allowed = (
        (own_sessions[:, None] == own_sessions[None, :]) & (local[:, None] <= local[None, :])
    ).astype(jnp.int32)
    tables = jnp.stack([cosine, sine]).reshape(2, 2, TOK, HALF).transpose(1, 0, 3, 2)
    place = jnp.stack([core, rank])
    (
        out_mine, out_other, qgrad_mine, qgrad_other, kv_keep, kv_send, short_keep, short_send
    ) = attention_call(
        place, q_keep, q_got, do_keep, do_got, context, other_context, short_rows,
        other_short, allowed, tables,
    )
    got = partner(jnp.concatenate([out_other, qgrad_other], 1))
    out_got, qgrad_got = got[:, :width], got[:, width:]
    attention = jnp.concatenate([role(out_mine, out_got), role(out_got, out_mine)], 1)
    query_grad = jnp.concatenate([role(qgrad_mine, qgrad_got), role(qgrad_got, qgrad_mine)], 1)

    kv_sums = kv_keep + partner(kv_send)
    short_kv = short_keep + partner(short_send)
    blocks, columns = after(kv_sums.reshape(plane, NZ, TOK, HD), columns)
    columns = columns.reshape(plane * TOK, 2 * NZ * TOK)
    arrived = plane_exchange(blocks).sum(0)
    here = jnp.where(upper, arrived[1], arrived[0])
    there = jnp.where(upper, arrived[0], arrived[1])
    grads = jnp.concatenate([here + across(there), short_kv], 0)
    grads = role(turn(grads, cosine, -sine), grads).astype(BF16)

    own_grads = role(grads[:TOK], grads[TOK:])
    got_grads = partner(role(grads[TOK:], grads[:TOK]))
    kv_grads = jnp.concatenate([role(own_grads, got_grads), role(got_grads, own_grads)], 1)

    by_step = [grads] + [along(grads, d) for d in range(1, NT)]
    terms = jnp.zeros((2 * TOK, weight.shape[1]), F32)
    for d in range(NT):
        head = lax.dynamic_index_in_dim(weight, (tp - d) & (NT - 1), 0, False)
        terms += product(by_step[d], head, 1, 1)
    own_terms = role(terms[:TOK], terms[TOK:])
    input_sum = own_terms + partner(role(terms[TOK:], terms[:TOK]))
    input_sum = input_sum.astype(BF16)
    input_grad = jnp.concatenate(
        [columns_at(input_sum, y * NZ + z) for z in range(NZ) for y in range(NY)], 1
    )

    plane_grads = plane_gather(kv_grads).reshape(plane * TOK, 2 * HD)
    owned = product(columns, plane_grads, 0, 0).reshape(2, NZ, TOK, 2 * HD)
    owned = role(owned[0], owned[1]) + partner(role(owned[1], owned[0]))
    owned = jnp.where(upper, owned[1], owned[0]) + across(jnp.where(upper, owned[0], owned[1]))
    return (attention, query_grad, owned[:, :HD], owned[:, HD:], input_grad)


def solution(mesh):
    rows = P(("group", "ctx"), "tp")
    return jax.shard_map(
        body,
        mesh=mesh,
        in_specs=(
            P(("group", "ctx"), None), rows, rows, P("ctx", "tp"), P("ctx", "tp"), P("ctx", None)
        ),
        out_specs=(rows, rows, rows, rows, rows),
        check_vma=False,
    )
```

profile of v0, /device:TPU:33, one launch (start us, length us, event | category | flops | bytes accessed | tf_op | source)
XLA Modules:
  0.0 244.9 jit_solution(13878185233560287145)
XLA Ops:
  1.5 6.6 %collective-permute-start.2 = (bf16[256,128]{1,0:T(8,128)(2,1)S(1)}, bf16[256,128]{1,0:T(8,128)(2,1)S(1)}, u32[]{:S(2)}, u32[]{:S(2)}) collective-permute-start(bf16[256,128]{1,0:T(8,128)(2,1)S(1)} %broadcast_select_fusion.10), channel_id=1, source_target_pairs={{0,16},{1,48},{2,80},{3,112},{4,20},{5,52},{6,84},{7,116},{8,24},{... | collective-permute-start | bytes 196616 | tf_op jit(solution)/shard_map/ppermute | solution.py:291
  8.1 2.6 %collective-permute-start.3 = (bf16[256,128]{1,0:T(8,128)(2,1)S(1)}, bf16[256,128]{1,0:T(8,128)(2,1)S(1)}, u32[]{:S(2)}, u32[]{:S(2)}) collective-permute-start(bf16[256,128]{1,0:T(8,128)(2,1)S(1)} %broadcast_select_fusion.10), channel_id=1, source_target_pairs={{0,0},{1,32},{2,64},{3,96},{4,4},{5,36},{6,68},{7,100},{8,8},{9,40... | collective-permute-start | bytes 196616 | tf_op jit(solution)/shard_map/ppermute | solution.py:290
  15.8 8.5 %all-to-all-start = ((bf16[16,2,256,128]{3,2,1,0:T(8,128)(2,1)}), bf16[16,2,256,128]{3,2,1,0:T(8,128)(2,1)S(1)}, u32[]{:S(2)}, u32[]{:S(2)}) async-start(bf16[16,2,256,128]{3,2,1,0:T(8,128)(2,1)} %broadcast_in_dim.14), calls=%async_computation | async-start | bytes 4194304 | tf_op jit(solution)/shard_map/all_to_all | solution.py:56
  29.4 2.2 collective-permute-start.4
  33.3 2.1 broadcast_select_fusion.1
  35.4 14.7 %all-to-all-done = bf16[16,2,256,128]{3,2,1,0:T(8,128)(2,1)S(1)} async-done(((bf16[16,2,256,128]{3,2,1,0:T(8,128)(2,1)}), bf16[16,2,256,128]{3,2,1,0:T(8,128)(2,1)S(1)}, u32[]{:S(2)}, u32[]{:S(2)}) %all-to-all-start) | async-done | bytes 2097184 | tf_op jit(solution)/shard_map/all_to_all | solution.py:56
  50.1 2.7 %fusion.1 = f32[4,128,256]{1,2,0:T(8,128)S(1)} fusion(bf16[4,2048,128]{2,1,0:T(8,128)(2,1)S(1)} %bitcast.138, bf16[128,2048]{1,0:T(8,128)(2,1)} %get-tuple-element.40, bf16[128,2048]{1,0:T(8,128)(2,1)} %get-tuple-element.39), kind=kOutput, calls=%fused_computation.5 | convolution fusion | flops 538968064 | bytes 3670016 | tf_op jit(solution)/shard_map/tk,hkn->htn/dot_general | solution.py:316
  53.1 3.0 %collective-permute-start.6 = (f32[128,128]{1,0:T(8,128)S(1)}, f32[128,128]{1,0:T(8,128)S(1)}, u32[]{:S(2)}, u32[]{:S(2)}) collective-permute-start(f32[128,128]{1,0:T(8,128)S(1)} %slice_bitcast_fusion.1), channel_id=1, source_target_pairs={{0,2},{1,3},{2,0},{3,1},{4,6},{5,7},{6,4},{7,5},{8,10},{9,11},{10,... | collective-permute-start | bytes 196616 | tf_op jit(solution)/shard_map/ppermute | solution.py:48
  56.2 2.3 collective-permute-done.6
  59.5 4.8 %collective-permute-start.8 = (bf16[128,128]{1,0:T(8,128)(2,1)S(1)}, bf16[128,128]{1,0:T(8,128)(2,1)S(1)}, u32[]{:S(2)}, u32[]{:S(2)}) collective-permute-start(bf16[128,128]{1,0:T(8,128)(2,1)S(1)} %fusion.28), channel_id=1, source_target_pairs={{0,16},{4,20},{8,24},{12,28},{16,0},{20,4},{24,8},{28,12},{32,48},... | collective-permute-start | bytes 98312 | tf_op jit(solution)/shard_map/ppermute | solution.py:44
  64.6 2.4 collective-permute-done.8
  68.2 6.9 %all-to-all-start.1 = ((bf16[16,2,128,128]{3,2,1,0:T(8,128)(2,1)}), bf16[16,2,128,128]{3,2,1,0:T(8,128)(2,1)S(1)}, u32[]{:S(2)}, u32[]{:S(2)}) async-start(bf16[16,2,128,128]{3,2,1,0:T(8,128)(2,1)} %broadcast_in_dim.17), calls=%async_computation.1 | async-start | bytes 2097152 | tf_op jit(solution)/shard_map/all_to_all | solution.py:56
  75.4 4.1 %collective-permute-start = (bf16[128,512]{1,0:T(8,128)(2,1)S(1)}, bf16[128,512]{1,0:T(8,128)(2,1)S(1)}, u32[]{:S(2)}, u32[]{:S(2)}) collective-permute-start(bf16[128,512]{1,0:T(8,128)(2,1)S(1)} %get-tuple-element.65), channel_id=1, source_target_pairs={{0,128},{128,0},{1,129},{129,1},{2,130},{130,2},{3,131},{131,3},{4... | collective-permute-start | bytes 393224 | tf_op jit(solution)/shard_map/ppermute | solution.py:40
  79.4 3.3 %pack.1 = bf16[16,128,512]{2,1,0:T(8,128)(2,1)} custom-call(bf16[128,8192]{1,0:T(8,128)(2,1)} %source.1), custom_call_target="tpu_custom_call" | custom-call | tf_op jit(solution)/shard_map/pack/pallas_call | solution.py:256
  83.1 4.3 %all-to-all-done.1 = bf16[16,2,128,128]{3,2,1,0:T(8,128)(2,1)S(1)} async-done(((bf16[16,2,128,128]{3,2,1,0:T(8,128)(2,1)}), bf16[16,2,128,128]{3,2,1,0:T(8,128)(2,1)S(1)}, u32[]{:S(2)}, u32[]{:S(2)}) %all-to-all-start.1) | async-done | bytes 1048608 | tf_op jit(solution)/shard_map/all_to_all | solution.py:56
  87.4 5.8 %collective-permute-start.9 = (bf16[32,128,128]{2,1,0:T(8,128)(2,1)S(1)}, bf16[32,128,128]{2,1,0:T(8,128)(2,1)S(1)}, u32[]{:S(2)}, u32[]{:S(2)}) collective-permute-start(bf16[32,128,128]{2,1,0:T(8,128)(2,1)S(1)} %bitcast.135), channel_id=1, source_target_pairs={{0,128},{128,0},{1,129},{129,1},{2,130},{130,2},{3,131},{131,3},{4... | collective-permute-start | bytes 3145736 | tf_op jit(solution)/shard_map/ppermute | solution.py:40
  98.3 3.0 %collective-permute-done.12 = f32[128,128]{1,0:T(8,128)S(1)} collective-permute-done((f32[128,128]{1,0:T(8,128)S(1)}, f32[128,128]{1,0:T(8,128)S(1)}, u32[]{:S(2)}, u32[]{:S(2)}) %collective-permute-start.12) | collective-permute-done | bytes 65568 | tf_op jit(solution)/shard_map/ppermute | solution.py:48
  103.2 4.8 %attention.1 = (bf16[128,512]{1,0:T(8,128)(2,1)S(1)}, bf16[128,512]{1,0:T(8,128)(2,1)S(1)}, bf16[128,512]{1,0:T(8,128)(2,1)S(1)}, bf16[128,512]{1,0:T(8,128)(2,1...) custom-call(s32[2]{0:T(128)S(1)} %pad_add_fusion.place_ref, ...), custom_call_target="tpu_custom_call" | custom-call | tf_op jit(solution)/shard_map/attention/pallas_call | solution.py:228
  112.2 11.9 %all-to-all-start.2 = ((bf16[16,128,512]{2,1,0:T(8,128)(2,1)}), bf16[16,128,512]{2,1,0:T(8,128)(2,1)}, u32[]{:S(2)}, u32[]{:S(2)}) async-start(bf16[16,128,512]{2,1,0:T(8,128)(2,1)} %pack.1), calls=%async_computation.2 | async-start | bytes 4194304 | tf_op jit(solution)/shard_map/all_to_all | solution.py:56
  124.1 3.2 %add.132 = f32[32,128,128]{2,1,0:T(8,128)} add(f32[32,128,128]{2,1,0:T(8,128)S(1)} %get-tuple-element.32, f32[32,128,128]{2,1,0:T(8,128)} %collective-permute-done.15) | non-fusion elementwise | flops 524288 | bytes 6291456 | tf_op jit(solution)/shard_map/add | solution.py:350
  127.3 26.0 %all-to-all-done.2 = bf16[16,128,512]{2,1,0:T(8,128)(2,1)} async-done(((bf16[16,128,512]{2,1,0:T(8,128)(2,1)}), bf16[16,128,512]{2,1,0:T(8,128)(2,1)}, u32[]{:S(2)}, u32[]{:S(2)}) %all-to-all-start.2) | async-done | bytes 2097184 | tf_op jit(solution)/shard_map/all_to_all | solution.py:56
  153.3 5.4 %all-to-all-start.3 = ((f32[16,2,128,128]{3,2,1,0:T(8,128)}), f32[16,2,128,128]{3,2,1,0:T(8,128)S(1)}, u32[]{:S(2)}, u32[]{:S(2)}) async-start(f32[16,2,128,128]{3,2,1,0:T(8,128)} %bitcast.137), calls=%async_computation.3 | async-start | bytes 4194304 | tf_op jit(solution)/shard_map/all_to_all | solution.py:56
  160.5 23.9 %all-to-all-done.3 = f32[16,2,128,128]{3,2,1,0:T(8,128)S(1)} async-done(((f32[16,2,128,128]{3,2,1,0:T(8,128)}), f32[16,2,128,128]{3,2,1,0:T(8,128)S(1)}, u32[]{:S(2)}, u32[]{:S(2)}) %all-to-all-start.3) | async-done | bytes 2097184 | tf_op jit(solution)/shard_map/all_to_all | solution.py:56
  184.6 5.0 %collective-permute-start.16 = (f32[128,128]{1,0:T(8,128)S(1)}, f32[128,128]{1,0:T(8,128)S(1)}, u32[]{:S(2)}, u32[]{:S(2)}) collective-permute-start(f32[128,128]{1,0:T(8,128)S(1)} %select_bitcast_fusion.1), channel_id=1, source_target_pairs={{0,16},{4,20},{8,24},{12,28},{16,0},{20,4},{24,8},{28,12},{32,48},... | collective-permute-start | bytes 196616 | tf_op jit(solution)/shard_map/ppermute | solution.py:44
  189.6 5.4 %collective-permute-start.14 = (bf16[128,1024]{1,0:T(8,128)(2,1)S(1)}, bf16[128,1024]{1,0:T(8,128)(2,1)}, u32[]{:S(2)}, u32[]{:S(2)}) collective-permute-start(bf16[128,1024]{1,0:T(8,128)(2,1)S(1)} %pad_maximum_fusion.1), channel_id=1, source_target_pairs={{0,128},{128,0},{1,129},{129,1},{2,130},{130,2},{3,131},{131,3},{4... | collective-permute-start | bytes 786440 | tf_op jit(solution)/shard_map/ppermute | solution.py:40
  198.4 3.8 %collective-permute-start.18 = (bf16[128,128]{1,0:T(8,128)(2,1)S(1)}, bf16[128,128]{1,0:T(8,128)(2,1)S(1)}, u32[]{:S(2)}, u32[]{:S(2)}) collective-permute-start(bf16[128,128]{1,0:T(8,128)(2,1)S(1)} %broadcast_select_fusion.13), channel_id=1, source_target_pairs={{0,128},{128,0},{1,129},{129,1},{2,130},{130,2},{3,131},{131,3},{4... | collective-permute-start | bytes 98312 | tf_op jit(solution)/shard_map/ppermute | solution.py:40
  204.9 4.3 %all-to-all-start.4 = ((bf16[16,128,256]{2,1,0:T(8,128)(2,1)}), bf16[16,128,256]{2,1,0:T(8,128)(2,1)S(1)}, u32[]{:S(2)}, u32[]{:S(2)}) async-start(bf16[16,128,256]{2,1,0:T(8,128)(2,1)} %broadcast_in_dim.20), calls=%async_computation.4 | async-start | bytes 2097152 | tf_op jit(solution)/shard_map/all_to_all | solution.py:56
  216.7 9.3 %all-to-all-done.4 = bf16[16,128,256]{2,1,0:T(8,128)(2,1)S(1)} async-done(((bf16[16,128,256]{2,1,0:T(8,128)(2,1)}), bf16[16,128,256]{2,1,0:T(8,128)(2,1)S(1)}, u32[]{:S(2)}, u32[]{:S(2)}) %all-to-all-start.4) | async-done | bytes 1048608 | tf_op jit(solution)/shard_map/all_to_all | solution.py:56
  226.0 2.3 convolution_bitcast_fusion
  228.4 2.1 collective-permute-start.19
  232.1 4.2 %collective-permute-start.20 = (f32[128,256]{1,0:T(8,128)S(1)}, f32[128,256]{1,0:T(8,128)S(1)}, u32[]{:S(2)}, u32[]{:S(2)}) collective-permute-start(f32[128,256]{1,0:T(8,128)S(1)} %select_bitcast_fusion), channel_id=1, source_target_pairs={{0,16},{4,20},{8,24},{12,28},{16,0},{20,4},{24,8},{28,12},{32,48},... | collective-permute-start | bytes 393224 | tf_op jit(solution)/shard_map/ppermute | solution.py:44
  236.3 7.8 %collective-permute-done.20 = f32[128,256]{1,0:T(8,128)S(1)} collective-permute-done((f32[128,256]{1,0:T(8,128)S(1)}, f32[128,256]{1,0:T(8,128)S(1)}, u32[]{:S(2)}, u32[]{:S(2)}) %collective-permute-start.20) | collective-permute-done | bytes 131104 | tf_op jit(solution)/shard_map/ppermute | solution.py:44
  (148 shorter events, 44.9 us)
Async XLA Ops:
  1.5 10.9 %collective-permute-start.2 = (bf16[256,128]{1,0:T(8,128)(2,1)S(1)}, bf16[256,128]{1,0:T(8,128)(2,1)S(1)}, u32[]{:S(2)}, u32[]{:S(2)}) collective-permute-start(bf16[256,128]{1,0:T(8,128)(2,1)S(1)} %broadcast_select_fusion.10), channel_id=1, source_target_pairs={{0,16},{1,48},{2,80},{3,112},{4,20},{5,52},{6,84},{7,116},{8,24},{... | collective-permute-start | bytes 196616 | tf_op jit(solution)/shard_map/ppermute | solution.py:291
  8.1 5.9 %collective-permute-start.3 = (bf16[256,128]{1,0:T(8,128)(2,1)S(1)}, bf16[256,128]{1,0:T(8,128)(2,1)S(1)}, u32[]{:S(2)}, u32[]{:S(2)}) collective-permute-start(bf16[256,128]{1,0:T(8,128)(2,1)S(1)} %broadcast_select_fusion.10), channel_id=1, source_target_pairs={{0,0},{1,32},{2,64},{3,96},{4,4},{5,36},{6,68},{7,100},{8,8},{9,40... | collective-permute-start | bytes 196616 | tf_op jit(solution)/shard_map/ppermute | solution.py:290
  15.8 34.3 %all-to-all-start = ((bf16[16,2,256,128]{3,2,1,0:T(8,128)(2,1)}), bf16[16,2,256,128]{3,2,1,0:T(8,128)(2,1)S(1)}, u32[]{:S(2)}, u32[]{:S(2)}) async-start(bf16[16,2,256,128]{3,2,1,0:T(8,128)(2,1)} %broadcast_in_dim.14), calls=%async_computation | async-start | bytes 4194304 | tf_op jit(solution)/shard_map/all_to_all | solution.py:56
  29.4 3.9 %collective-permute-start.4 = (bf16[128,2048]{1,0:T(8,128)(2,1)S(1)}, bf16[128,2048]{1,0:T(8,128)(2,1)}, u32[]{:S(2)}, u32[]{:S(2)}) collective-permute-start(bf16[128,2048]{1,0:T(8,128)(2,1)S(1)} %dynamic-slice_dynamic-update-slice_fusion), channel_id=1, source_target_pairs={{0,128},{128,0},{1,129},{129,1},{2,130},{130,2},{3,131},{131,3},{4... | collective-permute-start | bytes 1572872 | tf_op jit(solution)/shard_map/ppermute | solution.py:40
  52.8 3.4 %collective-permute-start.5 = (f32[128,128]{1,0:T(8,128)S(1)}, f32[128,128]{1,0:T(8,128)S(1)}, u32[]{:S(2)}, u32[]{:S(2)}) collective-permute-start(f32[128,128]{1,0:T(8,128)S(1)} %slice_bitcast_fusion.2), channel_id=1, source_target_pairs={{0,1},{1,2},{2,3},{3,0},{4,5},{5,6},{6,7},{7,4},{8,9},{9,10},{10,1... | collective-permute-start | bytes 196616 | tf_op jit(solution)/shard_map/ppermute | solution.py:48
  53.1 5.4 %collective-permute-start.6 = (f32[128,128]{1,0:T(8,128)S(1)}, f32[128,128]{1,0:T(8,128)S(1)}, u32[]{:S(2)}, u32[]{:S(2)}) collective-permute-start(f32[128,128]{1,0:T(8,128)S(1)} %slice_bitcast_fusion.1), channel_id=1, source_target_pairs={{0,2},{1,3},{2,0},{3,1},{4,6},{5,7},{6,4},{7,5},{8,10},{9,11},{10,... | collective-permute-start | bytes 196616 | tf_op jit(solution)/shard_map/ppermute | solution.py:48
  56.1 3.2 %collective-permute-start.7 = (f32[128,128]{1,0:T(8,128)S(1)}, f32[128,128]{1,0:T(8,128)S(1)}, u32[]{:S(2)}, u32[]{:S(2)}) collective-permute-start(f32[128,128]{1,0:T(8,128)S(1)} %slice_bitcast_fusion), channel_id=1, source_target_pairs={{0,3},{1,0},{2,1},{3,2},{4,7},{5,4},{6,5},{7,6},{8,11},{9,8},{10,9... | collective-permute-start | bytes 196616 | tf_op jit(solution)/shard_map/ppermute | solution.py:48
  59.5 7.4 %collective-permute-start.8 = (bf16[128,128]{1,0:T(8,128)(2,1)S(1)}, bf16[128,128]{1,0:T(8,128)(2,1)S(1)}, u32[]{:S(2)}, u32[]{:S(2)}) collective-permute-start(bf16[128,128]{1,0:T(8,128)(2,1)S(1)} %fusion.28), channel_id=1, source_target_pairs={{0,16},{4,20},{8,24},{12,28},{16,0},{20,4},{24,8},{28,12},{32,48},... | collective-permute-start | bytes 98312 | tf_op jit(solution)/shard_map/ppermute | solution.py:44
  68.2 19.2 %all-to-all-start.1 = ((bf16[16,2,128,128]{3,2,1,0:T(8,128)(2,1)}), bf16[16,2,128,128]{3,2,1,0:T(8,128)(2,1)S(1)}, u32[]{:S(2)}, u32[]{:S(2)}) async-start(bf16[16,2,128,128]{3,2,1,0:T(8,128)(2,1)} %broadcast_in_dim.17), calls=%async_computation.1 | async-start | bytes 2097152 | tf_op jit(solution)/shard_map/all_to_all | solution.py:56
  75.4 27.0 %collective-permute-start = (bf16[128,512]{1,0:T(8,128)(2,1)S(1)}, bf16[128,512]{1,0:T(8,128)(2,1)S(1)}, u32[]{:S(2)}, u32[]{:S(2)}) collective-permute-start(bf16[128,512]{1,0:T(8,128)(2,1)S(1)} %get-tuple-element.65), channel_id=1, source_target_pairs={{0,128},{128,0},{1,129},{129,1},{2,130},{130,2},{3,131},{131,3},{4... | collective-permute-start | bytes 393224 | tf_op jit(solution)/shard_map/ppermute | solution.py:40
  87.4 15.8 %collective-permute-start.9 = (bf16[32,128,128]{2,1,0:T(8,128)(2,1)S(1)}, bf16[32,128,128]{2,1,0:T(8,128)(2,1)S(1)}, u32[]{:S(2)}, u32[]{:S(2)}) collective-permute-start(bf16[32,128,128]{2,1,0:T(8,128)(2,1)S(1)} %bitcast.135), channel_id=1, source_target_pairs={{0,128},{128,0},{1,129},{129,1},{2,130},{130,2},{3,131},{131,3},{4... | collective-permute-start | bytes 3145736 | tf_op jit(solution)/shard_map/ppermute | solution.py:40
  93.3 3.7 %collective-permute-start.10 = (f32[128,128]{1,0:T(8,128)S(1)}, f32[128,128]{1,0:T(8,128)S(1)}, u32[]{:S(2)}, u32[]{:S(2)}) collective-permute-start(f32[128,128]{1,0:T(8,128)S(1)} %slice.223), channel_id=1, source_target_pairs={{0,1},{1,2},{2,3},{3,0},{4,5},{5,6},{6,7},{7,4},{8,9},{9,10},{10,1... | collective-permute-start | bytes 196616 | tf_op jit(solution)/shard_map/ppermute | solution.py:48
  93.4 4.9 %collective-permute-start.11 = (f32[128,128]{1,0:T(8,128)S(1)}, f32[128,128]{1,0:T(8,128)S(1)}, u32[]{:S(2)}, u32[]{:S(2)}) collective-permute-start(f32[128,128]{1,0:T(8,128)S(1)} %slice.224), channel_id=1, source_target_pairs={{0,2},{1,3},{2,0},{3,1},{4,6},{5,7},{6,4},{7,5},{8,10},{9,11},{10,... | collective-permute-start | bytes 196616 | tf_op jit(solution)/shard_map/ppermute | solution.py:48
  94.6 6.8 %collective-permute-start.12 = (f32[128,128]{1,0:T(8,128)S(1)}, f32[128,128]{1,0:T(8,128)S(1)}, u32[]{:S(2)}, u32[]{:S(2)}) collective-permute-start(f32[128,128]{1,0:T(8,128)S(1)} %slice.225), channel_id=1, source_target_pairs={{0,3},{1,0},{2,1},{3,2},{4,7},{5,4},{6,5},{7,6},{8,11},{9,8},{10,9... | collective-permute-start | bytes 196616 | tf_op jit(solution)/shard_map/ppermute | solution.py:48
  97.0 5.4 %collective-permute-start.1 = (bf16[128,512]{1,0:T(8,128)(2,1)S(1)}, bf16[128,512]{1,0:T(8,128)(2,1)S(1)}, u32[]{:S(2)}, u32[]{:S(2)}) collective-permute-start(bf16[128,512]{1,0:T(8,128)(2,1)S(1)} %get-tuple-element.63), channel_id=1, source_target_pairs={{0,128},{128,0},{1,129},{129,1},{2,130},{130,2},{3,131},{131,3},{4... | collective-permute-start | bytes 393224 | tf_op jit(solution)/shard_map/ppermute | solution.py:40
  101.6 1.6 collective-permute-start.13
  111.8 12.2 %collective-permute-start.15 = (f32[32,128,128]{2,1,0:T(8,128)}, f32[32,128,128]{2,1,0:T(8,128)}, u32[]{:S(2)}, u32[]{:S(2)}) collective-permute-start(f32[32,128,128]{2,1,0:T(8,128)} %get-tuple-element.33), channel_id=1, source_target_pairs={{0,128},{128,0},{1,129},{129,1},{2,130},{130,2},{3,131},{131,3},{4... | collective-permute-start | bytes 6291464 | tf_op jit(solution)/shard_map/ppermute | solution.py:40
  112.2 41.1 %all-to-all-start.2 = ((bf16[16,128,512]{2,1,0:T(8,128)(2,1)}), bf16[16,128,512]{2,1,0:T(8,128)(2,1)}, u32[]{:S(2)}, u32[]{:S(2)}) async-start(bf16[16,128,512]{2,1,0:T(8,128)(2,1)} %pack.1), calls=%async_computation.2 | async-start | bytes 4194304 | tf_op jit(solution)/shard_map/all_to_all | solution.py:56
  153.3 31.2 %all-to-all-start.3 = ((f32[16,2,128,128]{3,2,1,0:T(8,128)}), f32[16,2,128,128]{3,2,1,0:T(8,128)S(1)}, u32[]{:S(2)}, u32[]{:S(2)}) async-start(f32[16,2,128,128]{3,2,1,0:T(8,128)} %bitcast.137), calls=%async_computation.3 | async-start | bytes 4194304 | tf_op jit(solution)/shard_map/all_to_all | solution.py:56
  158.7 30.8 %copy-start.1 = (bf16[128,512]{1,0:T(8,128)(2,1)S(1)}, bf16[128,512]{1,0:T(8,128)(2,1)}, u32[]{:S(2)}) copy-start(bf16[128,512]{1,0:T(8,128)(2,1)} %copy-done) | copy-start | bytes 393220
  158.7 36.2 %copy-start.9 = (f32[128,128]{1,0:T(8,128)S(1)}, f32[128,128]{1,0:T(8,128)}, u32[]{:S(2)}) copy-start(f32[128,128]{1,0:T(8,128)} %copy-done.8) | copy-start | bytes 196612
  158.8 36.2 %collective-permute-start.17 = (f32[128,128]{1,0:T(8,128)S(1)}, f32[128,128]{1,0:T(8,128)S(1)}, u32[]{:S(2)}, u32[]{:S(2)}) collective-permute-start(f32[128,128]{1,0:T(8,128)S(1)} %copy-done.11), channel_id=1, source_target_pairs={{0,128},{128,0},{1,129},{129,1},{2,130},{130,2},{3,131},{131,3},{4... | collective-permute-start | bytes 196616 | tf_op jit(solution)/shard_map/ppermute | solution.py:40
  184.6 10.4 %collective-permute-start.16 = (f32[128,128]{1,0:T(8,128)S(1)}, f32[128,128]{1,0:T(8,128)S(1)}, u32[]{:S(2)}, u32[]{:S(2)}) collective-permute-start(f32[128,128]{1,0:T(8,128)S(1)} %select_bitcast_fusion.1), channel_id=1, source_target_pairs={{0,16},{4,20},{8,24},{12,28},{16,0},{20,4},{24,8},{28,12},{32,48},... | collective-permute-start | bytes 196616 | tf_op jit(solution)/shard_map/ppermute | solution.py:44
  189.6 24.6 %collective-permute-start.14 = (bf16[128,1024]{1,0:T(8,128)(2,1)S(1)}, bf16[128,1024]{1,0:T(8,128)(2,1)}, u32[]{:S(2)}, u32[]{:S(2)}) collective-permute-start(bf16[128,1024]{1,0:T(8,128)(2,1)S(1)} %pad_maximum_fusion.1), channel_id=1, source_target_pairs={{0,128},{128,0},{1,129},{129,1},{2,130},{130,2},{3,131},{131,3},{4... | collective-permute-start | bytes 786440 | tf_op jit(solution)/shard_map/ppermute | solution.py:40
  195.7 13.5 %collective-permute-start.21 = (bf16[256,128]{1,0:T(8,128)(2,1)S(1)}, bf16[256,128]{1,0:T(8,128)(2,1)}, u32[]{:S(2)}, u32[]{:S(2)}) collective-permute-start(bf16[256,128]{1,0:T(8,128)(2,1)S(1)} %fusion.22), channel_id=1, source_target_pairs={{0,1},{1,2},{2,3},{3,0},{4,5},{5,6},{6,7},{7,4},{8,9},{9,10},{10,1... | collective-permute-start | bytes 196616 | tf_op jit(solution)/shard_map/ppermute | solution.py:48
  195.8 15.1 %collective-permute-start.23 = (bf16[256,128]{1,0:T(8,128)(2,1)S(1)}, bf16[256,128]{1,0:T(8,128)(2,1)}, u32[]{:S(2)}, u32[]{:S(2)}) collective-permute-start(bf16[256,128]{1,0:T(8,128)(2,1)S(1)} %fusion.22), channel_id=1, source_target_pairs={{0,3},{1,0},{2,1},{3,2},{4,7},{5,4},{6,5},{7,6},{8,11},{9,8},{10,9... | collective-permute-start | bytes 196616 | tf_op jit(solution)/shard_map/ppermute | solution.py:48
  197.3 15.0 %collective-permute-start.22 = (bf16[256,128]{1,0:T(8,128)(2,1)S(1)}, bf16[256,128]{1,0:T(8,128)(2,1)S(1)}, u32[]{:S(2)}, u32[]{:S(2)}) collective-permute-start(bf16[256,128]{1,0:T(8,128)(2,1)S(1)} %fusion.22), channel_id=1, source_target_pairs={{0,2},{1,3},{2,0},{3,1},{4,6},{5,7},{6,4},{7,5},{8,10},{9,11},{10,... | collective-permute-start | bytes 196616 | tf_op jit(solution)/shard_map/ppermute | solution.py:48
  198.4 5.3 %collective-permute-start.18 = (bf16[128,128]{1,0:T(8,128)(2,1)S(1)}, bf16[128,128]{1,0:T(8,128)(2,1)S(1)}, u32[]{:S(2)}, u32[]{:S(2)}) collective-permute-start(bf16[128,128]{1,0:T(8,128)(2,1)S(1)} %broadcast_select_fusion.13), channel_id=1, source_target_pairs={{0,128},{128,0},{1,129},{129,1},{2,130},{130,2},{3,131},{131,3},{4... | collective-permute-start | bytes 98312 | tf_op jit(solution)/shard_map/ppermute | solution.py:40
  204.9 21.1 %all-to-all-start.4 = ((bf16[16,128,256]{2,1,0:T(8,128)(2,1)}), bf16[16,128,256]{2,1,0:T(8,128)(2,1)S(1)}, u32[]{:S(2)}, u32[]{:S(2)}) async-start(bf16[16,128,256]{2,1,0:T(8,128)(2,1)} %broadcast_in_dim.20), calls=%async_computation.4 | async-start | bytes 2097152 | tf_op jit(solution)/shard_map/all_to_all | solution.py:56
  213.9 16.5 %collective-permute-start.24 = (f32[128,2048]{1,0:T(8,128)}, f32[128,2048]{1,0:T(8,128)}, u32[]{:S(2)}, u32[]{:S(2)}) collective-permute-start(f32[128,2048]{1,0:T(8,128)} %slice_select_fusion), channel_id=1, source_target_pairs={{0,128},{128,0},{1,129},{129,1},{2,130},{130,2},{3,131},{131,3},{4... | collective-permute-start | bytes 3145736 | tf_op jit(solution)/shard_map/ppermute | solution.py:40
  228.4 3.6 %collective-permute-start.19 = (f32[2,128,256]{2,1,0:T(8,128)S(1)}, f32[2,128,256]{2,1,0:T(8,128)S(1)}, u32[]{:S(2)}, u32[]{:S(2)}) collective-permute-start(f32[2,128,256]{2,1,0:T(8,128)S(1)} %bitcast.151), channel_id=1, source_target_pairs={{0,128},{128,0},{1,129},{129,1},{2,130},{130,2},{3,131},{131,3},{4... | collective-permute-start | bytes 786440 | tf_op jit(solution)/shard_map/ppermute | solution.py:40
  232.1 12.1 %collective-permute-start.20 = (f32[128,256]{1,0:T(8,128)S(1)}, f32[128,256]{1,0:T(8,128)S(1)}, u32[]{:S(2)}, u32[]{:S(2)}) collective-permute-start(f32[128,256]{1,0:T(8,128)S(1)} %select_bitcast_fusion), channel_id=1, source_target_pairs={{0,16},{4,20},{8,24},{12,28},{16,0},{20,4},{24,8},{28,12},{32,48},... | collective-permute-start | bytes 393224 | tf_op jit(solution)/shard_map/ppermute | solution.py:44
  (15 other events, 81.7 us)
where the time goes:
time: 246 us; the launch traced here: 245 us
  waiting for transfers between devices  98.5 us (40%)
  starting transfers between devices  96.1 us (39%)
  local copies, waits for them, and re-layouts  15.9 us (6%)
  other arithmetic  15.1 us (6%)
  matrix products  9.88 us (4%)
  Pallas kernels  8.11 us (3%)
    all_to_all x5, waiting for transfers between devices, plane_exchange(): lax.all_to_all(blocks, 'ctx', split_axis=0, concat_axis=0, tiled=True, ax...  78.1 us
    all_to_all x5, starting transfers between devices, plane_exchange(): lax.all_to_all(blocks, 'ctx', split_axis=0, concat_axis=0, tiled=True, ax...  37 us
    ppermute x11, starting transfers between devices, partner(): return lax.ppermute(array, 'group', [(0, 1), (1, 0)])  27.9 us
    ppermute x3, starting transfers between devices, across(): return lax.ppermute(array, 'ctx', ACROSS)  14 us
    ppermute x3, waiting for transfers between devices, across(): return lax.ppermute(array, 'ctx', ACROSS)  10.3 us
    unnamed x50, local copies, waits for them, and re-layouts  10.2 us
    ppermute x9, starting transfers between devices, along(): return lax.ppermute(array, 'tp', [(t, (t + step) % NT) for t in range(NT)])  8.01 us
    ppermute x9, waiting for transfers between devices, along(): return lax.ppermute(array, 'tp', [(t, (t + step) % NT) for t in range(NT)])  7.69 us
  transfers between devices with their start and end apart: 30, of which 14 were waited for; matrix products, arithmetic and copies ran while one was open for 12% of the time, Pallas kernels for 1%

commit v1 on v0

--- a/solution.py
+++ b/solution.py
@@ -44,6 +44,13 @@
     return lax.ppermute(array, "ctx", ACROSS)
 
 
+def diagonal(array):
+    pairs = []
+    for source, target in ACROSS:
+        pairs += [(source, NX * NZ * NY + target), (NX * NZ * NY + source, target)]
+    return lax.ppermute(array, ("group", "ctx"), pairs)
+
+
 def along(array, step):
     return lax.ppermute(array, "tp", [(t, (t + step) % NT) for t in range(NT)])
 
@@ -80,7 +87,9 @@
 
 GH = 4
 ROWS = GH * TOK
-CHUNK = NY * TOK
+ZONES = 4
+CHUNK = ZONES * NY * TOK
+CHUNKS = NX * NZ // ZONES
 
 
 def attention_kernel(
@@ -93,7 +102,7 @@
     core = place_ref[0]
     rank = place_ref[1]
     long_core = core == 0
-    last = rank >> 2
+    last = rank // (ZONES * NY)
     count = last + 1
 
     def heads_down(ref_a, ref_b, take_a):
@@ -124,14 +133,17 @@
     q_short = heads_down(q_got, q_keep, long_core)
     do_short = heads_down(do_got, do_keep, long_core)
 
+    def block_places(j):
+        places = []
+        for zone in range(ZONES):
+            part = j * ZONES + zone
+            base = (part >> 1) * (NY * NZ) + (part & 1)
+            places += [base + y * NZ for y in range(NY)]
+        return places
+
     def blocks_of(j, take_mine):
-        base = (j >> 1) * (NY * NZ) + (j & 1)
         return jnp.concatenate(
-            [
-                jnp.where(take_mine, ctx_mine[base + y * NZ], ctx_other[base + y * NZ])
-                for y in range(NY)
-            ],
-            0,
+            [jnp.where(take_mine, ctx_mine[at], ctx_other[at]) for at in block_places(j)], 0
         )
 
     key_at = lax.broadcasted_iota(jnp.int32, (CHUNK, ROWS), 0)
@@ -179,24 +191,22 @@
         qacc[...] += product(keys, score_grad, 0, 0)
         key_part = product(score_grad, q_long, 1, 0) * SCALE
         value_part = product(weights.astype(BF16), do_long, 1, 0)
-        base = (j >> 1) * (NY * NZ) + (j & 1)
         keep = jnp.where(long_core, key_part, value_part)
         send = jnp.where(long_core, value_part, key_part)
-        for y in range(NY):
-            kv_keep[base + y * NZ] = keep[y * TOK : (y + 1) * TOK]
-            kv_send[base + y * NZ] = send[y * TOK : (y + 1) * TOK]
+        for i, at in enumerate(block_places(j)):
+            kv_keep[at] = keep[i * TOK : (i + 1) * TOK]
+            kv_send[at] = send[i * TOK : (i + 1) * TOK]
         return carry
 
     lax.fori_loop(0, count, grad_pass, 0)
 
     def clear_pass(j, carry):
-        base = (j >> 1) * (NY * NZ) + (j & 1)
-        for y in range(NY):
-            kv_keep[base + y * NZ] = jnp.zeros((TOK, HD), F32)
-            kv_send[base + y * NZ] = jnp.zeros((TOK, HD), F32)
+        for at in block_places(j):
+            kv_keep[at] = jnp.zeros((TOK, HD), F32)
+            kv_send[at] = jnp.zeros((TOK, HD), F32)
         return carry
 
-    lax.fori_loop(count, NX * NZ, clear_pass, 0)
+    lax.fori_loop(count, CHUNKS, clear_pass, 0)
 
     keys = jnp.where(long_core, short_mine[...], short_other[...])
     values = jnp.where(long_core, short_other[...], short_mine[...])
@@ -231,8 +241,8 @@
         in_specs=[pl.BlockSpec(memory_space=pltpu.SMEM)] + [vmem] * len(arrays),
         out_specs=(vmem,) * 8,
         scratch_shapes=[
-            pltpu.VMEM((NX * NZ, CHUNK, ROWS), F32),
-            pltpu.VMEM((NX * NZ, 1, ROWS), F32),
+            pltpu.VMEM((CHUNKS, CHUNK, ROWS), F32),
+            pltpu.VMEM((CHUNKS, 1, ROWS), F32),
             pltpu.VMEM((HD, ROWS), F32),
             pltpu.VMEM((HD, ROWS), F32),
         ],
@@ -249,6 +259,27 @@
                 target[x * NY + y, :, part * TOK : (part + 1) * TOK] = source[
                     :, column * TOK : (column + 1) * TOK
                 ]
+
+
+def finish_kernel(mine, other, target):
+    step = target.shape[1] // (NZ * NY)
+    for z in range(NZ):
+        for y in range(NY):
+            source = slice((y * NZ + z) * step, (y * NZ + z + 1) * step)
+            summed = mine[:, source] + other[:, source]
+            target[:, (z * NY + y) * step : (z * NY + y + 1) * step] = summed.astype(BF16)
+
+
+def finish_input(terms, other_terms):
+    whole = pl.BlockSpec(other_terms.shape, lambda i: (0, 0))
+    return pl.pallas_call(
+        finish_kernel,
+        grid=(1,),
+        out_shape=jax.ShapeDtypeStruct(other_terms.shape, BF16),
+        in_specs=[whole, whole],
+        out_specs=whole,
+        name="finish",
+    )(terms, other_terms)
 
 
 def pack_columns(activations):
@@ -279,6 +310,8 @@
     cosine, sine = jnp.cos(angles), jnp.sin(angles)
     own_cos = jnp.where(is_long, cosine[:TOK], cosine[TOK:])
     own_sin = jnp.where(is_long, sine[:TOK], sine[TOK:])
+    back_cos = jnp.concatenate([own_cos, jnp.where(is_long, cosine[TOK:], cosine[:TOK])], 0)
+    back_sin = jnp.concatenate([own_sin, jnp.where(is_long, sine[TOK:], sine[:TOK])], 0)
 
     def halves_by_zone(mine, other):
         return jnp.where(upper, jnp.stack([other, mine]), jnp.stack([mine, other]))
@@ -351,33 +384,39 @@
     short_kv = short_keep + partner(short_send)
     blocks, columns = after(kv_sums.reshape(plane, NZ, TOK, HD), columns)
     columns = columns.reshape(plane * TOK, 2 * NZ * TOK)
-    arrived = plane_exchange(blocks).sum(0)
+    other_columns = partner(columns)
+    arrived = plane_exchange(blocks)
+    arrived = arrived.sum(0)
     here = jnp.where(upper, arrived[1], arrived[0])
     there = jnp.where(upper, arrived[0], arrived[1])
-    grads = jnp.concatenate([here + across(there), short_kv], 0)
-    grads = role(turn(grads, cosine, -sine), grads).astype(BF16)
-
-    own_grads = role(grads[:TOK], grads[TOK:])
-    got_grads = partner(role(grads[TOK:], grads[:TOK]))
-    kv_grads = jnp.concatenate([role(own_grads, got_grads), role(got_grads, own_grads)], 1)
+    long_kv = here + across(there)
+    grads = jnp.concatenate([role(long_kv, short_kv), role(short_kv, long_kv)], 0)
+    grads = role(turn(grads, back_cos, -back_sin), grads).astype(BF16)
+    plane_grads = plane_gather(grads)
 
     by_step = [grads] + [along(grads, d) for d in range(1, NT)]
     terms = jnp.zeros((2 * TOK, weight.shape[1]), F32)
     for d in range(NT):
         head = lax.dynamic_index_in_dim(weight, (tp - d) & (NT - 1), 0, False)
         terms += product(by_step[d], head, 1, 1)
-    own_terms = role(terms[:TOK], terms[TOK:])
-    input_sum = own_terms + partner(role(terms[TOK:], terms[:TOK]))
-    input_sum = input_sum.astype(BF16)
-    input_grad = jnp.concatenate(
-        [columns_at(input_sum, y * NZ + z) for z in range(NZ) for y in range(NY)], 1
-    )
-
-    plane_grads = plane_gather(kv_grads).reshape(plane * TOK, 2 * HD)
-    owned = product(columns, plane_grads, 0, 0).reshape(2, NZ, TOK, 2 * HD)
-    owned = role(owned[0], owned[1]) + partner(role(owned[1], owned[0]))
-    owned = jnp.where(upper, owned[1], owned[0]) + across(jnp.where(upper, owned[0], owned[1]))
-    return (attention, query_grad, owned[:, :HD], owned[:, HD:], input_grad)
+    other_terms = partner(terms[TOK:])
+    input_grad = finish_input(terms, other_terms)
+
+    own_grads = plane_grads[:, :TOK].reshape(plane * TOK, HD)
+    got_grads = plane_grads[:, TOK:].reshape(plane * TOK, HD)
+    owned = product(columns, own_grads, 0, 0) + product(other_columns, got_grads, 0, 0)
+    owned = owned.reshape(2 * NZ, TOK, HD)
+    zone = (rank >> 2) & 1
+
+    def piece(group, part):
+        return lax.dynamic_index_in_dim(owned, group * NZ + part, 0, False)
+
+    diagonal_got = diagonal(piece(1 - core, 1 - zone))
+    across_got = across(piece(core, 1 - zone))
+    partner_got = partner(piece(1 - core, zone))
+    same = piece(core, zone) + across_got
+    cross = partner_got + diagonal_got
+    return (attention, query_grad, role(same, cross), role(cross, same), input_grad)
 
 
 def solution(mesh):

time: 246 us -> 243 us (0.988)
  the two profiles are of different devices: /device:TPU:33 before, /device:TPU:8 now
where the time goes in v1:
time: 243 us; the launch traced here: 238 us
  waiting for transfers between devices  104 us (43%)
  starting transfers between devices  76.1 us (31%)
  local copies, waits for them, and re-layouts  17.7 us (7%)
  other arithmetic  14.6 us (6%)
  Pallas kernels  13 us (5%)
  matrix products  11.9 us (5%)
    all_to_all x5, waiting for transfers between devices, plane_exchange(): lax.all_to_all(blocks, 'ctx', split_axis=0, concat_axis=0, tiled=True, ax...  85.7 us
    all_to_all x5, starting transfers between devices, plane_exchange(): lax.all_to_all(blocks, 'ctx', split_axis=0, concat_axis=0, tiled=True, ax...  40.3 us
    ppermute x9, starting transfers between devices, along(): return lax.ppermute(array, 'tp', [(t, (t + step) % NT) for t in range(NT)])  13 us
    unnamed x57, local copies, waits for them, and re-layouts  10.5 us
    ppermute x3, starting transfers between devices, across(): return lax.ppermute(array, 'ctx', ACROSS)  10.5 us
    dot_general x6, matrix products, product(): lax.dot_general(left, right, (((left_dim,), (right_dim,)), ((), ())), pre...  9.28 us
    ppermute x3, waiting for transfers between devices, across(): return lax.ppermute(array, 'ctx', ACROSS)  8 us
    ppermute x1, starting transfers between devices, body(): far = lax.ppermute(weight, ('ctx', 'tp'), FAR_TURN)  7.28 us
  transfers between devices with their start and end apart: 31, of which 15 were waited for; matrix products, arithmetic and copies ran while one was open for 14% of the time, Pallas kernels for 1%

profile of v1, /device:TPU:8, one launch (start us, length us, event | category | flops | bytes accessed | tf_op | source)
XLA Modules:
  0.0 238.1 jit_solution(5294597351332100408)
XLA Ops:
  1.5 7.3 %collective-permute-start.2 = (bf16[256,128]{1,0:T(8,128)(2,1)S(1)}, bf16[256,128]{1,0:T(8,128)(2,1)S(1)}, u32[]{:S(2)}, u32[]{:S(2)}) collective-permute-start(bf16[256,128]{1,0:T(8,128)(2,1)S(1)} %broadcast_select_fusion.10), channel_id=1, source_target_pairs={{0,16},{1,48},{2,80},{3,112},{4,20},{5,52},{6,84},{7,116},{8,24},{... | collective-permute-start | bytes 196616 | tf_op jit(solution)/shard_map/ppermute | solution.py:324
  13.0 14.3 %all-to-all-start = ((bf16[16,2,256,128]{3,2,1,0:T(8,128)(2,1)}), bf16[16,2,256,128]{3,2,1,0:T(8,128)(2,1)S(1)}, u32[]{:S(2)}, u32[]{:S(2)}) async-start(bf16[16,2,256,128]{3,2,1,0:T(8,128)(2,1)} %broadcast_in_dim.16), calls=%async_computation | async-start | bytes 4194304 | tf_op jit(solution)/shard_map/all_to_all | solution.py:63
  34.4 2.1 broadcast_select_fusion.1
  36.5 18.0 %all-to-all-done = bf16[16,2,256,128]{3,2,1,0:T(8,128)(2,1)S(1)} async-done(((bf16[16,2,256,128]{3,2,1,0:T(8,128)(2,1)}), bf16[16,2,256,128]{3,2,1,0:T(8,128)(2,1)S(1)}, u32[]{:S(2)}, u32[]{:S(2)}) %all-to-all-start) | async-done | bytes 2097184 | tf_op jit(solution)/shard_map/all_to_all | solution.py:63
  54.5 2.7 %fusion.1 = f32[4,128,256]{1,2,0:T(8,128)S(1)} fusion(bf16[4,2048,128]{2,1,0:T(8,128)(2,1)S(1)} %bitcast.158, bf16[128,2048]{1,0:T(8,128)(2,1)} %get-tuple-element.42, bf16[128,2048]{1,0:T(8,128)(2,1)} %get-tuple-element.41), kind=kOutput, calls=%fused_computation.6 | convolution fusion | flops 538968064 | bytes 3670016 | tf_op jit(solution)/shard_map/tk,hkn->htn/dot_general | solution.py:349
  58.1 1.8 collective-permute-start.6
  64.9 3.7 %collective-permute-start.8 = (bf16[128,128]{1,0:T(8,128)(2,1)S(1)}, bf16[128,128]{1,0:T(8,128)(2,1)S(1)}, u32[]{:S(2)}, u32[]{:S(2)}) collective-permute-start(bf16[128,128]{1,0:T(8,128)(2,1)S(1)} %fusion.22), channel_id=1, source_target_pairs={{0,16},{4,20},{8,24},{12,28},{16,0},{20,4},{24,8},{28,12},{32,48},... | collective-permute-start | bytes 98312 | tf_op jit(solution)/shard_map/ppermute | solution.py:44
  68.8 4.0 %collective-permute-done.8 = bf16[128,128]{1,0:T(8,128)(2,1)S(1)} collective-permute-done((bf16[128,128]{1,0:T(8,128)(2,1)S(1)}, bf16[128,128]{1,0:T(8,128)(2,1)S(1)}, u32[]{:S(2)}, u32[]{:S(2)}) %collective-permute-start.8) | collective-permute-done | bytes 32800 | tf_op jit(solution)/shard_map/ppermute | solution.py:44
  74.0 5.2 %all-to-all-start.1 = ((bf16[16,2,128,128]{3,2,1,0:T(8,128)(2,1)}), bf16[16,2,128,128]{3,2,1,0:T(8,128)(2,1)S(1)}, u32[]{:S(2)}, u32[]{:S(2)}) async-start(bf16[16,2,128,128]{3,2,1,0:T(8,128)(2,1)} %broadcast_in_dim.19), calls=%async_computation.1 | async-start | bytes 2097152 | tf_op jit(solution)/shard_map/all_to_all | solution.py:63
  79.6 3.3 %pack.1 = bf16[16,128,512]{2,1,0:T(8,128)(2,1)} custom-call(bf16[128,8192]{1,0:T(8,128)(2,1)} %source.1), custom_call_target="tpu_custom_call" | custom-call | tf_op jit(solution)/shard_map/pack/pallas_call | solution.py:287
  83.3 7.5 %all-to-all-done.1 = bf16[16,2,128,128]{3,2,1,0:T(8,128)(2,1)S(1)} async-done(((bf16[16,2,128,128]{3,2,1,0:T(8,128)(2,1)}), bf16[16,2,128,128]{3,2,1,0:T(8,128)(2,1)S(1)}, u32[]{:S(2)}, u32[]{:S(2)}) %all-to-all-start.1) | async-done | bytes 1048608 | tf_op jit(solution)/shard_map/all_to_all | solution.py:63
  90.9 2.7 %collective-permute-start.10 = (f32[128,128]{1,0:T(8,128)S(1)}, f32[128,128]{1,0:T(8,128)S(1)}, u32[]{:S(2)}, u32[]{:S(2)}) collective-permute-start(f32[128,128]{1,0:T(8,128)S(1)} %slice.172), channel_id=1, source_target_pairs={{0,1},{1,2},{2,3},{3,0},{4,5},{5,6},{6,7},{7,4},{8,9},{9,10},{10,1... | collective-permute-start | bytes 196616 | tf_op jit(solution)/shard_map/ppermute | solution.py:55
  97.4 2.7 %collective-permute-done.11 = f32[128,128]{1,0:T(8,128)S(1)} collective-permute-done((f32[128,128]{1,0:T(8,128)S(1)}, f32[128,128]{1,0:T(8,128)S(1)}, u32[]{:S(2)}, u32[]{:S(2)}) %collective-permute-start.11) | collective-permute-done | bytes 65568 | tf_op jit(solution)/shard_map/ppermute | solution.py:55
  102.7 7.2 %attention.1 = (bf16[128,512]{1,0:T(8,128)(2,1)S(1)}, bf16[128,512]{1,0:T(8,128)(2,1)S(1)}, bf16[128,512]{1,0:T(8,128)(2,1)S(1)}, bf16[128,512]{1,0:T(8,128)(2,1...) custom-call(s32[2]{0:T(128)S(1)} %pad_add_fusion.place_ref, ...), custom_call_target="tpu_custom_call" | custom-call | tf_op jit(solution)/shard_map/attention/pallas_call | solution.py:238
  112.7 9.2 %all-to-all-start.2 = ((bf16[16,128,512]{2,1,0:T(8,128)(2,1)}), bf16[16,128,512]{2,1,0:T(8,128)(2,1)}, u32[]{:S(2)}, u32[]{:S(2)}) async-start(bf16[16,128,512]{2,1,0:T(8,128)(2,1)} %pack.1), calls=%async_computation.2 | async-start | bytes 4194304 | tf_op jit(solution)/shard_map/all_to_all | solution.py:63
  121.9 3.2 %add.157 = f32[32,128,128]{2,1,0:T(8,128)} add(f32[32,128,128]{2,1,0:T(8,128)S(1)} %get-tuple-element.32, f32[32,128,128]{2,1,0:T(8,128)} %collective-permute-done.15) | non-fusion elementwise | flops 524288 | bytes 6291456 | tf_op jit(solution)/shard_map/add | solution.py:383
  125.1 26.4 %all-to-all-done.2 = bf16[16,128,512]{2,1,0:T(8,128)(2,1)} async-done(((bf16[16,128,512]{2,1,0:T(8,128)(2,1)}), bf16[16,128,512]{2,1,0:T(8,128)(2,1)}, u32[]{:S(2)}, u32[]{:S(2)}) %all-to-all-start.2) | async-done | bytes 2097184 | tf_op jit(solution)/shard_map/all_to_all | solution.py:63
  151.5 6.3 %all-to-all-start.3 = ((f32[16,2,128,128]{3,2,1,0:T(8,128)}), f32[16,2,128,128]{3,2,1,0:T(8,128)S(1)}, u32[]{:S(2)}, u32[]{:S(2)}) async-start(f32[16,2,128,128]{3,2,1,0:T(8,128)} %bitcast.157), calls=%async_computation.3 | async-start | bytes 4194304 | tf_op jit(solution)/shard_map/all_to_all | solution.py:63
  158.6 27.0 %all-to-all-done.3 = f32[16,2,128,128]{3,2,1,0:T(8,128)S(1)} async-done(((f32[16,2,128,128]{3,2,1,0:T(8,128)}), f32[16,2,128,128]{3,2,1,0:T(8,128)S(1)}, u32[]{:S(2)}, u32[]{:S(2)}) %all-to-all-start.3) | async-done | bytes 2097184 | tf_op jit(solution)/shard_map/all_to_all | solution.py:63
  185.7 4.0 %collective-permute-start.16 = (f32[128,128]{1,0:T(8,128)S(1)}, f32[128,128]{1,0:T(8,128)S(1)}, u32[]{:S(2)}, u32[]{:S(2)}) collective-permute-start(f32[128,128]{1,0:T(8,128)S(1)} %select_bitcast_fusion.1), channel_id=1, source_target_pairs={{0,16},{4,20},{8,24},{12,28},{16,0},{20,4},{24,8},{28,12},{32,48},... | collective-permute-start | bytes 196616 | tf_op jit(solution)/shard_map/ppermute | solution.py:44
  191.4 2.6 %collective-permute-done.16 = f32[128,128]{1,0:T(8,128)S(1)} collective-permute-done((f32[128,128]{1,0:T(8,128)S(1)}, f32[128,128]{1,0:T(8,128)S(1)}, u32[]{:S(2)}, u32[]{:S(2)}) %collective-permute-start.16) | collective-permute-done | bytes 65568 | tf_op jit(solution)/shard_map/ppermute | solution.py:44
  194.9 1.9 collective-permute-start.22
  196.8 1.9 collective-permute-start.24
  198.7 2.1 broadcast_in_dim.23
  200.8 5.4 %all-to-all-start.4 = ((bf16[16,256,128]{2,1,0:T(8,128)(2,1)}), bf16[16,256,128]{2,1,0:T(8,128)(2,1)S(1)}, u32[]{:S(2)}, u32[]{:S(2)}) async-start(bf16[16,256,128]{2,1,0:T(8,128)(2,1)} %broadcast_in_dim.23), calls=%async_computation.4 | async-start | bytes 2097152 | tf_op jit(solution)/shard_map/all_to_all | solution.py:63
  212.8 6.8 %all-to-all-done.4 = bf16[16,256,128]{2,1,0:T(8,128)(2,1)S(1)} async-done(((bf16[16,256,128]{2,1,0:T(8,128)(2,1)}), bf16[16,256,128]{2,1,0:T(8,128)(2,1)S(1)}, u32[]{:S(2)}, u32[]{:S(2)}) %all-to-all-start.4) | async-done | bytes 1048608 | tf_op jit(solution)/shard_map/all_to_all | solution.py:63
  219.7 2.3 convolution_bitcast_fusion
  222.0 2.4 convolution_add_fusion.2
  224.5 2.9 %collective-permute-start.19 = (f32[128,128]{1,0:T(8,128)S(1)}, f32[128,128]{1,0:T(8,128)S(1)}, u32[]{:S(2)}, u32[]{:S(2)}) collective-permute-start(f32[128,128]{1,0:T(8,128)S(1)} %get-tuple-element.65), channel_id=1, source_target_pairs={{0,16},{4,20},{8,24},{12,28},{16,0},{20,4},{24,8},{28,12},{32,48},... | collective-permute-start | bytes 196616 | tf_op jit(solution)/shard_map/ppermute | solution.py:44
  227.3 3.3 %collective-permute-start.21 = (f32[128,128]{1,0:T(8,128)S(1)}, f32[128,128]{1,0:T(8,128)S(1)}, u32[]{:S(2)}, u32[]{:S(2)}) collective-permute-start(f32[128,128]{1,0:T(8,128)S(1)} %get-tuple-element.66), channel_id=1, source_target_pairs={{0,144},{128,16},{4,148},{132,20},{8,152},{136,24},{12,156},{140,2... | collective-permute-start | bytes 196616 | tf_op jit(solution)/shard_map/ppermute | solution.py:51
  232.8 2.2 collective-permute-done.21
  235.7 2.5 %finish.1 = bf16[128,2048]{1,0:T(8,128)(2,1)} custom-call(f32[256,2048]{1,0:T(8,128)} %copy-done.10, f32[128,2048]{1,0:T(8,128)} %collective-permute-done.25.other), custom_call_target="tpu_custom_call" | custom-call | tf_op jit(solution)/shard_map/finish/pallas_call | solution.py:275
  (152 shorter events, 42.4 us)
Async XLA Ops:
  1.5 9.7 %collective-permute-start.2 = (bf16[256,128]{1,0:T(8,128)(2,1)S(1)}, bf16[256,128]{1,0:T(8,128)(2,1)S(1)}, u32[]{:S(2)}, u32[]{:S(2)}) collective-permute-start(bf16[256,128]{1,0:T(8,128)(2,1)S(1)} %broadcast_select_fusion.10), channel_id=1, source_target_pairs={{0,16},{1,48},{2,80},{3,112},{4,20},{5,52},{6,84},{7,116},{8,24},{... | collective-permute-start | bytes 196616 | tf_op jit(solution)/shard_map/ppermute | solution.py:324
  8.8 2.4 %collective-permute-start.3 = (bf16[256,128]{1,0:T(8,128)(2,1)S(1)}, bf16[256,128]{1,0:T(8,128)(2,1)S(1)}, u32[]{:S(2)}, u32[]{:S(2)}) collective-permute-start(bf16[256,128]{1,0:T(8,128)(2,1)S(1)} %broadcast_select_fusion.10), channel_id=1, source_target_pairs={{0,0},{1,32},{2,64},{3,96},{4,4},{5,36},{6,68},{7,100},{8,8},{9,40... | collective-permute-start | bytes 196616 | tf_op jit(solution)/shard_map/ppermute | solution.py:323
  13.0 41.5 %all-to-all-start = ((bf16[16,2,256,128]{3,2,1,0:T(8,128)(2,1)}), bf16[16,2,256,128]{3,2,1,0:T(8,128)(2,1)S(1)}, u32[]{:S(2)}, u32[]{:S(2)}) async-start(bf16[16,2,256,128]{3,2,1,0:T(8,128)(2,1)} %broadcast_in_dim.16), calls=%async_computation | async-start | bytes 4194304 | tf_op jit(solution)/shard_map/all_to_all | solution.py:63
  32.4 2.0 collective-permute-start.4
  57.3 6.2 %collective-permute-start.5 = (f32[128,128]{1,0:T(8,128)S(1)}, f32[128,128]{1,0:T(8,128)S(1)}, u32[]{:S(2)}, u32[]{:S(2)}) collective-permute-start(f32[128,128]{1,0:T(8,128)S(1)} %slice_bitcast_fusion.2), channel_id=1, source_target_pairs={{0,1},{1,2},{2,3},{3,0},{4,5},{5,6},{6,7},{7,4},{8,9},{9,10},{10,1... | collective-permute-start | bytes 196616 | tf_op jit(solution)/shard_map/ppermute | solution.py:55
  58.1 6.6 %collective-permute-start.6 = (f32[128,128]{1,0:T(8,128)S(1)}, f32[128,128]{1,0:T(8,128)S(1)}, u32[]{:S(2)}, u32[]{:S(2)}) collective-permute-start(f32[128,128]{1,0:T(8,128)S(1)} %slice_bitcast_fusion.1), channel_id=1, source_target_pairs={{0,2},{1,3},{2,0},{3,1},{4,6},{5,7},{6,4},{7,5},{8,10},{9,11},{10,... | collective-permute-start | bytes 196616 | tf_op jit(solution)/shard_map/ppermute | solution.py:55
  59.9 4.7 %collective-permute-start.7 = (f32[128,128]{1,0:T(8,128)S(1)}, f32[128,128]{1,0:T(8,128)S(1)}, u32[]{:S(2)}, u32[]{:S(2)}) collective-permute-start(f32[128,128]{1,0:T(8,128)S(1)} %slice_bitcast_fusion), channel_id=1, source_target_pairs={{0,3},{1,0},{2,1},{3,2},{4,7},{5,4},{6,5},{7,6},{8,11},{9,8},{10,9... | collective-permute-start | bytes 196616 | tf_op jit(solution)/shard_map/ppermute | solution.py:55
  64.9 7.9 %collective-permute-start.8 = (bf16[128,128]{1,0:T(8,128)(2,1)S(1)}, bf16[128,128]{1,0:T(8,128)(2,1)S(1)}, u32[]{:S(2)}, u32[]{:S(2)}) collective-permute-start(bf16[128,128]{1,0:T(8,128)(2,1)S(1)} %fusion.22), channel_id=1, source_target_pairs={{0,16},{4,20},{8,24},{12,28},{16,0},{20,4},{24,8},{28,12},{32,48},... | collective-permute-start | bytes 98312 | tf_op jit(solution)/shard_map/ppermute | solution.py:44
  74.0 16.7 %all-to-all-start.1 = ((bf16[16,2,128,128]{3,2,1,0:T(8,128)(2,1)}), bf16[16,2,128,128]{3,2,1,0:T(8,128)(2,1)S(1)}, u32[]{:S(2)}, u32[]{:S(2)}) async-start(bf16[16,2,128,128]{3,2,1,0:T(8,128)(2,1)} %broadcast_in_dim.19), calls=%async_computation.1 | async-start | bytes 2097152 | tf_op jit(solution)/shard_map/all_to_all | solution.py:63
  79.5 21.2 %collective-permute-start = (bf16[128,512]{1,0:T(8,128)(2,1)S(1)}, bf16[128,512]{1,0:T(8,128)(2,1)S(1)}, u32[]{:S(2)}, u32[]{:S(2)}) collective-permute-start(bf16[128,512]{1,0:T(8,128)(2,1)S(1)} %get-tuple-element.72), channel_id=1, source_target_pairs={{0,128},{128,0},{1,129},{129,1},{2,130},{130,2},{3,131},{131,3},{4... | collective-permute-start | bytes 393224 | tf_op jit(solution)/shard_map/ppermute | solution.py:40
  90.8 11.1 %collective-permute-start.9 = (bf16[32,128,128]{2,1,0:T(8,128)(2,1)S(1)}, bf16[32,128,128]{2,1,0:T(8,128)(2,1)S(1)}, u32[]{:S(2)}, u32[]{:S(2)}) collective-permute-start(bf16[32,128,128]{2,1,0:T(8,128)(2,1)S(1)} %bitcast.155), channel_id=1, source_target_pairs={{0,128},{128,0},{1,129},{129,1},{2,130},{130,2},{3,131},{131,3},{4... | collective-permute-start | bytes 3145736 | tf_op jit(solution)/shard_map/ppermute | solution.py:40
  90.9 6.5 %collective-permute-start.10 = (f32[128,128]{1,0:T(8,128)S(1)}, f32[128,128]{1,0:T(8,128)S(1)}, u32[]{:S(2)}, u32[]{:S(2)}) collective-permute-start(f32[128,128]{1,0:T(8,128)S(1)} %slice.172), channel_id=1, source_target_pairs={{0,1},{1,2},{2,3},{3,0},{4,5},{5,6},{6,7},{7,4},{8,9},{9,10},{10,1... | collective-permute-start | bytes 196616 | tf_op jit(solution)/shard_map/ppermute | solution.py:55
  93.6 6.6 %collective-permute-start.11 = (f32[128,128]{1,0:T(8,128)S(1)}, f32[128,128]{1,0:T(8,128)S(1)}, u32[]{:S(2)}, u32[]{:S(2)}) collective-permute-start(f32[128,128]{1,0:T(8,128)S(1)} %slice.173), channel_id=1, source_target_pairs={{0,2},{1,3},{2,0},{3,1},{4,6},{5,7},{6,4},{7,5},{8,10},{9,11},{10,... | collective-permute-start | bytes 196616 | tf_op jit(solution)/shard_map/ppermute | solution.py:55
  94.5 5.7 %collective-permute-start.12 = (f32[128,128]{1,0:T(8,128)S(1)}, f32[128,128]{1,0:T(8,128)S(1)}, u32[]{:S(2)}, u32[]{:S(2)}) collective-permute-start(f32[128,128]{1,0:T(8,128)S(1)} %slice.174), channel_id=1, source_target_pairs={{0,3},{1,0},{2,1},{3,2},{4,7},{5,4},{6,5},{7,6},{8,11},{9,8},{10,9... | collective-permute-start | bytes 196616 | tf_op jit(solution)/shard_map/ppermute | solution.py:55
  97.4 3.9 %collective-permute-start.1 = (bf16[128,512]{1,0:T(8,128)(2,1)S(1)}, bf16[128,512]{1,0:T(8,128)(2,1)S(1)}, u32[]{:S(2)}, u32[]{:S(2)}) collective-permute-start(bf16[128,512]{1,0:T(8,128)(2,1)S(1)} %get-tuple-element.70), channel_id=1, source_target_pairs={{0,128},{128,0},{1,129},{129,1},{2,130},{130,2},{3,131},{131,3},{4... | collective-permute-start | bytes 393224 | tf_op jit(solution)/shard_map/ppermute | solution.py:40
  100.4 1.5 collective-permute-start.13
  112.5 9.3 %collective-permute-start.15 = (f32[32,128,128]{2,1,0:T(8,128)}, f32[32,128,128]{2,1,0:T(8,128)}, u32[]{:S(2)}, u32[]{:S(2)}) collective-permute-start(f32[32,128,128]{2,1,0:T(8,128)} %get-tuple-element.33), channel_id=1, source_target_pairs={{0,128},{128,0},{1,129},{129,1},{2,130},{130,2},{3,131},{131,3},{4... | collective-permute-start | bytes 6291464 | tf_op jit(solution)/shard_map/ppermute | solution.py:40
  112.7 38.8 %all-to-all-start.2 = ((bf16[16,128,512]{2,1,0:T(8,128)(2,1)}), bf16[16,128,512]{2,1,0:T(8,128)(2,1)}, u32[]{:S(2)}, u32[]{:S(2)}) async-start(bf16[16,128,512]{2,1,0:T(8,128)(2,1)} %pack.1), calls=%async_computation.2 | async-start | bytes 4194304 | tf_op jit(solution)/shard_map/all_to_all | solution.py:63
  151.5 34.0 %all-to-all-start.3 = ((f32[16,2,128,128]{3,2,1,0:T(8,128)}), f32[16,2,128,128]{3,2,1,0:T(8,128)S(1)}, u32[]{:S(2)}, u32[]{:S(2)}) async-start(f32[16,2,128,128]{3,2,1,0:T(8,128)} %bitcast.157), calls=%async_computation.3 | async-start | bytes 4194304 | tf_op jit(solution)/shard_map/all_to_all | solution.py:63
  157.9 31.7 %collective-permute-start.14 = (bf16[128,1024]{1,0:T(8,128)(2,1)S(1)}, bf16[128,1024]{1,0:T(8,128)(2,1)}, u32[]{:S(2)}, u32[]{:S(2)}) collective-permute-start(bf16[128,1024]{1,0:T(8,128)(2,1)S(1)} %pad_maximum_fusion.1), channel_id=1, source_target_pairs={{0,128},{128,0},{1,129},{129,1},{2,130},{130,2},{3,131},{131,3},{4... | collective-permute-start | bytes 786440 | tf_op jit(solution)/shard_map/ppermute | solution.py:40
  158.0 36.0 %copy-start.14 = (f32[128,64]{1,0:T(8,128)S(1)}, f32[128,64]{1,0:T(8,128)}, u32[]{:S(2)}) copy-start(f32[128,64]{1,0:T(8,128)} %copy-done.13) | copy-start | bytes 98308
  158.1 33.3 %collective-permute-start.17 = (f32[128,128]{1,0:T(8,128)S(1)}, f32[128,128]{1,0:T(8,128)S(1)}, u32[]{:S(2)}, u32[]{:S(2)}) collective-permute-start(f32[128,128]{1,0:T(8,128)S(1)} %get-tuple-element.38), channel_id=1, source_target_pairs={{0,128},{128,0},{1,129},{129,1},{2,130},{130,2},{3,131},{131,3},{4... | collective-permute-start | bytes 196616 | tf_op jit(solution)/shard_map/ppermute | solution.py:40
  185.7 8.3 %collective-permute-start.16 = (f32[128,128]{1,0:T(8,128)S(1)}, f32[128,128]{1,0:T(8,128)S(1)}, u32[]{:S(2)}, u32[]{:S(2)}) collective-permute-start(f32[128,128]{1,0:T(8,128)S(1)} %select_bitcast_fusion.1), channel_id=1, source_target_pairs={{0,16},{4,20},{8,24},{12,28},{16,0},{20,4},{24,8},{28,12},{32,48},... | collective-permute-start | bytes 196616 | tf_op jit(solution)/shard_map/ppermute | solution.py:44
  191.4 30.7 %collective-permute-start.18 = (bf16[2048,512]{1,0:T(8,128)(2,1)}, bf16[2048,512]{1,0:T(8,128)(2,1)}, u32[]{:S(2)}, u32[]{:S(2)}) collective-permute-start(bf16[2048,512]{1,0:T(8,128)(2,1)} %bitcast.41), channel_id=1, source_target_pairs={{0,128},{128,0},{1,129},{129,1},{2,130},{130,2},{3,131},{131,3},{4... | collective-permute-start | bytes 6291464 | tf_op jit(solution)/shard_map/ppermute | solution.py:40
  194.9 11.8 %collective-permute-start.22 = (bf16[256,128]{1,0:T(8,128)(2,1)}, bf16[256,128]{1,0:T(8,128)(2,1)}, u32[]{:S(2)}, u32[]{:S(2)}) collective-permute-start(bf16[256,128]{1,0:T(8,128)(2,1)} %fusion.16), channel_id=1, source_target_pairs={{0,1},{1,2},{2,3},{3,0},{4,5},{5,6},{6,7},{7,4},{8,9},{9,10},{10,1... | collective-permute-start | bytes 196616 | tf_op jit(solution)/shard_map/ppermute | solution.py:55
  196.8 11.2 %collective-permute-start.24 = (bf16[256,128]{1,0:T(8,128)(2,1)}, bf16[256,128]{1,0:T(8,128)(2,1)}, u32[]{:S(2)}, u32[]{:S(2)}) collective-permute-start(bf16[256,128]{1,0:T(8,128)(2,1)} %fusion.16), channel_id=1, source_target_pairs={{0,3},{1,0},{2,1},{3,2},{4,7},{5,4},{6,5},{7,6},{8,11},{9,8},{10,9... | collective-permute-start | bytes 196616 | tf_op jit(solution)/shard_map/ppermute | solution.py:55
  198.7 10.6 %collective-permute-start.23 = (bf16[256,128]{1,0:T(8,128)(2,1)}, bf16[256,128]{1,0:T(8,128)(2,1)}, u32[]{:S(2)}, u32[]{:S(2)}) collective-permute-start(bf16[256,128]{1,0:T(8,128)(2,1)} %fusion.16), channel_id=1, source_target_pairs={{0,2},{1,3},{2,0},{3,1},{4,6},{5,7},{6,4},{7,5},{8,10},{9,11},{10,... | collective-permute-start | bytes 196616 | tf_op jit(solution)/shard_map/ppermute | solution.py:55
  200.8 18.8 %all-to-all-start.4 = ((bf16[16,256,128]{2,1,0:T(8,128)(2,1)}), bf16[16,256,128]{2,1,0:T(8,128)(2,1)S(1)}, u32[]{:S(2)}, u32[]{:S(2)}) async-start(bf16[16,256,128]{2,1,0:T(8,128)(2,1)} %broadcast_in_dim.23), calls=%async_computation.4 | async-start | bytes 2097152 | tf_op jit(solution)/shard_map/all_to_all | solution.py:63
  211.9 23.8 %collective-permute-start.25 = (f32[128,2048]{1,0:T(8,128)}, f32[128,2048]{1,0:T(8,128)}, u32[]{:S(2)}, u32[]{:S(2)}) collective-permute-start(f32[128,2048]{1,0:T(8,128)} %slice.210), channel_id=1, source_target_pairs={{0,128},{128,0},{1,129},{129,1},{2,130},{130,2},{3,131},{131,3},{4... | collective-permute-start | bytes 3145736 | tf_op jit(solution)/shard_map/ppermute | solution.py:40
  224.5 8.3 %collective-permute-start.19 = (f32[128,128]{1,0:T(8,128)S(1)}, f32[128,128]{1,0:T(8,128)S(1)}, u32[]{:S(2)}, u32[]{:S(2)}) collective-permute-start(f32[128,128]{1,0:T(8,128)S(1)} %get-tuple-element.65), channel_id=1, source_target_pairs={{0,16},{4,20},{8,24},{12,28},{16,0},{20,4},{24,8},{28,12},{32,48},... | collective-permute-start | bytes 196616 | tf_op jit(solution)/shard_map/ppermute | solution.py:44
  227.3 5.5 %collective-permute-start.20 = (f32[128,128]{1,0:T(8,128)S(1)}, f32[128,128]{1,0:T(8,128)S(1)}, u32[]{:S(2)}, u32[]{:S(2)}) collective-permute-start(f32[128,128]{1,0:T(8,128)S(1)} %get-tuple-element.67), channel_id=1, source_target_pairs={{0,128},{128,0},{1,129},{129,1},{2,130},{130,2},{3,131},{131,3},{4... | collective-permute-start | bytes 196616 | tf_op jit(solution)/shard_map/ppermute | solution.py:40
  227.3 7.7 %collective-permute-start.21 = (f32[128,128]{1,0:T(8,128)S(1)}, f32[128,128]{1,0:T(8,128)S(1)}, u32[]{:S(2)}, u32[]{:S(2)}) collective-permute-start(f32[128,128]{1,0:T(8,128)S(1)} %get-tuple-element.66), channel_id=1, source_target_pairs={{0,144},{128,16},{4,148},{132,20},{8,152},{136,24},{12,156},{140,2... | collective-permute-start | bytes 196616 | tf_op jit(solution)/shard_map/ppermute | solution.py:51
  (23 other events, 264.5 us)

commit v2 on v1

--- a/solution.py
+++ b/solution.py
@@ -251,14 +251,84 @@
     )(place, *arrays)
 
 
-def pack_kernel(source, target):
-    for x in range(NX):
-        for y in range(NY):
-            for part in range(2 * NZ):
-                column = (part // NZ) * (NX * NZ * NY) + ctx_of(x, part % NZ, y)
-                target[x * NY + y, :, part * TOK : (part + 1) * TOK] = source[
-                    :, column * TOK : (column + 1) * TOK
-                ]
+def join_kernel(place_ref, *refs):
+    first = place_ref[0] == 0
+    width = GH * HD
+    for mine, got, target in ((refs[0], refs[1], refs[4]), (refs[2], refs[3], refs[5])):
+        target[:, :width] = jnp.where(first, mine[...], got[...])
+        target[:, width:] = jnp.where(first, got[...], mine[...])
+
+
+def join_heads(place, *halves):
+    vmem = pl.BlockSpec(memory_space=pltpu.VMEM)
+    whole = jax.ShapeDtypeStruct((TOK, 2 * GH * HD), BF16)
+    return pl.pallas_call(
+        join_kernel,
+        out_shape=(whole, whole),
+        in_specs=[pl.BlockSpec(memory_space=pltpu.SMEM)] + [vmem] * len(halves),
+        out_specs=(vmem, vmem),
+        name="join",
+    )(place, *halves)
+
+
+def pack_kernel(source, *targets):
+    for group, target in enumerate(targets):
+        for x in range(NX):
+            for y in range(NY):
+                for z in range(NZ):
+                    column = group * (NX * NZ * NY) + ctx_of(x, z, y)
+                    target[x * NY + y, :, z * TOK : (z + 1) * TOK] = source[
+                        :, column * TOK : (column + 1) * TOK
+                    ]
+
+
+def owned_kernel(
+    place_ref, mine_first, mine_second, other_first, other_second, grads_ref,
+    here, above, beside, opposite,
+    sums, pieces,
+):
+    step = pl.program_id(0)
+
+    @pl.when(step == 0)
+    def _():
+        sums[...] = jnp.zeros_like(sums)
+
+    own = jnp.concatenate([grads_ref[i, :TOK] for i in range(NY)], 0)
+    got = jnp.concatenate([grads_ref[i, TOK:] for i in range(NY)], 0)
+    for group, (mine, other) in enumerate(
+        ((mine_first, other_first), (mine_second, other_second))
+    ):
+        sums[group] += product(own, mine[...], 0, 0) + product(got, other[...], 0, 0)
+
+    @pl.when(step == pl.num_programs(0) - 1)
+    def _():
+        for group in range(2):
+            for z in range(NZ):
+                pieces[group * NZ + z] = jnp.transpose(sums[group, :, z * TOK : (z + 1) * TOK])
+        core = place_ref[0]
+        zone = (place_ref[1] >> 2) & 1
+        here[...] = pieces[core * NZ + zone]
+        above[...] = pieces[core * NZ + 1 - zone]
+        beside[...] = pieces[(1 - core) * NZ + zone]
+        opposite[...] = pieces[(1 - core) * NZ + 1 - zone]
+
+
+def owned_pieces(place, *arrays):
+    columns = pl.BlockSpec((NY * TOK, NZ * TOK), lambda i: (i, 0))
+    grads = pl.BlockSpec((NY, 2 * TOK, HD), lambda i: (i, 0, 0))
+    piece = jax.ShapeDtypeStruct((TOK, HD), F32)
+    return pl.pallas_call(
+        owned_kernel,
+        grid=(NX,),
+        out_shape=(piece,) * 4,
+        in_specs=[pl.BlockSpec(memory_space=pltpu.SMEM)] + [columns] * 4 + [grads],
+        out_specs=(pl.BlockSpec((TOK, HD), lambda i: (0, 0)),) * 4,
+        scratch_shapes=[
+            pltpu.VMEM((2, HD, NZ * TOK), F32),
+            pltpu.VMEM((2 * NZ, TOK, HD), F32),
+        ],
+        name="owned",
+    )(place, *arrays)
 
 
 def finish_kernel(mine, other, target):
@@ -284,11 +354,12 @@
 
 def pack_columns(activations):
     vmem = pl.BlockSpec(memory_space=pltpu.VMEM)
+    packed = jax.ShapeDtypeStruct((NX * NY, TOK, NZ * TOK), activations.dtype)
     return pl.pallas_call(
         pack_kernel,
-        out_shape=jax.ShapeDtypeStruct((NX * NY, TOK, 2 * NZ * TOK), activations.dtype),
+        out_shape=(packed, packed),
         in_specs=[vmem],
-        out_specs=vmem,
+        out_specs=(vmem, vmem),
         name="pack",
     )(activations)
 
@@ -322,7 +393,9 @@
     weight = role(key_weight, value_weight)
     near = lax.ppermute(weight, ("ctx", "tp"), TURN)
     far = lax.ppermute(weight, ("ctx", "tp"), FAR_TURN)
-    weight = plane_gather(halves_by_zone(near, far))
+    weight = halves_by_zone(near, far)
+    weight = plane_gather(weight)
+    packed = pack_columns(activations)
     weight = weight.reshape(NX, NY * NZ * weight.shape[-2], HD)
 
     own_slice = lax.dynamic_slice_in_dim(activations, tp * slice_cols, slice_cols, 1)
@@ -348,18 +421,21 @@
 
     partial = jnp.einsum("tk,hkn->htn", both_slices, weight, preferred_element_type=F32)
     parts = [lax.dynamic_index_in_dim(partial, (tp + d) & (NT - 1), 0, False) for d in range(NT)]
-    long_sum = parts[0][:TOK] + sum(along(parts[d][:TOK], d) for d in range(1, NT))
+    arrivals = [along(parts[d][:TOK], d) for d in range(1, NT)]
+    first_columns = plane_exchange(packed[0])
+    long_sum = parts[0][:TOK] + sum(arrivals)
     long_rows = role(turn(long_sum, cosine[:TOK], sine[:TOK]), long_sum).astype(BF16)
     parts, long_rows = after(parts, long_rows)
     arrivals = [along(parts[d][TOK:], d) for d in range(1, NT)]
     short_sum = parts[0][TOK:] + sum(arrivals)
     short_rows = role(turn(short_sum, cosine[TOK:], sine[TOK:]), short_sum).astype(BF16)
     other_short = partner(short_rows)
-    context = halves_by_zone(long_rows, across(long_rows))
+    across_rows = across(long_rows)
+    context = halves_by_zone(long_rows, across_rows)
     context = plane_gather(context)
 
-    packed, context = after(pack_columns(activations), context)
-    columns = plane_exchange(packed)
+    second, context = after(packed[1], context)
+    second_columns = plane_exchange(second)
     context = context.reshape(plane * NZ, TOK, HD)
     other_context = partner(context)
 
@@ -375,16 +451,16 @@
         place, q_keep, q_got, do_keep, do_got, context, other_context, short_rows,
         other_short, allowed, tables,
     )
-    got = partner(jnp.concatenate([out_other, qgrad_other], 1))
-    out_got, qgrad_got = got[:, :width], got[:, width:]
-    attention = jnp.concatenate([role(out_mine, out_got), role(out_got, out_mine)], 1)
-    query_grad = jnp.concatenate([role(qgrad_mine, qgrad_got), role(qgrad_got, qgrad_mine)], 1)
+    out_got, qgrad_got = partner(out_other), partner(qgrad_other)
+    attention, query_grad = join_heads(place, out_mine, out_got, qgrad_mine, qgrad_got)
 
     kv_sums = kv_keep + partner(kv_send)
     short_kv = short_keep + partner(short_send)
-    blocks, columns = after(kv_sums.reshape(plane, NZ, TOK, HD), columns)
-    columns = columns.reshape(plane * TOK, 2 * NZ * TOK)
-    other_columns = partner(columns)
+    blocks, second_columns = after(kv_sums.reshape(plane, NZ, TOK, HD), second_columns)
+    columns = [
+        array.reshape(plane * TOK, NZ * TOK) for array in (first_columns, second_columns)
+    ]
+    other_columns = [partner(array) for array in columns]
     arrived = plane_exchange(blocks)
     arrived = arrived.sum(0)
     here = jnp.where(upper, arrived[1], arrived[0])
@@ -402,19 +478,13 @@
     other_terms = partner(terms[TOK:])
     input_grad = finish_input(terms, other_terms)
 
-    own_grads = plane_grads[:, :TOK].reshape(plane * TOK, HD)
-    got_grads = plane_grads[:, TOK:].reshape(plane * TOK, HD)
-    owned = product(columns, own_grads, 0, 0) + product(other_columns, got_grads, 0, 0)
-    owned = owned.reshape(2 * NZ, TOK, HD)
-    zone = (rank >> 2) & 1
-
-    def piece(group, part):
-        return lax.dynamic_index_in_dim(owned, group * NZ + part, 0, False)
-
-    diagonal_got = diagonal(piece(1 - core, 1 - zone))
-    across_got = across(piece(core, 1 - zone))
-    partner_got = partner(piece(1 - core, zone))
-    same = piece(core, zone) + across_got
+    here, above, beside, opposite = owned_pieces(
+        place, columns[0], columns[1], other_columns[0], other_columns[1], plane_grads
+    )
+    diagonal_got = diagonal(opposite)
+    across_got = across(above)
+    partner_got = partner(beside)
+    same = here + across_got
     cross = partner_got + diagonal_got
     return (attention, query_grad, role(same, cross), role(cross, same), input_grad)
 

time: 243 us -> 243 us (level)
  blocking collectives: 0 us -> 31 us
  waiting for transfers between devices: 104 us -> 75.4 us
  Pallas kernels: 13 us -> 19.4 us
  matrix products: 11.9 us -> 7.18 us
  other arithmetic: 14.6 us -> 11.6 us
    all_to_all x0 -> x1, blocking collectives: none -> 31 us  [plane_exchange(): lax.all_to_all(blocks, 'ctx', split_axis=0, concat_axis=0, tiled=True, ax...]
    all_to_all x5, waiting for transfers between devices: 85.7 us -> 59 us  [plane_exchange(): lax.all_to_all(blocks, 'ctx', split_axis=0, concat_axis=0, tiled=True, ax...]
    pallas_call x1 -> x3, Pallas kernels: 3.3 us -> 9.79 us  [the longest x1 4.57 us: owned_pieces(): pl.pallas_call(owned_kernel, grid=(NX,), out_shape=(piece,) * 4, in_specs...]
    dot_general x6 -> x4, matrix products: 9.28 us -> 4.52 us  [product(): lax.dot_general(left, right, (((left_dim,), (right_dim,)), ((), ())), pre...]
    ppermute x3, waiting for transfers between devices: 8 us -> 5.11 us  [across(): return lax.ppermute(array, 'ctx', ACROSS)]
    unnamed x57 -> x53, local copies, waits for them, and re-layouts: 10.5 us -> 11.8 us
    select_n x8 -> x7, other arithmetic: 5.42 us -> 4.54 us  [role(): return jnp.where(is_long, first, second)]
  transfers between devices with their start and end apart: 31 -> 33, of which waited for: 15 -> 14; matrix products, arithmetic and copies ran while one was open for 14% -> 10% of each run, Pallas kernels for 1% -> 4%
where the time goes in v2:
time: 243 us; the launch traced here: 240 us
  starting transfers between devices  75.7 us (31%)
  waiting for transfers between devices  75.4 us (31%)
  blocking collectives  31 us (13%)
  Pallas kernels  19.4 us (8%)
  local copies, waits for them, and re-layouts  18.1 us (7%)
  other arithmetic  11.6 us (5%)
  matrix products  7.18 us (3%)
    all_to_all x5, waiting for transfers between devices, plane_exchange(): lax.all_to_all(blocks, 'ctx', split_axis=0, concat_axis=0, tiled=True, ax...  59 us
    all_to_all x5, starting transfers between devices, plane_exchange(): lax.all_to_all(blocks, 'ctx', split_axis=0, concat_axis=0, tiled=True, ax...  39.1 us
    all_to_all x1, blocking collectives, plane_exchange(): lax.all_to_all(blocks, 'ctx', split_axis=0, concat_axis=0, tiled=True, ax...  31 us
    ppermute x9, starting transfers between devices, along(): return lax.ppermute(array, 'tp', [(t, (t + step) % NT) for t in range(NT)])  13.3 us
    unnamed x53, local copies, waits for them, and re-layouts  11.8 us
    ppermute x3, starting transfers between devices, across(): return lax.ppermute(array, 'ctx', ACROSS)  11.6 us
    ppermute x1, starting transfers between devices, body(): far = lax.ppermute(weight, ('ctx', 'tp'), FAR_TURN)  7.28 us
    pallas_call x1, Pallas kernels, attention_call(): pl.pallas_call(attention_kernel, out_shape=(rows, rows, rows, rows, block...  7.13 us
  transfers between devices with their start and end apart: 33, of which 14 were waited for; matrix products, arithmetic and copies ran while one was open for 10% of the time, Pallas kernels for 4%

profile of v2, /device:TPU:8, one launch (start us, length us, event | category | flops | bytes accessed | tf_op | source)
XLA Modules:
  0.0 239.5 jit_solution(16387448190520519743)
XLA Ops:
  1.5 7.3 %collective-permute-start.2 = (bf16[256,128]{1,0:T(8,128)(2,1)S(1)}, bf16[256,128]{1,0:T(8,128)(2,1)S(1)}, u32[]{:S(2)}, u32[]{:S(2)}) collective-permute-start(bf16[256,128]{1,0:T(8,128)(2,1)S(1)} %broadcast_select_fusion.6), channel_id=1, source_target_pairs={{0,16},{1,48},{2,80},{3,112},{4,20},{5,52},{6,84},{7,116},{8,24},{... | collective-permute-start | bytes 196616 | tf_op jit(solution)/shard_map/ppermute | solution.py:395
  11.2 1.8 broadcast_in_dim.16
  13.0 14.3 %all-to-all-start = ((bf16[16,2,256,128]{3,2,1,0:T(8,128)(2,1)}), bf16[16,2,256,128]{3,2,1,0:T(8,128)(2,1)S(1)}, u32[]{:S(2)}, u32[]{:S(2)}) async-start(bf16[16,2,256,128]{3,2,1,0:T(8,128)(2,1)} %broadcast_in_dim.16), calls=%async_computation | async-start | bytes 4194304 | tf_op jit(solution)/shard_map/all_to_all | solution.py:63
  34.4 2.1 broadcast_select_fusion.1
  36.5 18.0 %all-to-all-done = bf16[16,2,256,128]{3,2,1,0:T(8,128)(2,1)S(1)} async-done(((bf16[16,2,256,128]{3,2,1,0:T(8,128)(2,1)}), bf16[16,2,256,128]{3,2,1,0:T(8,128)(2,1)S(1)}, u32[]{:S(2)}, u32[]{:S(2)}) %all-to-all-start) | async-done | bytes 2097184 | tf_op jit(solution)/shard_map/all_to_all | solution.py:63
  54.5 2.7 %fusion.1 = f32[4,128,256]{1,2,0:T(8,128)S(1)} fusion(bf16[4,2048,128]{2,1,0:T(8,128)(2,1)S(1)} %bitcast.140, bf16[128,2048]{1,0:T(8,128)(2,1)} %get-tuple-element.58, bf16[128,2048]{1,0:T(8,128)(2,1)} %get-tuple-element.57), kind=kOutput, calls=%fused_computation.4 | convolution fusion | flops 538968064 | bytes 3670016 | tf_op jit(solution)/shard_map/tk,hkn->htn/dot_general | solution.py:422
  58.1 1.8 collective-permute-start.6
  64.9 3.7 %collective-permute-start.8 = (bf16[128,128]{1,0:T(8,128)(2,1)S(1)}, bf16[128,128]{1,0:T(8,128)(2,1)S(1)}, u32[]{:S(2)}, u32[]{:S(2)}) collective-permute-start(bf16[128,128]{1,0:T(8,128)(2,1)S(1)} %fusion.21), channel_id=1, source_target_pairs={{0,16},{4,20},{8,24},{12,28},{16,0},{20,4},{24,8},{28,12},{32,48},... | collective-permute-start | bytes 98312 | tf_op jit(solution)/shard_map/ppermute | solution.py:44
  68.8 4.0 %collective-permute-done.8 = bf16[128,128]{1,0:T(8,128)(2,1)S(1)} collective-permute-done((bf16[128,128]{1,0:T(8,128)(2,1)S(1)}, bf16[128,128]{1,0:T(8,128)(2,1)S(1)}, u32[]{:S(2)}, u32[]{:S(2)}) %collective-permute-start.8) | collective-permute-done | bytes 32800 | tf_op jit(solution)/shard_map/ppermute | solution.py:44
  74.0 5.2 %all-to-all-start.1 = ((bf16[16,2,128,128]{3,2,1,0:T(8,128)(2,1)}), bf16[16,2,128,128]{3,2,1,0:T(8,128)(2,1)S(1)}, u32[]{:S(2)}, u32[]{:S(2)}) async-start(bf16[16,2,128,128]{3,2,1,0:T(8,128)(2,1)} %broadcast_in_dim.19), calls=%async_computation.1 | async-start | bytes 2097152 | tf_op jit(solution)/shard_map/all_to_all | solution.py:63
  79.6 3.3 %pack.1 = (bf16[16,128,256]{2,1,0:T(8,128)(2,1)}, bf16[16,128,256]{2,1,0:T(8,128)(2,1)}) custom-call(bf16[128,8192]{1,0:T(8,128)(2,1)} %source.1), custom_call_target="tpu_custom_call" | custom-call | tf_op jit(solution)/shard_map/pack/pallas_call | solution.py:358
  83.3 7.5 %all-to-all-done.1 = bf16[16,2,128,128]{3,2,1,0:T(8,128)(2,1)S(1)} async-done(((bf16[16,2,128,128]{3,2,1,0:T(8,128)(2,1)}), bf16[16,2,128,128]{3,2,1,0:T(8,128)(2,1)S(1)}, u32[]{:S(2)}, u32[]{:S(2)}) %all-to-all-start.1) | async-done | bytes 1048608 | tf_op jit(solution)/shard_map/all_to_all | solution.py:63
  90.9 2.7 %collective-permute-start.10 = (f32[128,128]{1,0:T(8,128)S(1)}, f32[128,128]{1,0:T(8,128)S(1)}, u32[]{:S(2)}, u32[]{:S(2)}) collective-permute-start(f32[128,128]{1,0:T(8,128)S(1)} %slice.160), channel_id=1, source_target_pairs={{0,1},{1,2},{2,3},{3,0},{4,5},{5,6},{6,7},{7,4},{8,9},{9,10},{10,1... | collective-permute-start | bytes 196616 | tf_op jit(solution)/shard_map/ppermute | solution.py:55
  97.4 2.7 %collective-permute-done.11 = f32[128,128]{1,0:T(8,128)S(1)} collective-permute-done((f32[128,128]{1,0:T(8,128)S(1)}, f32[128,128]{1,0:T(8,128)S(1)}, u32[]{:S(2)}, u32[]{:S(2)}) %collective-permute-start.11) | collective-permute-done | bytes 65568 | tf_op jit(solution)/shard_map/ppermute | solution.py:55
  102.7 7.1 %attention.1 = (bf16[128,512]{1,0:T(8,128)(2,1)S(1)}, bf16[128,512]{1,0:T(8,128)(2,1)S(1)}, bf16[128,512]{1,0:T(8,128)(2,1)S(1)}, bf16[128,512]{1,0:T(8,128)(2,1...) custom-call(s32[2]{0:T(128)S(1)} %pad_add_fusion.place_ref, ...), custom_call_target="tpu_custom_call" | custom-call | tf_op jit(solution)/shard_map/attention/pallas_call | solution.py:238
  113.2 9.2 %all-to-all-start.3 = ((bf16[16,128,256]{2,1,0:T(8,128)(2,1)}), bf16[16,128,256]{2,1,0:T(8,128)(2,1)}, u32[]{:S(2)}, u32[]{:S(2)}) async-start(bf16[16,128,256]{2,1,0:T(8,128)(2,1)} %get-tuple-element.46), calls=%async_computation.3 | async-start | bytes 2097152 | tf_op jit(solution)/shard_map/all_to_all | solution.py:63
  122.4 3.2 %add.129 = f32[32,128,128]{2,1,0:T(8,128)} add(f32[32,128,128]{2,1,0:T(8,128)S(1)} %get-tuple-element.44, f32[32,128,128]{2,1,0:T(8,128)} %collective-permute-done.16) | non-fusion elementwise | flops 524288 | bytes 6291456 | tf_op jit(solution)/shard_map/add | solution.py:457
  125.6 13.9 %all-to-all-done.3 = bf16[16,128,256]{2,1,0:T(8,128)(2,1)} async-done(((bf16[16,128,256]{2,1,0:T(8,128)(2,1)}), bf16[16,128,256]{2,1,0:T(8,128)(2,1)}, u32[]{:S(2)}, u32[]{:S(2)}) %all-to-all-start.3) | async-done | bytes 1048608 | tf_op jit(solution)/shard_map/all_to_all | solution.py:63
  139.4 31.0 %all_to_all.30 = f32[16,2,128,128]{3,2,1,0:T(8,128)S(1)} all-to-all(f32[16,2,128,128]{3,2,1,0:T(8,128)} %bitcast.139), channel_id=1, replica_groups={{0,4,8,12,32,36,40,44,64,68,72,76,96,100,104,108},{16,20,24,28,48,52,56..., dimensions={0} | all-to-all | bytes 4194304 | tf_op jit(solution)/shard_map/all_to_all | solution.py:63
  170.4 5.5 %all-to-all-start.2 = ((bf16[16,128,256]{2,1,0:T(8,128)(2,1)}), bf16[16,128,256]{2,1,0:T(8,128)(2,1)}, u32[]{:S(2)}, u32[]{:S(2)}) async-start(bf16[16,128,256]{2,1,0:T(8,128)(2,1)} %get-tuple-element.43), calls=%async_computation.2 | async-start | bytes 2097152 | tf_op jit(solution)/shard_map/all_to_all | solution.py:63
  176.2 4.0 %collective-permute-start.19 = (f32[128,128]{1,0:T(8,128)S(1)}, f32[128,128]{1,0:T(8,128)S(1)}, u32[]{:S(2)}, u32[]{:S(2)}) collective-permute-start(f32[128,128]{1,0:T(8,128)S(1)} %select_bitcast_fusion.1), channel_id=1, source_target_pairs={{0,16},{4,20},{8,24},{12,28},{16,0},{20,4},{24,8},{28,12},{32,48},... | collective-permute-start | bytes 196616 | tf_op jit(solution)/shard_map/ppermute | solution.py:44
  180.2 9.7 %all-to-all-done.2 = bf16[16,128,256]{2,1,0:T(8,128)(2,1)} async-done(((bf16[16,128,256]{2,1,0:T(8,128)(2,1)}), bf16[16,128,256]{2,1,0:T(8,128)(2,1)}, u32[]{:S(2)}, u32[]{:S(2)}) %all-to-all-start.2) | async-done | bytes 1048608 | tf_op jit(solution)/shard_map/all_to_all | solution.py:63
  190.7 2.2 collective-permute-start.24
  192.9 1.9 collective-permute-start.26
  196.0 4.9 %all-to-all-start.5 = ((bf16[16,256,128]{2,1,0:T(8,128)(2,1)}), bf16[16,256,128]{2,1,0:T(8,128)(2,1)S(1)}, u32[]{:S(2)}, u32[]{:S(2)}) async-start(bf16[16,256,128]{2,1,0:T(8,128)(2,1)} %broadcast_in_dim.23), calls=%async_computation.5 | async-start | bytes 2097152 | tf_op jit(solution)/shard_map/all_to_all | solution.py:63
  207.3 9.9 %all-to-all-done.5.grads_ref = bf16[16,256,128]{2,1,0:T(8,128)(2,1)S(1)} async-done(((bf16[16,256,128]{2,1,0:T(8,128)(2,1)}), bf16[16,256,128]{2,1,0:T(8,128)(2,1)S(1)}, u32[]{:S(2)}, u32[]{:S(2)}) %all-to-all-start.5) | async-done | bytes 1048608 | tf_op jit(solution)/shard_map/all_to_all | solution.py:63
  218.2 4.6 %owned.1 = (f32[128,128]{1,0:T(8,128)}, f32[128,128]{1,0:T(8,128)}, f32[128,128]{1,0:T(8,128)}, f32[128,128]{1,0:T(8,128)}) custom-call(s32[2]{0:T(128)} %copy-done.4, bf16[2048,256]{1,0:T(8,128)(2,1)} %bitcast.32.mine_first, bf16[2048,256]{1,0:T(8,128)(2,1)} %bitcast.34.mine_second, bf16[2048,256]{1,0:T(8,128)(2,1)} %collective-permute-done.17.other_first, ...), custom_call_target="tpu_custom_call" | custom-call | tf_op jit(solution)/shard_map/owned/pallas_call | solution.py:320
  222.7 4.0 %collective-permute-start.21 = (f32[128,128]{1,0:T(8,128)}, f32[128,128]{1,0:T(8,128)S(1)}, u32[]{:S(2)}, u32[]{:S(2)}) collective-permute-start(f32[128,128]{1,0:T(8,128)} %get-tuple-element.52), channel_id=1, source_target_pairs={{0,16},{4,20},{8,24},{12,28},{16,0},{20,4},{24,8},{28,12},{32,48},... | collective-permute-start | bytes 196616 | tf_op jit(solution)/shard_map/ppermute | solution.py:44
  226.7 2.2 collective-permute-start.23
  228.9 1.9 join.1
  231.9 3.6 %collective-permute-done.23 = f32[128,128]{1,0:T(8,128)S(1)} collective-permute-done((f32[128,128]{1,0:T(8,128)}, f32[128,128]{1,0:T(8,128)S(1)}, u32[]{:S(2)}, u32[]{:S(2)}) %collective-permute-start.23) | collective-permute-done | bytes 65568 | tf_op jit(solution)/shard_map/ppermute | solution.py:51
  237.1 2.5 %finish.1 = bf16[128,2048]{1,0:T(8,128)(2,1)} custom-call(f32[256,2048]{1,0:T(8,128)} %copy-done.9, f32[128,2048]{1,0:T(8,128)} %collective-permute-done.27.other), custom_call_target="tpu_custom_call" | custom-call | tf_op jit(solution)/shard_map/finish/pallas_call | solution.py:345
  (147 shorter events, 40.3 us)
Async XLA Ops:
  1.5 9.7 %collective-permute-start.2 = (bf16[256,128]{1,0:T(8,128)(2,1)S(1)}, bf16[256,128]{1,0:T(8,128)(2,1)S(1)}, u32[]{:S(2)}, u32[]{:S(2)}) collective-permute-start(bf16[256,128]{1,0:T(8,128)(2,1)S(1)} %broadcast_select_fusion.6), channel_id=1, source_target_pairs={{0,16},{1,48},{2,80},{3,112},{4,20},{5,52},{6,84},{7,116},{8,24},{... | collective-permute-start | bytes 196616 | tf_op jit(solution)/shard_map/ppermute | solution.py:395
  8.8 2.4 %collective-permute-start.3 = (bf16[256,128]{1,0:T(8,128)(2,1)S(1)}, bf16[256,128]{1,0:T(8,128)(2,1)S(1)}, u32[]{:S(2)}, u32[]{:S(2)}) collective-permute-start(bf16[256,128]{1,0:T(8,128)(2,1)S(1)} %broadcast_select_fusion.6), channel_id=1, source_target_pairs={{0,0},{1,32},{2,64},{3,96},{4,4},{5,36},{6,68},{7,100},{8,8},{9,40... | collective-permute-start | bytes 196616 | tf_op jit(solution)/shard_map/ppermute | solution.py:394
  13.0 41.5 %all-to-all-start = ((bf16[16,2,256,128]{3,2,1,0:T(8,128)(2,1)}), bf16[16,2,256,128]{3,2,1,0:T(8,128)(2,1)S(1)}, u32[]{:S(2)}, u32[]{:S(2)}) async-start(bf16[16,2,256,128]{3,2,1,0:T(8,128)(2,1)} %broadcast_in_dim.16), calls=%async_computation | async-start | bytes 4194304 | tf_op jit(solution)/shard_map/all_to_all | solution.py:63
  32.4 2.0 collective-permute-start.4
  57.3 6.2 %collective-permute-start.5 = (f32[128,128]{1,0:T(8,128)S(1)}, f32[128,128]{1,0:T(8,128)S(1)}, u32[]{:S(2)}, u32[]{:S(2)}) collective-permute-start(f32[128,128]{1,0:T(8,128)S(1)} %slice_bitcast_fusion.2), channel_id=1, source_target_pairs={{0,1},{1,2},{2,3},{3,0},{4,5},{5,6},{6,7},{7,4},{8,9},{9,10},{10,1... | collective-permute-start | bytes 196616 | tf_op jit(solution)/shard_map/ppermute | solution.py:55
  58.1 6.6 %collective-permute-start.6 = (f32[128,128]{1,0:T(8,128)S(1)}, f32[128,128]{1,0:T(8,128)S(1)}, u32[]{:S(2)}, u32[]{:S(2)}) collective-permute-start(f32[128,128]{1,0:T(8,128)S(1)} %slice_bitcast_fusion.1), channel_id=1, source_target_pairs={{0,2},{1,3},{2,0},{3,1},{4,6},{5,7},{6,4},{7,5},{8,10},{9,11},{10,... | collective-permute-start | bytes 196616 | tf_op jit(solution)/shard_map/ppermute | solution.py:55
  59.9 4.7 %collective-permute-start.7 = (f32[128,128]{1,0:T(8,128)S(1)}, f32[128,128]{1,0:T(8,128)S(1)}, u32[]{:S(2)}, u32[]{:S(2)}) collective-permute-start(f32[128,128]{1,0:T(8,128)S(1)} %slice_bitcast_fusion), channel_id=1, source_target_pairs={{0,3},{1,0},{2,1},{3,2},{4,7},{5,4},{6,5},{7,6},{8,11},{9,8},{10,9... | collective-permute-start | bytes 196616 | tf_op jit(solution)/shard_map/ppermute | solution.py:55
  64.9 7.9 %collective-permute-start.8 = (bf16[128,128]{1,0:T(8,128)(2,1)S(1)}, bf16[128,128]{1,0:T(8,128)(2,1)S(1)}, u32[]{:S(2)}, u32[]{:S(2)}) collective-permute-start(bf16[128,128]{1,0:T(8,128)(2,1)S(1)} %fusion.21), channel_id=1, source_target_pairs={{0,16},{4,20},{8,24},{12,28},{16,0},{20,4},{24,8},{28,12},{32,48},... | collective-permute-start | bytes 98312 | tf_op jit(solution)/shard_map/ppermute | solution.py:44
  74.0 16.7 %all-to-all-start.1 = ((bf16[16,2,128,128]{3,2,1,0:T(8,128)(2,1)}), bf16[16,2,128,128]{3,2,1,0:T(8,128)(2,1)S(1)}, u32[]{:S(2)}, u32[]{:S(2)}) async-start(bf16[16,2,128,128]{3,2,1,0:T(8,128)(2,1)} %broadcast_in_dim.19), calls=%async_computation.1 | async-start | bytes 2097152 | tf_op jit(solution)/shard_map/all_to_all | solution.py:63
  79.5 21.2 %collective-permute-start = (bf16[128,512]{1,0:T(8,128)(2,1)S(1)}, bf16[128,512]{1,0:T(8,128)(2,1)S(1)}, u32[]{:S(2)}, u32[]{:S(2)}) collective-permute-start(bf16[128,512]{1,0:T(8,128)(2,1)S(1)} %get-tuple-element.79), channel_id=1, source_target_pairs={{0,128},{128,0},{1,129},{129,1},{2,130},{130,2},{3,131},{131,3},{4... | collective-permute-start | bytes 393224 | tf_op jit(solution)/shard_map/ppermute | solution.py:40
  90.8 11.1 %collective-permute-start.9 = (bf16[32,128,128]{2,1,0:T(8,128)(2,1)S(1)}, bf16[32,128,128]{2,1,0:T(8,128)(2,1)S(1)}, u32[]{:S(2)}, u32[]{:S(2)}) collective-permute-start(bf16[32,128,128]{2,1,0:T(8,128)(2,1)S(1)} %bitcast.137), channel_id=1, source_target_pairs={{0,128},{128,0},{1,129},{129,1},{2,130},{130,2},{3,131},{131,3},{4... | collective-permute-start | bytes 3145736 | tf_op jit(solution)/shard_map/ppermute | solution.py:40
  90.9 6.5 %collective-permute-start.10 = (f32[128,128]{1,0:T(8,128)S(1)}, f32[128,128]{1,0:T(8,128)S(1)}, u32[]{:S(2)}, u32[]{:S(2)}) collective-permute-start(f32[128,128]{1,0:T(8,128)S(1)} %slice.160), channel_id=1, source_target_pairs={{0,1},{1,2},{2,3},{3,0},{4,5},{5,6},{6,7},{7,4},{8,9},{9,10},{10,1... | collective-permute-start | bytes 196616 | tf_op jit(solution)/shard_map/ppermute | solution.py:55
  93.6 6.6 %collective-permute-start.11 = (f32[128,128]{1,0:T(8,128)S(1)}, f32[128,128]{1,0:T(8,128)S(1)}, u32[]{:S(2)}, u32[]{:S(2)}) collective-permute-start(f32[128,128]{1,0:T(8,128)S(1)} %slice.161), channel_id=1, source_target_pairs={{0,2},{1,3},{2,0},{3,1},{4,6},{5,7},{6,4},{7,5},{8,10},{9,11},{10,... | collective-permute-start | bytes 196616 | tf_op jit(solution)/shard_map/ppermute | solution.py:55
  94.5 5.7 %collective-permute-start.12 = (f32[128,128]{1,0:T(8,128)S(1)}, f32[128,128]{1,0:T(8,128)S(1)}, u32[]{:S(2)}, u32[]{:S(2)}) collective-permute-start(f32[128,128]{1,0:T(8,128)S(1)} %slice.162), channel_id=1, source_target_pairs={{0,3},{1,0},{2,1},{3,2},{4,7},{5,4},{6,5},{7,6},{8,11},{9,8},{10,9... | collective-permute-start | bytes 196616 | tf_op jit(solution)/shard_map/ppermute | solution.py:55
  97.4 3.9 %collective-permute-start.1 = (bf16[128,512]{1,0:T(8,128)(2,1)S(1)}, bf16[128,512]{1,0:T(8,128)(2,1)S(1)}, u32[]{:S(2)}, u32[]{:S(2)}) collective-permute-start(bf16[128,512]{1,0:T(8,128)(2,1)S(1)} %get-tuple-element.77), channel_id=1, source_target_pairs={{0,128},{128,0},{1,129},{129,1},{2,130},{130,2},{3,131},{131,3},{4... | collective-permute-start | bytes 393224 | tf_op jit(solution)/shard_map/ppermute | solution.py:40
  113.0 9.3 %collective-permute-start.16 = (f32[32,128,128]{2,1,0:T(8,128)}, f32[32,128,128]{2,1,0:T(8,128)}, u32[]{:S(2)}, u32[]{:S(2)}) collective-permute-start(f32[32,128,128]{2,1,0:T(8,128)} %get-tuple-element.45), channel_id=1, source_target_pairs={{0,128},{128,0},{1,129},{129,1},{2,130},{130,2},{3,131},{131,3},{4... | collective-permute-start | bytes 6291464 | tf_op jit(solution)/shard_map/ppermute | solution.py:40
  113.2 26.2 %all-to-all-start.3 = ((bf16[16,128,256]{2,1,0:T(8,128)(2,1)}), bf16[16,128,256]{2,1,0:T(8,128)(2,1)}, u32[]{:S(2)}, u32[]{:S(2)}) async-start(bf16[16,128,256]{2,1,0:T(8,128)(2,1)} %get-tuple-element.46), calls=%async_computation.3 | async-start | bytes 2097152 | tf_op jit(solution)/shard_map/all_to_all | solution.py:63
  170.4 19.5 %all-to-all-start.2 = ((bf16[16,128,256]{2,1,0:T(8,128)(2,1)}), bf16[16,128,256]{2,1,0:T(8,128)(2,1)}, u32[]{:S(2)}, u32[]{:S(2)}) async-start(bf16[16,128,256]{2,1,0:T(8,128)(2,1)} %get-tuple-element.43), calls=%async_computation.2 | async-start | bytes 2097152 | tf_op jit(solution)/shard_map/all_to_all | solution.py:63
  176.0 14.4 %collective-permute-start.20 = (f32[128,128]{1,0:T(8,128)S(1)}, f32[128,128]{1,0:T(8,128)S(1)}, u32[]{:S(2)}, u32[]{:S(2)}) collective-permute-start(f32[128,128]{1,0:T(8,128)S(1)} %get-tuple-element.50), channel_id=1, source_target_pairs={{0,128},{128,0},{1,129},{129,1},{2,130},{130,2},{3,131},{131,3},{4... | collective-permute-start | bytes 196616 | tf_op jit(solution)/shard_map/ppermute | solution.py:40
  176.2 14.2 %collective-permute-start.19 = (f32[128,128]{1,0:T(8,128)S(1)}, f32[128,128]{1,0:T(8,128)S(1)}, u32[]{:S(2)}, u32[]{:S(2)}) collective-permute-start(f32[128,128]{1,0:T(8,128)S(1)} %select_bitcast_fusion.1), channel_id=1, source_target_pairs={{0,16},{4,20},{8,24},{12,28},{16,0},{20,4},{24,8},{28,12},{32,48},... | collective-permute-start | bytes 196616 | tf_op jit(solution)/shard_map/ppermute | solution.py:44
  189.9 17.4 %collective-permute-start.17 = (bf16[2048,256]{1,0:T(8,128)(2,1)}, bf16[2048,256]{1,0:T(8,128)(2,1)}, u32[]{:S(2)}, u32[]{:S(2)}) collective-permute-start(bf16[2048,256]{1,0:T(8,128)(2,1)} %bitcast.32.mine_first), channel_id=1, source_target_pairs={{0,128},{128,0},{1,129},{129,1},{2,130},{130,2},{3,131},{131,3},{4... | collective-permute-start | bytes 3145736 | tf_op jit(solution)/shard_map/ppermute | solution.py:40
  189.9 17.4 %collective-permute-start.18 = (bf16[2048,256]{1,0:T(8,128)(2,1)}, bf16[2048,256]{1,0:T(8,128)(2,1)}, u32[]{:S(2)}, u32[]{:S(2)}) collective-permute-start(bf16[2048,256]{1,0:T(8,128)(2,1)} %bitcast.34.mine_second), channel_id=1, source_target_pairs={{0,128},{128,0},{1,129},{129,1},{2,130},{130,2},{3,131},{131,3},{4... | collective-permute-start | bytes 3145736 | tf_op jit(solution)/shard_map/ppermute | solution.py:40
  190.7 10.7 %collective-permute-start.24 = (bf16[256,128]{1,0:T(8,128)(2,1)S(1)}, bf16[256,128]{1,0:T(8,128)(2,1)}, u32[]{:S(2)}, u32[]{:S(2)}) collective-permute-start(bf16[256,128]{1,0:T(8,128)(2,1)S(1)} %fusion.15), channel_id=1, source_target_pairs={{0,1},{1,2},{2,3},{3,0},{4,5},{5,6},{6,7},{7,4},{8,9},{9,10},{10,1... | collective-permute-start | bytes 196616 | tf_op jit(solution)/shard_map/ppermute | solution.py:55
  192.9 9.8 %collective-permute-start.26 = (bf16[256,128]{1,0:T(8,128)(2,1)S(1)}, bf16[256,128]{1,0:T(8,128)(2,1)}, u32[]{:S(2)}, u32[]{:S(2)}) collective-permute-start(bf16[256,128]{1,0:T(8,128)(2,1)S(1)} %fusion.15), channel_id=1, source_target_pairs={{0,3},{1,0},{2,1},{3,2},{4,7},{5,4},{6,5},{7,6},{8,11},{9,8},{10,9... | collective-permute-start | bytes 196616 | tf_op jit(solution)/shard_map/ppermute | solution.py:55
  194.8 9.1 %collective-permute-start.25 = (bf16[256,128]{1,0:T(8,128)(2,1)S(1)}, bf16[256,128]{1,0:T(8,128)(2,1)S(1)}, u32[]{:S(2)}, u32[]{:S(2)}) collective-permute-start(bf16[256,128]{1,0:T(8,128)(2,1)S(1)} %fusion.15), channel_id=1, source_target_pairs={{0,2},{1,3},{2,0},{3,1},{4,6},{5,7},{6,4},{7,5},{8,10},{9,11},{10,... | collective-permute-start | bytes 196616 | tf_op jit(solution)/shard_map/ppermute | solution.py:55
  196.0 21.2 %all-to-all-start.5 = ((bf16[16,256,128]{2,1,0:T(8,128)(2,1)}), bf16[16,256,128]{2,1,0:T(8,128)(2,1)S(1)}, u32[]{:S(2)}, u32[]{:S(2)}) async-start(bf16[16,256,128]{2,1,0:T(8,128)(2,1)} %broadcast_in_dim.23), calls=%async_computation.5 | async-start | bytes 2097152 | tf_op jit(solution)/shard_map/all_to_all | solution.py:63
  206.6 30.4 %collective-permute-start.27 = (f32[128,2048]{1,0:T(8,128)}, f32[128,2048]{1,0:T(8,128)}, u32[]{:S(2)}, u32[]{:S(2)}) collective-permute-start(f32[128,2048]{1,0:T(8,128)} %slice.190), channel_id=1, source_target_pairs={{0,128},{128,0},{1,129},{129,1},{2,130},{130,2},{3,131},{131,3},{4... | collective-permute-start | bytes 3145736 | tf_op jit(solution)/shard_map/ppermute | solution.py:40
  206.6 20.0 %collective-permute-start.14 = (bf16[128,512]{1,0:T(8,128)(2,1)S(1)}, bf16[128,512]{1,0:T(8,128)(2,1)S(1)}, u32[]{:S(2)}, u32[]{:S(2)}) collective-permute-start(bf16[128,512]{1,0:T(8,128)(2,1)S(1)} %copy-done.8), channel_id=1, source_target_pairs={{0,128},{128,0},{1,129},{129,1},{2,130},{130,2},{3,131},{131,3},{4... | collective-permute-start | bytes 393224 | tf_op jit(solution)/shard_map/ppermute | solution.py:40
  207.2 21.7 %collective-permute-start.15 = (bf16[128,512]{1,0:T(8,128)(2,1)S(1)}, bf16[128,512]{1,0:T(8,128)(2,1)}, u32[]{:S(2)}, u32[]{:S(2)}) collective-permute-start(bf16[128,512]{1,0:T(8,128)(2,1)S(1)} %copy-done.6), channel_id=1, source_target_pairs={{0,128},{128,0},{1,129},{129,1},{2,130},{130,2},{3,131},{131,3},{4... | collective-permute-start | bytes 393224 | tf_op jit(solution)/shard_map/ppermute | solution.py:40
  222.7 9.2 %collective-permute-start.21 = (f32[128,128]{1,0:T(8,128)}, f32[128,128]{1,0:T(8,128)S(1)}, u32[]{:S(2)}, u32[]{:S(2)}) collective-permute-start(f32[128,128]{1,0:T(8,128)} %get-tuple-element.52), channel_id=1, source_target_pairs={{0,16},{4,20},{8,24},{12,28},{16,0},{20,4},{24,8},{28,12},{32,48},... | collective-permute-start | bytes 196616 | tf_op jit(solution)/shard_map/ppermute | solution.py:44
  226.7 5.2 %collective-permute-start.22 = (f32[128,128]{1,0:T(8,128)}, f32[128,128]{1,0:T(8,128)S(1)}, u32[]{:S(2)}, u32[]{:S(2)}) collective-permute-start(f32[128,128]{1,0:T(8,128)} %get-tuple-element.53), channel_id=1, source_target_pairs={{0,128},{128,0},{1,129},{129,1},{2,130},{130,2},{3,131},{131,3},{4... | collective-permute-start | bytes 196616 | tf_op jit(solution)/shard_map/ppermute | solution.py:40
  226.7 8.9 %collective-permute-start.23 = (f32[128,128]{1,0:T(8,128)}, f32[128,128]{1,0:T(8,128)S(1)}, u32[]{:S(2)}, u32[]{:S(2)}) collective-permute-start(f32[128,128]{1,0:T(8,128)} %get-tuple-element.54), channel_id=1, source_target_pairs={{0,144},{128,16},{4,148},{132,20},{8,152},{136,24},{12,156},{140,2... | collective-permute-start | bytes 196616 | tf_op jit(solution)/shard_map/ppermute | solution.py:51
  (23 other events, 140.1 us)

commit v3 on v2

--- a/solution.py
+++ b/solution.py
@@ -1,3 +1,4 @@
+import functools
 import math
 
 import jax
@@ -44,13 +45,6 @@
     return lax.ppermute(array, "ctx", ACROSS)
 
 
-def diagonal(array):
-    pairs = []
-    for source, target in ACROSS:
-        pairs += [(source, NX * NZ * NY + target), (NX * NZ * NY + source, target)]
-    return lax.ppermute(array, ("group", "ctx"), pairs)
-
-
 def along(array, step):
     return lax.ppermute(array, "tp", [(t, (t + step) % NT) for t in range(NT)])
 
@@ -65,8 +59,32 @@
     )
 
 
-def plane_gather(block):
-    return plane_exchange(jnp.broadcast_to(block[None], (NX * NY, *block.shape)))
+def copies_kernel(by_zone, place_ref, mine, other, target, pair, sems):
+    upper = jnp.logical_and(by_zone, ((place_ref[1] >> 2) & 1) == 1)
+    rows = mine.shape[0]
+    pair[:rows] = jnp.where(upper, other[...], mine[...])
+    pair[rows:] = jnp.where(upper, mine[...], other[...])
+    copies = [pltpu.make_async_copy(pair, target.at[i], sems.at[i]) for i in range(NX * NY)]
+    for copy in copies:
+        copy.start()
+    for copy in copies:
+        copy.wait()
+
+
+def plane_copies(place, mine, other, by_zone=True):
+    rows, width = mine.shape
+    vmem = pl.BlockSpec(memory_space=pltpu.VMEM)
+    return pl.pallas_call(
+        functools.partial(copies_kernel, by_zone),
+        out_shape=jax.ShapeDtypeStruct((NX * NY, 2 * rows, width), mine.dtype),
+        in_specs=[pl.BlockSpec(memory_space=pltpu.SMEM), vmem, vmem],
+        out_specs=pl.BlockSpec(memory_space=pl.ANY),
+        scratch_shapes=[
+            pltpu.VMEM((2 * rows, width), mine.dtype),
+            pltpu.SemaphoreType.DMA((NX * NY,)),
+        ],
+        name="copies",
+    )(place, mine, other)
 
 
 def turn(rows, cosine, sine):
@@ -92,11 +110,33 @@
 CHUNKS = NX * NZ // ZONES
 
 
+def heads_down(ref_a, ref_b, take_a):
+    picked = jnp.where(take_a, ref_a[...], ref_b[...])
+    return jnp.concatenate([picked[:, h * HD : (h + 1) * HD] for h in range(GH)], 0)
+
+
+def store_heads(target, transposed):
+    for h in range(GH):
+        target[:, h * HD : (h + 1) * HD] = jnp.transpose(
+            transposed[:, h * TOK : (h + 1) * TOK]
+        ).astype(BF16)
+
+
+def unturn(transposed, table_ref, which):
+    cosine = jnp.concatenate([table_ref[which, 0]] * GH, 1)
+    sine = jnp.concatenate([table_ref[which, 1]] * GH, 1)
+    first, second = transposed[:HALF], transposed[HALF:]
+    return jnp.concatenate([first * cosine + second * sine, second * cosine - first * sine], 0)
+
+
+def dots(grads, attended_t):
+    grads_t = jnp.transpose(grads.astype(F32))
+    return jnp.sum(grads_t * attended_t.astype(BF16).astype(F32), 0, keepdims=True)
+
+
 def attention_kernel(
-    place_ref,
-    q_keep, q_got, do_keep, do_got, ctx_mine, ctx_other, short_mine, short_other,
-    allowed_ref, table_ref,
-    out_mine, out_other, qgrad_mine, qgrad_other, kv_keep, kv_send, short_keep, short_send,
+    place_ref, q_keep, q_got, do_keep, do_got, ctx_mine, ctx_other, table_ref,
+    out_ref, qgrad_ref, kv_keep, kv_send,
     scores, tops, acc, qacc,
 ):
     core = place_ref[0]
@@ -104,34 +144,8 @@
     long_core = core == 0
     last = rank // (ZONES * NY)
     count = last + 1
-
-    def heads_down(ref_a, ref_b, take_a):
-        picked = jnp.where(take_a, ref_a[...], ref_b[...])
-        return jnp.concatenate([picked[:, h * HD : (h + 1) * HD] for h in range(GH)], 0)
-
-    def store_out(mine, other, long_part, short_part):
-        for h in range(GH):
-            long_head = long_part[:, h * TOK : (h + 1) * TOK]
-            short_head = short_part[:, h * TOK : (h + 1) * TOK]
-            here = (slice(None), slice(h * HD, (h + 1) * HD))
-            mine[here] = jnp.transpose(jnp.where(long_core, long_head, short_head)).astype(BF16)
-            other[here] = jnp.transpose(jnp.where(long_core, short_head, long_head)).astype(BF16)
-
-    def unturn(transposed, which):
-        cosine = jnp.concatenate([table_ref[which, 0]] * GH, 1)
-        sine = jnp.concatenate([table_ref[which, 1]] * GH, 1)
-        first, second = transposed[:HALF], transposed[HALF:]
-        return jnp.concatenate(
-            [first * cosine + second * sine, second * cosine - first * sine], 0
-        )
-
-    def dots(grads_t, attended_t):
-        return jnp.sum(grads_t * attended_t.astype(BF16).astype(F32), 0, keepdims=True)
-
     q_long = heads_down(q_keep, q_got, long_core)
     do_long = heads_down(do_keep, do_got, long_core)
-    q_short = heads_down(q_got, q_keep, long_core)
-    do_short = heads_down(do_got, do_keep, long_core)
 
     def block_places(j):
         places = []
@@ -179,8 +193,8 @@
 
     lax.fori_loop(0, count, out_pass, 0)
     attended = acc[...]
-    do_long_t = jnp.transpose(do_long.astype(F32))
-    out_dot = dots(do_long_t, attended)
+    store_heads(out_ref, attended)
+    out_dot = dots(do_long, attended)
 
     def grad_pass(j, carry):
         keys = blocks_of(j, long_core)
@@ -199,6 +213,7 @@
         return carry
 
     lax.fori_loop(0, count, grad_pass, 0)
+    store_heads(qgrad_ref, unturn(qacc[...] * SCALE, table_ref, 0))
 
     def clear_pass(j, carry):
         for at in block_places(j):
@@ -208,6 +223,14 @@
 
     lax.fori_loop(count, CHUNKS, clear_pass, 0)
 
+
+def short_kernel(
+    place_ref, q_keep, q_got, do_keep, do_got, short_mine, short_other, allowed_ref, table_ref,
+    out_ref, qgrad_ref, keep_ref, send_ref,
+):
+    long_core = place_ref[0] == 0
+    q_short = heads_down(q_got, q_keep, long_core)
+    do_short = heads_down(do_got, do_keep, long_core)
     keys = jnp.where(long_core, short_mine[...], short_other[...])
     values = jnp.where(long_core, short_other[...], short_mine[...])
     allowed = jnp.concatenate([allowed_ref[...]] * GH, 1) > 0
@@ -215,31 +238,41 @@
     powers = jnp.exp(scored - jnp.max(scored, 0, keepdims=True))
     weights = powers * (1.0 / jnp.sum(powers, 0, keepdims=True))
     rounded = weights.astype(BF16)
-    short_attended = product(values, rounded, 0, 0)
-    store_out(out_mine, out_other, attended, short_attended)
-    short_dot = dots(jnp.transpose(do_short.astype(F32)), short_attended)
+    attended = product(values, rounded, 0, 0)
+    store_heads(out_ref, attended)
+    out_dot = dots(do_short, attended)
     prob_grad = product(values, do_short, 1, 1)
-    score_grad = (weights * (prob_grad - short_dot)).astype(BF16)
-    short_qgrad = product(keys, score_grad, 0, 0)
-    store_out(
-        qgrad_mine, qgrad_other, unturn(qacc[...] * SCALE, 0), unturn(short_qgrad * SCALE, 1)
-    )
+    score_grad = (weights * (prob_grad - out_dot)).astype(BF16)
+    qgrad = product(keys, score_grad, 0, 0)
+    store_heads(qgrad_ref, unturn(qgrad * SCALE, table_ref, 1))
     key_part = product(score_grad, q_short, 1, 0) * SCALE
     value_part = product(rounded, do_short, 1, 0)
-    short_keep[...] = jnp.where(long_core, key_part, value_part)
-    short_send[...] = jnp.where(long_core, value_part, key_part)
+    keep_ref[...] = jnp.where(long_core, key_part, value_part)
+    send_ref[...] = jnp.where(long_core, value_part, key_part)
+
+
+def short_call(place, *arrays):
+    rows = jax.ShapeDtypeStruct((TOK, GH * HD), BF16)
+    block = jax.ShapeDtypeStruct((TOK, HD), F32)
+    vmem = pl.BlockSpec(memory_space=pltpu.VMEM)
+    return pl.pallas_call(
+        short_kernel,
+        out_shape=(rows, rows, block, block),
+        in_specs=[pl.BlockSpec(memory_space=pltpu.SMEM)] + [vmem] * len(arrays),
+        out_specs=(vmem,) * 4,
+        name="short_attention",
+    )(place, *arrays)
 
 
 def attention_call(place, *arrays):
     rows = jax.ShapeDtypeStruct((TOK, GH * HD), BF16)
     blocks = jax.ShapeDtypeStruct((NX * NZ * NY, TOK, HD), F32)
-    block = jax.ShapeDtypeStruct((TOK, HD), F32)
     vmem = pl.BlockSpec(memory_space=pltpu.VMEM)
     return pl.pallas_call(
         attention_kernel,
-        out_shape=(rows, rows, rows, rows, blocks, blocks, block, block),
+        out_shape=(rows, rows, blocks, blocks),
         in_specs=[pl.BlockSpec(memory_space=pltpu.SMEM)] + [vmem] * len(arrays),
-        out_specs=(vmem,) * 8,
+        out_specs=(vmem,) * 4,
         scratch_shapes=[
             pltpu.VMEM((CHUNKS, CHUNK, ROWS), F32),
             pltpu.VMEM((CHUNKS, 1, ROWS), F32),
@@ -251,12 +284,16 @@
     )(place, *arrays)
 
 
-def join_kernel(place_ref, *refs):
+def join_kernel(
+    place_ref, long_out, short_out, long_qgrad, short_qgrad, out_got, qgrad_got, out, qgrad
+):
     first = place_ref[0] == 0
     width = GH * HD
-    for mine, got, target in ((refs[0], refs[1], refs[4]), (refs[2], refs[3], refs[5])):
-        target[:, :width] = jnp.where(first, mine[...], got[...])
-        target[:, width:] = jnp.where(first, got[...], mine[...])
+    for long_part, short_part, got, target in (
+        (long_out, short_out, out_got, out), (long_qgrad, short_qgrad, qgrad_got, qgrad)
+    ):
+        target[:, :width] = jnp.where(first, long_part[...], got[...])
+        target[:, width:] = jnp.where(first, got[...], short_part[...])
 
 
 def join_heads(place, *halves):
@@ -284,7 +321,7 @@
 
 def owned_kernel(
     place_ref, mine_first, mine_second, other_first, other_second, grads_ref,
-    here, above, beside, opposite,
+    here, beside, leaving,
     sums, pieces,
 ):
     step = pl.program_id(0)
@@ -308,9 +345,9 @@
         core = place_ref[0]
         zone = (place_ref[1] >> 2) & 1
         here[...] = pieces[core * NZ + zone]
-        above[...] = pieces[core * NZ + 1 - zone]
+        leaving[0] = pieces[core * NZ + 1 - zone]
         beside[...] = pieces[(1 - core) * NZ + zone]
-        opposite[...] = pieces[(1 - core) * NZ + 1 - zone]
+        leaving[1] = pieces[(1 - core) * NZ + 1 - zone]
 
 
 def owned_pieces(place, *arrays):
@@ -320,9 +357,13 @@
     return pl.pallas_call(
         owned_kernel,
         grid=(NX,),
-        out_shape=(piece,) * 4,
+        out_shape=(piece, piece, jax.ShapeDtypeStruct((2, TOK, HD), F32)),
         in_specs=[pl.BlockSpec(memory_space=pltpu.SMEM)] + [columns] * 4 + [grads],
-        out_specs=(pl.BlockSpec((TOK, HD), lambda i: (0, 0)),) * 4,
+        out_specs=(
+            pl.BlockSpec((TOK, HD), lambda i: (0, 0)),
+            pl.BlockSpec((TOK, HD), lambda i: (0, 0)),
+            pl.BlockSpec((2, TOK, HD), lambda i: (0, 0, 0)),
+        ),
         scratch_shapes=[
             pltpu.VMEM((2, HD, NZ * TOK), F32),
             pltpu.VMEM((2 * NZ, TOK, HD), F32),
@@ -331,25 +372,63 @@
     )(place, *arrays)
 
 
-def finish_kernel(mine, other, target):
+def input_kernel(place_ref, weight, other_weight, *refs):
+    grads, target = refs[:NT], refs[NT]
+    heads = [(place_ref[2] - d) & (NT - 1) for d in range(NT)]
+    left = jnp.concatenate([g[part] for g in grads for part in range(2)], 1)
     step = target.shape[1] // (NZ * NY)
-    for z in range(NZ):
-        for y in range(NY):
+    for y in range(NY):
+        for z in range(NZ):
             source = slice((y * NZ + z) * step, (y * NZ + z + 1) * step)
-            summed = mine[:, source] + other[:, source]
-            target[:, (z * NY + y) * step : (z * NY + y + 1) * step] = summed.astype(BF16)
-
-
-def finish_input(terms, other_terms):
-    whole = pl.BlockSpec(other_terms.shape, lambda i: (0, 0))
-    return pl.pallas_call(
-        finish_kernel,
-        grid=(1,),
-        out_shape=jax.ShapeDtypeStruct(other_terms.shape, BF16),
-        in_specs=[whole, whole],
-        out_specs=whole,
-        name="finish",
-    )(terms, other_terms)
+            right = jnp.concatenate(
+                [w[head, source] for head in heads for w in (weight, other_weight)], 1
+            )
+            target[:, (z * NY + y) * step : (z * NY + y + 1) * step] = product(
+                left, right, 1, 1
+            ).astype(BF16)
+
+
+def input_product(place, weight, other_weight, *grads):
+    vmem = pl.BlockSpec(memory_space=pltpu.VMEM)
+    return pl.pallas_call(
+        input_kernel,
+        out_shape=jax.ShapeDtypeStruct((TOK, weight.shape[1]), BF16),
+        in_specs=[pl.BlockSpec(memory_space=pltpu.SMEM)] + [vmem] * (2 + NT),
+        out_specs=vmem,
+        name="input",
+    )(place, weight, other_weight, *grads)
+
+
+def slice_kernel(place_ref, source, target, sems):
+    step = target.shape[1] // (NZ * NY)
+    copies = []
+    for y in range(NY):
+        for z in range(NZ):
+            i = y * NZ + z
+            first = pl.multiple_of((place_ref[2] * (NZ * NY) + z * NY + y) * step, step)
+            copies.append(
+                pltpu.make_async_copy(
+                    source.at[:, pl.ds(first, step)],
+                    target.at[:, i * step : (i + 1) * step],
+                    sems.at[i],
+                )
+            )
+    for copy in copies:
+        copy.start()
+    for copy in copies:
+        copy.wait()
+
+
+def feature_slice(place, activations):
+    rows, features = activations.shape
+    return pl.pallas_call(
+        slice_kernel,
+        out_shape=jax.ShapeDtypeStruct((rows, features // NT), activations.dtype),
+        in_specs=[pl.BlockSpec(memory_space=pltpu.SMEM), pl.BlockSpec(memory_space=pl.ANY)],
+        out_specs=pl.BlockSpec(memory_space=pl.ANY),
+        scratch_shapes=[pltpu.SemaphoreType.DMA((NZ * NY,))],
+        name="feature_slice",
+    )(place, activations)
 
 
 def pack_columns(activations):
@@ -370,9 +449,8 @@
     tp = lax.axis_index("tp").astype(jnp.int32)
     is_long = core == 0
     upper = ((rank >> 2) & 1) == 1
-    features = activations.shape[1]
-    slice_cols = features // NT
     plane = NX * NY
+    place = jnp.stack([core, rank, tp])
 
     local = jnp.arange(TOK, dtype=jnp.int32)
     frequency = THETA ** (-2.0 * jnp.arange(HALF, dtype=F32) / HD)
@@ -384,29 +462,19 @@
     back_cos = jnp.concatenate([own_cos, jnp.where(is_long, cosine[TOK:], cosine[:TOK])], 0)
     back_sin = jnp.concatenate([own_sin, jnp.where(is_long, sine[TOK:], sine[:TOK])], 0)
 
-    def halves_by_zone(mine, other):
-        return jnp.where(upper, jnp.stack([other, mine]), jnp.stack([mine, other]))
-
     def role(first, second):
         return jnp.where(is_long, first, second)
 
     weight = role(key_weight, value_weight)
     near = lax.ppermute(weight, ("ctx", "tp"), TURN)
     far = lax.ppermute(weight, ("ctx", "tp"), FAR_TURN)
-    weight = halves_by_zone(near, far)
-    weight = plane_gather(weight)
+    weight = plane_copies(place, near, far)
+    weight = plane_exchange(weight)
     packed = pack_columns(activations)
-    weight = weight.reshape(NX, NY * NZ * weight.shape[-2], HD)
-
-    own_slice = lax.dynamic_slice_in_dim(activations, tp * slice_cols, slice_cols, 1)
-    step = slice_cols // (NZ * NY)
-
-    def columns_at(array, block):
-        return array[:, block * step : (block + 1) * step]
-
-    own_slice = jnp.concatenate(
-        [columns_at(own_slice, z * NY + y) for y in range(NY) for z in range(NZ)], 1
-    )
+    weight = weight.reshape(NX, NY * weight.shape[-2], HD)
+    other_weight = partner(weight)
+
+    own_slice = feature_slice(place, activations)
     other_slice = partner(own_slice)
     both_slices = jnp.concatenate(
         [role(own_slice, other_slice), role(other_slice, own_slice)], 0
@@ -431,8 +499,8 @@
     short_rows = role(turn(short_sum, cosine[TOK:], sine[TOK:]), short_sum).astype(BF16)
     other_short = partner(short_rows)
     across_rows = across(long_rows)
-    context = halves_by_zone(long_rows, across_rows)
-    context = plane_gather(context)
+    context = plane_copies(place, long_rows, across_rows)
+    context = plane_exchange(context)
 
     second, context = after(packed[1], context)
     second_columns = plane_exchange(second)
@@ -444,48 +512,42 @@
         (own_sessions[:, None] == own_sessions[None, :]) & (local[:, None] <= local[None, :])
     ).astype(jnp.int32)
     tables = jnp.stack([cosine, sine]).reshape(2, 2, TOK, HALF).transpose(1, 0, 3, 2)
-    place = jnp.stack([core, rank])
-    (
-        out_mine, out_other, qgrad_mine, qgrad_other, kv_keep, kv_send, short_keep, short_send
-    ) = attention_call(
-        place, q_keep, q_got, do_keep, do_got, context, other_context, short_rows,
-        other_short, allowed, tables,
-    )
-    out_got, qgrad_got = partner(out_other), partner(qgrad_other)
-    attention, query_grad = join_heads(place, out_mine, out_got, qgrad_mine, qgrad_got)
-
+    short_out, short_qgrad, short_keep, short_send = short_call(
+        place, q_keep, q_got, do_keep, do_got, short_rows, other_short, allowed, tables
+    )
+    long_out, long_qgrad, kv_keep, kv_send = attention_call(
+        place, q_keep, q_got, do_keep, do_got, context, other_context, tables
+    )
+    out_parts = (long_out, short_out, long_qgrad, short_qgrad)
+    out_got, qgrad_got = partner(role(short_out, long_out)), partner(role(short_qgrad, long_qgrad))
+    attention, query_grad = join_heads(place, *out_parts, out_got, qgrad_got)
     kv_sums = kv_keep + partner(kv_send)
     short_kv = short_keep + partner(short_send)
-    blocks, second_columns = after(kv_sums.reshape(plane, NZ, TOK, HD), second_columns)
+    blocks, second_columns = after(kv_sums.reshape(plane, NZ * TOK, HD), second_columns)
     columns = [
         array.reshape(plane * TOK, NZ * TOK) for array in (first_columns, second_columns)
     ]
     other_columns = [partner(array) for array in columns]
     arrived = plane_exchange(blocks)
-    arrived = arrived.sum(0)
+    arrived = arrived.reshape(plane, NZ, TOK, HD).sum(0)
     here = jnp.where(upper, arrived[1], arrived[0])
     there = jnp.where(upper, arrived[0], arrived[1])
     long_kv = here + across(there)
     grads = jnp.concatenate([role(long_kv, short_kv), role(short_kv, long_kv)], 0)
     grads = role(turn(grads, back_cos, -back_sin), grads).astype(BF16)
-    plane_grads = plane_gather(grads)
-
-    by_step = [grads] + [along(grads, d) for d in range(1, NT)]
-    terms = jnp.zeros((2 * TOK, weight.shape[1]), F32)
-    for d in range(NT):
-        head = lax.dynamic_index_in_dim(weight, (tp - d) & (NT - 1), 0, False)
-        terms += product(by_step[d], head, 1, 1)
-    other_terms = partner(terms[TOK:])
-    input_grad = finish_input(terms, other_terms)
-
-    here, above, beside, opposite = owned_pieces(
+    grads_copies = plane_copies(place, grads[:TOK], grads[TOK:], False)
+    plane_grads = plane_exchange(grads_copies)
+
+    pair = jnp.stack([grads[:TOK], partner(grads[TOK:])])
+    by_step = [pair] + [along(pair, d) for d in range(1, NT)]
+    input_grad = input_product(place, weight, other_weight, *by_step)
+
+    here, beside, leaving = owned_pieces(
         place, columns[0], columns[1], other_columns[0], other_columns[1], plane_grads
     )
-    diagonal_got = diagonal(opposite)
-    across_got = across(above)
-    partner_got = partner(beside)
-    same = here + across_got
-    cross = partner_got + diagonal_got
+    arrived_pieces = across(leaving)
+    cross = partner(beside + arrived_pieces[1])
+    same = here + arrived_pieces[0]
     return (attention, query_grad, role(same, cross), role(cross, same), input_grad)
 
 

time: 243 us -> 249 us (1.025)
  blocking collectives: 31 us -> 0 us
  Pallas kernels: 19.4 us -> 48.4 us
  waiting for transfers between devices: 75.4 us -> 93.2 us
  local copies, waits for them, and re-layouts: 18.1 us -> 11.1 us
  other arithmetic: 11.6 us -> 17.4 us
  matrix products: 7.18 us -> 2.1 us
    all_to_all x1 -> x0, blocking collectives: 31 us -> none  [plane_exchange(): lax.all_to_all(blocks, 'ctx', split_axis=0, concat_axis=0, tiled=True, ax...]
    pallas_call x3 -> x8, Pallas kernels: 14.2 us -> 43.1 us  [the longest x1 17.7 us: feature_slice(): pl.pallas_call(slice_kernel, out_shape=jax.ShapeDtypeStruct((rows, featur...]
    ppermute x3, waiting for transfers between devices: 5.11 us -> 13.5 us  [across(): return lax.ppermute(array, 'ctx', ACROSS)]
    ppermute x9, starting transfers between devices: 13.3 us -> 6.28 us  [along(): return lax.ppermute(array, 'tp', [(t, (t + step) % NT) for t in range(NT)])]
    all_to_all x5 -> x6, waiting for transfers between devices: 59 us -> 65.8 us  [plane_exchange(): lax.all_to_all(blocks, 'ctx', split_axis=0, concat_axis=0, tiled=True, ax...]
    all_to_all x5 -> x6, starting transfers between devices: 39.1 us -> 44.6 us  [plane_exchange(): lax.all_to_all(blocks, 'ctx', split_axis=0, concat_axis=0, tiled=True, ax...]
    dot_general x4 -> x0, matrix products: 4.52 us -> none  [product(): lax.dot_general(left, right, (((left_dim,), (right_dim,)), ((), ())), pre...]
    broadcast_in_dim x3 -> x0, local copies, waits for them, and re-layouts: 4.18 us -> none  [plane_gather(): jnp.broadcast_to(block[None], (NX * NY, *block.shape))]
  transfers between devices with their start and end apart: 33 -> 34, of which waited for: 14 -> 19; matrix products, arithmetic and copies ran while one was open for 10% -> 7% of each run, Pallas kernels for 4% -> 15%
where the time goes in v3:
time: 249 us; the launch traced here: 247 us
  waiting for transfers between devices  93.2 us (37%)
  starting transfers between devices  73.5 us (30%)
  Pallas kernels  48.4 us (19%)
  other arithmetic  17.4 us (7%)
  local copies, waits for them, and re-layouts  11.1 us (4%)
    all_to_all x6, waiting for transfers between devices, plane_exchange(): lax.all_to_all(blocks, 'ctx', split_axis=0, concat_axis=0, tiled=True, ax...  65.8 us
    all_to_all x6, starting transfers between devices, plane_exchange(): lax.all_to_all(blocks, 'ctx', split_axis=0, concat_axis=0, tiled=True, ax...  44.6 us
    pallas_call x1, Pallas kernels, feature_slice(): pl.pallas_call(slice_kernel, out_shape=jax.ShapeDtypeStruct((rows, featur...  17.7 us
    ppermute x3, waiting for transfers between devices, across(): return lax.ppermute(array, 'ctx', ACROSS)  13.5 us
    ppermute x3, starting transfers between devices, across(): return lax.ppermute(array, 'ctx', ACROSS)  12 us
    ppermute x9, waiting for transfers between devices, along(): return lax.ppermute(array, 'tp', [(t, (t + step) % NT) for t in range(NT)])  7.95 us
    unnamed x94, local copies, waits for them, and re-layouts  7.72 us
    pallas_call x1, Pallas kernels, attention_call(): pl.pallas_call(attention_kernel, out_shape=(rows, rows, blocks, blocks),...  7.37 us
  transfers between devices with their start and end apart: 34, of which 19 were waited for; matrix products, arithmetic and copies ran while one was open for 7% of the time, Pallas kernels for 15%

profile of v3, /device:TPU:8, one launch (start us, length us, event | category | flops | bytes accessed | tf_op | source)
XLA Modules:
  0.0 246.9 jit_solution(4204711567457032375)
XLA Ops:
  2.2 7.3 %collective-permute-start.3 = (bf16[256,128]{1,0:T(8,128)(2,1)S(1)}, bf16[256,128]{1,0:T(8,128)(2,1)S(1)}, u32[]{:S(2)}, u32[]{:S(2)}) collective-permute-start(bf16[256,128]{1,0:T(8,128)(2,1)S(1)} %broadcast_select_fusion.8), channel_id=1, source_target_pairs={{0,16},{1,48},{2,80},{3,112},{4,20},{5,52},{6,84},{7,116},{8,24},{... | collective-permute-start | bytes 196616 | tf_op jit(solution)/shard_map/ppermute | solution.py:470
  12.3 2.4 copies.3
  14.7 12.6 %all-to-all-start = ((bf16[16,512,128]{2,1,0:T(8,128)(2,1)}), bf16[16,512,128]{2,1,0:T(8,128)(2,1)S(1)}, u32[]{:S(2)}, u32[]{:S(2)}) async-start(bf16[16,512,128]{2,1,0:T(8,128)(2,1)} %copies.3), calls=%async_computation | async-start | bytes 4194304 | tf_op jit(solution)/shard_map/all_to_all | solution.py:57
  27.3 17.7 %feature_slice.1 = bf16[128,2048]{1,0:T(8,128)(2,1)} custom-call(s32[3]{0:T(128)} %pad_add_fusion.place_ref, bf16[128,8192]{1,0:T(8,128)(2,1)} %source.3), custom_call_target="tpu_custom_call" | custom-call | tf_op jit(solution)/shard_map/feature_slice/pallas_call | solution.py:424
  45.2 2.0 collective-permute-done.4
  49.1 7.5 %all-to-all-done = bf16[16,512,128]{2,1,0:T(8,128)(2,1)S(1)} async-done(((bf16[16,512,128]{2,1,0:T(8,128)(2,1)}), bf16[16,512,128]{2,1,0:T(8,128)(2,1)S(1)}, u32[]{:S(2)}, u32[]{:S(2)}) %all-to-all-start) | async-done | bytes 2097184 | tf_op jit(solution)/shard_map/all_to_all | solution.py:57
  56.7 2.1 fusion
  62.3 2.0 collective-permute-done.7
  64.3 2.7 %collective-permute-done.5 = f32[128,128]{1,0:T(8,128)S(1)} collective-permute-done((f32[128,128]{1,0:T(8,128)S(1)}, f32[128,128]{1,0:T(8,128)S(1)}, u32[]{:S(2)}, u32[]{:S(2)}) %collective-permute-start.5) | collective-permute-done | bytes 65568 | tf_op jit(solution)/shard_map/ppermute | solution.py:49
  68.5 3.9 %collective-permute-start.8 = (bf16[128,128]{1,0:T(8,128)(2,1)S(1)}, bf16[128,128]{1,0:T(8,128)(2,1)S(1)}, u32[]{:S(2)}, u32[]{:S(2)}) collective-permute-start(bf16[128,128]{1,0:T(8,128)(2,1)S(1)} %fusion.10.mine), channel_id=1, source_target_pairs={{0,16},{4,20},{8,24},{12,28},{16,0},{20,4},{24,8},{28,12},{32,48},... | collective-permute-start | bytes 98312 | tf_op jit(solution)/shard_map/ppermute | solution.py:45
  72.4 4.0 %collective-permute-done.8.other = bf16[128,128]{1,0:T(8,128)(2,1)S(1)} collective-permute-done((bf16[128,128]{1,0:T(8,128)(2,1)S(1)}, bf16[128,128]{1,0:T(8,128)(2,1)S(1)}, u32[]{:S(2)}, u32[]{:S(2)}) %collective-permute-start.8) | collective-permute-done | bytes 32800 | tf_op jit(solution)/shard_map/ppermute | solution.py:45
  79.0 5.1 %all-to-all-start.1 = ((bf16[16,256,128]{2,1,0:T(8,128)(2,1)}), bf16[16,256,128]{2,1,0:T(8,128)(2,1)S(1)}, u32[]{:S(2)}, u32[]{:S(2)}) async-start(bf16[16,256,128]{2,1,0:T(8,128)(2,1)} %copies.4), calls=%async_computation.1 | async-start | bytes 2097152 | tf_op jit(solution)/shard_map/all_to_all | solution.py:57
  84.0 3.3 %pack.1 = (bf16[16,128,256]{2,1,0:T(8,128)(2,1)}, bf16[16,128,256]{2,1,0:T(8,128)(2,1)}) custom-call(bf16[128,8192]{1,0:T(8,128)(2,1)} %source.3), custom_call_target="tpu_custom_call" | custom-call | tf_op jit(solution)/shard_map/pack/pallas_call | solution.py:437
  89.2 6.5 %all-to-all-done.1 = bf16[16,256,128]{2,1,0:T(8,128)(2,1)S(1)} async-done(((bf16[16,256,128]{2,1,0:T(8,128)(2,1)}), bf16[16,256,128]{2,1,0:T(8,128)(2,1)S(1)}, u32[]{:S(2)}, u32[]{:S(2)}) %all-to-all-start.1) | async-done | bytes 1048608 | tf_op jit(solution)/shard_map/all_to_all | solution.py:57
  98.7 7.4 %attention.1 = (bf16[128,512]{1,0:T(8,128)(2,1)S(1)}, bf16[128,512]{1,0:T(8,128)(2,1)S(1)}, f32[32,128,128]{2,1,0:T(8,128)S(1)}, f32[32,128,128]{2,1,0:T(8,128)}) custom-call(s32[3]{0:T(128)S(1)} %copy-done.9, bf16[128,512]{1,0:T(8,128)(2,1)S(1)} %get-tuple-element.78.q_keep, bf16[128,512]{1,0:T(8,128)(2,1)S(1)} %collective-permute-done.q_got, ...), custom_call_target="tpu_custom_call" | custom-call | tf_op jit(solution)/shard_map/attention/pallas_call | solution.py:271
  107.5 9.2 %all-to-all-start.3 = ((bf16[16,128,256]{2,1,0:T(8,128)(2,1)}), bf16[16,128,256]{2,1,0:T(8,128)(2,1)S(1)}, u32[]{:S(2)}, u32[]{:S(2)}) async-start(bf16[16,128,256]{2,1,0:T(8,128)(2,1)} %get-tuple-element.45), calls=%async_computation.3 | async-start | bytes 2097152 | tf_op jit(solution)/shard_map/all_to_all | solution.py:57
  116.7 3.3 %add.102 = f32[32,128,128]{2,1,0:T(8,128)} add(f32[32,128,128]{2,1,0:T(8,128)S(1)} %get-tuple-element.43, f32[32,128,128]{2,1,0:T(8,128)} %collective-permute-done.16) | non-fusion elementwise | flops 524288 | bytes 6291456 | tf_op jit(solution)/shard_map/add | solution.py:524
  120.0 13.7 %all-to-all-done.3 = bf16[16,128,256]{2,1,0:T(8,128)(2,1)S(1)} async-done(((bf16[16,128,256]{2,1,0:T(8,128)(2,1)}), bf16[16,128,256]{2,1,0:T(8,128)(2,1)S(1)}, u32[]{:S(2)}, u32[]{:S(2)}) %all-to-all-start.3) | async-done | bytes 1048608 | tf_op jit(solution)/shard_map/all_to_all | solution.py:57
  134.7 5.0 %all-to-all-start.4 = ((f32[16,256,128]{2,1,0:T(8,128)}), f32[16,256,128]{2,1,0:T(8,128)S(1)}, u32[]{:S(2)}, u32[]{:S(2)}) async-start(f32[16,256,128]{2,1,0:T(8,128)} %bitcast.129), calls=%async_computation.4 | async-start | bytes 4194304 | tf_op jit(solution)/shard_map/all_to_all | solution.py:57
  140.3 2.3 collective-permute-start.12
  144.5 22.6 %all-to-all-done.4 = f32[16,256,128]{2,1,0:T(8,128)S(1)} async-done(((f32[16,256,128]{2,1,0:T(8,128)}), f32[16,256,128]{2,1,0:T(8,128)S(1)}, u32[]{:S(2)}, u32[]{:S(2)}) %all-to-all-start.4) | async-done | bytes 2097184 | tf_op jit(solution)/shard_map/all_to_all | solution.py:57
  168.4 5.5 %all-to-all-start.2 = ((bf16[16,128,256]{2,1,0:T(8,128)(2,1)}), bf16[16,128,256]{2,1,0:T(8,128)(2,1)}, u32[]{:S(2)}, u32[]{:S(2)}) async-start(bf16[16,128,256]{2,1,0:T(8,128)(2,1)} %get-tuple-element.42), calls=%async_computation.2 | async-start | bytes 2097152 | tf_op jit(solution)/shard_map/all_to_all | solution.py:57
  177.2 2.7 %short_attention.1 = (bf16[128,512]{1,0:T(8,128)(2,1)}, bf16[128,512]{1,0:T(8,128)(2,1)}, f32[128,128]{1,0:T(8,128)}, f32[128,128]{1,0:T(8,128)}) custom-call(s32[3]{0:T(128)} %pad_add_fusion.place_ref, bf16[128,512]{1,0:T(8,128)(2,1)} %copy-done, bf16[128,512]{1,0:T(8,128)(2,1)} %copy-done.3, bf16[128,512]{1,0:T(8,128)(2,1)} %copy-done.1, ...), custom_call_target="tpu_custom_call" | custom-call | tf_op jit(solution)/shard_map/short_attention/pallas_call | solution.py:258
  182.4 3.8 %collective-permute-start.19 = (f32[128,128]{1,0:T(8,128)}, f32[128,128]{1,0:T(8,128)}, u32[]{:S(2)}, u32[]{:S(2)}) collective-permute-start(f32[128,128]{1,0:T(8,128)} %slice_select_fusion), channel_id=1, source_target_pairs={{0,16},{4,20},{8,24},{12,28},{16,0},{20,4},{24,8},{28,12},{32,48},... | collective-permute-start | bytes 196616 | tf_op jit(solution)/shard_map/ppermute | solution.py:45
  187.8 3.2 %collective-permute-done.19 = f32[128,128]{1,0:T(8,128)} collective-permute-done((f32[128,128]{1,0:T(8,128)}, f32[128,128]{1,0:T(8,128)}, u32[]{:S(2)}, u32[]{:S(2)}) %collective-permute-start.19) | collective-permute-done | bytes 65568 | tf_op jit(solution)/shard_map/ppermute | solution.py:45
  195.7 7.3 %all-to-all-start.5 = ((bf16[16,256,128]{2,1,0:T(8,128)(2,1)}), bf16[16,256,128]{2,1,0:T(8,128)(2,1)}, u32[]{:S(2)}, u32[]{:S(2)}) async-start(bf16[16,256,128]{2,1,0:T(8,128)(2,1)} %copies.5), calls=%async_computation.5 | async-start | bytes 2097152 | tf_op jit(solution)/shard_map/all_to_all | solution.py:57
  204.2 14.7 %all-to-all-done.5.grads_ref = bf16[16,256,128]{2,1,0:T(8,128)(2,1)} async-done(((bf16[16,256,128]{2,1,0:T(8,128)(2,1)}), bf16[16,256,128]{2,1,0:T(8,128)(2,1)}, u32[]{:S(2)}, u32[]{:S(2)}) %all-to-all-start.5) | async-done | bytes 1048608 | tf_op jit(solution)/shard_map/all_to_all | solution.py:57
  218.9 4.6 %owned.1 = (f32[128,128]{1,0:T(8,128)}, f32[128,128]{1,0:T(8,128)}, f32[2,128,128]{2,1,0:T(8,128)}) custom-call(s32[3]{0:T(128)} %pad_add_fusion.place_ref, bf16[2048,256]{1,0:T(8,128)(2,1)} %bitcast.29.mine_first, bf16[2048,256]{1,0:T(8,128)(2,1)} %bitcast.134, bf16[2048,256]{1,0:T(8,128)(2,1)} %collective-permute-done.17.other_first, ...), custom_call_target="tpu_custom_call" | custom-call | tf_op jit(solution)/shard_map/owned/pallas_call | solution.py:357
  223.5 4.2 %collective-permute-start.21 = (f32[2,128,128]{2,1,0:T(8,128)}, f32[2,128,128]{2,1,0:T(8,128)S(1)}, u32[]{:S(2)}, u32[]{:S(2)}) collective-permute-start(f32[2,128,128]{2,1,0:T(8,128)} %get-tuple-element.51), channel_id=1, source_target_pairs={{0,16},{4,20},{8,24},{12,28},{16,0},{20,4},{24,8},{28,12},{32,48},... | collective-permute-start | bytes 393224 | tf_op jit(solution)/shard_map/ppermute | solution.py:45
  228.9 6.3 %collective-permute-done.21 = f32[2,128,128]{2,1,0:T(8,128)S(1)} collective-permute-done((f32[2,128,128]{2,1,0:T(8,128)}, f32[2,128,128]{2,1,0:T(8,128)S(1)}, u32[]{:S(2)}, u32[]{:S(2)}) %collective-permute-start.21) | collective-permute-done | bytes 131104 | tf_op jit(solution)/shard_map/ppermute | solution.py:45
  237.0 2.0 join.1
  241.7 4.5 %input.1 = bf16[128,2048]{1,0:T(8,128)(2,1)} custom-call(s32[3]{0:T(128)} %pad_add_fusion.place_ref, bf16[4,2048,128]{2,1,0:T(8,128)(2,1)} %bitcast.131, bf16[4,2048,128]{2,1,0:T(8,128)(2,1)} %collective-permute-done.23.other_weight, bf16[2,128,128]{2,1,0:T(8,128)(2,1)} %copy-done.29, bf16[2,128,128]{2,1,0:T(8,128)(2,1)} %copy-done.37, ...), custom_call_target="tpu_custom_call" | custom-call | tf_op jit(solution)/shard_map/input/pallas_call | solution.py:393
  (188 shorter events, 44.1 us)
Async XLA Ops:
  1.5 8.5 %collective-permute-start.2 = (bf16[256,128]{1,0:T(8,128)(2,1)S(1)}, bf16[256,128]{1,0:T(8,128)(2,1)S(1)}, u32[]{:S(2)}, u32[]{:S(2)}) collective-permute-start(bf16[256,128]{1,0:T(8,128)(2,1)S(1)} %broadcast_select_fusion.8), channel_id=1, source_target_pairs={{0,0},{1,32},{2,64},{3,96},{4,4},{5,36},{6,68},{7,100},{8,8},{9,40... | collective-permute-start | bytes 196616 | tf_op jit(solution)/shard_map/ppermute | solution.py:469
  2.2 9.5 %collective-permute-start.3 = (bf16[256,128]{1,0:T(8,128)(2,1)S(1)}, bf16[256,128]{1,0:T(8,128)(2,1)S(1)}, u32[]{:S(2)}, u32[]{:S(2)}) collective-permute-start(bf16[256,128]{1,0:T(8,128)(2,1)S(1)} %broadcast_select_fusion.8), channel_id=1, source_target_pairs={{0,16},{1,48},{2,80},{3,112},{4,20},{5,52},{6,84},{7,116},{8,24},{... | collective-permute-start | bytes 196616 | tf_op jit(solution)/shard_map/ppermute | solution.py:470
  14.7 42.0 %all-to-all-start = ((bf16[16,512,128]{2,1,0:T(8,128)(2,1)}), bf16[16,512,128]{2,1,0:T(8,128)(2,1)S(1)}, u32[]{:S(2)}, u32[]{:S(2)}) async-start(bf16[16,512,128]{2,1,0:T(8,128)(2,1)} %copies.3), calls=%async_computation | async-start | bytes 4194304 | tf_op jit(solution)/shard_map/all_to_all | solution.py:57
  45.0 2.2 collective-permute-start.4
  59.6 4.7 %collective-permute-start.7 = (f32[128,128]{1,0:T(8,128)S(1)}, f32[128,128]{1,0:T(8,128)S(1)}, u32[]{:S(2)}, u32[]{:S(2)}) collective-permute-start(f32[128,128]{1,0:T(8,128)S(1)} %slice_bitcast_fusion.2), channel_id=1, source_target_pairs={{0,3},{1,0},{2,1},{3,2},{4,7},{5,4},{6,5},{7,6},{8,11},{9,8},{10,9... | collective-permute-start | bytes 196616 | tf_op jit(solution)/shard_map/ppermute | solution.py:49
  60.9 6.2 %collective-permute-start.5 = (f32[128,128]{1,0:T(8,128)S(1)}, f32[128,128]{1,0:T(8,128)S(1)}, u32[]{:S(2)}, u32[]{:S(2)}) collective-permute-start(f32[128,128]{1,0:T(8,128)S(1)} %slice_bitcast_fusion.4), channel_id=1, source_target_pairs={{0,1},{1,2},{2,3},{3,0},{4,5},{5,6},{6,7},{7,4},{8,9},{9,10},{10,1... | collective-permute-start | bytes 196616 | tf_op jit(solution)/shard_map/ppermute | solution.py:49
  61.7 6.6 %collective-permute-start.6 = (f32[128,128]{1,0:T(8,128)S(1)}, f32[128,128]{1,0:T(8,128)S(1)}, u32[]{:S(2)}, u32[]{:S(2)}) collective-permute-start(f32[128,128]{1,0:T(8,128)S(1)} %slice_bitcast_fusion.3), channel_id=1, source_target_pairs={{0,2},{1,3},{2,0},{3,1},{4,6},{5,7},{6,4},{7,5},{8,10},{9,11},{10,... | collective-permute-start | bytes 196616 | tf_op jit(solution)/shard_map/ppermute | solution.py:49
  68.5 7.9 %collective-permute-start.8 = (bf16[128,128]{1,0:T(8,128)(2,1)S(1)}, bf16[128,128]{1,0:T(8,128)(2,1)S(1)}, u32[]{:S(2)}, u32[]{:S(2)}) collective-permute-start(bf16[128,128]{1,0:T(8,128)(2,1)S(1)} %fusion.10.mine), channel_id=1, source_target_pairs={{0,16},{4,20},{8,24},{12,28},{16,0},{20,4},{24,8},{28,12},{32,48},... | collective-permute-start | bytes 98312 | tf_op jit(solution)/shard_map/ppermute | solution.py:45
  79.0 16.7 %all-to-all-start.1 = ((bf16[16,256,128]{2,1,0:T(8,128)(2,1)}), bf16[16,256,128]{2,1,0:T(8,128)(2,1)S(1)}, u32[]{:S(2)}, u32[]{:S(2)}) async-start(bf16[16,256,128]{2,1,0:T(8,128)(2,1)} %copies.4), calls=%async_computation.1 | async-start | bytes 2097152 | tf_op jit(solution)/shard_map/all_to_all | solution.py:57
  95.7 3.0 %collective-permute-start.9 = (bf16[32,128,128]{2,1,0:T(8,128)(2,1)S(1)}, bf16[32,128,128]{2,1,0:T(8,128)(2,1)S(1)}, u32[]{:S(2)}, u32[]{:S(2)}) collective-permute-start(bf16[32,128,128]{2,1,0:T(8,128)(2,1)S(1)} %bitcast.127), channel_id=1, source_target_pairs={{0,128},{128,0},{1,129},{129,1},{2,130},{130,2},{3,131},{131,3},{4... | collective-permute-start | bytes 3145736 | tf_op jit(solution)/shard_map/ppermute | solution.py:41
  95.9 2.6 %collective-permute-start = (bf16[128,512]{1,0:T(8,128)(2,1)S(1)}, bf16[128,512]{1,0:T(8,128)(2,1)S(1)}, u32[]{:S(2)}, u32[]{:S(2)}) collective-permute-start(bf16[128,512]{1,0:T(8,128)(2,1)S(1)} %get-tuple-element.77), channel_id=1, source_target_pairs={{0,128},{128,0},{1,129},{129,1},{2,130},{130,2},{3,131},{131,3},{4... | collective-permute-start | bytes 393224 | tf_op jit(solution)/shard_map/ppermute | solution.py:41
  107.4 9.3 %collective-permute-start.16 = (f32[32,128,128]{2,1,0:T(8,128)}, f32[32,128,128]{2,1,0:T(8,128)}, u32[]{:S(2)}, u32[]{:S(2)}) collective-permute-start(f32[32,128,128]{2,1,0:T(8,128)} %get-tuple-element.44), channel_id=1, source_target_pairs={{0,128},{128,0},{1,129},{129,1},{2,130},{130,2},{3,131},{131,3},{4... | collective-permute-start | bytes 6291464 | tf_op jit(solution)/shard_map/ppermute | solution.py:41
  107.5 26.1 %all-to-all-start.3 = ((bf16[16,128,256]{2,1,0:T(8,128)(2,1)}), bf16[16,128,256]{2,1,0:T(8,128)(2,1)S(1)}, u32[]{:S(2)}, u32[]{:S(2)}) async-start(bf16[16,128,256]{2,1,0:T(8,128)(2,1)} %get-tuple-element.45), calls=%async_computation.3 | async-start | bytes 2097152 | tf_op jit(solution)/shard_map/all_to_all | solution.py:57
  134.7 32.4 %all-to-all-start.4 = ((f32[16,256,128]{2,1,0:T(8,128)}), f32[16,256,128]{2,1,0:T(8,128)S(1)}, u32[]{:S(2)}, u32[]{:S(2)}) async-start(f32[16,256,128]{2,1,0:T(8,128)} %bitcast.129), calls=%async_computation.4 | async-start | bytes 4194304 | tf_op jit(solution)/shard_map/all_to_all | solution.py:57
  140.3 33.6 %collective-permute-start.12 = (f32[128,128]{1,0:T(8,128)}, f32[128,128]{1,0:T(8,128)}, u32[]{:S(2)}, u32[]{:S(2)}) collective-permute-start(f32[128,128]{1,0:T(8,128)} %slice.143), channel_id=1, source_target_pairs={{0,3},{1,0},{2,1},{3,2},{4,7},{5,4},{6,5},{7,6},{8,11},{9,8},{10,9... | collective-permute-start | bytes 196616 | tf_op jit(solution)/shard_map/ppermute | solution.py:49
  143.3 30.7 %collective-permute-start.10 = (f32[128,128]{1,0:T(8,128)}, f32[128,128]{1,0:T(8,128)}, u32[]{:S(2)}, u32[]{:S(2)}) collective-permute-start(f32[128,128]{1,0:T(8,128)} %slice.141), channel_id=1, source_target_pairs={{0,1},{1,2},{2,3},{3,0},{4,5},{5,6},{6,7},{7,4},{8,9},{9,10},{10,1... | collective-permute-start | bytes 196616 | tf_op jit(solution)/shard_map/ppermute | solution.py:49
  143.9 30.1 %collective-permute-start.11 = (f32[128,128]{1,0:T(8,128)}, f32[128,128]{1,0:T(8,128)}, u32[]{:S(2)}, u32[]{:S(2)}) collective-permute-start(f32[128,128]{1,0:T(8,128)} %slice.142), channel_id=1, source_target_pairs={{0,2},{1,3},{2,0},{3,1},{4,6},{5,7},{6,4},{7,5},{8,10},{9,11},{10,... | collective-permute-start | bytes 196616 | tf_op jit(solution)/shard_map/ppermute | solution.py:49
  168.4 18.6 %all-to-all-start.2 = ((bf16[16,128,256]{2,1,0:T(8,128)(2,1)}), bf16[16,128,256]{2,1,0:T(8,128)(2,1)}, u32[]{:S(2)}, u32[]{:S(2)}) async-start(bf16[16,128,256]{2,1,0:T(8,128)(2,1)} %get-tuple-element.42), calls=%async_computation.2 | async-start | bytes 2097152 | tf_op jit(solution)/shard_map/all_to_all | solution.py:57
  179.9 8.0 %collective-permute-start.20 = (f32[128,128]{1,0:T(8,128)}, f32[128,128]{1,0:T(8,128)S(1)}, u32[]{:S(2)}, u32[]{:S(2)}) collective-permute-start(f32[128,128]{1,0:T(8,128)} %get-tuple-element.49), channel_id=1, source_target_pairs={{0,128},{128,0},{1,129},{129,1},{2,130},{130,2},{3,131},{131,3},{4... | collective-permute-start | bytes 196616 | tf_op jit(solution)/shard_map/ppermute | solution.py:41
  182.4 8.6 %collective-permute-start.19 = (f32[128,128]{1,0:T(8,128)}, f32[128,128]{1,0:T(8,128)}, u32[]{:S(2)}, u32[]{:S(2)}) collective-permute-start(f32[128,128]{1,0:T(8,128)} %slice_select_fusion), channel_id=1, source_target_pairs={{0,16},{4,20},{8,24},{12,28},{16,0},{20,4},{24,8},{28,12},{32,48},... | collective-permute-start | bytes 196616 | tf_op jit(solution)/shard_map/ppermute | solution.py:45
  187.0 17.2 %collective-permute-start.17 = (bf16[2048,256]{1,0:T(8,128)(2,1)}, bf16[2048,256]{1,0:T(8,128)(2,1)}, u32[]{:S(2)}, u32[]{:S(2)}) collective-permute-start(bf16[2048,256]{1,0:T(8,128)(2,1)} %bitcast.29.mine_first), channel_id=1, source_target_pairs={{0,128},{128,0},{1,129},{129,1},{2,130},{130,2},{3,131},{131,3},{4... | collective-permute-start | bytes 3145736 | tf_op jit(solution)/shard_map/ppermute | solution.py:41
  187.0 52.1 %collective-permute-start.23 = (bf16[4,2048,128]{2,1,0:T(8,128)(2,1)S(1)}, bf16[4,2048,128]{2,1,0:T(8,128)(2,1)}, u32[]{:S(2)}, u32[]{:S(2)}) collective-permute-start(bf16[4,2048,128]{2,1,0:T(8,128)(2,1)S(1)} %bitcast.132), channel_id=1, source_target_pairs={{0,128},{128,0},{1,129},{129,1},{2,130},{130,2},{3,131},{131,3},{4... | collective-permute-start | bytes 6291464 | tf_op jit(solution)/shard_map/ppermute | solution.py:41
  187.5 16.7 %collective-permute-start.18 = (bf16[2048,256]{1,0:T(8,128)(2,1)S(1)}, bf16[2048,256]{1,0:T(8,128)(2,1)}, u32[]{:S(2)}, u32[]{:S(2)}) collective-permute-start(bf16[2048,256]{1,0:T(8,128)(2,1)S(1)} %bitcast.135), channel_id=1, source_target_pairs={{0,128},{128,0},{1,129},{129,1},{2,130},{130,2},{3,131},{131,3},{4... | collective-permute-start | bytes 3145736 | tf_op jit(solution)/shard_map/ppermute | solution.py:41
  195.7 23.3 %all-to-all-start.5 = ((bf16[16,256,128]{2,1,0:T(8,128)(2,1)}), bf16[16,256,128]{2,1,0:T(8,128)(2,1)}, u32[]{:S(2)}, u32[]{:S(2)}) async-start(bf16[16,256,128]{2,1,0:T(8,128)(2,1)} %copies.5), calls=%async_computation.5 | async-start | bytes 2097152 | tf_op jit(solution)/shard_map/all_to_all | solution.py:57
  203.6 32.4 %collective-permute-start.14 = (bf16[128,512]{1,0:T(8,128)(2,1)}, bf16[128,512]{1,0:T(8,128)(2,1)}, u32[]{:S(2)}, u32[]{:S(2)}) collective-permute-start(bf16[128,512]{1,0:T(8,128)(2,1)} %broadcast_select_fusion.3), channel_id=1, source_target_pairs={{0,128},{128,0},{1,129},{129,1},{2,130},{130,2},{3,131},{131,3},{4... | collective-permute-start | bytes 393224 | tf_op jit(solution)/shard_map/ppermute | solution.py:41
  203.7 24.2 %collective-permute-start.24 = (bf16[128,128]{1,0:T(8,128)(2,1)}, bf16[128,128]{1,0:T(8,128)(2,1)S(1)}, u32[]{:S(2)}, u32[]{:S(2)}) collective-permute-start(bf16[128,128]{1,0:T(8,128)(2,1)} %get-tuple-element.84.other), channel_id=1, source_target_pairs={{0,128},{128,0},{1,129},{129,1},{2,130},{130,2},{3,131},{131,3},{4... | collective-permute-start | bytes 98312 | tf_op jit(solution)/shard_map/ppermute | solution.py:41
  223.5 11.7 %collective-permute-start.21 = (f32[2,128,128]{2,1,0:T(8,128)}, f32[2,128,128]{2,1,0:T(8,128)S(1)}, u32[]{:S(2)}, u32[]{:S(2)}) collective-permute-start(f32[2,128,128]{2,1,0:T(8,128)} %get-tuple-element.51), channel_id=1, source_target_pairs={{0,16},{4,20},{8,24},{12,28},{16,0},{20,4},{24,8},{28,12},{32,48},... | collective-permute-start | bytes 393224 | tf_op jit(solution)/shard_map/ppermute | solution.py:45
  227.8 8.6 %collective-permute-start.15 = (bf16[128,512]{1,0:T(8,128)(2,1)S(1)}, bf16[128,512]{1,0:T(8,128)(2,1)S(1)}, u32[]{:S(2)}, u32[]{:S(2)}) collective-permute-start(bf16[128,512]{1,0:T(8,128)(2,1)S(1)} %broadcast_select_fusion.2), channel_id=1, source_target_pairs={{0,128},{128,0},{1,129},{129,1},{2,130},{130,2},{3,131},{131,3},{4... | collective-permute-start | bytes 393224 | tf_op jit(solution)/shard_map/ppermute | solution.py:41
  227.9 11.2 %collective-permute-start.25 = (bf16[2,128,128]{2,1,0:T(8,128)(2,1)S(1)}, bf16[2,128,128]{2,1,0:T(8,128)(2,1)S(1)}, u32[]{:S(2)}, u32[]{:S(2)}) collective-permute-start(bf16[2,128,128]{2,1,0:T(8,128)(2,1)S(1)} %pad_maximum_fusion.2.refs_0_), channel_id=1, source_target_pairs={{0,1},{1,2},{2,3},{3,0},{4,5},{5,6},{6,7},{7,4},{8,9},{9,10},{10,1... | collective-permute-start | bytes 196616 | tf_op jit(solution)/shard_map/ppermute | solution.py:49
  235.2 5.2 %collective-permute-start.26 = (bf16[2,128,128]{2,1,0:T(8,128)(2,1)S(1)}, bf16[2,128,128]{2,1,0:T(8,128)(2,1)S(1)}, u32[]{:S(2)}, u32[]{:S(2)}) collective-permute-start(bf16[2,128,128]{2,1,0:T(8,128)(2,1)S(1)} %pad_maximum_fusion.2.refs_0_), channel_id=1, source_target_pairs={{0,2},{1,3},{2,0},{3,1},{4,6},{5,7},{6,4},{7,5},{8,10},{9,11},{10,... | collective-permute-start | bytes 196616 | tf_op jit(solution)/shard_map/ppermute | solution.py:49
  236.0 5.0 %collective-permute-start.27 = (bf16[2,128,128]{2,1,0:T(8,128)(2,1)S(1)}, bf16[2,128,128]{2,1,0:T(8,128)(2,1)S(1)}, u32[]{:S(2)}, u32[]{:S(2)}) collective-permute-start(bf16[2,128,128]{2,1,0:T(8,128)(2,1)S(1)} %pad_maximum_fusion.2.refs_0_), channel_id=1, source_target_pairs={{0,3},{1,0},{2,1},{3,2},{4,7},{5,4},{6,5},{7,6},{8,11},{9,8},{10,9... | collective-permute-start | bytes 196616 | tf_op jit(solution)/shard_map/ppermute | solution.py:49
  236.4 9.8 %collective-permute-start.22 = (f32[128,128]{1,0:T(8,128)S(1)}, f32[128,128]{1,0:T(8,128)S(1)}, u32[]{:S(2)}, u32[]{:S(2)}) collective-permute-start(f32[128,128]{1,0:T(8,128)S(1)} %fusion.6), channel_id=1, source_target_pairs={{0,128},{128,0},{1,129},{129,1},{2,130},{130,2},{3,131},{131,3},{4... | collective-permute-start | bytes 196616 | tf_op jit(solution)/shard_map/ppermute | solution.py:41
  (48 other events, 503.8 us)

commit v4 on v3

--- a/solution.py
+++ b/solution.py
@@ -1,4 +1,3 @@
-import functools
 import math
 
 import jax
@@ -45,6 +44,20 @@
     return lax.ppermute(array, "ctx", ACROSS)
 
 
+def diagonal(array):
+    pairs = []
+    for source, target in ACROSS:
+        pairs += [(source, NX * NZ * NY + target), (NX * NZ * NY + source, target)]
+    return lax.ppermute(array, ("group", "ctx"), pairs)
+
+
+def across_cores(array, step):
+    pairs = [
+        (core * NT + t, (1 - core) * NT + (t + step) % NT) for core in range(2) for t in range(NT)
+    ]
+    return lax.ppermute(array, ("group", "tp"), pairs)
+
+
 def along(array, step):
     return lax.ppermute(array, "tp", [(t, (t + step) % NT) for t in range(NT)])
 
@@ -59,32 +72,8 @@
     )
 
 
-def copies_kernel(by_zone, place_ref, mine, other, target, pair, sems):
-    upper = jnp.logical_and(by_zone, ((place_ref[1] >> 2) & 1) == 1)
-    rows = mine.shape[0]
-    pair[:rows] = jnp.where(upper, other[...], mine[...])
-    pair[rows:] = jnp.where(upper, mine[...], other[...])
-    copies = [pltpu.make_async_copy(pair, target.at[i], sems.at[i]) for i in range(NX * NY)]
-    for copy in copies:
-        copy.start()
-    for copy in copies:
-        copy.wait()
-
-
-def plane_copies(place, mine, other, by_zone=True):
-    rows, width = mine.shape
-    vmem = pl.BlockSpec(memory_space=pltpu.VMEM)
-    return pl.pallas_call(
-        functools.partial(copies_kernel, by_zone),
-        out_shape=jax.ShapeDtypeStruct((NX * NY, 2 * rows, width), mine.dtype),
-        in_specs=[pl.BlockSpec(memory_space=pltpu.SMEM), vmem, vmem],
-        out_specs=pl.BlockSpec(memory_space=pl.ANY),
-        scratch_shapes=[
-            pltpu.VMEM((2 * rows, width), mine.dtype),
-            pltpu.SemaphoreType.DMA((NX * NY,)),
-        ],
-        name="copies",
-    )(place, mine, other)
+def plane_copies(block):
+    return jnp.broadcast_to(block[None], (NX * NY, *block.shape))
 
 
 def turn(rows, cosine, sine):
@@ -321,7 +310,7 @@
 
 def owned_kernel(
     place_ref, mine_first, mine_second, other_first, other_second, grads_ref,
-    here, beside, leaving,
+    here, above, beside, opposite,
     sums, pieces,
 ):
     step = pl.program_id(0)
@@ -345,9 +334,9 @@
         core = place_ref[0]
         zone = (place_ref[1] >> 2) & 1
         here[...] = pieces[core * NZ + zone]
-        leaving[0] = pieces[core * NZ + 1 - zone]
+        above[...] = pieces[core * NZ + 1 - zone]
         beside[...] = pieces[(1 - core) * NZ + zone]
-        leaving[1] = pieces[(1 - core) * NZ + 1 - zone]
+        opposite[...] = pieces[(1 - core) * NZ + 1 - zone]
 
 
 def owned_pieces(place, *arrays):
@@ -357,13 +346,9 @@
     return pl.pallas_call(
         owned_kernel,
         grid=(NX,),
-        out_shape=(piece, piece, jax.ShapeDtypeStruct((2, TOK, HD), F32)),
+        out_shape=(piece,) * 4,
         in_specs=[pl.BlockSpec(memory_space=pltpu.SMEM)] + [columns] * 4 + [grads],
-        out_specs=(
-            pl.BlockSpec((TOK, HD), lambda i: (0, 0)),
-            pl.BlockSpec((TOK, HD), lambda i: (0, 0)),
-            pl.BlockSpec((2, TOK, HD), lambda i: (0, 0, 0)),
-        ),
+        out_specs=(pl.BlockSpec((TOK, HD), lambda i: (0, 0)),) * 4,
         scratch_shapes=[
             pltpu.VMEM((2, HD, NZ * TOK), F32),
             pltpu.VMEM((2 * NZ, TOK, HD), F32),
@@ -373,60 +358,90 @@
 
 
 def input_kernel(place_ref, weight, other_weight, *refs):
-    grads, target = refs[:NT], refs[NT]
+    grads, target = refs[: 2 * NT], refs[2 * NT]
     heads = [(place_ref[2] - d) & (NT - 1) for d in range(NT)]
-    left = jnp.concatenate([g[part] for g in grads for part in range(2)], 1)
+    left = jnp.concatenate([g[...] for g in grads], 1)
+    right = jnp.concatenate([w[head] for head in heads for w in (weight, other_weight)], 1)
+    target[...] = product(left, right, 1, 1).astype(BF16)
+
+
+def input_product(place, weight, other_weight, *grads):
+    heads, features, width = weight.shape
+    step = features // (NZ * NY)
+    weights = pl.BlockSpec((heads, step, width), lambda y, z: (0, y * NZ + z, 0))
+    whole = pl.BlockSpec((TOK, HD), lambda y, z: (0, 0))
+    return pl.pallas_call(
+        input_kernel,
+        grid=(NY, NZ),
+        out_shape=jax.ShapeDtypeStruct((TOK, features), BF16),
+        in_specs=[pl.BlockSpec(memory_space=pltpu.SMEM)] + [weights] * 2 + [whole] * (2 * NT),
+        out_specs=pl.BlockSpec((TOK, step), lambda y, z: (0, z * NY + y)),
+        name="input",
+    )(place, weight, other_weight, *grads)
+
+
+def grads_kernel(
+    place_ref, here, got, short_keep, short_got, cosine_ref, sine_ref,
+    own_ref, other_ref, target, block, sems,
+):
+    long_core = place_ref[0] == 0
+    long_part = here[...] + got[...]
+    short_part = short_keep[...] + short_got[...]
+    rows = jnp.concatenate(
+        [
+            jnp.where(long_core, long_part, short_part),
+            jnp.where(long_core, short_part, long_part),
+        ],
+        0,
+    )
+    turned = rows * cosine_ref[...] + pltpu.roll(rows, HALF, 1) * sine_ref[...]
+    rows = jnp.where(long_core, turned, rows).astype(BF16)
+    block[...] = rows
+    copies = [pltpu.make_async_copy(block, target.at[i], sems.at[i]) for i in range(NX * NY)]
+    for copy in copies:
+        copy.start()
+    own_ref[...] = rows[:TOK]
+    other_ref[...] = rows[TOK:]
+    for copy in copies:
+        copy.wait()
+
+
+def grads_call(place, *arrays):
+    vmem = pl.BlockSpec(memory_space=pltpu.VMEM)
+    half = jax.ShapeDtypeStruct((TOK, HD), BF16)
+    return pl.pallas_call(
+        grads_kernel,
+        out_shape=(half, half, jax.ShapeDtypeStruct((NX * NY, 2 * TOK, HD), BF16)),
+        in_specs=[pl.BlockSpec(memory_space=pltpu.SMEM)] + [vmem] * len(arrays),
+        out_specs=(vmem, vmem, pl.BlockSpec(memory_space=pl.ANY)),
+        scratch_shapes=[
+            pltpu.VMEM((2 * TOK, HD), BF16),
+            pltpu.SemaphoreType.DMA((NX * NY,)),
+        ],
+        name="grads",
+    )(place, *arrays)
+
+
+def slice_kernel(place_ref, source, target):
     step = target.shape[1] // (NZ * NY)
     for y in range(NY):
         for z in range(NZ):
-            source = slice((y * NZ + z) * step, (y * NZ + z + 1) * step)
-            right = jnp.concatenate(
-                [w[head, source] for head in heads for w in (weight, other_weight)], 1
-            )
-            target[:, (z * NY + y) * step : (z * NY + y + 1) * step] = product(
-                left, right, 1, 1
-            ).astype(BF16)
-
-
-def input_product(place, weight, other_weight, *grads):
-    vmem = pl.BlockSpec(memory_space=pltpu.VMEM)
-    return pl.pallas_call(
-        input_kernel,
-        out_shape=jax.ShapeDtypeStruct((TOK, weight.shape[1]), BF16),
-        in_specs=[pl.BlockSpec(memory_space=pltpu.SMEM)] + [vmem] * (2 + NT),
-        out_specs=vmem,
-        name="input",
-    )(place, weight, other_weight, *grads)
-
-
-def slice_kernel(place_ref, source, target, sems):
-    step = target.shape[1] // (NZ * NY)
-    copies = []
-    for y in range(NY):
-        for z in range(NZ):
-            i = y * NZ + z
-            first = pl.multiple_of((place_ref[2] * (NZ * NY) + z * NY + y) * step, step)
-            copies.append(
-                pltpu.make_async_copy(
-                    source.at[:, pl.ds(first, step)],
-                    target.at[:, i * step : (i + 1) * step],
-                    sems.at[i],
-                )
-            )
-    for copy in copies:
-        copy.start()
-    for copy in copies:
-        copy.wait()
+            i, j = y * NZ + z, z * NY + y
+            target[:, i * step : (i + 1) * step] = source[:, j * step : (j + 1) * step]
 
 
 def feature_slice(place, activations):
     rows, features = activations.shape
+    block = (rows, features // NT)
     return pl.pallas_call(
         slice_kernel,
-        out_shape=jax.ShapeDtypeStruct((rows, features // NT), activations.dtype),
-        in_specs=[pl.BlockSpec(memory_space=pltpu.SMEM), pl.BlockSpec(memory_space=pl.ANY)],
-        out_specs=pl.BlockSpec(memory_space=pl.ANY),
-        scratch_shapes=[pltpu.SemaphoreType.DMA((NZ * NY,))],
+        grid_spec=pltpu.PrefetchScalarGridSpec(
+            num_scalar_prefetch=1,
+            grid=(1,),
+            in_specs=[pl.BlockSpec(block, lambda i, place: (0, place[2]))],
+            out_specs=pl.BlockSpec(block, lambda i, place: (0, 0)),
+        ),
+        out_shape=jax.ShapeDtypeStruct(block, activations.dtype),
         name="feature_slice",
     )(place, activations)
 
@@ -461,6 +476,13 @@
     own_sin = jnp.where(is_long, sine[:TOK], sine[TOK:])
     back_cos = jnp.concatenate([own_cos, jnp.where(is_long, cosine[TOK:], cosine[:TOK])], 0)
     back_sin = jnp.concatenate([own_sin, jnp.where(is_long, sine[TOK:], sine[:TOK])], 0)
+    back_cos = jnp.concatenate([back_cos, back_cos], 1)
+    back_sin = jnp.concatenate([back_sin, -back_sin], 1)
+
+    def by_zone(mine, other):
+        return jnp.concatenate(
+            [jnp.where(upper, other, mine), jnp.where(upper, mine, other)], 0
+        )
 
     def role(first, second):
         return jnp.where(is_long, first, second)
@@ -468,7 +490,7 @@
     weight = role(key_weight, value_weight)
     near = lax.ppermute(weight, ("ctx", "tp"), TURN)
     far = lax.ppermute(weight, ("ctx", "tp"), FAR_TURN)
-    weight = plane_copies(place, near, far)
+    weight = plane_copies(by_zone(near, far))
     weight = plane_exchange(weight)
     packed = pack_columns(activations)
     weight = weight.reshape(NX, NY * weight.shape[-2], HD)
@@ -483,8 +505,8 @@
     rotated = turn(queries.astype(F32), own_cos, own_sin).astype(BF16)
     width = GH * HD
     q_keep = role(rotated[:, :width], rotated[:, width:])
+    do_keep = role(out_grad[:, :width], out_grad[:, width:])
     q_got = partner(role(rotated[:, width:], rotated[:, :width]))
-    do_keep = role(out_grad[:, :width], out_grad[:, width:])
     do_got = partner(role(out_grad[:, width:], out_grad[:, :width]))
 
     partial = jnp.einsum("tk,hkn->htn", both_slices, weight, preferred_element_type=F32)
@@ -499,7 +521,7 @@
     short_rows = role(turn(short_sum, cosine[TOK:], sine[TOK:]), short_sum).astype(BF16)
     other_short = partner(short_rows)
     across_rows = across(long_rows)
-    context = plane_copies(place, long_rows, across_rows)
+    context = plane_copies(by_zone(long_rows, across_rows))
     context = plane_exchange(context)
 
     second, context = after(packed[1], context)
@@ -522,7 +544,7 @@
     out_got, qgrad_got = partner(role(short_out, long_out)), partner(role(short_qgrad, long_qgrad))
     attention, query_grad = join_heads(place, *out_parts, out_got, qgrad_got)
     kv_sums = kv_keep + partner(kv_send)
-    short_kv = short_keep + partner(short_send)
+    short_got = partner(short_send)
     blocks, second_columns = after(kv_sums.reshape(plane, NZ * TOK, HD), second_columns)
     columns = [
         array.reshape(plane * TOK, NZ * TOK) for array in (first_columns, second_columns)
@@ -532,22 +554,23 @@
     arrived = arrived.reshape(plane, NZ, TOK, HD).sum(0)
     here = jnp.where(upper, arrived[1], arrived[0])
     there = jnp.where(upper, arrived[0], arrived[1])
-    long_kv = here + across(there)
-    grads = jnp.concatenate([role(long_kv, short_kv), role(short_kv, long_kv)], 0)
-    grads = role(turn(grads, back_cos, -back_sin), grads).astype(BF16)
-    grads_copies = plane_copies(place, grads[:TOK], grads[TOK:], False)
-    plane_grads = plane_exchange(grads_copies)
-
-    pair = jnp.stack([grads[:TOK], partner(grads[TOK:])])
-    by_step = [pair] + [along(pair, d) for d in range(1, NT)]
-    input_grad = input_product(place, weight, other_weight, *by_step)
-
-    here, beside, leaving = owned_pieces(
+    own_grads, got_grads, copies = grads_call(
+        place, here, across(there), short_keep, short_got, back_cos, back_sin
+    )
+    plane_grads = plane_exchange(copies)
+
+    mine = [own_grads] + [along(own_grads, d) for d in range(1, NT)]
+    swapped = [partner(got_grads)] + [across_cores(got_grads, d) for d in range(1, NT)]
+    input_grad = input_product(
+        place, weight, other_weight, *[g for pair in zip(mine, swapped) for g in pair]
+    )
+
+    here, above, beside, opposite = owned_pieces(
         place, columns[0], columns[1], other_columns[0], other_columns[1], plane_grads
     )
-    arrived_pieces = across(leaving)
-    cross = partner(beside + arrived_pieces[1])
-    same = here + arrived_pieces[0]
+    opposite = diagonal(opposite)
+    same = here + across(above)
+    cross = partner(beside) + opposite
     return (attention, query_grad, role(same, cross), role(cross, same), input_grad)
 
 

time: 249 us -> 249 us (level)
  blocking collectives: 0 us -> 25.3 us
  Pallas kernels: 48.4 us -> 32.3 us
  waiting for transfers between devices: 93.2 us -> 81.8 us
  other arithmetic: 17.4 us -> 21.1 us
    all_to_all x0 -> x1, blocking collectives: none -> 25.3 us  [plane_exchange(): lax.all_to_all(blocks, 'ctx', split_axis=0, concat_axis=0, tiled=True, ax...]
    pallas_call x6 -> x4, Pallas kernels: 33 us -> 16.9 us  [the longest x1 6.88 us: input_product(): pl.pallas_call(input_kernel, grid=(NY, NZ), out_shape=jax.ShapeDtypeStruc...]
    all_to_all x6 -> x5, waiting for transfers between devices: 65.8 us -> 56.2 us  [plane_exchange(): lax.all_to_all(blocks, 'ctx', split_axis=0, concat_axis=0, tiled=True, ax...]
    all_to_all x6 -> x5, starting transfers between devices: 44.6 us -> 36.4 us  [plane_exchange(): lax.all_to_all(blocks, 'ctx', split_axis=0, concat_axis=0, tiled=True, ax...]
    unnamed x94 -> x62, local copies, waits for them, and re-layouts: 7.72 us -> 2.74 us
    ppermute x3, waiting for transfers between devices: 13.5 us -> 8.59 us  [across(): return lax.ppermute(array, 'ctx', ACROSS)]
    ppermute x9, starting transfers between devices: 6.28 us -> 10.2 us  [along(): return lax.ppermute(array, 'tp', [(t, (t + step) % NT) for t in range(NT)])]
    ppermute x0 -> x4, starting transfers between devices: none -> 2.99 us  [the longest x1 2.89 us: diagonal(): return lax.ppermute(array, ('group', 'ctx'), pairs)]
  transfers between devices with their start and end apart: 34 -> 37, of which waited for: 19 -> 17; matrix products, arithmetic and copies ran while one was open for 7% -> 9% of each run, Pallas kernels for 15% -> 10%
where the time goes in v4:
time: 249 us; the launch traced here: 245 us
  waiting for transfers between devices  81.8 us (33%)
  starting transfers between devices  72.3 us (29%)
  Pallas kernels  32.3 us (13%)
  blocking collectives  25.3 us (10%)
  other arithmetic  21.1 us (8%)
  local copies, waits for them, and re-layouts  8.98 us (4%)
    all_to_all x5, waiting for transfers between devices, plane_exchange(): lax.all_to_all(blocks, 'ctx', split_axis=0, concat_axis=0, tiled=True, ax...  56.2 us
    all_to_all x5, starting transfers between devices, plane_exchange(): lax.all_to_all(blocks, 'ctx', split_axis=0, concat_axis=0, tiled=True, ax...  36.4 us
    all_to_all x1, blocking collectives, plane_exchange(): lax.all_to_all(blocks, 'ctx', split_axis=0, concat_axis=0, tiled=True, ax...  25.3 us
    ppermute x9, starting transfers between devices, along(): return lax.ppermute(array, 'tp', [(t, (t + step) % NT) for t in range(NT)])  10.2 us
    ppermute x9, waiting for transfers between devices, along(): return lax.ppermute(array, 'tp', [(t, (t + step) % NT) for t in range(NT)])  9.29 us
    ppermute x3, starting transfers between devices, across(): return lax.ppermute(array, 'ctx', ACROSS)  9.15 us
    ppermute x3, waiting for transfers between devices, across(): return lax.ppermute(array, 'ctx', ACROSS)  8.59 us
    pallas_call x1, Pallas kernels, attention_call(): pl.pallas_call(attention_kernel, out_shape=(rows, rows, blocks, blocks),...  7.4 us
  transfers between devices with their start and end apart: 37, of which 17 were waited for; matrix products, arithmetic and copies ran while one was open for 9% of the time, Pallas kernels for 10%

profile of v4, /device:TPU:8, one launch (start us, length us, event | category | flops | bytes accessed | tf_op | source)
XLA Modules:
  0.0 245.0 jit_solution(10582125169194586513)
XLA Ops:
  1.5 7.3 %collective-permute-start.2 = (bf16[256,128]{1,0:T(8,128)(2,1)S(1)}, bf16[256,128]{1,0:T(8,128)(2,1)S(1)}, u32[]{:S(2)}, u32[]{:S(2)}) collective-permute-start(bf16[256,128]{1,0:T(8,128)(2,1)S(1)} %broadcast_select_fusion.8), channel_id=1, source_target_pairs={{0,16},{1,48},{2,80},{3,112},{4,20},{5,52},{6,84},{7,116},{8,24},{... | collective-permute-start | bytes 196616 | tf_op jit(solution)/shard_map/ppermute | solution.py:492
  12.9 14.3 %all-to-all-start = ((bf16[16,512,128]{2,1,0:T(8,128)(2,1)}), bf16[16,512,128]{2,1,0:T(8,128)(2,1)S(1)}, u32[]{:S(2)}, u32[]{:S(2)}) async-start(bf16[16,512,128]{2,1,0:T(8,128)(2,1)} %broadcast_in_dim.12), calls=%async_computation | async-start | bytes 4194304 | tf_op jit(solution)/shard_map/all_to_all | solution.py:70
  27.8 2.5 %feature_slice.1 = bf16[128,2048]{1,0:T(8,128)(2,1)} custom-call(s32[3]{0:T(128)} %pad_add_fusion.place_ref, bf16[128,8192]{1,0:T(8,128)(2,1)} %source.3), custom_call_target="tpu_custom_call" | custom-call | tf_op jit(solution)/shard_map/feature_slice/pallas_call | solution.py:436
  34.4 20.1 %all-to-all-done = bf16[16,512,128]{2,1,0:T(8,128)(2,1)S(1)} async-done(((bf16[16,512,128]{2,1,0:T(8,128)(2,1)}), bf16[16,512,128]{2,1,0:T(8,128)(2,1)S(1)}, u32[]{:S(2)}, u32[]{:S(2)}) %all-to-all-start) | async-done | bytes 2097184 | tf_op jit(solution)/shard_map/all_to_all | solution.py:70
  61.7 3.8 %collective-permute-done.5 = f32[128,128]{1,0:T(8,128)S(1)} collective-permute-done((f32[128,128]{1,0:T(8,128)S(1)}, f32[128,128]{1,0:T(8,128)S(1)}, u32[]{:S(2)}, u32[]{:S(2)}) %collective-permute-start.5) | collective-permute-done | bytes 65568 | tf_op jit(solution)/shard_map/ppermute | solution.py:62
  65.8 3.4 %collective-permute-start.8 = (bf16[128,128]{1,0:T(8,128)(2,1)S(1)}, bf16[128,128]{1,0:T(8,128)(2,1)S(1)}, u32[]{:S(2)}, u32[]{:S(2)}) collective-permute-start(bf16[128,128]{1,0:T(8,128)(2,1)S(1)} %fusion.5), channel_id=1, source_target_pairs={{0,16},{4,20},{8,24},{12,28},{16,0},{20,4},{24,8},{28,12},{32,48},... | collective-permute-start | bytes 98312 | tf_op jit(solution)/shard_map/ppermute | solution.py:44
  69.1 4.5 %collective-permute-done.8 = bf16[128,128]{1,0:T(8,128)(2,1)S(1)} collective-permute-done((bf16[128,128]{1,0:T(8,128)(2,1)S(1)}, bf16[128,128]{1,0:T(8,128)(2,1)S(1)}, u32[]{:S(2)}, u32[]{:S(2)}) %collective-permute-start.8) | collective-permute-done | bytes 32800 | tf_op jit(solution)/shard_map/ppermute | solution.py:44
  74.9 5.3 %all-to-all-start.1 = ((bf16[16,256,128]{2,1,0:T(8,128)(2,1)}), bf16[16,256,128]{2,1,0:T(8,128)(2,1)S(1)}, u32[]{:S(2)}, u32[]{:S(2)}) async-start(bf16[16,256,128]{2,1,0:T(8,128)(2,1)} %broadcast_in_dim.15), calls=%async_computation.1 | async-start | bytes 2097152 | tf_op jit(solution)/shard_map/all_to_all | solution.py:70
  80.2 3.3 %pack.1 = (bf16[16,128,256]{2,1,0:T(8,128)(2,1)}, bf16[16,128,256]{2,1,0:T(8,128)(2,1)}) custom-call(bf16[128,8192]{1,0:T(8,128)(2,1)} %source.3), custom_call_target="tpu_custom_call" | custom-call | tf_op jit(solution)/shard_map/pack/pallas_call | solution.py:452
  84.6 7.8 %all-to-all-done.1 = bf16[16,256,128]{2,1,0:T(8,128)(2,1)S(1)} async-done(((bf16[16,256,128]{2,1,0:T(8,128)(2,1)}), bf16[16,256,128]{2,1,0:T(8,128)(2,1)S(1)}, u32[]{:S(2)}, u32[]{:S(2)}) %all-to-all-start.1) | async-done | bytes 1048608 | tf_op jit(solution)/shard_map/all_to_all | solution.py:70
  95.5 7.4 %attention.1 = (bf16[128,512]{1,0:T(8,128)(2,1)S(1)}, bf16[128,512]{1,0:T(8,128)(2,1)S(1)}, f32[32,128,128]{2,1,0:T(8,128)S(1)}, f32[32,128,128]{2,1,0:T(8,128)}) custom-call(s32[3]{0:T(128)S(1)} %copy-done.9, bf16[128,512]{1,0:T(8,128)(2,1)S(1)} %get-tuple-element.82.q_keep, bf16[128,512]{1,0:T(8,128)(2,1)S(1)} %collective-permute-done.q_got, ...), custom_call_target="tpu_custom_call" | custom-call | tf_op jit(solution)/shard_map/attention/pallas_call | solution.py:260
  104.3 25.3 %all_to_all.30 = bf16[16,128,256]{2,1,0:T(8,128)(2,1)} all-to-all(bf16[16,128,256]{2,1,0:T(8,128)(2,1)S(1)} %copy-done.13), channel_id=1, replica_groups={{0,4,8,12,32,36,40,44,64,68,72,76,96,100,104,108},{16,20,24,28,48,52,56..., dimensions={0} | all-to-all | bytes 2097152 | tf_op jit(solution)/shard_map/all_to_all | solution.py:70
  129.6 5.5 %all-to-all-start.2 = ((bf16[16,128,256]{2,1,0:T(8,128)(2,1)}), bf16[16,128,256]{2,1,0:T(8,128)(2,1)}, u32[]{:S(2)}, u32[]{:S(2)}) async-start(bf16[16,128,256]{2,1,0:T(8,128)(2,1)} %get-tuple-element.46), calls=%async_computation.2 | async-start | bytes 2097152 | tf_op jit(solution)/shard_map/all_to_all | solution.py:70
  135.2 3.2 %add.93 = f32[32,128,128]{2,1,0:T(8,128)} add(f32[32,128,128]{2,1,0:T(8,128)S(1)} %get-tuple-element.47, f32[32,128,128]{2,1,0:T(8,128)} %collective-permute-done.16) | non-fusion elementwise | flops 524288 | bytes 6291456 | tf_op jit(solution)/shard_map/add | solution.py:546
  138.4 11.4 %all-to-all-done.2 = bf16[16,128,256]{2,1,0:T(8,128)(2,1)} async-done(((bf16[16,128,256]{2,1,0:T(8,128)(2,1)}), bf16[16,128,256]{2,1,0:T(8,128)(2,1)}, u32[]{:S(2)}, u32[]{:S(2)}) %all-to-all-start.2) | async-done | bytes 1048608 | tf_op jit(solution)/shard_map/all_to_all | solution.py:70
  149.8 5.6 %all-to-all-start.4 = ((f32[16,256,128]{2,1,0:T(8,128)}), f32[16,256,128]{2,1,0:T(8,128)}, u32[]{:S(2)}, u32[]{:S(2)}) async-start(f32[16,256,128]{2,1,0:T(8,128)} %bitcast.97), calls=%async_computation.4 | async-start | bytes 4194304 | tf_op jit(solution)/shard_map/all_to_all | solution.py:70
  156.9 3.6 %collective-permute-start.12 = (f32[128,128]{1,0:T(8,128)S(1)}, f32[128,128]{1,0:T(8,128)S(1)}, u32[]{:S(2)}, u32[]{:S(2)}) collective-permute-start(f32[128,128]{1,0:T(8,128)S(1)} %slice.123), channel_id=1, source_target_pairs={{0,3},{1,0},{2,1},{3,2},{4,7},{5,4},{6,5},{7,6},{8,11},{9,8},{10,9... | collective-permute-start | bytes 196616 | tf_op jit(solution)/shard_map/ppermute | solution.py:62
  164.5 3.0 %collective-permute-done.10 = f32[128,128]{1,0:T(8,128)S(1)} collective-permute-done((f32[128,128]{1,0:T(8,128)S(1)}, f32[128,128]{1,0:T(8,128)S(1)}, u32[]{:S(2)}, u32[]{:S(2)}) %collective-permute-start.10) | collective-permute-done | bytes 65568 | tf_op jit(solution)/shard_map/ppermute | solution.py:62
  171.8 2.7 %short_attention.1 = (bf16[128,512]{1,0:T(8,128)(2,1)}, bf16[128,512]{1,0:T(8,128)(2,1)}, f32[128,128]{1,0:T(8,128)}, f32[128,128]{1,0:T(8,128)}) custom-call(s32[3]{0:T(128)} %pad_add_fusion.place_ref, bf16[128,512]{1,0:T(8,128)(2,1)} %copy-done, bf16[128,512]{1,0:T(8,128)(2,1)} %copy-done.3, bf16[128,512]{1,0:T(8,128)(2,1)} %copy-done.1, ...), custom_call_target="tpu_custom_call" | custom-call | tf_op jit(solution)/shard_map/short_attention/pallas_call | solution.py:247
  175.0 7.0 %all-to-all-done.4 = f32[16,256,128]{2,1,0:T(8,128)} async-done(((f32[16,256,128]{2,1,0:T(8,128)}), f32[16,256,128]{2,1,0:T(8,128)}, u32[]{:S(2)}, u32[]{:S(2)}) %all-to-all-start.4) | async-done | bytes 2097184 | tf_op jit(solution)/shard_map/all_to_all | solution.py:70
  182.0 2.4 reduce_sum.9
  185.9 3.0 %collective-permute-start.19 = (f32[128,128]{1,0:T(8,128)S(1)}, f32[128,128]{1,0:T(8,128)}, u32[]{:S(2)}, u32[]{:S(2)}) collective-permute-start(f32[128,128]{1,0:T(8,128)S(1)} %get-tuple-element.87), channel_id=1, source_target_pairs={{0,16},{4,20},{8,24},{12,28},{16,0},{20,4},{24,8},{28,12},{32,48},... | collective-permute-start | bytes 196616 | tf_op jit(solution)/shard_map/ppermute | solution.py:44
  190.6 4.0 %collective-permute-done.19.got = f32[128,128]{1,0:T(8,128)} collective-permute-done((f32[128,128]{1,0:T(8,128)S(1)}, f32[128,128]{1,0:T(8,128)}, u32[]{:S(2)}, u32[]{:S(2)}) %collective-permute-start.19) | collective-permute-done | bytes 65568 | tf_op jit(solution)/shard_map/ppermute | solution.py:44
  194.7 2.9 %grads.1 = (bf16[128,128]{1,0:T(8,128)(2,1)}, bf16[128,128]{1,0:T(8,128)(2,1)}, bf16[16,256,128]{2,1,0:T(8,128)(2,1)}) custom-call(s32[3]{0:T(128)} %pad_add_fusion.place_ref, f32[128,128]{1,0:T(8,128)} %get-tuple-element.88.here, f32[128,128]{1,0:T(8,128)} %collective-permute-done.19.got, f32[128,128]{1,0:T(8,128)} %get-tuple-element.52.short_keep, ...), custom_call_target="tpu_custom_call" | custom-call | tf_op jit(solution)/shard_map/grads/pallas_call | solution.py:412
  197.6 5.6 %all-to-all-start.5 = ((bf16[16,256,128]{2,1,0:T(8,128)(2,1)}), bf16[16,256,128]{2,1,0:T(8,128)(2,1)}, u32[]{:S(2)}, u32[]{:S(2)}) async-start(bf16[16,256,128]{2,1,0:T(8,128)(2,1)} %get-tuple-element.54), calls=%async_computation.5 | async-start | bytes 2097152 | tf_op jit(solution)/shard_map/all_to_all | solution.py:70
  206.0 9.9 %all-to-all-done.5.grads_ref = bf16[16,256,128]{2,1,0:T(8,128)(2,1)} async-done(((bf16[16,256,128]{2,1,0:T(8,128)(2,1)}), bf16[16,256,128]{2,1,0:T(8,128)(2,1)}, u32[]{:S(2)}, u32[]{:S(2)}) %all-to-all-start.5) | async-done | bytes 1048608 | tf_op jit(solution)/shard_map/all_to_all | solution.py:70
  215.8 4.6 %owned.1 = (f32[128,128]{1,0:T(8,128)}, f32[128,128]{1,0:T(8,128)}, f32[128,128]{1,0:T(8,128)}, f32[128,128]{1,0:T(8,128)}) custom-call(s32[3]{0:T(128)} %pad_add_fusion.place_ref, bf16[2048,256]{1,0:T(8,128)(2,1)} %bitcast.29.mine_first, bf16[2048,256]{1,0:T(8,128)(2,1)} %bitcast.102, bf16[2048,256]{1,0:T(8,128)(2,1)} %collective-permute-done.17.other_first, ...), custom_call_target="tpu_custom_call" | custom-call | tf_op jit(solution)/shard_map/owned/pallas_call | solution.py:346
  220.7 3.0 %collective-permute-start.22 = (f32[128,128]{1,0:T(8,128)}, f32[128,128]{1,0:T(8,128)S(1)}, u32[]{:S(2)}, u32[]{:S(2)}) collective-permute-start(f32[128,128]{1,0:T(8,128)} %get-tuple-element.57), channel_id=1, source_target_pairs={{0,128},{128,0},{1,129},{129,1},{2,130},{130,2},{3,131},{131,3},{4... | collective-permute-start | bytes 196616 | tf_op jit(solution)/shard_map/ppermute | solution.py:40
  223.7 2.9 %collective-permute-start.23 = (f32[128,128]{1,0:T(8,128)}, f32[128,128]{1,0:T(8,128)S(1)}, u32[]{:S(2)}, u32[]{:S(2)}) collective-permute-start(f32[128,128]{1,0:T(8,128)} %get-tuple-element.58), channel_id=1, source_target_pairs={{0,144},{128,16},{4,148},{132,20},{8,152},{136,24},{12,156},{140,2... | collective-permute-start | bytes 196616 | tf_op jit(solution)/shard_map/ppermute | solution.py:51
  226.6 2.7 %collective-permute-start.21 = (f32[128,128]{1,0:T(8,128)}, f32[128,128]{1,0:T(8,128)S(1)}, u32[]{:S(2)}, u32[]{:S(2)}) collective-permute-start(f32[128,128]{1,0:T(8,128)} %get-tuple-element.56), channel_id=1, source_target_pairs={{0,16},{4,20},{8,24},{12,28},{16,0},{20,4},{24,8},{28,12},{32,48},... | collective-permute-start | bytes 196616 | tf_op jit(solution)/shard_map/ppermute | solution.py:44
  229.3 3.1 %collective-permute-start.30 = (bf16[128,128]{1,0:T(8,128)(2,1)S(1)}, bf16[128,128]{1,0:T(8,128)(2,1)S(1)}, u32[]{:S(2)}, u32[]{:S(2)}) collective-permute-start(bf16[128,128]{1,0:T(8,128)(2,1)S(1)} %copy-done.20), channel_id=1, source_target_pairs={{0,3},{1,0},{2,1},{3,2},{4,7},{5,4},{6,5},{7,6},{8,11},{9,8},{10,9... | collective-permute-start | bytes 98312 | tf_op jit(solution)/shard_map/ppermute | solution.py:62
  237.4 6.9 %input.1 = bf16[128,2048]{1,0:T(8,128)(2,1)} custom-call(s32[3]{0:T(128)} %pad_add_fusion.place_ref, bf16[4,2048,128]{2,1,0:T(8,128)(2,1)} %bitcast.99, bf16[4,2048,128]{2,1,0:T(8,128)(2,1)} %collective-permute-done.24.other_weight, bf16[128,128]{1,0:T(8,128)(2,1)} %get-tuple-element.59.refs_0_, bf16[128,128]{1,0:T(8,128)(2,1)} %collective-permute-done.25.refs_1_, ...), custom_call_target="tpu_custom_call" | custom-call | tf_op jit(solution)/shard_map/input/pallas_call | solution.py:373
  (162 shorter events, 45.6 us)
Async XLA Ops:
  1.5 9.7 %collective-permute-start.2 = (bf16[256,128]{1,0:T(8,128)(2,1)S(1)}, bf16[256,128]{1,0:T(8,128)(2,1)S(1)}, u32[]{:S(2)}, u32[]{:S(2)}) collective-permute-start(bf16[256,128]{1,0:T(8,128)(2,1)S(1)} %broadcast_select_fusion.8), channel_id=1, source_target_pairs={{0,16},{1,48},{2,80},{3,112},{4,20},{5,52},{6,84},{7,116},{8,24},{... | collective-permute-start | bytes 196616 | tf_op jit(solution)/shard_map/ppermute | solution.py:492
  12.9 41.5 %all-to-all-start = ((bf16[16,512,128]{2,1,0:T(8,128)(2,1)}), bf16[16,512,128]{2,1,0:T(8,128)(2,1)S(1)}, u32[]{:S(2)}, u32[]{:S(2)}) async-start(bf16[16,512,128]{2,1,0:T(8,128)(2,1)} %broadcast_in_dim.12), calls=%async_computation | async-start | bytes 4194304 | tf_op jit(solution)/shard_map/all_to_all | solution.py:70
  57.4 4.3 %collective-permute-start.7 = (f32[128,128]{1,0:T(8,128)S(1)}, f32[128,128]{1,0:T(8,128)S(1)}, u32[]{:S(2)}, u32[]{:S(2)}) collective-permute-start(f32[128,128]{1,0:T(8,128)S(1)} %slice_bitcast_fusion), channel_id=1, source_target_pairs={{0,3},{1,0},{2,1},{3,2},{4,7},{5,4},{6,5},{7,6},{8,11},{9,8},{10,9... | collective-permute-start | bytes 196616 | tf_op jit(solution)/shard_map/ppermute | solution.py:62
  59.4 6.1 %collective-permute-start.5 = (f32[128,128]{1,0:T(8,128)S(1)}, f32[128,128]{1,0:T(8,128)S(1)}, u32[]{:S(2)}, u32[]{:S(2)}) collective-permute-start(f32[128,128]{1,0:T(8,128)S(1)} %slice_bitcast_fusion.2), channel_id=1, source_target_pairs={{0,1},{1,2},{2,3},{3,0},{4,5},{5,6},{6,7},{7,4},{8,9},{9,10},{10,1... | collective-permute-start | bytes 196616 | tf_op jit(solution)/shard_map/ppermute | solution.py:62
  59.5 6.1 %collective-permute-start.6 = (f32[128,128]{1,0:T(8,128)S(1)}, f32[128,128]{1,0:T(8,128)S(1)}, u32[]{:S(2)}, u32[]{:S(2)}) collective-permute-start(f32[128,128]{1,0:T(8,128)S(1)} %slice_bitcast_fusion.1), channel_id=1, source_target_pairs={{0,2},{1,3},{2,0},{3,1},{4,6},{5,7},{6,4},{7,5},{8,10},{9,11},{10,... | collective-permute-start | bytes 196616 | tf_op jit(solution)/shard_map/ppermute | solution.py:62
  65.8 7.9 %collective-permute-start.8 = (bf16[128,128]{1,0:T(8,128)(2,1)S(1)}, bf16[128,128]{1,0:T(8,128)(2,1)S(1)}, u32[]{:S(2)}, u32[]{:S(2)}) collective-permute-start(bf16[128,128]{1,0:T(8,128)(2,1)S(1)} %fusion.5), channel_id=1, source_target_pairs={{0,16},{4,20},{8,24},{12,28},{16,0},{20,4},{24,8},{28,12},{32,48},... | collective-permute-start | bytes 98312 | tf_op jit(solution)/shard_map/ppermute | solution.py:44
  74.9 17.6 %all-to-all-start.1 = ((bf16[16,256,128]{2,1,0:T(8,128)(2,1)}), bf16[16,256,128]{2,1,0:T(8,128)(2,1)S(1)}, u32[]{:S(2)}, u32[]{:S(2)}) async-start(bf16[16,256,128]{2,1,0:T(8,128)(2,1)} %broadcast_in_dim.15), calls=%async_computation.1 | async-start | bytes 2097152 | tf_op jit(solution)/shard_map/all_to_all | solution.py:70
  92.4 3.0 %collective-permute-start.9 = (bf16[32,128,128]{2,1,0:T(8,128)(2,1)S(1)}, bf16[32,128,128]{2,1,0:T(8,128)(2,1)S(1)}, u32[]{:S(2)}, u32[]{:S(2)}) collective-permute-start(bf16[32,128,128]{2,1,0:T(8,128)(2,1)S(1)} %bitcast.95), channel_id=1, source_target_pairs={{0,128},{128,0},{1,129},{129,1},{2,130},{130,2},{3,131},{131,3},{4... | collective-permute-start | bytes 3145736 | tf_op jit(solution)/shard_map/ppermute | solution.py:40
  104.2 31.0 %collective-permute-start.16 = (f32[32,128,128]{2,1,0:T(8,128)}, f32[32,128,128]{2,1,0:T(8,128)}, u32[]{:S(2)}, u32[]{:S(2)}) collective-permute-start(f32[32,128,128]{2,1,0:T(8,128)} %get-tuple-element.48), channel_id=1, source_target_pairs={{0,128},{128,0},{1,129},{129,1},{2,130},{130,2},{3,131},{131,3},{4... | collective-permute-start | bytes 6291464 | tf_op jit(solution)/shard_map/ppermute | solution.py:40
  129.6 20.2 %all-to-all-start.2 = ((bf16[16,128,256]{2,1,0:T(8,128)(2,1)}), bf16[16,128,256]{2,1,0:T(8,128)(2,1)}, u32[]{:S(2)}, u32[]{:S(2)}) async-start(bf16[16,128,256]{2,1,0:T(8,128)(2,1)} %get-tuple-element.46), calls=%async_computation.2 | async-start | bytes 2097152 | tf_op jit(solution)/shard_map/all_to_all | solution.py:70
  149.8 32.3 %all-to-all-start.4 = ((f32[16,256,128]{2,1,0:T(8,128)}), f32[16,256,128]{2,1,0:T(8,128)}, u32[]{:S(2)}, u32[]{:S(2)}) async-start(f32[16,256,128]{2,1,0:T(8,128)} %bitcast.97), calls=%async_computation.4 | async-start | bytes 4194304 | tf_op jit(solution)/shard_map/all_to_all | solution.py:70
  156.9 7.6 %collective-permute-start.12 = (f32[128,128]{1,0:T(8,128)S(1)}, f32[128,128]{1,0:T(8,128)S(1)}, u32[]{:S(2)}, u32[]{:S(2)}) collective-permute-start(f32[128,128]{1,0:T(8,128)S(1)} %slice.123), channel_id=1, source_target_pairs={{0,3},{1,0},{2,1},{3,2},{4,7},{5,4},{6,5},{7,6},{8,11},{9,8},{10,9... | collective-permute-start | bytes 196616 | tf_op jit(solution)/shard_map/ppermute | solution.py:62
  161.4 6.2 %collective-permute-start.10 = (f32[128,128]{1,0:T(8,128)S(1)}, f32[128,128]{1,0:T(8,128)S(1)}, u32[]{:S(2)}, u32[]{:S(2)}) collective-permute-start(f32[128,128]{1,0:T(8,128)S(1)} %slice.121), channel_id=1, source_target_pairs={{0,1},{1,2},{2,3},{3,0},{4,5},{5,6},{6,7},{7,4},{8,9},{9,10},{10,1... | collective-permute-start | bytes 196616 | tf_op jit(solution)/shard_map/ppermute | solution.py:62
  162.3 6.6 %collective-permute-start.11 = (f32[128,128]{1,0:T(8,128)S(1)}, f32[128,128]{1,0:T(8,128)S(1)}, u32[]{:S(2)}, u32[]{:S(2)}) collective-permute-start(f32[128,128]{1,0:T(8,128)S(1)} %slice.122), channel_id=1, source_target_pairs={{0,2},{1,3},{2,0},{3,1},{4,6},{5,7},{6,4},{7,5},{8,10},{9,11},{10,... | collective-permute-start | bytes 196616 | tf_op jit(solution)/shard_map/ppermute | solution.py:62
  164.5 41.3 %collective-permute-start.24 = (bf16[4,2048,128]{2,1,0:T(8,128)(2,1)S(1)}, bf16[4,2048,128]{2,1,0:T(8,128)(2,1)}, u32[]{:S(2)}, u32[]{:S(2)}) collective-permute-start(bf16[4,2048,128]{2,1,0:T(8,128)(2,1)S(1)} %bitcast.100), channel_id=1, source_target_pairs={{0,128},{128,0},{1,129},{129,1},{2,130},{130,2},{3,131},{131,3},{4... | collective-permute-start | bytes 6291464 | tf_op jit(solution)/shard_map/ppermute | solution.py:40
  170.7 34.7 %collective-permute-start.17 = (bf16[2048,256]{1,0:T(8,128)(2,1)}, bf16[2048,256]{1,0:T(8,128)(2,1)}, u32[]{:S(2)}, u32[]{:S(2)}) collective-permute-start(bf16[2048,256]{1,0:T(8,128)(2,1)} %bitcast.29.mine_first), channel_id=1, source_target_pairs={{0,128},{128,0},{1,129},{129,1},{2,130},{130,2},{3,131},{131,3},{4... | collective-permute-start | bytes 3145736 | tf_op jit(solution)/shard_map/ppermute | solution.py:40
  174.5 16.2 %collective-permute-start.20 = (f32[128,128]{1,0:T(8,128)}, f32[128,128]{1,0:T(8,128)}, u32[]{:S(2)}, u32[]{:S(2)}) collective-permute-start(f32[128,128]{1,0:T(8,128)} %get-tuple-element.53), channel_id=1, source_target_pairs={{0,128},{128,0},{1,129},{129,1},{2,130},{130,2},{3,131},{131,3},{4... | collective-permute-start | bytes 196616 | tf_op jit(solution)/shard_map/ppermute | solution.py:40
  174.6 31.4 %collective-permute-start.18 = (bf16[2048,256]{1,0:T(8,128)(2,1)S(1)}, bf16[2048,256]{1,0:T(8,128)(2,1)}, u32[]{:S(2)}, u32[]{:S(2)}) collective-permute-start(bf16[2048,256]{1,0:T(8,128)(2,1)S(1)} %bitcast.103), channel_id=1, source_target_pairs={{0,128},{128,0},{1,129},{129,1},{2,130},{130,2},{3,131},{131,3},{4... | collective-permute-start | bytes 3145736 | tf_op jit(solution)/shard_map/ppermute | solution.py:40
  185.9 8.8 %collective-permute-start.19 = (f32[128,128]{1,0:T(8,128)S(1)}, f32[128,128]{1,0:T(8,128)}, u32[]{:S(2)}, u32[]{:S(2)}) collective-permute-start(f32[128,128]{1,0:T(8,128)S(1)} %get-tuple-element.87), channel_id=1, source_target_pairs={{0,16},{4,20},{8,24},{12,28},{16,0},{20,4},{24,8},{28,12},{32,48},... | collective-permute-start | bytes 196616 | tf_op jit(solution)/shard_map/ppermute | solution.py:44
  197.6 18.2 %all-to-all-start.5 = ((bf16[16,256,128]{2,1,0:T(8,128)(2,1)}), bf16[16,256,128]{2,1,0:T(8,128)(2,1)}, u32[]{:S(2)}, u32[]{:S(2)}) async-start(bf16[16,256,128]{2,1,0:T(8,128)(2,1)} %get-tuple-element.54), calls=%async_computation.5 | async-start | bytes 2097152 | tf_op jit(solution)/shard_map/all_to_all | solution.py:70
  204.2 16.2 %collective-permute-start.14 = (bf16[128,512]{1,0:T(8,128)(2,1)S(1)}, bf16[128,512]{1,0:T(8,128)(2,1)}, u32[]{:S(2)}, u32[]{:S(2)}) collective-permute-start(bf16[128,512]{1,0:T(8,128)(2,1)S(1)} %broadcast_select_fusion.3), channel_id=1, source_target_pairs={{0,128},{128,0},{1,129},{129,1},{2,130},{130,2},{3,131},{131,3},{4... | collective-permute-start | bytes 393224 | tf_op jit(solution)/shard_map/ppermute | solution.py:40
  205.3 15.3 %collective-permute-start.15 = (bf16[128,512]{1,0:T(8,128)(2,1)S(1)}, bf16[128,512]{1,0:T(8,128)(2,1)S(1)}, u32[]{:S(2)}, u32[]{:S(2)}) collective-permute-start(bf16[128,512]{1,0:T(8,128)(2,1)S(1)} %broadcast_select_fusion.2), channel_id=1, source_target_pairs={{0,128},{128,0},{1,129},{129,1},{2,130},{130,2},{3,131},{131,3},{4... | collective-permute-start | bytes 393224 | tf_op jit(solution)/shard_map/ppermute | solution.py:40
  205.4 15.3 %collective-permute-start.25 = (bf16[128,128]{1,0:T(8,128)(2,1)}, bf16[128,128]{1,0:T(8,128)(2,1)}, u32[]{:S(2)}, u32[]{:S(2)}) collective-permute-start(bf16[128,128]{1,0:T(8,128)(2,1)} %get-tuple-element.60), channel_id=1, source_target_pairs={{0,128},{128,0},{1,129},{129,1},{2,130},{130,2},{3,131},{131,3},{4... | collective-permute-start | bytes 98312 | tf_op jit(solution)/shard_map/ppermute | solution.py:40
  205.9 17.8 %collective-permute-start.26 = (bf16[128,128]{1,0:T(8,128)(2,1)}, bf16[128,128]{1,0:T(8,128)(2,1)S(1)}, u32[]{:S(2)}, u32[]{:S(2)}) collective-permute-start(bf16[128,128]{1,0:T(8,128)(2,1)} %get-tuple-element.59.refs_0_), channel_id=1, source_target_pairs={{0,1},{1,2},{2,3},{3,0},{4,5},{5,6},{6,7},{7,4},{8,9},{9,10},{10,1... | collective-permute-start | bytes 98312 | tf_op jit(solution)/shard_map/ppermute | solution.py:62
  206.0 20.6 %collective-permute-start.27 = (bf16[128,128]{1,0:T(8,128)(2,1)}, bf16[128,128]{1,0:T(8,128)(2,1)S(1)}, u32[]{:S(2)}, u32[]{:S(2)}) collective-permute-start(bf16[128,128]{1,0:T(8,128)(2,1)} %get-tuple-element.60), channel_id=1, source_target_pairs={{0,129},{1,130},{2,131},{3,128},{128,1},{129,2},{130,3},{131,0},{4... | collective-permute-start | bytes 98312 | tf_op jit(solution)/shard_map/ppermute | solution.py:58
  220.4 8.9 %collective-permute-start.28 = (bf16[128,128]{1,0:T(8,128)(2,1)S(1)}, bf16[128,128]{1,0:T(8,128)(2,1)S(1)}, u32[]{:S(2)}, u32[]{:S(2)}) collective-permute-start(bf16[128,128]{1,0:T(8,128)(2,1)S(1)} %copy-done.20), channel_id=1, source_target_pairs={{0,2},{1,3},{2,0},{3,1},{4,6},{5,7},{6,4},{7,5},{8,10},{9,11},{10,... | collective-permute-start | bytes 98312 | tf_op jit(solution)/shard_map/ppermute | solution.py:62
  220.6 11.9 %collective-permute-start.29 = (bf16[128,128]{1,0:T(8,128)(2,1)S(1)}, bf16[128,128]{1,0:T(8,128)(2,1)S(1)}, u32[]{:S(2)}, u32[]{:S(2)}) collective-permute-start(bf16[128,128]{1,0:T(8,128)(2,1)S(1)} %copy-done.29), channel_id=1, source_target_pairs={{0,130},{1,131},{2,128},{3,129},{128,2},{129,3},{130,0},{131,1},{4... | collective-permute-start | bytes 98312 | tf_op jit(solution)/shard_map/ppermute | solution.py:58
  220.7 23.7 %collective-permute-start.22 = (f32[128,128]{1,0:T(8,128)}, f32[128,128]{1,0:T(8,128)S(1)}, u32[]{:S(2)}, u32[]{:S(2)}) collective-permute-start(f32[128,128]{1,0:T(8,128)} %get-tuple-element.57), channel_id=1, source_target_pairs={{0,128},{128,0},{1,129},{129,1},{2,130},{130,2},{3,131},{131,3},{4... | collective-permute-start | bytes 196616 | tf_op jit(solution)/shard_map/ppermute | solution.py:40
  223.7 20.7 %collective-permute-start.23 = (f32[128,128]{1,0:T(8,128)}, f32[128,128]{1,0:T(8,128)S(1)}, u32[]{:S(2)}, u32[]{:S(2)}) collective-permute-start(f32[128,128]{1,0:T(8,128)} %get-tuple-element.58), channel_id=1, source_target_pairs={{0,144},{128,16},{4,148},{132,20},{8,152},{136,24},{12,156},{140,2... | collective-permute-start | bytes 196616 | tf_op jit(solution)/shard_map/ppermute | solution.py:51
  226.6 17.8 %collective-permute-start.21 = (f32[128,128]{1,0:T(8,128)}, f32[128,128]{1,0:T(8,128)S(1)}, u32[]{:S(2)}, u32[]{:S(2)}) collective-permute-start(f32[128,128]{1,0:T(8,128)} %get-tuple-element.56), channel_id=1, source_target_pairs={{0,16},{4,20},{8,24},{12,28},{16,0},{20,4},{24,8},{28,12},{32,48},... | collective-permute-start | bytes 196616 | tf_op jit(solution)/shard_map/ppermute | solution.py:44
  229.3 5.3 %collective-permute-start.30 = (bf16[128,128]{1,0:T(8,128)(2,1)S(1)}, bf16[128,128]{1,0:T(8,128)(2,1)S(1)}, u32[]{:S(2)}, u32[]{:S(2)}) collective-permute-start(bf16[128,128]{1,0:T(8,128)(2,1)S(1)} %copy-done.20), channel_id=1, source_target_pairs={{0,3},{1,0},{2,1},{3,2},{4,7},{5,4},{6,5},{7,6},{8,11},{9,8},{10,9... | collective-permute-start | bytes 98312 | tf_op jit(solution)/shard_map/ppermute | solution.py:62
  232.4 4.4 %collective-permute-start.31 = (bf16[128,128]{1,0:T(8,128)(2,1)S(1)}, bf16[128,128]{1,0:T(8,128)(2,1)S(1)}, u32[]{:S(2)}, u32[]{:S(2)}) collective-permute-start(bf16[128,128]{1,0:T(8,128)(2,1)S(1)} %copy-done.29), channel_id=1, source_target_pairs={{0,131},{1,128},{2,129},{3,130},{128,3},{129,0},{130,1},{131,2},{4... | collective-permute-start | bytes 98312 | tf_op jit(solution)/shard_map/ppermute | solution.py:58
  (35 other events, 434.3 us)

commit v5 on v4

--- a/solution.py
+++ b/solution.py
@@ -49,13 +49,6 @@
     for source, target in ACROSS:
         pairs += [(source, NX * NZ * NY + target), (NX * NZ * NY + source, target)]
     return lax.ppermute(array, ("group", "ctx"), pairs)
-
-
-def across_cores(array, step):
-    pairs = [
-        (core * NT + t, (1 - core) * NT + (t + step) % NT) for core in range(2) for t in range(NT)
-    ]
-    return lax.ppermute(array, ("group", "tp"), pairs)
 
 
 def along(array, step):
@@ -357,69 +350,25 @@
     )(place, *arrays)
 
 
-def input_kernel(place_ref, weight, other_weight, *refs):
-    grads, target = refs[: 2 * NT], refs[2 * NT]
-    heads = [(place_ref[2] - d) & (NT - 1) for d in range(NT)]
-    left = jnp.concatenate([g[...] for g in grads], 1)
-    right = jnp.concatenate([w[head] for head in heads for w in (weight, other_weight)], 1)
-    target[...] = product(left, right, 1, 1).astype(BF16)
-
-
-def input_product(place, weight, other_weight, *grads):
-    heads, features, width = weight.shape
-    step = features // (NZ * NY)
-    weights = pl.BlockSpec((heads, step, width), lambda y, z: (0, y * NZ + z, 0))
-    whole = pl.BlockSpec((TOK, HD), lambda y, z: (0, 0))
-    return pl.pallas_call(
-        input_kernel,
-        grid=(NY, NZ),
-        out_shape=jax.ShapeDtypeStruct((TOK, features), BF16),
-        in_specs=[pl.BlockSpec(memory_space=pltpu.SMEM)] + [weights] * 2 + [whole] * (2 * NT),
-        out_specs=pl.BlockSpec((TOK, step), lambda y, z: (0, z * NY + y)),
-        name="input",
-    )(place, weight, other_weight, *grads)
-
-
-def grads_kernel(
-    place_ref, here, got, short_keep, short_got, cosine_ref, sine_ref,
-    own_ref, other_ref, target, block, sems,
-):
-    long_core = place_ref[0] == 0
-    long_part = here[...] + got[...]
-    short_part = short_keep[...] + short_got[...]
-    rows = jnp.concatenate(
-        [
-            jnp.where(long_core, long_part, short_part),
-            jnp.where(long_core, short_part, long_part),
-        ],
-        0,
-    )
-    turned = rows * cosine_ref[...] + pltpu.roll(rows, HALF, 1) * sine_ref[...]
-    rows = jnp.where(long_core, turned, rows).astype(BF16)
-    block[...] = rows
-    copies = [pltpu.make_async_copy(block, target.at[i], sems.at[i]) for i in range(NX * NY)]
-    for copy in copies:
-        copy.start()
-    own_ref[...] = rows[:TOK]
-    other_ref[...] = rows[TOK:]
-    for copy in copies:
-        copy.wait()
-
-
-def grads_call(place, *arrays):
-    vmem = pl.BlockSpec(memory_space=pltpu.VMEM)
-    half = jax.ShapeDtypeStruct((TOK, HD), BF16)
-    return pl.pallas_call(
-        grads_kernel,
-        out_shape=(half, half, jax.ShapeDtypeStruct((NX * NY, 2 * TOK, HD), BF16)),
-        in_specs=[pl.BlockSpec(memory_space=pltpu.SMEM)] + [vmem] * len(arrays),
-        out_specs=(vmem, vmem, pl.BlockSpec(memory_space=pl.ANY)),
-        scratch_shapes=[
-            pltpu.VMEM((2 * TOK, HD), BF16),
-            pltpu.SemaphoreType.DMA((NX * NY,)),
-        ],
-        name="grads",
-    )(place, *arrays)
+def finish_kernel(mine, other, target):
+    step = target.shape[1] // (NZ * NY)
+    for z in range(NZ):
+        for y in range(NY):
+            source = slice((y * NZ + z) * step, (y * NZ + z + 1) * step)
+            summed = mine[:, source] + other[:, source]
+            target[:, (z * NY + y) * step : (z * NY + y + 1) * step] = summed.astype(BF16)
+
+
+def finish_input(terms, other_terms):
+    whole = pl.BlockSpec(other_terms.shape, lambda i: (0, 0))
+    return pl.pallas_call(
+        finish_kernel,
+        grid=(1,),
+        out_shape=jax.ShapeDtypeStruct(other_terms.shape, BF16),
+        in_specs=[whole, whole],
+        out_specs=whole,
+        name="finish",
+    )(terms, other_terms)
 
 
 def slice_kernel(place_ref, source, target):
@@ -476,8 +425,6 @@
     own_sin = jnp.where(is_long, sine[:TOK], sine[TOK:])
     back_cos = jnp.concatenate([own_cos, jnp.where(is_long, cosine[TOK:], cosine[:TOK])], 0)
     back_sin = jnp.concatenate([own_sin, jnp.where(is_long, sine[TOK:], sine[:TOK])], 0)
-    back_cos = jnp.concatenate([back_cos, back_cos], 1)
-    back_sin = jnp.concatenate([back_sin, -back_sin], 1)
 
     def by_zone(mine, other):
         return jnp.concatenate(
@@ -494,7 +441,6 @@
     weight = plane_exchange(weight)
     packed = pack_columns(activations)
     weight = weight.reshape(NX, NY * weight.shape[-2], HD)
-    other_weight = partner(weight)
 
     own_slice = feature_slice(place, activations)
     other_slice = partner(own_slice)
@@ -544,7 +490,7 @@
     out_got, qgrad_got = partner(role(short_out, long_out)), partner(role(short_qgrad, long_qgrad))
     attention, query_grad = join_heads(place, *out_parts, out_got, qgrad_got)
     kv_sums = kv_keep + partner(kv_send)
-    short_got = partner(short_send)
+    short_kv = short_keep + partner(short_send)
     blocks, second_columns = after(kv_sums.reshape(plane, NZ * TOK, HD), second_columns)
     columns = [
         array.reshape(plane * TOK, NZ * TOK) for array in (first_columns, second_columns)
@@ -554,16 +500,18 @@
     arrived = arrived.reshape(plane, NZ, TOK, HD).sum(0)
     here = jnp.where(upper, arrived[1], arrived[0])
     there = jnp.where(upper, arrived[0], arrived[1])
-    own_grads, got_grads, copies = grads_call(
-        place, here, across(there), short_keep, short_got, back_cos, back_sin
-    )
-    plane_grads = plane_exchange(copies)
-
-    mine = [own_grads] + [along(own_grads, d) for d in range(1, NT)]
-    swapped = [partner(got_grads)] + [across_cores(got_grads, d) for d in range(1, NT)]
-    input_grad = input_product(
-        place, weight, other_weight, *[g for pair in zip(mine, swapped) for g in pair]
-    )
+    long_kv = here + across(there)
+    grads = jnp.concatenate([role(long_kv, short_kv), role(short_kv, long_kv)], 0)
+    grads = role(turn(grads, back_cos, -back_sin), grads).astype(BF16)
+    plane_grads = plane_exchange(plane_copies(grads))
+
+    by_step = [grads] + [along(grads, d) for d in range(1, NT)]
+    terms = jnp.zeros((2 * TOK, weight.shape[1]), F32)
+    for d in range(NT):
+        head = lax.dynamic_index_in_dim(weight, (tp - d) & (NT - 1), 0, False)
+        terms += product(by_step[d], head, 1, 1)
+    other_terms = partner(terms[TOK:])
+    input_grad = finish_input(terms, other_terms)
 
     here, above, beside, opposite = owned_pieces(
         place, columns[0], columns[1], other_columns[0], other_columns[1], plane_grads

time: 249 us -> 241 us (0.968)
  the two profiles are of different devices: /device:TPU:8 before, /device:TPU:33 now
where the time goes in v5:
time: 241 us; the launch traced here: 240 us
  starting transfers between devices  102 us (42%)
  waiting for transfers between devices  74.3 us (31%)
  Pallas kernels  25 us (10%)
  local copies, waits for them, and re-layouts  15.5 us (6%)
  other arithmetic  15.4 us (6%)
  matrix products  6.62 us (3%)
    all_to_all x6, waiting for transfers between devices, plane_exchange(): lax.all_to_all(blocks, 'ctx', split_axis=0, concat_axis=0, tiled=True, ax...  57.6 us
    all_to_all x6, starting transfers between devices, plane_exchange(): lax.all_to_all(blocks, 'ctx', split_axis=0, concat_axis=0, tiled=True, ax...  37.5 us
    ppermute x13, starting transfers between devices, partner(): return lax.ppermute(array, 'group', [(0, 1), (1, 0)])  25.9 us
    ppermute x9, starting transfers between devices, along(): return lax.ppermute(array, 'tp', [(t, (t + step) % NT) for t in range(NT)])  18 us
    pallas_call x1, Pallas kernels, attention_call(): pl.pallas_call(attention_kernel, out_shape=(rows, rows, blocks, blocks),...  7.4 us
    ppermute x3, starting transfers between devices, across(): return lax.ppermute(array, 'ctx', ACROSS)  7.24 us
    ppermute x3, waiting for transfers between devices, across(): return lax.ppermute(array, 'ctx', ACROSS)  7.07 us
    ppermute x1, starting transfers between devices, body(): far = lax.ppermute(weight, ('ctx', 'tp'), FAR_TURN)  6.57 us
  transfers between devices with their start and end apart: 34, of which 16 were waited for; matrix products, arithmetic and copies ran while one was open for 11% of the time, Pallas kernels for 6%

profile of v5, /device:TPU:33, one launch (start us, length us, event | category | flops | bytes accessed | tf_op | source)
XLA Modules:
  0.0 239.8 jit_solution(14892768677286476237)
XLA Ops:
  1.5 6.6 %collective-permute-start.2 = (bf16[256,128]{1,0:T(8,128)(2,1)S(1)}, bf16[256,128]{1,0:T(8,128)(2,1)S(1)}, u32[]{:S(2)}, u32[]{:S(2)}) collective-permute-start(bf16[256,128]{1,0:T(8,128)(2,1)S(1)} %broadcast_select_fusion.8), channel_id=1, source_target_pairs={{0,16},{1,48},{2,80},{3,112},{4,20},{5,52},{6,84},{7,116},{8,24},{... | collective-permute-start | bytes 196616 | tf_op jit(solution)/shard_map/ppermute | solution.py:439
  8.1 2.6 %collective-permute-start.3 = (bf16[256,128]{1,0:T(8,128)(2,1)S(1)}, bf16[256,128]{1,0:T(8,128)(2,1)S(1)}, u32[]{:S(2)}, u32[]{:S(2)}) collective-permute-start(bf16[256,128]{1,0:T(8,128)(2,1)S(1)} %broadcast_select_fusion.8), channel_id=1, source_target_pairs={{0,0},{1,32},{2,64},{3,96},{4,4},{5,36},{6,68},{7,100},{8,8},{9,40... | collective-permute-start | bytes 196616 | tf_op jit(solution)/shard_map/ppermute | solution.py:438
  11.6 2.4 collective-permute-done.3
  15.7 8.5 %all-to-all-start = ((bf16[16,512,128]{2,1,0:T(8,128)(2,1)}), bf16[16,512,128]{2,1,0:T(8,128)(2,1)S(1)}, u32[]{:S(2)}, u32[]{:S(2)}) async-start(bf16[16,512,128]{2,1,0:T(8,128)(2,1)} %broadcast_in_dim.16), calls=%async_computation | async-start | bytes 4194304 | tf_op jit(solution)/shard_map/all_to_all | solution.py:63
  24.8 2.5 %feature_slice.1 = bf16[128,2048]{1,0:T(8,128)(2,1)} custom-call(s32[3]{0:T(128)} %pad_add_fusion.place_ref, bf16[128,8192]{1,0:T(8,128)(2,1)} %source.3), custom_call_target="tpu_custom_call" | custom-call | tf_op jit(solution)/shard_map/feature_slice/pallas_call | solution.py:385
  33.3 16.7 %all-to-all-done = bf16[16,512,128]{2,1,0:T(8,128)(2,1)S(1)} async-done(((bf16[16,512,128]{2,1,0:T(8,128)(2,1)}), bf16[16,512,128]{2,1,0:T(8,128)(2,1)S(1)}, u32[]{:S(2)}, u32[]{:S(2)}) %all-to-all-start) | async-done | bytes 2097184 | tf_op jit(solution)/shard_map/all_to_all | solution.py:63
  54.5 3.0 %collective-permute-start.6 = (f32[128,128]{1,0:T(8,128)S(1)}, f32[128,128]{1,0:T(8,128)S(1)}, u32[]{:S(2)}, u32[]{:S(2)}) collective-permute-start(f32[128,128]{1,0:T(8,128)S(1)} %slice_bitcast_fusion.1), channel_id=1, source_target_pairs={{0,2},{1,3},{2,0},{3,1},{4,6},{5,7},{6,4},{7,5},{8,10},{9,11},{10,... | collective-permute-start | bytes 196616 | tf_op jit(solution)/shard_map/ppermute | solution.py:55
  60.0 3.5 %collective-permute-start.8 = (bf16[128,128]{1,0:T(8,128)(2,1)S(1)}, bf16[128,128]{1,0:T(8,128)(2,1)S(1)}, u32[]{:S(2)}, u32[]{:S(2)}) collective-permute-start(bf16[128,128]{1,0:T(8,128)(2,1)S(1)} %fusion.21), channel_id=1, source_target_pairs={{0,16},{4,20},{8,24},{12,28},{16,0},{20,4},{24,8},{28,12},{32,48},... | collective-permute-start | bytes 98312 | tf_op jit(solution)/shard_map/ppermute | solution.py:44
  63.6 3.4 %collective-permute-done.8 = bf16[128,128]{1,0:T(8,128)(2,1)S(1)} collective-permute-done((bf16[128,128]{1,0:T(8,128)(2,1)S(1)}, bf16[128,128]{1,0:T(8,128)(2,1)S(1)}, u32[]{:S(2)}, u32[]{:S(2)}) %collective-permute-start.8) | collective-permute-done | bytes 32800 | tf_op jit(solution)/shard_map/ppermute | solution.py:44
  68.2 6.4 %all-to-all-start.1 = ((bf16[16,256,128]{2,1,0:T(8,128)(2,1)}), bf16[16,256,128]{2,1,0:T(8,128)(2,1)S(1)}, u32[]{:S(2)}, u32[]{:S(2)}) async-start(bf16[16,256,128]{2,1,0:T(8,128)(2,1)} %broadcast_in_dim.19), calls=%async_computation.1 | async-start | bytes 2097152 | tf_op jit(solution)/shard_map/all_to_all | solution.py:63
  74.5 3.4 %pack.1 = (bf16[16,128,256]{2,1,0:T(8,128)(2,1)}, bf16[16,128,256]{2,1,0:T(8,128)(2,1)}) custom-call(bf16[128,8192]{1,0:T(8,128)(2,1)} %source.3), custom_call_target="tpu_custom_call" | custom-call | tf_op jit(solution)/shard_map/pack/pallas_call | solution.py:401
  79.7 6.7 %all-to-all-done.1 = bf16[16,256,128]{2,1,0:T(8,128)(2,1)S(1)} async-done(((bf16[16,256,128]{2,1,0:T(8,128)(2,1)}), bf16[16,256,128]{2,1,0:T(8,128)(2,1)S(1)}, u32[]{:S(2)}, u32[]{:S(2)}) %all-to-all-start.1) | async-done | bytes 1048608 | tf_op jit(solution)/shard_map/all_to_all | solution.py:63
  86.4 6.4 %collective-permute-start.9 = (bf16[32,128,128]{2,1,0:T(8,128)(2,1)S(1)}, bf16[32,128,128]{2,1,0:T(8,128)(2,1)S(1)}, u32[]{:S(2)}, u32[]{:S(2)}) collective-permute-start(bf16[32,128,128]{2,1,0:T(8,128)(2,1)S(1)} %bitcast.129), channel_id=1, source_target_pairs={{0,128},{128,0},{1,129},{129,1},{2,130},{130,2},{3,131},{131,3},{4... | collective-permute-start | bytes 3145736 | tf_op jit(solution)/shard_map/ppermute | solution.py:40
  95.5 7.4 %attention.1 = (bf16[128,512]{1,0:T(8,128)(2,1)S(1)}, bf16[128,512]{1,0:T(8,128)(2,1)S(1)}, f32[32,128,128]{2,1,0:T(8,128)S(1)}, f32[32,128,128]{2,1,0:T(8,128)}) custom-call(s32[3]{0:T(128)S(1)} %copy-done.9, bf16[128,512]{1,0:T(8,128)(2,1)S(1)} %get-tuple-element.80.q_keep, bf16[128,512]{1,0:T(8,128)(2,1)S(1)} %collective-permute-done.q_got, ...), custom_call_target="tpu_custom_call" | custom-call | tf_op jit(solution)/shard_map/attention/pallas_call | solution.py:253
  104.6 7.4 %all-to-all-start.3 = ((bf16[16,128,256]{2,1,0:T(8,128)(2,1)}), bf16[16,128,256]{2,1,0:T(8,128)(2,1)S(1)}, u32[]{:S(2)}, u32[]{:S(2)}) async-start(bf16[16,128,256]{2,1,0:T(8,128)(2,1)} %get-tuple-element.46), calls=%async_computation.3 | async-start | bytes 2097152 | tf_op jit(solution)/shard_map/all_to_all | solution.py:63
  112.0 3.3 %add.125 = f32[32,128,128]{2,1,0:T(8,128)} add(f32[32,128,128]{2,1,0:T(8,128)S(1)} %get-tuple-element.44, f32[32,128,128]{2,1,0:T(8,128)} %collective-permute-done.16) | non-fusion elementwise | flops 524288 | bytes 6291456 | tf_op jit(solution)/shard_map/add | solution.py:492
  115.3 12.8 %all-to-all-done.3 = bf16[16,128,256]{2,1,0:T(8,128)(2,1)S(1)} async-done(((bf16[16,128,256]{2,1,0:T(8,128)(2,1)}), bf16[16,128,256]{2,1,0:T(8,128)(2,1)S(1)}, u32[]{:S(2)}, u32[]{:S(2)}) %all-to-all-start.3) | async-done | bytes 1048608 | tf_op jit(solution)/shard_map/all_to_all | solution.py:63
  129.1 4.4 %all-to-all-start.4 = ((f32[16,256,128]{2,1,0:T(8,128)}), f32[16,256,128]{2,1,0:T(8,128)S(1)}, u32[]{:S(2)}, u32[]{:S(2)}) async-start(f32[16,256,128]{2,1,0:T(8,128)} %bitcast.131), calls=%async_computation.4 | async-start | bytes 4194304 | tf_op jit(solution)/shard_map/all_to_all | solution.py:63
  139.4 5.1 %collective-permute-start.11 = (f32[128,128]{1,0:T(8,128)}, f32[128,128]{1,0:T(8,128)}, u32[]{:S(2)}, u32[]{:S(2)}) collective-permute-start(f32[128,128]{1,0:T(8,128)} %slice.131), channel_id=1, source_target_pairs={{0,2},{1,3},{2,0},{3,1},{4,6},{5,7},{6,4},{7,5},{8,10},{9,11},{10,... | collective-permute-start | bytes 196616 | tf_op jit(solution)/shard_map/ppermute | solution.py:55
  144.5 14.7 %all-to-all-done.4 = f32[16,256,128]{2,1,0:T(8,128)S(1)} async-done(((f32[16,256,128]{2,1,0:T(8,128)}), f32[16,256,128]{2,1,0:T(8,128)S(1)}, u32[]{:S(2)}, u32[]{:S(2)}) %all-to-all-start.4) | async-done | bytes 2097184 | tf_op jit(solution)/shard_map/all_to_all | solution.py:63
  159.3 5.3 %all-to-all-start.2 = ((bf16[16,128,256]{2,1,0:T(8,128)(2,1)}), bf16[16,128,256]{2,1,0:T(8,128)(2,1)}, u32[]{:S(2)}, u32[]{:S(2)}) async-start(bf16[16,128,256]{2,1,0:T(8,128)(2,1)} %get-tuple-element.43), calls=%async_computation.2 | async-start | bytes 2097152 | tf_op jit(solution)/shard_map/all_to_all | solution.py:63
  165.9 4.0 %collective-permute-start.13 = (bf16[128,128]{1,0:T(8,128)(2,1)S(1)}, bf16[128,128]{1,0:T(8,128)(2,1)S(1)}, u32[]{:S(2)}, u32[]{:S(2)}) collective-permute-start(bf16[128,128]{1,0:T(8,128)(2,1)S(1)} %fusion.23.short_mine), channel_id=1, source_target_pairs={{0,128},{128,0},{1,129},{129,1},{2,130},{130,2},{3,131},{131,3},{4... | collective-permute-start | bytes 98312 | tf_op jit(solution)/shard_map/ppermute | solution.py:40
  171.3 2.7 %short_attention.1 = (bf16[128,512]{1,0:T(8,128)(2,1)}, bf16[128,512]{1,0:T(8,128)(2,1)}, f32[128,128]{1,0:T(8,128)}, f32[128,128]{1,0:T(8,128)}) custom-call(s32[3]{0:T(128)} %pad_add_fusion.place_ref, bf16[128,512]{1,0:T(8,128)(2,1)} %copy-done, bf16[128,512]{1,0:T(8,128)(2,1)} %copy-done.3, bf16[128,512]{1,0:T(8,128)(2,1)} %copy-done.1, ...), custom_call_target="tpu_custom_call" | custom-call | tf_op jit(solution)/shard_map/short_attention/pallas_call | solution.py:240
  177.0 5.7 %collective-permute-start.17 = (bf16[2048,256]{1,0:T(8,128)(2,1)}, bf16[2048,256]{1,0:T(8,128)(2,1)}, u32[]{:S(2)}, u32[]{:S(2)}) collective-permute-start(bf16[2048,256]{1,0:T(8,128)(2,1)} %bitcast.29.mine_first), channel_id=1, source_target_pairs={{0,128},{128,0},{1,129},{129,1},{2,130},{130,2},{3,131},{131,3},{4... | collective-permute-start | bytes 3145736 | tf_op jit(solution)/shard_map/ppermute | solution.py:40
  188.2 5.1 %collective-permute-start.25 = (bf16[256,128]{1,0:T(8,128)(2,1)S(1)}, bf16[256,128]{1,0:T(8,128)(2,1)S(1)}, u32[]{:S(2)}, u32[]{:S(2)}) collective-permute-start(bf16[256,128]{1,0:T(8,128)(2,1)S(1)} %fusion.15), channel_id=1, source_target_pairs={{0,2},{1,3},{2,0},{3,1},{4,6},{5,7},{6,4},{7,5},{8,10},{9,11},{10,... | collective-permute-start | bytes 196616 | tf_op jit(solution)/shard_map/ppermute | solution.py:55
  194.5 5.5 %all-to-all-start.5 = ((bf16[16,256,128]{2,1,0:T(8,128)(2,1)}), bf16[16,256,128]{2,1,0:T(8,128)(2,1)}, u32[]{:S(2)}, u32[]{:S(2)}) async-start(bf16[16,256,128]{2,1,0:T(8,128)(2,1)} %broadcast_in_dim.23), calls=%async_computation.5 | async-start | bytes 2097152 | tf_op jit(solution)/shard_map/all_to_all | solution.py:63
  208.6 6.3 %all-to-all-done.5.grads_ref = bf16[16,256,128]{2,1,0:T(8,128)(2,1)} async-done(((bf16[16,256,128]{2,1,0:T(8,128)(2,1)}), bf16[16,256,128]{2,1,0:T(8,128)(2,1)}, u32[]{:S(2)}, u32[]{:S(2)}) %all-to-all-start.5) | async-done | bytes 1048608 | tf_op jit(solution)/shard_map/all_to_all | solution.py:63
  214.9 4.6 %owned.1 = (f32[128,128]{1,0:T(8,128)}, f32[128,128]{1,0:T(8,128)}, f32[128,128]{1,0:T(8,128)}, f32[128,128]{1,0:T(8,128)}) custom-call(s32[3]{0:T(128)} %pad_add_fusion.place_ref, bf16[2048,256]{1,0:T(8,128)(2,1)} %bitcast.29.mine_first, bf16[2048,256]{1,0:T(8,128)(2,1)} %bitcast.138, bf16[2048,256]{1,0:T(8,128)(2,1)} %collective-permute-done.17.other_first, ...), custom_call_target="tpu_custom_call" | custom-call | tf_op jit(solution)/shard_map/owned/pallas_call | solution.py:339
  219.5 3.3 %collective-permute-start.22 = (f32[128,128]{1,0:T(8,128)}, f32[128,128]{1,0:T(8,128)S(1)}, u32[]{:S(2)}, u32[]{:S(2)}) collective-permute-start(f32[128,128]{1,0:T(8,128)} %get-tuple-element.53), channel_id=1, source_target_pairs={{0,128},{128,0},{1,129},{129,1},{2,130},{130,2},{3,131},{131,3},{4... | collective-permute-start | bytes 196616 | tf_op jit(solution)/shard_map/ppermute | solution.py:40
  222.7 3.7 %collective-permute-start.23 = (f32[128,128]{1,0:T(8,128)}, f32[128,128]{1,0:T(8,128)S(1)}, u32[]{:S(2)}, u32[]{:S(2)}) collective-permute-start(f32[128,128]{1,0:T(8,128)} %get-tuple-element.54), channel_id=1, source_target_pairs={{0,144},{128,16},{4,148},{132,20},{8,152},{136,24},{12,156},{140,2... | collective-permute-start | bytes 196616 | tf_op jit(solution)/shard_map/ppermute | solution.py:51
  232.1 3.7 %collective-permute-done.21 = f32[128,128]{1,0:T(8,128)S(1)} collective-permute-done((f32[128,128]{1,0:T(8,128)}, f32[128,128]{1,0:T(8,128)S(1)}, u32[]{:S(2)}, u32[]{:S(2)}) %collective-permute-start.21) | collective-permute-done | bytes 65568 | tf_op jit(solution)/shard_map/ppermute | solution.py:44
  237.3 2.5 %finish.1 = bf16[128,2048]{1,0:T(8,128)(2,1)} custom-call(f32[256,2048]{1,0:T(8,128)} %copy-done.10, f32[128,2048]{1,0:T(8,128)} %collective-permute-done.27.other), custom_call_target="tpu_custom_call" | custom-call | tf_op jit(solution)/shard_map/finish/pallas_call | solution.py:364
  (170 shorter events, 59.0 us)
Async XLA Ops:
  1.5 10.1 %collective-permute-start.2 = (bf16[256,128]{1,0:T(8,128)(2,1)S(1)}, bf16[256,128]{1,0:T(8,128)(2,1)S(1)}, u32[]{:S(2)}, u32[]{:S(2)}) collective-permute-start(bf16[256,128]{1,0:T(8,128)(2,1)S(1)} %broadcast_select_fusion.8), channel_id=1, source_target_pairs={{0,16},{1,48},{2,80},{3,112},{4,20},{5,52},{6,84},{7,116},{8,24},{... | collective-permute-start | bytes 196616 | tf_op jit(solution)/shard_map/ppermute | solution.py:439
  8.1 5.9 %collective-permute-start.3 = (bf16[256,128]{1,0:T(8,128)(2,1)S(1)}, bf16[256,128]{1,0:T(8,128)(2,1)S(1)}, u32[]{:S(2)}, u32[]{:S(2)}) collective-permute-start(bf16[256,128]{1,0:T(8,128)(2,1)S(1)} %broadcast_select_fusion.8), channel_id=1, source_target_pairs={{0,0},{1,32},{2,64},{3,96},{4,4},{5,36},{6,68},{7,100},{8,8},{9,40... | collective-permute-start | bytes 196616 | tf_op jit(solution)/shard_map/ppermute | solution.py:438
  15.7 34.3 %all-to-all-start = ((bf16[16,512,128]{2,1,0:T(8,128)(2,1)}), bf16[16,512,128]{2,1,0:T(8,128)(2,1)S(1)}, u32[]{:S(2)}, u32[]{:S(2)}) async-start(bf16[16,512,128]{2,1,0:T(8,128)(2,1)} %broadcast_in_dim.16), calls=%async_computation | async-start | bytes 4194304 | tf_op jit(solution)/shard_map/all_to_all | solution.py:63
  27.4 4.0 %collective-permute-start.4 = (bf16[128,2048]{1,0:T(8,128)(2,1)}, bf16[128,2048]{1,0:T(8,128)(2,1)S(1)}, u32[]{:S(2)}, u32[]{:S(2)}) collective-permute-start(bf16[128,2048]{1,0:T(8,128)(2,1)} %feature_slice.1), channel_id=1, source_target_pairs={{0,128},{128,0},{1,129},{129,1},{2,130},{130,2},{3,131},{131,3},{4... | collective-permute-start | bytes 1572872 | tf_op jit(solution)/shard_map/ppermute | solution.py:40
  52.9 5.1 %collective-permute-start.7 = (f32[128,128]{1,0:T(8,128)S(1)}, f32[128,128]{1,0:T(8,128)S(1)}, u32[]{:S(2)}, u32[]{:S(2)}) collective-permute-start(f32[128,128]{1,0:T(8,128)S(1)} %slice_bitcast_fusion), channel_id=1, source_target_pairs={{0,3},{1,0},{2,1},{3,2},{4,7},{5,4},{6,5},{7,6},{8,11},{9,8},{10,9... | collective-permute-start | bytes 196616 | tf_op jit(solution)/shard_map/ppermute | solution.py:55
  54.1 4.0 %collective-permute-start.5 = (f32[128,128]{1,0:T(8,128)S(1)}, f32[128,128]{1,0:T(8,128)S(1)}, u32[]{:S(2)}, u32[]{:S(2)}) collective-permute-start(f32[128,128]{1,0:T(8,128)S(1)} %slice_bitcast_fusion.2), channel_id=1, source_target_pairs={{0,1},{1,2},{2,3},{3,0},{4,5},{5,6},{6,7},{7,4},{8,9},{9,10},{10,1... | collective-permute-start | bytes 196616 | tf_op jit(solution)/shard_map/ppermute | solution.py:55
  54.5 5.4 %collective-permute-start.6 = (f32[128,128]{1,0:T(8,128)S(1)}, f32[128,128]{1,0:T(8,128)S(1)}, u32[]{:S(2)}, u32[]{:S(2)}) collective-permute-start(f32[128,128]{1,0:T(8,128)S(1)} %slice_bitcast_fusion.1), channel_id=1, source_target_pairs={{0,2},{1,3},{2,0},{3,1},{4,6},{5,7},{6,4},{7,5},{8,10},{9,11},{10,... | collective-permute-start | bytes 196616 | tf_op jit(solution)/shard_map/ppermute | solution.py:55
  60.0 6.9 %collective-permute-start.8 = (bf16[128,128]{1,0:T(8,128)(2,1)S(1)}, bf16[128,128]{1,0:T(8,128)(2,1)S(1)}, u32[]{:S(2)}, u32[]{:S(2)}) collective-permute-start(bf16[128,128]{1,0:T(8,128)(2,1)S(1)} %fusion.21), channel_id=1, source_target_pairs={{0,16},{4,20},{8,24},{12,28},{16,0},{20,4},{24,8},{28,12},{32,48},... | collective-permute-start | bytes 98312 | tf_op jit(solution)/shard_map/ppermute | solution.py:44
  68.2 18.2 %all-to-all-start.1 = ((bf16[16,256,128]{2,1,0:T(8,128)(2,1)}), bf16[16,256,128]{2,1,0:T(8,128)(2,1)S(1)}, u32[]{:S(2)}, u32[]{:S(2)}) async-start(bf16[16,256,128]{2,1,0:T(8,128)(2,1)} %broadcast_in_dim.19), calls=%async_computation.1 | async-start | bytes 2097152 | tf_op jit(solution)/shard_map/all_to_all | solution.py:63
  86.4 9.1 %collective-permute-start.9 = (bf16[32,128,128]{2,1,0:T(8,128)(2,1)S(1)}, bf16[32,128,128]{2,1,0:T(8,128)(2,1)S(1)}, u32[]{:S(2)}, u32[]{:S(2)}) collective-permute-start(bf16[32,128,128]{2,1,0:T(8,128)(2,1)S(1)} %bitcast.129), channel_id=1, source_target_pairs={{0,128},{128,0},{1,129},{129,1},{2,130},{130,2},{3,131},{131,3},{4... | collective-permute-start | bytes 3145736 | tf_op jit(solution)/shard_map/ppermute | solution.py:40
  104.2 7.8 %collective-permute-start.16 = (f32[32,128,128]{2,1,0:T(8,128)}, f32[32,128,128]{2,1,0:T(8,128)}, u32[]{:S(2)}, u32[]{:S(2)}) collective-permute-start(f32[32,128,128]{2,1,0:T(8,128)} %get-tuple-element.45), channel_id=1, source_target_pairs={{0,128},{128,0},{1,129},{129,1},{2,130},{130,2},{3,131},{131,3},{4... | collective-permute-start | bytes 6291464 | tf_op jit(solution)/shard_map/ppermute | solution.py:40
  104.6 23.5 %all-to-all-start.3 = ((bf16[16,128,256]{2,1,0:T(8,128)(2,1)}), bf16[16,128,256]{2,1,0:T(8,128)(2,1)S(1)}, u32[]{:S(2)}, u32[]{:S(2)}) async-start(bf16[16,128,256]{2,1,0:T(8,128)(2,1)} %get-tuple-element.46), calls=%async_computation.3 | async-start | bytes 2097152 | tf_op jit(solution)/shard_map/all_to_all | solution.py:63
  129.1 30.2 %all-to-all-start.4 = ((f32[16,256,128]{2,1,0:T(8,128)}), f32[16,256,128]{2,1,0:T(8,128)S(1)}, u32[]{:S(2)}, u32[]{:S(2)}) async-start(f32[16,256,128]{2,1,0:T(8,128)} %bitcast.131), calls=%async_computation.4 | async-start | bytes 4194304 | tf_op jit(solution)/shard_map/all_to_all | solution.py:63
  135.0 29.6 %collective-permute-start.12 = (f32[128,128]{1,0:T(8,128)}, f32[128,128]{1,0:T(8,128)}, u32[]{:S(2)}, u32[]{:S(2)}) collective-permute-start(f32[128,128]{1,0:T(8,128)} %slice.132), channel_id=1, source_target_pairs={{0,3},{1,0},{2,1},{3,2},{4,7},{5,4},{6,5},{7,6},{8,11},{9,8},{10,9... | collective-permute-start | bytes 196616 | tf_op jit(solution)/shard_map/ppermute | solution.py:55
  137.6 27.0 %collective-permute-start.10 = (f32[128,128]{1,0:T(8,128)}, f32[128,128]{1,0:T(8,128)}, u32[]{:S(2)}, u32[]{:S(2)}) collective-permute-start(f32[128,128]{1,0:T(8,128)} %slice.130), channel_id=1, source_target_pairs={{0,1},{1,2},{2,3},{3,0},{4,5},{5,6},{6,7},{7,4},{8,9},{9,10},{10,1... | collective-permute-start | bytes 196616 | tf_op jit(solution)/shard_map/ppermute | solution.py:55
  139.4 25.2 %collective-permute-start.11 = (f32[128,128]{1,0:T(8,128)}, f32[128,128]{1,0:T(8,128)}, u32[]{:S(2)}, u32[]{:S(2)}) collective-permute-start(f32[128,128]{1,0:T(8,128)} %slice.131), channel_id=1, source_target_pairs={{0,2},{1,3},{2,0},{3,1},{4,6},{5,7},{6,4},{7,5},{8,10},{9,11},{10,... | collective-permute-start | bytes 196616 | tf_op jit(solution)/shard_map/ppermute | solution.py:55
  159.3 17.7 %all-to-all-start.2 = ((bf16[16,128,256]{2,1,0:T(8,128)(2,1)}), bf16[16,128,256]{2,1,0:T(8,128)(2,1)}, u32[]{:S(2)}, u32[]{:S(2)}) async-start(bf16[16,128,256]{2,1,0:T(8,128)(2,1)} %get-tuple-element.43), calls=%async_computation.2 | async-start | bytes 2097152 | tf_op jit(solution)/shard_map/all_to_all | solution.py:63
  165.9 4.8 %collective-permute-start.13 = (bf16[128,128]{1,0:T(8,128)(2,1)S(1)}, bf16[128,128]{1,0:T(8,128)(2,1)S(1)}, u32[]{:S(2)}, u32[]{:S(2)}) collective-permute-start(bf16[128,128]{1,0:T(8,128)(2,1)S(1)} %fusion.23.short_mine), channel_id=1, source_target_pairs={{0,128},{128,0},{1,129},{129,1},{2,130},{130,2},{3,131},{131,3},{4... | collective-permute-start | bytes 98312 | tf_op jit(solution)/shard_map/ppermute | solution.py:40
  174.0 8.8 %collective-permute-start.20 = (f32[128,128]{1,0:T(8,128)}, f32[128,128]{1,0:T(8,128)S(1)}, u32[]{:S(2)}, u32[]{:S(2)}) collective-permute-start(f32[128,128]{1,0:T(8,128)} %get-tuple-element.50), channel_id=1, source_target_pairs={{0,128},{128,0},{1,129},{129,1},{2,130},{130,2},{3,131},{131,3},{4... | collective-permute-start | bytes 196616 | tf_op jit(solution)/shard_map/ppermute | solution.py:40
  174.5 8.2 %collective-permute-start.19 = (f32[128,128]{1,0:T(8,128)S(1)}, f32[128,128]{1,0:T(8,128)S(1)}, u32[]{:S(2)}, u32[]{:S(2)}) collective-permute-start(f32[128,128]{1,0:T(8,128)S(1)} %slice_select_fusion), channel_id=1, source_target_pairs={{0,16},{4,20},{8,24},{12,28},{16,0},{20,4},{24,8},{28,12},{32,48},... | collective-permute-start | bytes 196616 | tf_op jit(solution)/shard_map/ppermute | solution.py:44
  177.0 31.6 %collective-permute-start.17 = (bf16[2048,256]{1,0:T(8,128)(2,1)}, bf16[2048,256]{1,0:T(8,128)(2,1)}, u32[]{:S(2)}, u32[]{:S(2)}) collective-permute-start(bf16[2048,256]{1,0:T(8,128)(2,1)} %bitcast.29.mine_first), channel_id=1, source_target_pairs={{0,128},{128,0},{1,129},{129,1},{2,130},{130,2},{3,131},{131,3},{4... | collective-permute-start | bytes 3145736 | tf_op jit(solution)/shard_map/ppermute | solution.py:40
  182.7 25.9 %collective-permute-start.18 = (bf16[2048,256]{1,0:T(8,128)(2,1)S(1)}, bf16[2048,256]{1,0:T(8,128)(2,1)}, u32[]{:S(2)}, u32[]{:S(2)}) collective-permute-start(bf16[2048,256]{1,0:T(8,128)(2,1)S(1)} %bitcast.139), channel_id=1, source_target_pairs={{0,128},{128,0},{1,129},{129,1},{2,130},{130,2},{3,131},{131,3},{4... | collective-permute-start | bytes 3145736 | tf_op jit(solution)/shard_map/ppermute | solution.py:40
  186.4 15.4 %collective-permute-start.26 = (bf16[256,128]{1,0:T(8,128)(2,1)S(1)}, bf16[256,128]{1,0:T(8,128)(2,1)}, u32[]{:S(2)}, u32[]{:S(2)}) collective-permute-start(bf16[256,128]{1,0:T(8,128)(2,1)S(1)} %fusion.15), channel_id=1, source_target_pairs={{0,3},{1,0},{2,1},{3,2},{4,7},{5,4},{6,5},{7,6},{8,11},{9,8},{10,9... | collective-permute-start | bytes 196616 | tf_op jit(solution)/shard_map/ppermute | solution.py:55
  188.2 12.3 %collective-permute-start.24 = (bf16[256,128]{1,0:T(8,128)(2,1)S(1)}, bf16[256,128]{1,0:T(8,128)(2,1)}, u32[]{:S(2)}, u32[]{:S(2)}) collective-permute-start(bf16[256,128]{1,0:T(8,128)(2,1)S(1)} %fusion.15), channel_id=1, source_target_pairs={{0,1},{1,2},{2,3},{3,0},{4,5},{5,6},{6,7},{7,4},{8,9},{9,10},{10,1... | collective-permute-start | bytes 196616 | tf_op jit(solution)/shard_map/ppermute | solution.py:55
  188.2 14.8 %collective-permute-start.25 = (bf16[256,128]{1,0:T(8,128)(2,1)S(1)}, bf16[256,128]{1,0:T(8,128)(2,1)S(1)}, u32[]{:S(2)}, u32[]{:S(2)}) collective-permute-start(bf16[256,128]{1,0:T(8,128)(2,1)S(1)} %fusion.15), channel_id=1, source_target_pairs={{0,2},{1,3},{2,0},{3,1},{4,6},{5,7},{6,4},{7,5},{8,10},{9,11},{10,... | collective-permute-start | bytes 196616 | tf_op jit(solution)/shard_map/ppermute | solution.py:55
  194.5 20.4 %all-to-all-start.5 = ((bf16[16,256,128]{2,1,0:T(8,128)(2,1)}), bf16[16,256,128]{2,1,0:T(8,128)(2,1)}, u32[]{:S(2)}, u32[]{:S(2)}) async-start(bf16[16,256,128]{2,1,0:T(8,128)(2,1)} %broadcast_in_dim.23), calls=%async_computation.5 | async-start | bytes 2097152 | tf_op jit(solution)/shard_map/all_to_all | solution.py:63
  205.8 31.6 %collective-permute-start.27 = (f32[128,2048]{1,0:T(8,128)}, f32[128,2048]{1,0:T(8,128)}, u32[]{:S(2)}, u32[]{:S(2)}) collective-permute-start(f32[128,2048]{1,0:T(8,128)} %slice.160), channel_id=1, source_target_pairs={{0,128},{128,0},{1,129},{129,1},{2,130},{130,2},{3,131},{131,3},{4... | collective-permute-start | bytes 3145736 | tf_op jit(solution)/shard_map/ppermute | solution.py:40
  207.9 18.5 %collective-permute-start.14 = (bf16[128,512]{1,0:T(8,128)(2,1)S(1)}, bf16[128,512]{1,0:T(8,128)(2,1)}, u32[]{:S(2)}, u32[]{:S(2)}) collective-permute-start(bf16[128,512]{1,0:T(8,128)(2,1)S(1)} %broadcast_select_fusion.3), channel_id=1, source_target_pairs={{0,128},{128,0},{1,129},{129,1},{2,130},{130,2},{3,131},{131,3},{4... | collective-permute-start | bytes 393224 | tf_op jit(solution)/shard_map/ppermute | solution.py:40
  208.1 20.0 %collective-permute-start.15 = (bf16[128,512]{1,0:T(8,128)(2,1)S(1)}, bf16[128,512]{1,0:T(8,128)(2,1)S(1)}, u32[]{:S(2)}, u32[]{:S(2)}) collective-permute-start(bf16[128,512]{1,0:T(8,128)(2,1)S(1)} %broadcast_select_fusion.2), channel_id=1, source_target_pairs={{0,128},{128,0},{1,129},{129,1},{2,130},{130,2},{3,131},{131,3},{4... | collective-permute-start | bytes 393224 | tf_op jit(solution)/shard_map/ppermute | solution.py:40
  219.5 11.3 %collective-permute-start.22 = (f32[128,128]{1,0:T(8,128)}, f32[128,128]{1,0:T(8,128)S(1)}, u32[]{:S(2)}, u32[]{:S(2)}) collective-permute-start(f32[128,128]{1,0:T(8,128)} %get-tuple-element.53), channel_id=1, source_target_pairs={{0,128},{128,0},{1,129},{129,1},{2,130},{130,2},{3,131},{131,3},{4... | collective-permute-start | bytes 196616 | tf_op jit(solution)/shard_map/ppermute | solution.py:40
  222.7 9.4 %collective-permute-start.23 = (f32[128,128]{1,0:T(8,128)}, f32[128,128]{1,0:T(8,128)S(1)}, u32[]{:S(2)}, u32[]{:S(2)}) collective-permute-start(f32[128,128]{1,0:T(8,128)} %get-tuple-element.54), channel_id=1, source_target_pairs={{0,144},{128,16},{4,148},{132,20},{8,152},{136,24},{12,156},{140,2... | collective-permute-start | bytes 196616 | tf_op jit(solution)/shard_map/ppermute | solution.py:51
  226.4 9.4 %collective-permute-start.21 = (f32[128,128]{1,0:T(8,128)}, f32[128,128]{1,0:T(8,128)S(1)}, u32[]{:S(2)}, u32[]{:S(2)}) collective-permute-start(f32[128,128]{1,0:T(8,128)} %get-tuple-element.52), channel_id=1, source_target_pairs={{0,16},{4,20},{8,24},{12,28},{16,0},{20,4},{24,8},{28,12},{32,48},... | collective-permute-start | bytes 196616 | tf_op jit(solution)/shard_map/ppermute | solution.py:44
  (36 other events, 379.5 us)

commit v6 on v5

--- a/solution.py
+++ b/solution.py
@@ -290,22 +290,17 @@
     )(place, *halves)
 
 
-def pack_kernel(source, *targets):
-    for group, target in enumerate(targets):
-        for x in range(NX):
-            for y in range(NY):
-                for z in range(NZ):
-                    column = group * (NX * NZ * NY) + ctx_of(x, z, y)
-                    target[x * NY + y, :, z * TOK : (z + 1) * TOK] = source[
-                        :, column * TOK : (column + 1) * TOK
-                    ]
-
-
-def owned_kernel(
-    place_ref, mine_first, mine_second, other_first, other_second, grads_ref,
-    here, above, beside, opposite,
-    sums, pieces,
-):
+def pack_kernel(place_ref, source, target):
+    group, z = place_ref[2] >> 1, place_ref[2] & 1
+    for x in range(NX):
+        for y in range(NY):
+            column = group * (NX * NZ * NY) + (x * NZ + z) * NY + y
+            target[x * NY + y] = source[:, pl.ds(pl.multiple_of(column * TOK, TOK), TOK)]
+
+
+def owned_kernel(place_ref, *refs):
+    mine, other, grads_ref = refs[:NT], refs[NT : 2 * NT], refs[2 * NT]
+    here, above, beside, opposite, sums, pieces = refs[2 * NT + 1 :]
     step = pl.program_id(0)
 
     @pl.when(step == 0)
@@ -314,38 +309,37 @@
 
     own = jnp.concatenate([grads_ref[i, :TOK] for i in range(NY)], 0)
     got = jnp.concatenate([grads_ref[i, TOK:] for i in range(NY)], 0)
-    for group, (mine, other) in enumerate(
-        ((mine_first, other_first), (mine_second, other_second))
-    ):
-        sums[group] += product(own, mine[...], 0, 0) + product(got, other[...], 0, 0)
+    own_columns = jnp.concatenate([ref[...] for ref in mine], 1)
+    got_columns = jnp.concatenate([ref[...] for ref in other], 1)
+    sums[...] += product(own, own_columns, 0, 0) + product(got, got_columns, 0, 0)
 
     @pl.when(step == pl.num_programs(0) - 1)
     def _():
-        for group in range(2):
-            for z in range(NZ):
-                pieces[group * NZ + z] = jnp.transpose(sums[group, :, z * TOK : (z + 1) * TOK])
+        for d in range(NT):
+            pieces[d] = jnp.transpose(sums[:, d * TOK : (d + 1) * TOK])
         core = place_ref[0]
         zone = (place_ref[1] >> 2) & 1
-        here[...] = pieces[core * NZ + zone]
-        above[...] = pieces[core * NZ + 1 - zone]
-        beside[...] = pieces[(1 - core) * NZ + zone]
-        opposite[...] = pieces[(1 - core) * NZ + 1 - zone]
+
+        def piece(group, part):
+            return pieces[(place_ref[2] - group * NZ - part) & (NT - 1)]
+
+        here[...] = piece(core, zone)
+        above[...] = piece(core, 1 - zone)
+        beside[...] = piece(1 - core, zone)
+        opposite[...] = piece(1 - core, 1 - zone)
 
 
 def owned_pieces(place, *arrays):
-    columns = pl.BlockSpec((NY * TOK, NZ * TOK), lambda i: (i, 0))
+    columns = pl.BlockSpec((NY * TOK, TOK), lambda i: (i, 0))
     grads = pl.BlockSpec((NY, 2 * TOK, HD), lambda i: (i, 0, 0))
     piece = jax.ShapeDtypeStruct((TOK, HD), F32)
     return pl.pallas_call(
         owned_kernel,
         grid=(NX,),
         out_shape=(piece,) * 4,
-        in_specs=[pl.BlockSpec(memory_space=pltpu.SMEM)] + [columns] * 4 + [grads],
+        in_specs=[pl.BlockSpec(memory_space=pltpu.SMEM)] + [columns] * (2 * NT) + [grads],
         out_specs=(pl.BlockSpec((TOK, HD), lambda i: (0, 0)),) * 4,
-        scratch_shapes=[
-            pltpu.VMEM((2, HD, NZ * TOK), F32),
-            pltpu.VMEM((2 * NZ, TOK, HD), F32),
-        ],
+        scratch_shapes=[pltpu.VMEM((HD, NT * TOK), F32), pltpu.VMEM((NT, TOK, HD), F32)],
         name="owned",
     )(place, *arrays)
 
@@ -395,16 +389,15 @@
     )(place, activations)
 
 
-def pack_columns(activations):
+def pack_columns(place, activations):
     vmem = pl.BlockSpec(memory_space=pltpu.VMEM)
-    packed = jax.ShapeDtypeStruct((NX * NY, TOK, NZ * TOK), activations.dtype)
     return pl.pallas_call(
         pack_kernel,
-        out_shape=(packed, packed),
-        in_specs=[vmem],
-        out_specs=(vmem, vmem),
+        out_shape=jax.ShapeDtypeStruct((NX * NY, TOK, TOK), activations.dtype),
+        in_specs=[pl.BlockSpec(memory_space=pltpu.SMEM), vmem],
+        out_specs=vmem,
         name="pack",
-    )(activations)
+    )(place, activations)
 
 
 def body(activations, queries, out_grad, key_weight, value_weight, sessions):
@@ -439,7 +432,7 @@
     far = lax.ppermute(weight, ("ctx", "tp"), FAR_TURN)
     weight = plane_copies(by_zone(near, far))
     weight = plane_exchange(weight)
-    packed = pack_columns(activations)
+    packed = pack_columns(place, activations)
     weight = weight.reshape(NX, NY * weight.shape[-2], HD)
 
     own_slice = feature_slice(place, activations)
@@ -458,7 +451,8 @@
     partial = jnp.einsum("tk,hkn->htn", both_slices, weight, preferred_element_type=F32)
     parts = [lax.dynamic_index_in_dim(partial, (tp + d) & (NT - 1), 0, False) for d in range(NT)]
     arrivals = [along(parts[d][:TOK], d) for d in range(1, NT)]
-    first_columns = plane_exchange(packed[0])
+    columns = plane_exchange(packed).reshape(plane * TOK, TOK)
+    columns = [columns] + [along(columns, d) for d in range(1, NT)]
     long_sum = parts[0][:TOK] + sum(arrivals)
     long_rows = role(turn(long_sum, cosine[:TOK], sine[:TOK]), long_sum).astype(BF16)
     parts, long_rows = after(parts, long_rows)
@@ -470,8 +464,6 @@
     context = plane_copies(by_zone(long_rows, across_rows))
     context = plane_exchange(context)
 
-    second, context = after(packed[1], context)
-    second_columns = plane_exchange(second)
     context = context.reshape(plane * NZ, TOK, HD)
     other_context = partner(context)
 
@@ -491,10 +483,7 @@
     attention, query_grad = join_heads(place, *out_parts, out_got, qgrad_got)
     kv_sums = kv_keep + partner(kv_send)
     short_kv = short_keep + partner(short_send)
-    blocks, second_columns = after(kv_sums.reshape(plane, NZ * TOK, HD), second_columns)
-    columns = [
-        array.reshape(plane * TOK, NZ * TOK) for array in (first_columns, second_columns)
-    ]
+    blocks = kv_sums.reshape(plane, NZ * TOK, HD)
     other_columns = [partner(array) for array in columns]
     arrived = plane_exchange(blocks)
     arrived = arrived.reshape(plane, NZ, TOK, HD).sum(0)
@@ -514,7 +503,7 @@
     input_grad = finish_input(terms, other_terms)
 
     here, above, beside, opposite = owned_pieces(
-        place, columns[0], columns[1], other_columns[0], other_columns[1], plane_grads
+        place, *columns, *other_columns, plane_grads
     )
     opposite = diagonal(opposite)
     same = here + across(above)

time: 241 us -> 252 us (1.046)
  the two profiles are of different devices: /device:TPU:33 before, /device:TPU:8 now
where the time goes in v6:
time: 252 us; the launch traced here: 247 us
  waiting for transfers between devices  98.5 us (39%)
  starting transfers between devices  97.4 us (39%)
  Pallas kernels  24.4 us (10%)
  other arithmetic  10.8 us (4%)
  local copies, waits for them, and re-layouts  9.44 us (4%)
  matrix products  5.59 us (2%)
    all_to_all x5, waiting for transfers between devices, plane_exchange(): lax.all_to_all(blocks, 'ctx', split_axis=0, concat_axis=0, tiled=True, ax...  52.4 us
    all_to_all x5, starting transfers between devices, plane_exchange(): lax.all_to_all(blocks, 'ctx', split_axis=0, concat_axis=0, tiled=True, ax...  42.3 us
    ppermute x12, starting transfers between devices, along(): return lax.ppermute(array, 'tp', [(t, (t + step) % NT) for t in range(NT)])  31.3 us
    ppermute x12, waiting for transfers between devices, along(): return lax.ppermute(array, 'tp', [(t, (t + step) % NT) for t in range(NT)])  28.4 us
    ppermute x15, waiting for transfers between devices, partner(): return lax.ppermute(array, 'group', [(0, 1), (1, 0)])  10.2 us
    ppermute x3, starting transfers between devices, across(): return lax.ppermute(array, 'ctx', ACROSS)  9.79 us
    pallas_call x1, Pallas kernels, attention_call(): pl.pallas_call(attention_kernel, out_shape=(rows, rows, blocks, blocks),...  7.38 us
    ppermute x1, starting transfers between devices, body(): far = lax.ppermute(weight, ('ctx', 'tp'), FAR_TURN)  7.28 us
  transfers between devices with their start and end apart: 38, of which 19 were waited for; matrix products, arithmetic and copies ran while one was open for 6% of the time, Pallas kernels for 6%

profile of v6, /device:TPU:8, one launch (start us, length us, event | category | flops | bytes accessed | tf_op | source)
XLA Modules:
  0.0 247.3 jit_solution(13052729431819317838)
XLA Ops:
  1.5 7.3 %collective-permute-start.2 = (bf16[256,128]{1,0:T(8,128)(2,1)S(1)}, bf16[256,128]{1,0:T(8,128)(2,1)S(1)}, u32[]{:S(2)}, u32[]{:S(2)}) collective-permute-start(bf16[256,128]{1,0:T(8,128)(2,1)S(1)} %broadcast_select_fusion.8), channel_id=1, source_target_pairs={{0,16},{1,48},{2,80},{3,112},{4,20},{5,52},{6,84},{7,116},{8,24},{... | collective-permute-start | bytes 196616 | tf_op jit(solution)/shard_map/ppermute | solution.py:432
  12.9 14.3 %all-to-all-start = ((bf16[16,512,128]{2,1,0:T(8,128)(2,1)}), bf16[16,512,128]{2,1,0:T(8,128)(2,1)S(1)}, u32[]{:S(2)}, u32[]{:S(2)}) async-start(bf16[16,512,128]{2,1,0:T(8,128)(2,1)} %broadcast_in_dim.16), calls=%async_computation | async-start | bytes 4194304 | tf_op jit(solution)/shard_map/all_to_all | solution.py:63
  27.8 2.5 %feature_slice.1 = bf16[128,2048]{1,0:T(8,128)(2,1)} custom-call(s32[3]{0:T(128)} %pad_add_fusion.place_ref, bf16[128,8192]{1,0:T(8,128)(2,1)} %source.3), custom_call_target="tpu_custom_call" | custom-call | tf_op jit(solution)/shard_map/feature_slice/pallas_call | solution.py:379
  30.4 2.1 collective-permute-done.4
  34.4 20.1 %all-to-all-done = bf16[16,512,128]{2,1,0:T(8,128)(2,1)S(1)} async-done(((bf16[16,512,128]{2,1,0:T(8,128)(2,1)}), bf16[16,512,128]{2,1,0:T(8,128)(2,1)S(1)}, u32[]{:S(2)}, u32[]{:S(2)}) %all-to-all-start) | async-done | bytes 2097184 | tf_op jit(solution)/shard_map/all_to_all | solution.py:63
  54.5 2.1 fusion.1
  64.3 3.7 %collective-permute-start.8 = (bf16[128,128]{1,0:T(8,128)(2,1)S(1)}, bf16[128,128]{1,0:T(8,128)(2,1)S(1)}, u32[]{:S(2)}, u32[]{:S(2)}) collective-permute-start(bf16[128,128]{1,0:T(8,128)(2,1)S(1)} %fusion.21), channel_id=1, source_target_pairs={{0,16},{4,20},{8,24},{12,28},{16,0},{20,4},{24,8},{28,12},{32,48},... | collective-permute-start | bytes 98312 | tf_op jit(solution)/shard_map/ppermute | solution.py:44
  67.9 4.3 %collective-permute-done.8 = bf16[128,128]{1,0:T(8,128)(2,1)S(1)} collective-permute-done((bf16[128,128]{1,0:T(8,128)(2,1)S(1)}, bf16[128,128]{1,0:T(8,128)(2,1)S(1)}, u32[]{:S(2)}, u32[]{:S(2)}) %collective-permute-start.8) | collective-permute-done | bytes 32800 | tf_op jit(solution)/shard_map/ppermute | solution.py:44
  73.4 5.2 %all-to-all-start.1 = ((bf16[16,256,128]{2,1,0:T(8,128)(2,1)}), bf16[16,256,128]{2,1,0:T(8,128)(2,1)S(1)}, u32[]{:S(2)}, u32[]{:S(2)}) async-start(bf16[16,256,128]{2,1,0:T(8,128)(2,1)} %broadcast_in_dim.19), calls=%async_computation.1 | async-start | bytes 2097152 | tf_op jit(solution)/shard_map/all_to_all | solution.py:63
  79.1 11.1 %all-to-all-done.1 = bf16[16,256,128]{2,1,0:T(8,128)(2,1)S(1)} async-done(((bf16[16,256,128]{2,1,0:T(8,128)(2,1)}), bf16[16,256,128]{2,1,0:T(8,128)(2,1)S(1)}, u32[]{:S(2)}, u32[]{:S(2)}) %all-to-all-start.1) | async-done | bytes 1048608 | tf_op jit(solution)/shard_map/all_to_all | solution.py:63
  93.2 7.4 %attention.1 = (bf16[128,512]{1,0:T(8,128)(2,1)S(1)}, bf16[128,512]{1,0:T(8,128)(2,1)S(1)}, f32[32,128,128]{2,1,0:T(8,128)S(1)}, f32[32,128,128]{2,1,0:T(8,128)}) custom-call(s32[3]{0:T(128)S(1)} %copy-done.7, bf16[128,512]{1,0:T(8,128)(2,1)S(1)} %get-tuple-element.68.q_keep, bf16[128,512]{1,0:T(8,128)(2,1)S(1)} %collective-permute-done.q_got, ...), custom_call_target="tpu_custom_call" | custom-call | tf_op jit(solution)/shard_map/attention/pallas_call | solution.py:253
  100.7 4.2 %collective-permute-done.23 = f32[32,128,128]{2,1,0:T(8,128)S(1)} collective-permute-done((f32[32,128,128]{2,1,0:T(8,128)}, f32[32,128,128]{2,1,0:T(8,128)S(1)}, u32[]{:S(2)}, u32[]{:S(2)}) %collective-permute-start.23) | collective-permute-done | bytes 2097184 | tf_op jit(solution)/shard_map/ppermute | solution.py:40
  106.6 9.2 %all-to-all-start.3 = ((f32[16,256,128]{2,1,0:T(8,128)}), f32[16,256,128]{2,1,0:T(8,128)S(1)}, u32[]{:S(2)}, u32[]{:S(2)}) async-start(f32[16,256,128]{2,1,0:T(8,128)} %bitcast.30), calls=%async_computation.3 | async-start | bytes 4194304 | tf_op jit(solution)/shard_map/all_to_all | solution.py:63
  115.8 2.7 %collective-permute-start.10 = (f32[128,128]{1,0:T(8,128)S(1)}, f32[128,128]{1,0:T(8,128)S(1)}, u32[]{:S(2)}, u32[]{:S(2)}) collective-permute-start(f32[128,128]{1,0:T(8,128)S(1)} %slice.130), channel_id=1, source_target_pairs={{0,1},{1,2},{2,3},{3,0},{4,5},{5,6},{6,7},{7,4},{8,9},{9,10},{10,1... | collective-permute-start | bytes 196616 | tf_op jit(solution)/shard_map/ppermute | solution.py:55
  121.1 2.5 %pack.1 = bf16[16,128,128]{2,1,0:T(8,128)(2,1)} custom-call(s32[3]{0:T(128)} %pad_add_fusion.place_ref, bf16[128,8192]{1,0:T(8,128)(2,1)} %source.3), custom_call_target="tpu_custom_call" | custom-call | tf_op jit(solution)/shard_map/pack/pallas_call | solution.py:394
  125.2 20.4 %all-to-all-done.3 = f32[16,256,128]{2,1,0:T(8,128)S(1)} async-done(((f32[16,256,128]{2,1,0:T(8,128)}), f32[16,256,128]{2,1,0:T(8,128)S(1)}, u32[]{:S(2)}, u32[]{:S(2)}) %all-to-all-start.3) | async-done | bytes 2097184 | tf_op jit(solution)/shard_map/all_to_all | solution.py:63
  145.6 5.4 %all-to-all-start.2 = ((bf16[16,128,128]{2,1,0:T(8,128)(2,1)}), bf16[16,128,128]{2,1,0:T(8,128)(2,1)}, u32[]{:S(2)}, u32[]{:S(2)}) async-start(bf16[16,128,128]{2,1,0:T(8,128)(2,1)} %pack.1), calls=%async_computation.2 | async-start | bytes 1048576 | tf_op jit(solution)/shard_map/all_to_all | solution.py:63
  152.4 2.7 %short_attention.1 = (bf16[128,512]{1,0:T(8,128)(2,1)}, bf16[128,512]{1,0:T(8,128)(2,1)}, f32[128,128]{1,0:T(8,128)}, f32[128,128]{1,0:T(8,128)}) custom-call(s32[3]{0:T(128)} %pad_add_fusion.place_ref, bf16[128,512]{1,0:T(8,128)(2,1)} %copy-done, bf16[128,512]{1,0:T(8,128)(2,1)} %copy-done.3, bf16[128,512]{1,0:T(8,128)(2,1)} %copy-done.1, ...), custom_call_target="tpu_custom_call" | custom-call | tf_op jit(solution)/shard_map/short_attention/pallas_call | solution.py:240
  155.2 3.8 %collective-permute-start.24 = (f32[128,128]{1,0:T(8,128)S(1)}, f32[128,128]{1,0:T(8,128)S(1)}, u32[]{:S(2)}, u32[]{:S(2)}) collective-permute-start(f32[128,128]{1,0:T(8,128)S(1)} %slice_select_fusion), channel_id=1, source_target_pairs={{0,16},{4,20},{8,24},{12,28},{16,0},{20,4},{24,8},{28,12},{32,48},... | collective-permute-start | bytes 196616 | tf_op jit(solution)/shard_map/ppermute | solution.py:44
  160.0 2.6 %collective-permute-start.16 = (bf16[2048,128]{1,0:T(8,128)(2,1)}, bf16[2048,128]{1,0:T(8,128)(2,1)}, u32[]{:S(2)}, u32[]{:S(2)}) collective-permute-start(bf16[2048,128]{1,0:T(8,128)(2,1)} %bitcast.29.refs_0_), channel_id=1, source_target_pairs={{0,1},{1,2},{2,3},{3,0},{4,5},{5,6},{6,7},{7,4},{8,9},{9,10},{10,1... | collective-permute-start | bytes 1572872 | tf_op jit(solution)/shard_map/ppermute | solution.py:55
  165.9 13.1 %collective-permute-start.29 = (bf16[256,128]{1,0:T(8,128)(2,1)}, bf16[256,128]{1,0:T(8,128)(2,1)}, u32[]{:S(2)}, u32[]{:S(2)}) collective-permute-start(bf16[256,128]{1,0:T(8,128)(2,1)} %fusion.15), channel_id=1, source_target_pairs={{0,1},{1,2},{2,3},{3,0},{4,5},{5,6},{6,7},{7,4},{8,9},{9,10},{10,1... | collective-permute-start | bytes 196616 | tf_op jit(solution)/shard_map/ppermute | solution.py:55
  179.0 2.1 broadcast_in_dim.23
  181.1 8.2 %all-to-all-start.4 = ((bf16[16,256,128]{2,1,0:T(8,128)(2,1)}), bf16[16,256,128]{2,1,0:T(8,128)(2,1)S(1)}, u32[]{:S(2)}, u32[]{:S(2)}) async-start(bf16[16,256,128]{2,1,0:T(8,128)(2,1)} %broadcast_in_dim.23), calls=%async_computation.4 | async-start | bytes 2097152 | tf_op jit(solution)/shard_map/all_to_all | solution.py:63
  190.7 10.8 %collective-permute-done.29 = bf16[256,128]{1,0:T(8,128)(2,1)} collective-permute-done((bf16[256,128]{1,0:T(8,128)(2,1)}, bf16[256,128]{1,0:T(8,128)(2,1)}, u32[]{:S(2)}, u32[]{:S(2)}) %collective-permute-start.29) | collective-permute-done | bytes 65568 | tf_op jit(solution)/shard_map/ppermute | solution.py:55
  202.8 11.4 %collective-permute-done.31 = bf16[256,128]{1,0:T(8,128)(2,1)S(1)} collective-permute-done((bf16[256,128]{1,0:T(8,128)(2,1)}, bf16[256,128]{1,0:T(8,128)(2,1)S(1)}, u32[]{:S(2)}, u32[]{:S(2)}) %collective-permute-start.31) | collective-permute-done | bytes 65568 | tf_op jit(solution)/shard_map/ppermute | solution.py:55
  214.2 3.9 %collective-permute-start.30 = (bf16[256,128]{1,0:T(8,128)(2,1)}, bf16[256,128]{1,0:T(8,128)(2,1)S(1)}, u32[]{:S(2)}, u32[]{:S(2)}) collective-permute-start(bf16[256,128]{1,0:T(8,128)(2,1)} %fusion.15), channel_id=1, source_target_pairs={{0,2},{1,3},{2,0},{3,1},{4,6},{5,7},{6,4},{7,5},{8,10},{9,11},{10,... | collective-permute-start | bytes 196616 | tf_op jit(solution)/shard_map/ppermute | solution.py:55
  218.6 2.0 collective-permute-done.30
  227.3 4.8 %owned.1 = (f32[128,128]{1,0:T(8,128)}, f32[128,128]{1,0:T(8,128)}, f32[128,128]{1,0:T(8,128)}, f32[128,128]{1,0:T(8,128)}) custom-call(s32[3]{0:T(128)} %pad_add_fusion.place_ref, bf16[2048,128]{1,0:T(8,128)(2,1)} %bitcast.29.refs_0_, bf16[2048,128]{1,0:T(8,128)(2,1)} %collective-permute-done.16.refs_1_, bf16[2048,128]{1,0:T(8,128)(2,1)} %collective-permute-done.17.refs_2_, ...), custom_call_target="tpu_custom_call" | custom-call | tf_op jit(solution)/shard_map/owned/pallas_call | solution.py:336
  232.0 2.3 collective-permute-start.26
  234.4 3.8 %collective-permute-start.28 = (f32[128,128]{1,0:T(8,128)}, f32[128,128]{1,0:T(8,128)S(1)}, u32[]{:S(2)}, u32[]{:S(2)}) collective-permute-start(f32[128,128]{1,0:T(8,128)} %get-tuple-element.42), channel_id=1, source_target_pairs={{0,144},{128,16},{4,148},{132,20},{8,152},{136,24},{12,156},{140,2... | collective-permute-start | bytes 196616 | tf_op jit(solution)/shard_map/ppermute | solution.py:51
  238.8 2.0 join.1
  244.8 2.5 finish.1
  (162 shorter events, 45.7 us)
Async XLA Ops:
  1.5 9.7 %collective-permute-start.2 = (bf16[256,128]{1,0:T(8,128)(2,1)S(1)}, bf16[256,128]{1,0:T(8,128)(2,1)S(1)}, u32[]{:S(2)}, u32[]{:S(2)}) collective-permute-start(bf16[256,128]{1,0:T(8,128)(2,1)S(1)} %broadcast_select_fusion.8), channel_id=1, source_target_pairs={{0,16},{1,48},{2,80},{3,112},{4,20},{5,52},{6,84},{7,116},{8,24},{... | collective-permute-start | bytes 196616 | tf_op jit(solution)/shard_map/ppermute | solution.py:432
  12.9 41.5 %all-to-all-start = ((bf16[16,512,128]{2,1,0:T(8,128)(2,1)}), bf16[16,512,128]{2,1,0:T(8,128)(2,1)S(1)}, u32[]{:S(2)}, u32[]{:S(2)}) async-start(bf16[16,512,128]{2,1,0:T(8,128)(2,1)} %broadcast_in_dim.16), calls=%async_computation | async-start | bytes 4194304 | tf_op jit(solution)/shard_map/all_to_all | solution.py:63
  56.7 6.2 %collective-permute-start.5 = (f32[128,128]{1,0:T(8,128)S(1)}, f32[128,128]{1,0:T(8,128)S(1)}, u32[]{:S(2)}, u32[]{:S(2)}) collective-permute-start(f32[128,128]{1,0:T(8,128)S(1)} %slice_bitcast_fusion.2), channel_id=1, source_target_pairs={{0,1},{1,2},{2,3},{3,0},{4,5},{5,6},{6,7},{7,4},{8,9},{9,10},{10,1... | collective-permute-start | bytes 196616 | tf_op jit(solution)/shard_map/ppermute | solution.py:55
  57.5 6.6 %collective-permute-start.6 = (f32[128,128]{1,0:T(8,128)S(1)}, f32[128,128]{1,0:T(8,128)S(1)}, u32[]{:S(2)}, u32[]{:S(2)}) collective-permute-start(f32[128,128]{1,0:T(8,128)S(1)} %slice_bitcast_fusion.1), channel_id=1, source_target_pairs={{0,2},{1,3},{2,0},{3,1},{4,6},{5,7},{6,4},{7,5},{8,10},{9,11},{10,... | collective-permute-start | bytes 196616 | tf_op jit(solution)/shard_map/ppermute | solution.py:55
  59.3 4.7 %collective-permute-start.7 = (f32[128,128]{1,0:T(8,128)S(1)}, f32[128,128]{1,0:T(8,128)S(1)}, u32[]{:S(2)}, u32[]{:S(2)}) collective-permute-start(f32[128,128]{1,0:T(8,128)S(1)} %slice_bitcast_fusion), channel_id=1, source_target_pairs={{0,3},{1,0},{2,1},{3,2},{4,7},{5,4},{6,5},{7,6},{8,11},{9,8},{10,9... | collective-permute-start | bytes 196616 | tf_op jit(solution)/shard_map/ppermute | solution.py:55
  64.3 7.9 %collective-permute-start.8 = (bf16[128,128]{1,0:T(8,128)(2,1)S(1)}, bf16[128,128]{1,0:T(8,128)(2,1)S(1)}, u32[]{:S(2)}, u32[]{:S(2)}) collective-permute-start(bf16[128,128]{1,0:T(8,128)(2,1)S(1)} %fusion.21), channel_id=1, source_target_pairs={{0,16},{4,20},{8,24},{12,28},{16,0},{20,4},{24,8},{28,12},{32,48},... | collective-permute-start | bytes 98312 | tf_op jit(solution)/shard_map/ppermute | solution.py:44
  73.4 16.7 %all-to-all-start.1 = ((bf16[16,256,128]{2,1,0:T(8,128)(2,1)}), bf16[16,256,128]{2,1,0:T(8,128)(2,1)S(1)}, u32[]{:S(2)}, u32[]{:S(2)}) async-start(bf16[16,256,128]{2,1,0:T(8,128)(2,1)} %broadcast_in_dim.19), calls=%async_computation.1 | async-start | bytes 2097152 | tf_op jit(solution)/shard_map/all_to_all | solution.py:63
  100.5 4.4 %collective-permute-start.23 = (f32[32,128,128]{2,1,0:T(8,128)}, f32[32,128,128]{2,1,0:T(8,128)S(1)}, u32[]{:S(2)}, u32[]{:S(2)}) collective-permute-start(f32[32,128,128]{2,1,0:T(8,128)} %get-tuple-element.36), channel_id=1, source_target_pairs={{0,128},{128,0},{1,129},{129,1},{2,130},{130,2},{3,131},{131,3},{4... | collective-permute-start | bytes 6291464 | tf_op jit(solution)/shard_map/ppermute | solution.py:40
  106.6 38.9 %all-to-all-start.3 = ((f32[16,256,128]{2,1,0:T(8,128)}), f32[16,256,128]{2,1,0:T(8,128)S(1)}, u32[]{:S(2)}, u32[]{:S(2)}) async-start(f32[16,256,128]{2,1,0:T(8,128)} %bitcast.30), calls=%async_computation.3 | async-start | bytes 4194304 | tf_op jit(solution)/shard_map/all_to_all | solution.py:63
  115.8 7.8 %collective-permute-start.10 = (f32[128,128]{1,0:T(8,128)S(1)}, f32[128,128]{1,0:T(8,128)S(1)}, u32[]{:S(2)}, u32[]{:S(2)}) collective-permute-start(f32[128,128]{1,0:T(8,128)S(1)} %slice.130), channel_id=1, source_target_pairs={{0,1},{1,2},{2,3},{3,0},{4,5},{5,6},{6,7},{7,4},{8,9},{9,10},{10,1... | collective-permute-start | bytes 196616 | tf_op jit(solution)/shard_map/ppermute | solution.py:55
  118.5 6.3 %collective-permute-start.11 = (f32[128,128]{1,0:T(8,128)S(1)}, f32[128,128]{1,0:T(8,128)S(1)}, u32[]{:S(2)}, u32[]{:S(2)}) collective-permute-start(f32[128,128]{1,0:T(8,128)S(1)} %slice.131), channel_id=1, source_target_pairs={{0,2},{1,3},{2,0},{3,1},{4,6},{5,7},{6,4},{7,5},{8,10},{9,11},{10,... | collective-permute-start | bytes 196616 | tf_op jit(solution)/shard_map/ppermute | solution.py:55
  119.4 5.5 %collective-permute-start.12 = (f32[128,128]{1,0:T(8,128)S(1)}, f32[128,128]{1,0:T(8,128)S(1)}, u32[]{:S(2)}, u32[]{:S(2)}) collective-permute-start(f32[128,128]{1,0:T(8,128)S(1)} %slice.132), channel_id=1, source_target_pairs={{0,3},{1,0},{2,1},{3,2},{4,7},{5,4},{6,5},{7,6},{8,11},{9,8},{10,9... | collective-permute-start | bytes 196616 | tf_op jit(solution)/shard_map/ppermute | solution.py:55
  125.1 26.6 %collective-permute-start.13 = (bf16[128,128]{1,0:T(8,128)(2,1)S(1)}, bf16[128,128]{1,0:T(8,128)(2,1)S(1)}, u32[]{:S(2)}, u32[]{:S(2)}) collective-permute-start(bf16[128,128]{1,0:T(8,128)(2,1)S(1)} %fusion.23.short_mine), channel_id=1, source_target_pairs={{0,128},{128,0},{1,129},{129,1},{2,130},{130,2},{3,131},{131,3},{4... | collective-permute-start | bytes 98312 | tf_op jit(solution)/shard_map/ppermute | solution.py:40
  145.6 14.4 %all-to-all-start.2 = ((bf16[16,128,128]{2,1,0:T(8,128)(2,1)}), bf16[16,128,128]{2,1,0:T(8,128)(2,1)}, u32[]{:S(2)}, u32[]{:S(2)}) async-start(bf16[16,128,128]{2,1,0:T(8,128)(2,1)} %pack.1), calls=%async_computation.2 | async-start | bytes 1048576 | tf_op jit(solution)/shard_map/all_to_all | solution.py:63
  155.0 9.9 %collective-permute-start.25 = (f32[128,128]{1,0:T(8,128)}, f32[128,128]{1,0:T(8,128)S(1)}, u32[]{:S(2)}, u32[]{:S(2)}) collective-permute-start(f32[128,128]{1,0:T(8,128)} %get-tuple-element.38), channel_id=1, source_target_pairs={{0,128},{128,0},{1,129},{129,1},{2,130},{130,2},{3,131},{131,3},{4... | collective-permute-start | bytes 196616 | tf_op jit(solution)/shard_map/ppermute | solution.py:40
  155.2 9.7 %collective-permute-start.24 = (f32[128,128]{1,0:T(8,128)S(1)}, f32[128,128]{1,0:T(8,128)S(1)}, u32[]{:S(2)}, u32[]{:S(2)}) collective-permute-start(f32[128,128]{1,0:T(8,128)S(1)} %slice_select_fusion), channel_id=1, source_target_pairs={{0,16},{4,20},{8,24},{12,28},{16,0},{20,4},{24,8},{28,12},{32,48},... | collective-permute-start | bytes 196616 | tf_op jit(solution)/shard_map/ppermute | solution.py:44
  160.0 61.3 %collective-permute-start.16 = (bf16[2048,128]{1,0:T(8,128)(2,1)}, bf16[2048,128]{1,0:T(8,128)(2,1)}, u32[]{:S(2)}, u32[]{:S(2)}) collective-permute-start(bf16[2048,128]{1,0:T(8,128)(2,1)} %bitcast.29.refs_0_), channel_id=1, source_target_pairs={{0,1},{1,2},{2,3},{3,0},{4,5},{5,6},{6,7},{7,4},{8,9},{9,10},{10,1... | collective-permute-start | bytes 1572872 | tf_op jit(solution)/shard_map/ppermute | solution.py:55
  162.6 59.2 %collective-permute-start.17 = (bf16[2048,128]{1,0:T(8,128)(2,1)}, bf16[2048,128]{1,0:T(8,128)(2,1)}, u32[]{:S(2)}, u32[]{:S(2)}) collective-permute-start(bf16[2048,128]{1,0:T(8,128)(2,1)} %bitcast.29.refs_0_), channel_id=1, source_target_pairs={{0,2},{1,3},{2,0},{3,1},{4,6},{5,7},{6,4},{7,5},{8,10},{9,11},{10,... | collective-permute-start | bytes 1572872 | tf_op jit(solution)/shard_map/ppermute | solution.py:55
  163.4 58.5 %collective-permute-start.18 = (bf16[2048,128]{1,0:T(8,128)(2,1)}, bf16[2048,128]{1,0:T(8,128)(2,1)}, u32[]{:S(2)}, u32[]{:S(2)}) collective-permute-start(bf16[2048,128]{1,0:T(8,128)(2,1)} %bitcast.29.refs_0_), channel_id=1, source_target_pairs={{0,3},{1,0},{2,1},{3,2},{4,7},{5,4},{6,5},{7,6},{8,11},{9,8},{10,9... | collective-permute-start | bytes 1572872 | tf_op jit(solution)/shard_map/ppermute | solution.py:55
  165.0 58.0 %collective-permute-start.19 = (bf16[2048,128]{1,0:T(8,128)(2,1)}, bf16[2048,128]{1,0:T(8,128)(2,1)}, u32[]{:S(2)}, u32[]{:S(2)}) collective-permute-start(bf16[2048,128]{1,0:T(8,128)(2,1)} %bitcast.29.refs_0_), channel_id=1, source_target_pairs={{0,128},{128,0},{1,129},{129,1},{2,130},{130,2},{3,131},{131,3},{4... | collective-permute-start | bytes 1572872 | tf_op jit(solution)/shard_map/ppermute | solution.py:40
  165.9 35.6 %collective-permute-start.29 = (bf16[256,128]{1,0:T(8,128)(2,1)}, bf16[256,128]{1,0:T(8,128)(2,1)}, u32[]{:S(2)}, u32[]{:S(2)}) collective-permute-start(bf16[256,128]{1,0:T(8,128)(2,1)} %fusion.15), channel_id=1, source_target_pairs={{0,1},{1,2},{2,3},{3,0},{4,5},{5,6},{6,7},{7,4},{8,9},{9,10},{10,1... | collective-permute-start | bytes 196616 | tf_op jit(solution)/shard_map/ppermute | solution.py:55
  181.1 45.2 %all-to-all-start.4 = ((bf16[16,256,128]{2,1,0:T(8,128)(2,1)}), bf16[16,256,128]{2,1,0:T(8,128)(2,1)S(1)}, u32[]{:S(2)}, u32[]{:S(2)}) async-start(bf16[16,256,128]{2,1,0:T(8,128)(2,1)} %broadcast_in_dim.23), calls=%async_computation.4 | async-start | bytes 2097152 | tf_op jit(solution)/shard_map/all_to_all | solution.py:63
  201.5 12.7 %collective-permute-start.31 = (bf16[256,128]{1,0:T(8,128)(2,1)}, bf16[256,128]{1,0:T(8,128)(2,1)S(1)}, u32[]{:S(2)}, u32[]{:S(2)}) collective-permute-start(bf16[256,128]{1,0:T(8,128)(2,1)} %fusion.15), channel_id=1, source_target_pairs={{0,3},{1,0},{2,1},{3,2},{4,7},{5,4},{6,5},{7,6},{8,11},{9,8},{10,9... | collective-permute-start | bytes 196616 | tf_op jit(solution)/shard_map/ppermute | solution.py:55
  214.2 6.4 %collective-permute-start.30 = (bf16[256,128]{1,0:T(8,128)(2,1)}, bf16[256,128]{1,0:T(8,128)(2,1)S(1)}, u32[]{:S(2)}, u32[]{:S(2)}) collective-permute-start(bf16[256,128]{1,0:T(8,128)(2,1)} %fusion.15), channel_id=1, source_target_pairs={{0,2},{1,3},{2,0},{3,1},{4,6},{5,7},{6,4},{7,5},{8,10},{9,11},{10,... | collective-permute-start | bytes 196616 | tf_op jit(solution)/shard_map/ppermute | solution.py:55
  221.2 22.6 %collective-permute-start.32 = (f32[128,2048]{1,0:T(8,128)S(1)}, f32[128,2048]{1,0:T(8,128)S(1)}, u32[]{:S(2)}, u32[]{:S(2)}) collective-permute-start(f32[128,2048]{1,0:T(8,128)S(1)} %slice.160), channel_id=1, source_target_pairs={{0,128},{128,0},{1,129},{129,1},{2,130},{130,2},{3,131},{131,3},{4... | collective-permute-start | bytes 3145736 | tf_op jit(solution)/shard_map/ppermute | solution.py:40
  221.8 3.6 %collective-permute-start.21 = (bf16[2048,128]{1,0:T(8,128)(2,1)}, bf16[2048,128]{1,0:T(8,128)(2,1)S(1)}, u32[]{:S(2)}, u32[]{:S(2)}) collective-permute-start(bf16[2048,128]{1,0:T(8,128)(2,1)} %collective-permute-done.17.refs_2_), channel_id=1, source_target_pairs={{0,128},{128,0},{1,129},{129,1},{2,130},{130,2},{3,131},{131,3},{4... | collective-permute-start | bytes 1572872 | tf_op jit(solution)/shard_map/ppermute | solution.py:40
  221.9 4.4 %collective-permute-start.22 = (bf16[2048,128]{1,0:T(8,128)(2,1)}, bf16[2048,128]{1,0:T(8,128)(2,1)}, u32[]{:S(2)}, u32[]{:S(2)}) collective-permute-start(bf16[2048,128]{1,0:T(8,128)(2,1)} %collective-permute-done.18.refs_3_), channel_id=1, source_target_pairs={{0,128},{128,0},{1,129},{129,1},{2,130},{130,2},{3,131},{131,3},{4... | collective-permute-start | bytes 1572872 | tf_op jit(solution)/shard_map/ppermute | solution.py:40
  223.0 11.4 %collective-permute-start.15 = (bf16[128,512]{1,0:T(8,128)(2,1)}, bf16[128,512]{1,0:T(8,128)(2,1)}, u32[]{:S(2)}, u32[]{:S(2)}) collective-permute-start(bf16[128,512]{1,0:T(8,128)(2,1)} %broadcast_select_fusion.2), channel_id=1, source_target_pairs={{0,128},{128,0},{1,129},{129,1},{2,130},{130,2},{3,131},{131,3},{4... | collective-permute-start | bytes 393224 | tf_op jit(solution)/shard_map/ppermute | solution.py:40
  224.7 13.5 %collective-permute-start.14 = (bf16[128,512]{1,0:T(8,128)(2,1)S(1)}, bf16[128,512]{1,0:T(8,128)(2,1)S(1)}, u32[]{:S(2)}, u32[]{:S(2)}) collective-permute-start(bf16[128,512]{1,0:T(8,128)(2,1)S(1)} %broadcast_select_fusion.3), channel_id=1, source_target_pairs={{0,128},{128,0},{1,129},{129,1},{2,130},{130,2},{3,131},{131,3},{4... | collective-permute-start | bytes 393224 | tf_op jit(solution)/shard_map/ppermute | solution.py:40
  232.0 8.8 %collective-permute-start.26 = (f32[128,128]{1,0:T(8,128)}, f32[128,128]{1,0:T(8,128)S(1)}, u32[]{:S(2)}, u32[]{:S(2)}) collective-permute-start(f32[128,128]{1,0:T(8,128)} %get-tuple-element.40), channel_id=1, source_target_pairs={{0,16},{4,20},{8,24},{12,28},{16,0},{20,4},{24,8},{28,12},{32,48},... | collective-permute-start | bytes 196616 | tf_op jit(solution)/shard_map/ppermute | solution.py:44
  234.4 6.5 %collective-permute-start.27 = (f32[128,128]{1,0:T(8,128)}, f32[128,128]{1,0:T(8,128)S(1)}, u32[]{:S(2)}, u32[]{:S(2)}) collective-permute-start(f32[128,128]{1,0:T(8,128)} %get-tuple-element.41), channel_id=1, source_target_pairs={{0,128},{128,0},{1,129},{129,1},{2,130},{130,2},{3,131},{131,3},{4... | collective-permute-start | bytes 196616 | tf_op jit(solution)/shard_map/ppermute | solution.py:40
  234.4 7.9 %collective-permute-start.28 = (f32[128,128]{1,0:T(8,128)}, f32[128,128]{1,0:T(8,128)S(1)}, u32[]{:S(2)}, u32[]{:S(2)}) collective-permute-start(f32[128,128]{1,0:T(8,128)} %get-tuple-element.42), channel_id=1, source_target_pairs={{0,144},{128,16},{4,148},{132,20},{8,152},{136,24},{12,156},{140,2... | collective-permute-start | bytes 196616 | tf_op jit(solution)/shard_map/ppermute | solution.py:51
  (32 other events, 511.9 us)

commit v7 on v6

--- a/solution.py
+++ b/solution.py
@@ -86,6 +86,7 @@
 
 
 GH = 4
+VMEM_LIMIT = 22 << 20
 ROWS = GH * TOK
 ZONES = 4
 CHUNK = ZONES * NY * TOK
@@ -242,6 +243,7 @@
         out_shape=(rows, rows, block, block),
         in_specs=[pl.BlockSpec(memory_space=pltpu.SMEM)] + [vmem] * len(arrays),
         out_specs=(vmem,) * 4,
+        compiler_params=pltpu.CompilerParams(vmem_limit_bytes=6 << 20),
         name="short_attention",
     )(place, *arrays)
 
@@ -261,7 +263,7 @@
             pltpu.VMEM((HD, ROWS), F32),
             pltpu.VMEM((HD, ROWS), F32),
         ],
-        compiler_params=pltpu.CompilerParams(vmem_limit_bytes=48 << 20),
+        compiler_params=pltpu.CompilerParams(vmem_limit_bytes=VMEM_LIMIT),
         name="attention",
     )(place, *arrays)
 
@@ -286,8 +288,36 @@
         out_shape=(whole, whole),
         in_specs=[pl.BlockSpec(memory_space=pltpu.SMEM)] + [vmem] * len(halves),
         out_specs=(vmem, vmem),
+        compiler_params=pltpu.CompilerParams(vmem_limit_bytes=5 << 20),
         name="join",
     )(place, *halves)
+
+
+def query_kernel(place_ref, queries, cosine_ref, sine_ref, keep, send):
+    first = place_ref[0] == 0
+
+    def turned(head):
+        rows = queries[:, head * HD : (head + 1) * HD].astype(F32)
+        rows = rows * cosine_ref[...] + pltpu.roll(rows, HALF, 1) * sine_ref[...]
+        return rows.astype(BF16)
+
+    for h in range(GH):
+        low, high = turned(h), turned(h + GH)
+        keep[:, h * HD : (h + 1) * HD] = jnp.where(first, low, high)
+        send[:, h * HD : (h + 1) * HD] = jnp.where(first, high, low)
+
+
+def turn_queries(place, *arrays):
+    vmem = pl.BlockSpec(memory_space=pltpu.VMEM)
+    half = jax.ShapeDtypeStruct((TOK, GH * HD), BF16)
+    return pl.pallas_call(
+        query_kernel,
+        out_shape=(half, half),
+        in_specs=[pl.BlockSpec(memory_space=pltpu.SMEM)] + [vmem] * len(arrays),
+        out_specs=(vmem, vmem),
+        compiler_params=pltpu.CompilerParams(vmem_limit_bytes=4 << 20),
+        name="query_turn",
+    )(place, *arrays)
 
 
 def pack_kernel(place_ref, source, target):
@@ -340,6 +370,7 @@
         in_specs=[pl.BlockSpec(memory_space=pltpu.SMEM)] + [columns] * (2 * NT) + [grads],
         out_specs=(pl.BlockSpec((TOK, HD), lambda i: (0, 0)),) * 4,
         scratch_shapes=[pltpu.VMEM((HD, NT * TOK), F32), pltpu.VMEM((NT, TOK, HD), F32)],
+        compiler_params=pltpu.CompilerParams(vmem_limit_bytes=8 << 20),
         name="owned",
     )(place, *arrays)
 
@@ -361,6 +392,7 @@
         out_shape=jax.ShapeDtypeStruct(other_terms.shape, BF16),
         in_specs=[whole, whole],
         out_specs=whole,
+        compiler_params=pltpu.CompilerParams(vmem_limit_bytes=8 << 20),
         name="finish",
     )(terms, other_terms)
 
@@ -385,6 +417,7 @@
             out_specs=pl.BlockSpec(block, lambda i, place: (0, 0)),
         ),
         out_shape=jax.ShapeDtypeStruct(block, activations.dtype),
+        compiler_params=pltpu.CompilerParams(vmem_limit_bytes=5 << 20),
         name="feature_slice",
     )(place, activations)
 
@@ -396,6 +429,7 @@
         out_shape=jax.ShapeDtypeStruct((NX * NY, TOK, TOK), activations.dtype),
         in_specs=[pl.BlockSpec(memory_space=pltpu.SMEM), vmem],
         out_specs=vmem,
+        compiler_params=pltpu.CompilerParams(vmem_limit_bytes=6 << 20),
         name="pack",
     )(place, activations)
 
@@ -441,11 +475,12 @@
         [role(own_slice, other_slice), role(other_slice, own_slice)], 0
     )
 
-    rotated = turn(queries.astype(F32), own_cos, own_sin).astype(BF16)
     width = GH * HD
-    q_keep = role(rotated[:, :width], rotated[:, width:])
+    full_cos = jnp.concatenate([own_cos, own_cos], 1)
+    full_sin = jnp.concatenate([-own_sin, own_sin], 1)
+    q_keep, q_send = turn_queries(place, queries, full_cos, full_sin)
     do_keep = role(out_grad[:, :width], out_grad[:, width:])
-    q_got = partner(role(rotated[:, width:], rotated[:, :width]))
+    q_got = partner(q_send)
     do_got = partner(role(out_grad[:, width:], out_grad[:, :width]))
 
     partial = jnp.einsum("tk,hkn->htn", both_slices, weight, preferred_element_type=F32)
@@ -506,8 +541,10 @@
         place, *columns, *other_columns, plane_grads
     )
     opposite = diagonal(opposite)
-    same = here + across(above)
-    cross = partner(beside) + opposite
+    above = across(above)
+    beside = partner(beside)
+    same = here + above
+    cross = beside + opposite
     return (attention, query_grad, role(same, cross), role(cross, same), input_grad)
 
 

time: 252 us -> 253 us (level)
  blocking collectives: 0 us -> 16.5 us
  waiting for transfers between devices: 98.5 us -> 88 us
  Pallas kernels: 24.4 us -> 18 us
  starting transfers between devices: 97.4 us -> 91.8 us
  local copies, waits for them, and re-layouts: 9.44 us -> 15 us
  matrix products: 5.59 us -> 8.76 us
    all_to_all x0 -> x1, blocking collectives: none -> 16.5 us  [plane_exchange(): lax.all_to_all(blocks, 'ctx', split_axis=0, concat_axis=0, tiled=True, ax...]
    all_to_all x5 -> x4, waiting for transfers between devices: 52.4 us -> 44.2 us  [plane_exchange(): lax.all_to_all(blocks, 'ctx', split_axis=0, concat_axis=0, tiled=True, ax...]
    all_to_all x5 -> x4, starting transfers between devices: 42.3 us -> 37.4 us  [plane_exchange(): lax.all_to_all(blocks, 'ctx', split_axis=0, concat_axis=0, tiled=True, ax...]
    dot_general x4, matrix products: 3.49 us -> 6.14 us  [product(): lax.dot_general(left, right, (((left_dim,), (right_dim,)), ((), ())), pre...]
    unnamed x54 -> x38, local copies, waits for them, and re-layouts: 4.29 us -> 6.61 us
  transfers between devices with their start and end apart: 38 -> 37, of which waited for: 19 -> 19; matrix products, arithmetic and copies ran while one was open for 6% -> 8% of each run, Pallas kernels for 6% -> 4%
where the time goes in v7:
time: 253 us; the launch traced here: 250 us
  starting transfers between devices  91.8 us (36%)
  waiting for transfers between devices  88 us (35%)
  Pallas kernels  18 us (7%)
  blocking collectives  16.5 us (7%)
  local copies, waits for them, and re-layouts  15 us (6%)
  other arithmetic  10.5 us (4%)
  matrix products  8.76 us (3%)
    all_to_all x4, waiting for transfers between devices, plane_exchange(): lax.all_to_all(blocks, 'ctx', split_axis=0, concat_axis=0, tiled=True, ax...  44.2 us
    all_to_all x4, starting transfers between devices, plane_exchange(): lax.all_to_all(blocks, 'ctx', split_axis=0, concat_axis=0, tiled=True, ax...  37.4 us
    ppermute x12, starting transfers between devices, along(): return lax.ppermute(array, 'tp', [(t, (t + step) % NT) for t in range(NT)])  30.8 us
    ppermute x12, waiting for transfers between devices, along(): return lax.ppermute(array, 'tp', [(t, (t + step) % NT) for t in range(NT)])  27.2 us
    all_to_all x1, blocking collectives, plane_exchange(): lax.all_to_all(blocks, 'ctx', split_axis=0, concat_axis=0, tiled=True, ax...  16.5 us
    ppermute x3, starting transfers between devices, across(): return lax.ppermute(array, 'ctx', ACROSS)  9.83 us
    ppermute x15, waiting for transfers between devices, partner(): return lax.ppermute(array, 'group', [(0, 1), (1, 0)])  7.99 us
    ppermute x1, starting transfers between devices, body(): far = lax.ppermute(weight, ('ctx', 'tp'), FAR_TURN)  7.28 us
  transfers between devices with their start and end apart: 37, of which 19 were waited for; matrix products, arithmetic and copies ran while one was open for 8% of the time, Pallas kernels for 4%

profile of v7, /device:TPU:8, one launch (start us, length us, event | category | flops | bytes accessed | tf_op | source)
XLA Modules:
  0.0 249.7 jit_solution(5472940328740441265)
XLA Ops:
  1.5 7.3 %collective-permute-start.2 = (bf16[256,128]{1,0:T(8,128)(2,1)S(1)}, bf16[256,128]{1,0:T(8,128)(2,1)S(1)}, u32[]{:S(2)}, u32[]{:S(2)}) collective-permute-start(bf16[256,128]{1,0:T(8,128)(2,1)S(1)} %broadcast_select_fusion.6), channel_id=1, source_target_pairs={{0,16},{1,48},{2,80},{3,112},{4,20},{5,52},{6,84},{7,116},{8,24},{... | collective-permute-start | bytes 196616 | tf_op jit(solution)/shard_map/ppermute | solution.py:466
  9.4 1.7 collective-permute-done.2
  11.2 1.8 broadcast_in_dim.16
  13.0 14.4 %all-to-all-start = ((bf16[16,512,128]{2,1,0:T(8,128)(2,1)}), bf16[16,512,128]{2,1,0:T(8,128)(2,1)}, u32[]{:S(2)}, u32[]{:S(2)}) async-start(bf16[16,512,128]{2,1,0:T(8,128)(2,1)} %broadcast_in_dim.16), calls=%async_computation | async-start | bytes 4194304 | tf_op jit(solution)/shard_map/all_to_all | solution.py:63
  28.2 1.8 collective-permute-done.4
  31.1 23.6 %all-to-all-done = bf16[16,512,128]{2,1,0:T(8,128)(2,1)} async-done(((bf16[16,512,128]{2,1,0:T(8,128)(2,1)}), bf16[16,512,128]{2,1,0:T(8,128)(2,1)}, u32[]{:S(2)}, u32[]{:S(2)}) %all-to-all-start) | async-done | bytes 2097184 | tf_op jit(solution)/shard_map/all_to_all | solution.py:63
  54.7 2.6 %fusion.1 = f32[4,128,256]{1,2,0:T(8,128)S(1)} fusion(bf16[4,2048,128]{2,1,0:T(8,128)(2,1)} %bitcast.3, bf16[128,2048]{1,0:T(8,128)(2,1)} %get-tuple-element.52, bf16[128,2048]{1,0:T(8,128)(2,1)} %get-tuple-element.51), kind=kOutput, calls=%fused_computation.4 | convolution fusion | flops 538968064 | bytes 3670016 | tf_op jit(solution)/shard_map/tk,hkn->htn/dot_general | solution.py:486
  58.9 1.8 collective-permute-start.6
  65.7 3.7 %collective-permute-start.8 = (bf16[128,128]{1,0:T(8,128)(2,1)S(1)}, bf16[128,128]{1,0:T(8,128)(2,1)S(1)}, u32[]{:S(2)}, u32[]{:S(2)}) collective-permute-start(bf16[128,128]{1,0:T(8,128)(2,1)S(1)} %fusion.21), channel_id=1, source_target_pairs={{0,16},{4,20},{8,24},{12,28},{16,0},{20,4},{24,8},{28,12},{32,48},... | collective-permute-start | bytes 98312 | tf_op jit(solution)/shard_map/ppermute | solution.py:44
  69.3 4.3 %collective-permute-done.8 = bf16[128,128]{1,0:T(8,128)(2,1)S(1)} collective-permute-done((bf16[128,128]{1,0:T(8,128)(2,1)S(1)}, bf16[128,128]{1,0:T(8,128)(2,1)S(1)}, u32[]{:S(2)}, u32[]{:S(2)}) %collective-permute-start.8) | collective-permute-done | bytes 32800 | tf_op jit(solution)/shard_map/ppermute | solution.py:44
  73.8 16.5 %all_to_all.25 = bf16[16,256,128]{2,1,0:T(8,128)(2,1)S(1)} all-to-all(bf16[16,256,128]{2,1,0:T(8,128)(2,1)S(1)} %broadcast_in_dim.19), channel_id=1, replica_groups={{0,4,8,12,32,36,40,44,64,68,72,76,96,100,104,108},{16,20,24,28,48,52,56..., dimensions={0} | all-to-all | bytes 2097152 | tf_op jit(solution)/shard_map/all_to_all | solution.py:63
  94.0 6.2 %attention.1 = (bf16[128,512]{1,0:T(8,128)(2,1)S(1)}, bf16[128,512]{1,0:T(8,128)(2,1)S(1)}, f32[32,128,128]{2,1,0:T(8,128)S(1)}, f32[32,128,128]{2,1,0:T(8,128)S(1)}) custom-call(s32[3]{0:T(128)S(1)} %pad_add_fusion.place_ref, bf16[128,512]{1,0:T(8,128)(2,1)S(1)} %get-tuple-element.26.q_keep, bf16[128,512]{1,0:T(8,128)(2,1)S(1)} %collective-permute-done.q_got, ...), custom_call_target="tpu_custom_call" | custom-call | tf_op jit(solution)/shard_map/attention/pallas_call | solution.py:255
  100.5 4.0 %collective-permute-done.23 = f32[32,128,128]{2,1,0:T(8,128)S(1)} collective-permute-done((f32[32,128,128]{2,1,0:T(8,128)S(1)}, f32[32,128,128]{2,1,0:T(8,128)S(1)}, u32[]{:S(2)}, u32[]{:S(2)}) %collective-permute-start.23) | collective-permute-done | bytes 2097184 | tf_op jit(solution)/shard_map/ppermute | solution.py:40
  106.1 9.2 %all-to-all-start.3 = ((f32[16,256,128]{2,1,0:T(8,128)}), f32[16,256,128]{2,1,0:T(8,128)}, u32[]{:S(2)}, u32[]{:S(2)}) async-start(f32[16,256,128]{2,1,0:T(8,128)} %bitcast.123), calls=%async_computation.3 | async-start | bytes 4194304 | tf_op jit(solution)/shard_map/all_to_all | solution.py:63
  116.2 2.6 %collective-permute-start.10 = (f32[128,128]{1,0:T(8,128)S(1)}, f32[128,128]{1,0:T(8,128)S(1)}, u32[]{:S(2)}, u32[]{:S(2)}) collective-permute-start(f32[128,128]{1,0:T(8,128)S(1)} %slice.112), channel_id=1, source_target_pairs={{0,1},{1,2},{2,3},{3,0},{4,5},{5,6},{6,7},{7,4},{8,9},{9,10},{10,1... | collective-permute-start | bytes 196616 | tf_op jit(solution)/shard_map/ppermute | solution.py:55
  126.3 19.0 %all-to-all-done.3 = f32[16,256,128]{2,1,0:T(8,128)} async-done(((f32[16,256,128]{2,1,0:T(8,128)}), f32[16,256,128]{2,1,0:T(8,128)}, u32[]{:S(2)}, u32[]{:S(2)}) %all-to-all-start.3) | async-done | bytes 2097184 | tf_op jit(solution)/shard_map/all_to_all | solution.py:63
  145.3 5.4 %all-to-all-start.2 = ((bf16[16,128,128]{2,1,0:T(8,128)(2,1)}), bf16[16,128,128]{2,1,0:T(8,128)(2,1)}, u32[]{:S(2)}, u32[]{:S(2)}) async-start(bf16[16,128,128]{2,1,0:T(8,128)(2,1)} %pack.1), calls=%async_computation.2 | async-start | bytes 1048576 | tf_op jit(solution)/shard_map/all_to_all | solution.py:63
  152.8 1.7 reduce_sum.9
  154.5 3.5 %collective-permute-start.24 = (f32[128,128]{1,0:T(8,128)S(1)}, f32[128,128]{1,0:T(8,128)S(1)}, u32[]{:S(2)}, u32[]{:S(2)}) collective-permute-start(f32[128,128]{1,0:T(8,128)S(1)} %slice_select_fusion), channel_id=1, source_target_pairs={{0,16},{4,20},{8,24},{12,28},{16,0},{20,4},{24,8},{28,12},{32,48},... | collective-permute-start | bytes 196616 | tf_op jit(solution)/shard_map/ppermute | solution.py:44
  159.6 2.6 %collective-permute-start.16 = (bf16[2048,128]{1,0:T(8,128)(2,1)}, bf16[2048,128]{1,0:T(8,128)(2,1)}, u32[]{:S(2)}, u32[]{:S(2)}) collective-permute-start(bf16[2048,128]{1,0:T(8,128)(2,1)} %bitcast.29.refs_0_), channel_id=1, source_target_pairs={{0,1},{1,2},{2,3},{3,0},{4,5},{5,6},{6,7},{7,4},{8,9},{9,10},{10,1... | collective-permute-start | bytes 1572872 | tf_op jit(solution)/shard_map/ppermute | solution.py:55
  166.0 12.5 %collective-permute-start.29 = (bf16[256,128]{1,0:T(8,128)(2,1)}, bf16[256,128]{1,0:T(8,128)(2,1)}, u32[]{:S(2)}, u32[]{:S(2)}) collective-permute-start(bf16[256,128]{1,0:T(8,128)(2,1)} %fusion.15), channel_id=1, source_target_pairs={{0,1},{1,2},{2,3},{3,0},{4,5},{5,6},{6,7},{7,4},{8,9},{9,10},{10,1... | collective-permute-start | bytes 196616 | tf_op jit(solution)/shard_map/ppermute | solution.py:55
  178.5 2.1 broadcast_in_dim.45
  180.6 8.4 %all-to-all-start.4 = ((bf16[16,256,128]{2,1,0:T(8,128)(2,1)}), bf16[16,256,128]{2,1,0:T(8,128)(2,1)S(1)}, u32[]{:S(2)}, u32[]{:S(2)}) async-start(bf16[16,256,128]{2,1,0:T(8,128)(2,1)} %broadcast_in_dim.45), calls=%async_computation.4 | async-start | bytes 2097152 | tf_op jit(solution)/shard_map/all_to_all | solution.py:63
  190.7 10.1 %collective-permute-done.29 = bf16[256,128]{1,0:T(8,128)(2,1)} collective-permute-done((bf16[256,128]{1,0:T(8,128)(2,1)}, bf16[256,128]{1,0:T(8,128)(2,1)}, u32[]{:S(2)}, u32[]{:S(2)}) %collective-permute-start.29) | collective-permute-done | bytes 65568 | tf_op jit(solution)/shard_map/ppermute | solution.py:55
  202.3 10.9 %collective-permute-done.31 = bf16[256,128]{1,0:T(8,128)(2,1)S(1)} collective-permute-done((bf16[256,128]{1,0:T(8,128)(2,1)}, bf16[256,128]{1,0:T(8,128)(2,1)S(1)}, u32[]{:S(2)}, u32[]{:S(2)}) %collective-permute-start.31) | collective-permute-done | bytes 65568 | tf_op jit(solution)/shard_map/ppermute | solution.py:55
  213.3 4.3 %collective-permute-start.30 = (bf16[256,128]{1,0:T(8,128)(2,1)}, bf16[256,128]{1,0:T(8,128)(2,1)S(1)}, u32[]{:S(2)}, u32[]{:S(2)}) collective-permute-start(bf16[256,128]{1,0:T(8,128)(2,1)} %fusion.15), channel_id=1, source_target_pairs={{0,2},{1,3},{2,0},{3,1},{4,6},{5,7},{6,4},{7,5},{8,10},{9,11},{10,... | collective-permute-start | bytes 196616 | tf_op jit(solution)/shard_map/ppermute | solution.py:55
  232.6 3.7 %owned.1 = (f32[128,128]{1,0:T(8,128)S(1)}, f32[128,128]{1,0:T(8,128)S(1)}, f32[128,128]{1,0:T(8,128)S(1)}, f32[128,128]{1,0:T(8,128)S(1)}) custom-call(s32[3]{0:T(128)S(1)} %pad_add_fusion.place_ref, bf16[2048,128]{1,0:T(8,128)(2,1)} %bitcast.29.refs_0_, bf16[2048,128]{1,0:T(8,128)(2,1)} %collective-permute-done.16.refs_1_, ...), custom_call_target="tpu_custom_call" | custom-call | tf_op jit(solution)/shard_map/owned/pallas_call | solution.py:366
  236.3 2.7 %collective-permute-start.26 = (f32[128,128]{1,0:T(8,128)S(1)}, f32[128,128]{1,0:T(8,128)S(1)}, u32[]{:S(2)}, u32[]{:S(2)}) collective-permute-start(f32[128,128]{1,0:T(8,128)S(1)} %get-tuple-element.44), channel_id=1, source_target_pairs={{0,16},{4,20},{8,24},{12,28},{16,0},{20,4},{24,8},{28,12},{32,48},... | collective-permute-start | bytes 196616 | tf_op jit(solution)/shard_map/ppermute | solution.py:44
  239.0 3.4 %collective-permute-start.28 = (f32[128,128]{1,0:T(8,128)S(1)}, f32[128,128]{1,0:T(8,128)S(1)}, u32[]{:S(2)}, u32[]{:S(2)}) collective-permute-start(f32[128,128]{1,0:T(8,128)S(1)} %get-tuple-element.46), channel_id=1, source_target_pairs={{0,144},{128,16},{4,148},{132,20},{8,152},{136,24},{12,156},{140,2... | collective-permute-start | bytes 196616 | tf_op jit(solution)/shard_map/ppermute | solution.py:51
  242.4 1.8 join.1
  244.7 2.1 collective-permute-done.28
  247.5 2.2 finish.1
  (144 shorter events, 50.6 us)
Async XLA Ops:
  1.5 9.7 %collective-permute-start.2 = (bf16[256,128]{1,0:T(8,128)(2,1)S(1)}, bf16[256,128]{1,0:T(8,128)(2,1)S(1)}, u32[]{:S(2)}, u32[]{:S(2)}) collective-permute-start(bf16[256,128]{1,0:T(8,128)(2,1)S(1)} %broadcast_select_fusion.6), channel_id=1, source_target_pairs={{0,16},{1,48},{2,80},{3,112},{4,20},{5,52},{6,84},{7,116},{8,24},{... | collective-permute-start | bytes 196616 | tf_op jit(solution)/shard_map/ppermute | solution.py:466
  13.0 41.8 %all-to-all-start = ((bf16[16,512,128]{2,1,0:T(8,128)(2,1)}), bf16[16,512,128]{2,1,0:T(8,128)(2,1)}, u32[]{:S(2)}, u32[]{:S(2)}) async-start(bf16[16,512,128]{2,1,0:T(8,128)(2,1)} %broadcast_in_dim.16), calls=%async_computation | async-start | bytes 4194304 | tf_op jit(solution)/shard_map/all_to_all | solution.py:63
  58.2 6.2 %collective-permute-start.5 = (f32[128,128]{1,0:T(8,128)S(1)}, f32[128,128]{1,0:T(8,128)S(1)}, u32[]{:S(2)}, u32[]{:S(2)}) collective-permute-start(f32[128,128]{1,0:T(8,128)S(1)} %slice_bitcast_fusion.2), channel_id=1, source_target_pairs={{0,1},{1,2},{2,3},{3,0},{4,5},{5,6},{6,7},{7,4},{8,9},{9,10},{10,1... | collective-permute-start | bytes 196616 | tf_op jit(solution)/shard_map/ppermute | solution.py:55
  58.9 6.6 %collective-permute-start.6 = (f32[128,128]{1,0:T(8,128)S(1)}, f32[128,128]{1,0:T(8,128)S(1)}, u32[]{:S(2)}, u32[]{:S(2)}) collective-permute-start(f32[128,128]{1,0:T(8,128)S(1)} %slice_bitcast_fusion.1), channel_id=1, source_target_pairs={{0,2},{1,3},{2,0},{3,1},{4,6},{5,7},{6,4},{7,5},{8,10},{9,11},{10,... | collective-permute-start | bytes 196616 | tf_op jit(solution)/shard_map/ppermute | solution.py:55
  60.7 4.7 %collective-permute-start.7 = (f32[128,128]{1,0:T(8,128)S(1)}, f32[128,128]{1,0:T(8,128)S(1)}, u32[]{:S(2)}, u32[]{:S(2)}) collective-permute-start(f32[128,128]{1,0:T(8,128)S(1)} %slice_bitcast_fusion), channel_id=1, source_target_pairs={{0,3},{1,0},{2,1},{3,2},{4,7},{5,4},{6,5},{7,6},{8,11},{9,8},{10,9... | collective-permute-start | bytes 196616 | tf_op jit(solution)/shard_map/ppermute | solution.py:55
  65.7 7.9 %collective-permute-start.8 = (bf16[128,128]{1,0:T(8,128)(2,1)S(1)}, bf16[128,128]{1,0:T(8,128)(2,1)S(1)}, u32[]{:S(2)}, u32[]{:S(2)}) collective-permute-start(bf16[128,128]{1,0:T(8,128)(2,1)S(1)} %fusion.21), channel_id=1, source_target_pairs={{0,16},{4,20},{8,24},{12,28},{16,0},{20,4},{24,8},{28,12},{32,48},... | collective-permute-start | bytes 98312 | tf_op jit(solution)/shard_map/ppermute | solution.py:44
  90.4 3.7 %collective-permute-start.9 = (bf16[32,128,128]{2,1,0:T(8,128)(2,1)S(1)}, bf16[32,128,128]{2,1,0:T(8,128)(2,1)S(1)}, u32[]{:S(2)}, u32[]{:S(2)}) collective-permute-start(bf16[32,128,128]{2,1,0:T(8,128)(2,1)S(1)} %bitcast.121), channel_id=1, source_target_pairs={{0,128},{128,0},{1,129},{129,1},{2,130},{130,2},{3,131},{131,3},{4... | collective-permute-start | bytes 3145736 | tf_op jit(solution)/shard_map/ppermute | solution.py:40
  100.2 4.2 %collective-permute-start.23 = (f32[32,128,128]{2,1,0:T(8,128)S(1)}, f32[32,128,128]{2,1,0:T(8,128)S(1)}, u32[]{:S(2)}, u32[]{:S(2)}) collective-permute-start(f32[32,128,128]{2,1,0:T(8,128)S(1)} %get-tuple-element.40), channel_id=1, source_target_pairs={{0,128},{128,0},{1,129},{129,1},{2,130},{130,2},{3,131},{131,3},{4... | collective-permute-start | bytes 6291464 | tf_op jit(solution)/shard_map/ppermute | solution.py:40
  106.1 39.1 %all-to-all-start.3 = ((f32[16,256,128]{2,1,0:T(8,128)}), f32[16,256,128]{2,1,0:T(8,128)}, u32[]{:S(2)}, u32[]{:S(2)}) async-start(f32[16,256,128]{2,1,0:T(8,128)} %bitcast.123), calls=%async_computation.3 | async-start | bytes 4194304 | tf_op jit(solution)/shard_map/all_to_all | solution.py:63
  116.2 8.2 %collective-permute-start.10 = (f32[128,128]{1,0:T(8,128)S(1)}, f32[128,128]{1,0:T(8,128)S(1)}, u32[]{:S(2)}, u32[]{:S(2)}) collective-permute-start(f32[128,128]{1,0:T(8,128)S(1)} %slice.112), channel_id=1, source_target_pairs={{0,1},{1,2},{2,3},{3,0},{4,5},{5,6},{6,7},{7,4},{8,9},{9,10},{10,1... | collective-permute-start | bytes 196616 | tf_op jit(solution)/shard_map/ppermute | solution.py:55
  119.7 6.2 %collective-permute-start.11 = (f32[128,128]{1,0:T(8,128)S(1)}, f32[128,128]{1,0:T(8,128)S(1)}, u32[]{:S(2)}, u32[]{:S(2)}) collective-permute-start(f32[128,128]{1,0:T(8,128)S(1)} %slice.113), channel_id=1, source_target_pairs={{0,2},{1,3},{2,0},{3,1},{4,6},{5,7},{6,4},{7,5},{8,10},{9,11},{10,... | collective-permute-start | bytes 196616 | tf_op jit(solution)/shard_map/ppermute | solution.py:55
  121.3 4.7 %collective-permute-start.12 = (f32[128,128]{1,0:T(8,128)S(1)}, f32[128,128]{1,0:T(8,128)S(1)}, u32[]{:S(2)}, u32[]{:S(2)}) collective-permute-start(f32[128,128]{1,0:T(8,128)S(1)} %slice.114), channel_id=1, source_target_pairs={{0,3},{1,0},{2,1},{3,2},{4,7},{5,4},{6,5},{7,6},{8,11},{9,8},{10,9... | collective-permute-start | bytes 196616 | tf_op jit(solution)/shard_map/ppermute | solution.py:55
  126.2 24.6 %collective-permute-start.13 = (bf16[128,128]{1,0:T(8,128)(2,1)S(1)}, bf16[128,128]{1,0:T(8,128)(2,1)S(1)}, u32[]{:S(2)}, u32[]{:S(2)}) collective-permute-start(bf16[128,128]{1,0:T(8,128)(2,1)S(1)} %fusion.23.short_mine), channel_id=1, source_target_pairs={{0,128},{128,0},{1,129},{129,1},{2,130},{130,2},{3,131},{131,3},{4... | collective-permute-start | bytes 98312 | tf_op jit(solution)/shard_map/ppermute | solution.py:40
  145.3 14.3 %all-to-all-start.2 = ((bf16[16,128,128]{2,1,0:T(8,128)(2,1)}), bf16[16,128,128]{2,1,0:T(8,128)(2,1)}, u32[]{:S(2)}, u32[]{:S(2)}) async-start(bf16[16,128,128]{2,1,0:T(8,128)(2,1)} %pack.1), calls=%async_computation.2 | async-start | bytes 1048576 | tf_op jit(solution)/shard_map/all_to_all | solution.py:63
  152.8 11.9 %collective-permute-start.25 = (f32[128,128]{1,0:T(8,128)S(1)}, f32[128,128]{1,0:T(8,128)S(1)}, u32[]{:S(2)}, u32[]{:S(2)}) collective-permute-start(f32[128,128]{1,0:T(8,128)S(1)} %get-tuple-element.42), channel_id=1, source_target_pairs={{0,128},{128,0},{1,129},{129,1},{2,130},{130,2},{3,131},{131,3},{4... | collective-permute-start | bytes 196616 | tf_op jit(solution)/shard_map/ppermute | solution.py:40
  154.5 10.1 %collective-permute-start.24 = (f32[128,128]{1,0:T(8,128)S(1)}, f32[128,128]{1,0:T(8,128)S(1)}, u32[]{:S(2)}, u32[]{:S(2)}) collective-permute-start(f32[128,128]{1,0:T(8,128)S(1)} %slice_select_fusion), channel_id=1, source_target_pairs={{0,16},{4,20},{8,24},{12,28},{16,0},{20,4},{24,8},{28,12},{32,48},... | collective-permute-start | bytes 196616 | tf_op jit(solution)/shard_map/ppermute | solution.py:44
  159.6 63.7 %collective-permute-start.16 = (bf16[2048,128]{1,0:T(8,128)(2,1)}, bf16[2048,128]{1,0:T(8,128)(2,1)}, u32[]{:S(2)}, u32[]{:S(2)}) collective-permute-start(bf16[2048,128]{1,0:T(8,128)(2,1)} %bitcast.29.refs_0_), channel_id=1, source_target_pairs={{0,1},{1,2},{2,3},{3,0},{4,5},{5,6},{6,7},{7,4},{8,9},{9,10},{10,1... | collective-permute-start | bytes 1572872 | tf_op jit(solution)/shard_map/ppermute | solution.py:55
  162.2 61.6 %collective-permute-start.17 = (bf16[2048,128]{1,0:T(8,128)(2,1)}, bf16[2048,128]{1,0:T(8,128)(2,1)}, u32[]{:S(2)}, u32[]{:S(2)}) collective-permute-start(bf16[2048,128]{1,0:T(8,128)(2,1)} %bitcast.29.refs_0_), channel_id=1, source_target_pairs={{0,2},{1,3},{2,0},{3,1},{4,6},{5,7},{6,4},{7,5},{8,10},{9,11},{10,... | collective-permute-start | bytes 1572872 | tf_op jit(solution)/shard_map/ppermute | solution.py:55
  163.0 60.9 %collective-permute-start.18 = (bf16[2048,128]{1,0:T(8,128)(2,1)}, bf16[2048,128]{1,0:T(8,128)(2,1)}, u32[]{:S(2)}, u32[]{:S(2)}) collective-permute-start(bf16[2048,128]{1,0:T(8,128)(2,1)} %bitcast.29.refs_0_), channel_id=1, source_target_pairs={{0,3},{1,0},{2,1},{3,2},{4,7},{5,4},{6,5},{7,6},{8,11},{9,8},{10,9... | collective-permute-start | bytes 1572872 | tf_op jit(solution)/shard_map/ppermute | solution.py:55
  164.6 60.4 %collective-permute-start.19 = (bf16[2048,128]{1,0:T(8,128)(2,1)}, bf16[2048,128]{1,0:T(8,128)(2,1)}, u32[]{:S(2)}, u32[]{:S(2)}) collective-permute-start(bf16[2048,128]{1,0:T(8,128)(2,1)} %bitcast.29.refs_0_), channel_id=1, source_target_pairs={{0,128},{128,0},{1,129},{129,1},{2,130},{130,2},{3,131},{131,3},{4... | collective-permute-start | bytes 1572872 | tf_op jit(solution)/shard_map/ppermute | solution.py:40
  166.0 34.8 %collective-permute-start.29 = (bf16[256,128]{1,0:T(8,128)(2,1)}, bf16[256,128]{1,0:T(8,128)(2,1)}, u32[]{:S(2)}, u32[]{:S(2)}) collective-permute-start(bf16[256,128]{1,0:T(8,128)(2,1)} %fusion.15), channel_id=1, source_target_pairs={{0,1},{1,2},{2,3},{3,0},{4,5},{5,6},{6,7},{7,4},{8,9},{9,10},{10,1... | collective-permute-start | bytes 196616 | tf_op jit(solution)/shard_map/ppermute | solution.py:55
  180.6 48.8 %all-to-all-start.4 = ((bf16[16,256,128]{2,1,0:T(8,128)(2,1)}), bf16[16,256,128]{2,1,0:T(8,128)(2,1)S(1)}, u32[]{:S(2)}, u32[]{:S(2)}) async-start(bf16[16,256,128]{2,1,0:T(8,128)(2,1)} %broadcast_in_dim.45), calls=%async_computation.4 | async-start | bytes 2097152 | tf_op jit(solution)/shard_map/all_to_all | solution.py:63
  200.8 12.5 %collective-permute-start.31 = (bf16[256,128]{1,0:T(8,128)(2,1)}, bf16[256,128]{1,0:T(8,128)(2,1)S(1)}, u32[]{:S(2)}, u32[]{:S(2)}) collective-permute-start(bf16[256,128]{1,0:T(8,128)(2,1)} %fusion.15), channel_id=1, source_target_pairs={{0,3},{1,0},{2,1},{3,2},{4,7},{5,4},{6,5},{7,6},{8,11},{9,8},{10,9... | collective-permute-start | bytes 196616 | tf_op jit(solution)/shard_map/ppermute | solution.py:55
  213.3 7.5 %collective-permute-start.30 = (bf16[256,128]{1,0:T(8,128)(2,1)}, bf16[256,128]{1,0:T(8,128)(2,1)S(1)}, u32[]{:S(2)}, u32[]{:S(2)}) collective-permute-start(bf16[256,128]{1,0:T(8,128)(2,1)} %fusion.15), channel_id=1, source_target_pairs={{0,2},{1,3},{2,0},{3,1},{4,6},{5,7},{6,4},{7,5},{8,10},{9,11},{10,... | collective-permute-start | bytes 196616 | tf_op jit(solution)/shard_map/ppermute | solution.py:55
  223.3 24.2 %collective-permute-start.32 = (f32[128,2048]{1,0:T(8,128)}, f32[128,2048]{1,0:T(8,128)}, u32[]{:S(2)}, u32[]{:S(2)}) collective-permute-start(f32[128,2048]{1,0:T(8,128)} %slice.138), channel_id=1, source_target_pairs={{0,128},{128,0},{1,129},{129,1},{2,130},{130,2},{3,131},{131,3},{4... | collective-permute-start | bytes 3145736 | tf_op jit(solution)/shard_map/ppermute | solution.py:40
  223.8 4.0 %collective-permute-start.21 = (bf16[2048,128]{1,0:T(8,128)(2,1)}, bf16[2048,128]{1,0:T(8,128)(2,1)S(1)}, u32[]{:S(2)}, u32[]{:S(2)}) collective-permute-start(bf16[2048,128]{1,0:T(8,128)(2,1)} %collective-permute-done.17.refs_2_), channel_id=1, source_target_pairs={{0,128},{128,0},{1,129},{129,1},{2,130},{130,2},{3,131},{131,3},{4... | collective-permute-start | bytes 1572872 | tf_op jit(solution)/shard_map/ppermute | solution.py:40
  223.9 4.7 %collective-permute-start.22 = (bf16[2048,128]{1,0:T(8,128)(2,1)}, bf16[2048,128]{1,0:T(8,128)(2,1)S(1)}, u32[]{:S(2)}, u32[]{:S(2)}) collective-permute-start(bf16[2048,128]{1,0:T(8,128)(2,1)} %collective-permute-done.18.refs_3_), channel_id=1, source_target_pairs={{0,128},{128,0},{1,129},{129,1},{2,130},{130,2},{3,131},{131,3},{4... | collective-permute-start | bytes 1572872 | tf_op jit(solution)/shard_map/ppermute | solution.py:40
  225.0 14.0 %collective-permute-start.15 = (bf16[128,512]{1,0:T(8,128)(2,1)}, bf16[128,512]{1,0:T(8,128)(2,1)}, u32[]{:S(2)}, u32[]{:S(2)}) collective-permute-start(bf16[128,512]{1,0:T(8,128)(2,1)} %broadcast_select_fusion.2), channel_id=1, source_target_pairs={{0,128},{128,0},{1,129},{129,1},{2,130},{130,2},{3,131},{131,3},{4... | collective-permute-start | bytes 393224 | tf_op jit(solution)/shard_map/ppermute | solution.py:40
  227.7 14.7 %collective-permute-start.14 = (bf16[128,512]{1,0:T(8,128)(2,1)}, bf16[128,512]{1,0:T(8,128)(2,1)}, u32[]{:S(2)}, u32[]{:S(2)}) collective-permute-start(bf16[128,512]{1,0:T(8,128)(2,1)} %broadcast_select_fusion.3), channel_id=1, source_target_pairs={{0,128},{128,0},{1,129},{129,1},{2,130},{130,2},{3,131},{131,3},{4... | collective-permute-start | bytes 393224 | tf_op jit(solution)/shard_map/ppermute | solution.py:40
  236.3 8.5 %collective-permute-start.26 = (f32[128,128]{1,0:T(8,128)S(1)}, f32[128,128]{1,0:T(8,128)S(1)}, u32[]{:S(2)}, u32[]{:S(2)}) collective-permute-start(f32[128,128]{1,0:T(8,128)S(1)} %get-tuple-element.44), channel_id=1, source_target_pairs={{0,16},{4,20},{8,24},{12,28},{16,0},{20,4},{24,8},{28,12},{32,48},... | collective-permute-start | bytes 196616 | tf_op jit(solution)/shard_map/ppermute | solution.py:44
  238.9 5.8 %collective-permute-start.27 = (f32[128,128]{1,0:T(8,128)S(1)}, f32[128,128]{1,0:T(8,128)S(1)}, u32[]{:S(2)}, u32[]{:S(2)}) collective-permute-start(f32[128,128]{1,0:T(8,128)S(1)} %get-tuple-element.45), channel_id=1, source_target_pairs={{0,128},{128,0},{1,129},{129,1},{2,130},{130,2},{3,131},{131,3},{4... | collective-permute-start | bytes 196616 | tf_op jit(solution)/shard_map/ppermute | solution.py:40
  239.0 7.8 %collective-permute-start.28 = (f32[128,128]{1,0:T(8,128)S(1)}, f32[128,128]{1,0:T(8,128)S(1)}, u32[]{:S(2)}, u32[]{:S(2)}) collective-permute-start(f32[128,128]{1,0:T(8,128)S(1)} %get-tuple-element.46), channel_id=1, source_target_pairs={{0,144},{128,16},{4,148},{132,20},{8,152},{136,24},{12,156},{140,2... | collective-permute-start | bytes 196616 | tf_op jit(solution)/shard_map/ppermute | solution.py:51
  (24 other events, 187.7 us)

commit v8 on v7

--- a/solution.py
+++ b/solution.py
@@ -521,9 +521,9 @@
     blocks = kv_sums.reshape(plane, NZ * TOK, HD)
     other_columns = [partner(array) for array in columns]
     arrived = plane_exchange(blocks)
-    arrived = arrived.reshape(plane, NZ, TOK, HD).sum(0)
-    here = jnp.where(upper, arrived[1], arrived[0])
-    there = jnp.where(upper, arrived[0], arrived[1])
+    zone = (rank >> 2) & 1
+    there = lax.dynamic_slice_in_dim(arrived, (1 - zone) * TOK, TOK, 1).sum(0)
+    here = lax.dynamic_slice_in_dim(arrived, zone * TOK, TOK, 1).sum(0)
     long_kv = here + across(there)
     grads = jnp.concatenate([role(long_kv, short_kv), role(short_kv, long_kv)], 0)
     grads = role(turn(grads, back_cos, -back_sin), grads).astype(BF16)

time: 253 us -> 254 us (level)
  transfers between devices with their start and end apart: 37 -> 37, of which waited for: 19 -> 20; matrix products, arithmetic and copies ran while one was open for 8% -> 8% of each run, Pallas kernels for 4% -> 4%
where the time goes in v8:
time: 254 us; the launch traced here: 251 us
  starting transfers between devices  92.8 us (37%)
  waiting for transfers between devices  88.6 us (35%)
  Pallas kernels  18 us (7%)
  blocking collectives  16.5 us (6%)
  local copies, waits for them, and re-layouts  15.1 us (6%)
  other arithmetic  10.4 us (4%)
  matrix products  8.77 us (3%)
    all_to_all x4, waiting for transfers between devices, plane_exchange(): lax.all_to_all(blocks, 'ctx', split_axis=0, concat_axis=0, tiled=True, ax...  43 us
    all_to_all x4, starting transfers between devices, plane_exchange(): lax.all_to_all(blocks, 'ctx', split_axis=0, concat_axis=0, tiled=True, ax...  37 us
    ppermute x12, starting transfers between devices, along(): return lax.ppermute(array, 'tp', [(t, (t + step) % NT) for t in range(NT)])  32 us
    ppermute x12, waiting for transfers between devices, along(): return lax.ppermute(array, 'tp', [(t, (t + step) % NT) for t in range(NT)])  26.5 us
    all_to_all x1, blocking collectives, plane_exchange(): lax.all_to_all(blocks, 'ctx', split_axis=0, concat_axis=0, tiled=True, ax...  16.5 us
    ppermute x3, starting transfers between devices, across(): return lax.ppermute(array, 'ctx', ACROSS)  9.77 us
    ppermute x15, waiting for transfers between devices, partner(): return lax.ppermute(array, 'group', [(0, 1), (1, 0)])  9.09 us
    ppermute x1, starting transfers between devices, body(): far = lax.ppermute(weight, ('ctx', 'tp'), FAR_TURN)  7.28 us
  transfers between devices with their start and end apart: 37, of which 20 were waited for; matrix products, arithmetic and copies ran while one was open for 8% of the time, Pallas kernels for 4%

profile of v8, /device:TPU:8, one launch (start us, length us, event | category | flops | bytes accessed | tf_op | source)
XLA Modules:
  0.0 251.3 jit_solution(4968232616877990465)
XLA Ops:
  1.5 7.3 %collective-permute-start.2 = (bf16[256,128]{1,0:T(8,128)(2,1)S(1)}, bf16[256,128]{1,0:T(8,128)(2,1)S(1)}, u32[]{:S(2)}, u32[]{:S(2)}) collective-permute-start(bf16[256,128]{1,0:T(8,128)(2,1)S(1)} %broadcast_select_fusion.6), channel_id=1, source_target_pairs={{0,16},{1,48},{2,80},{3,112},{4,20},{5,52},{6,84},{7,116},{8,24},{... | collective-permute-start | bytes 196616 | tf_op jit(solution)/shard_map/ppermute | solution.py:466
  9.4 1.7 collective-permute-done.2
  11.2 1.7 broadcast_in_dim.16
  13.0 14.4 %all-to-all-start = ((bf16[16,512,128]{2,1,0:T(8,128)(2,1)}), bf16[16,512,128]{2,1,0:T(8,128)(2,1)}, u32[]{:S(2)}, u32[]{:S(2)}) async-start(bf16[16,512,128]{2,1,0:T(8,128)(2,1)} %broadcast_in_dim.16), calls=%async_computation | async-start | bytes 4194304 | tf_op jit(solution)/shard_map/all_to_all | solution.py:63
  28.2 1.8 collective-permute-done.4
  31.1 23.6 %all-to-all-done = bf16[16,512,128]{2,1,0:T(8,128)(2,1)} async-done(((bf16[16,512,128]{2,1,0:T(8,128)(2,1)}), bf16[16,512,128]{2,1,0:T(8,128)(2,1)}, u32[]{:S(2)}, u32[]{:S(2)}) %all-to-all-start) | async-done | bytes 2097184 | tf_op jit(solution)/shard_map/all_to_all | solution.py:63
  54.7 2.6 %fusion.1 = f32[4,128,256]{1,2,0:T(8,128)S(1)} fusion(bf16[4,2048,128]{2,1,0:T(8,128)(2,1)} %bitcast.3, bf16[128,2048]{1,0:T(8,128)(2,1)} %get-tuple-element.52, bf16[128,2048]{1,0:T(8,128)(2,1)} %get-tuple-element.51), kind=kOutput, calls=%fused_computation.4 | convolution fusion | flops 538968064 | bytes 3670016 | tf_op jit(solution)/shard_map/tk,hkn->htn/dot_general | solution.py:486
  58.9 1.8 collective-permute-start.6
  62.6 1.7 collective-permute-done.5
  65.7 3.7 %collective-permute-start.8 = (bf16[128,128]{1,0:T(8,128)(2,1)S(1)}, bf16[128,128]{1,0:T(8,128)(2,1)S(1)}, u32[]{:S(2)}, u32[]{:S(2)}) collective-permute-start(bf16[128,128]{1,0:T(8,128)(2,1)S(1)} %fusion.21), channel_id=1, source_target_pairs={{0,16},{4,20},{8,24},{12,28},{16,0},{20,4},{24,8},{28,12},{32,48},... | collective-permute-start | bytes 98312 | tf_op jit(solution)/shard_map/ppermute | solution.py:44
  69.3 4.3 %collective-permute-done.8 = bf16[128,128]{1,0:T(8,128)(2,1)S(1)} collective-permute-done((bf16[128,128]{1,0:T(8,128)(2,1)S(1)}, bf16[128,128]{1,0:T(8,128)(2,1)S(1)}, u32[]{:S(2)}, u32[]{:S(2)}) %collective-permute-start.8) | collective-permute-done | bytes 32800 | tf_op jit(solution)/shard_map/ppermute | solution.py:44
  73.8 16.5 %all_to_all.25 = bf16[16,256,128]{2,1,0:T(8,128)(2,1)S(1)} all-to-all(bf16[16,256,128]{2,1,0:T(8,128)(2,1)S(1)} %broadcast_in_dim.19), channel_id=1, replica_groups={{0,4,8,12,32,36,40,44,64,68,72,76,96,100,104,108},{16,20,24,28,48,52,56..., dimensions={0} | all-to-all | bytes 2097152 | tf_op jit(solution)/shard_map/all_to_all | solution.py:63
  94.0 6.2 %attention.1 = (bf16[128,512]{1,0:T(8,128)(2,1)S(1)}, bf16[128,512]{1,0:T(8,128)(2,1)S(1)}, f32[32,128,128]{2,1,0:T(8,128)S(1)}, f32[32,128,128]{2,1,0:T(8,128)S(1)}) custom-call(s32[3]{0:T(128)S(1)} %pad_add_fusion.place_ref, bf16[128,512]{1,0:T(8,128)(2,1)S(1)} %get-tuple-element.26.q_keep, bf16[128,512]{1,0:T(8,128)(2,1)S(1)} %collective-permute-done.q_got, ...), custom_call_target="tpu_custom_call" | custom-call | tf_op jit(solution)/shard_map/attention/pallas_call | solution.py:255
  100.5 4.0 %collective-permute-done.23 = f32[32,128,128]{2,1,0:T(8,128)S(1)} collective-permute-done((f32[32,128,128]{2,1,0:T(8,128)S(1)}, f32[32,128,128]{2,1,0:T(8,128)S(1)}, u32[]{:S(2)}, u32[]{:S(2)}) %collective-permute-start.23) | collective-permute-done | bytes 2097184 | tf_op jit(solution)/shard_map/ppermute | solution.py:40
  106.1 9.2 %all-to-all-start.3 = ((f32[16,256,128]{2,1,0:T(8,128)}), f32[16,256,128]{2,1,0:T(8,128)}, u32[]{:S(2)}, u32[]{:S(2)}) async-start(f32[16,256,128]{2,1,0:T(8,128)} %bitcast.123), calls=%async_computation.3 | async-start | bytes 4194304 | tf_op jit(solution)/shard_map/all_to_all | solution.py:63
  116.2 2.6 %collective-permute-start.10 = (f32[128,128]{1,0:T(8,128)S(1)}, f32[128,128]{1,0:T(8,128)S(1)}, u32[]{:S(2)}, u32[]{:S(2)}) collective-permute-start(f32[128,128]{1,0:T(8,128)S(1)} %slice.102), channel_id=1, source_target_pairs={{0,1},{1,2},{2,3},{3,0},{4,5},{5,6},{6,7},{7,4},{8,9},{9,10},{10,1... | collective-permute-start | bytes 196616 | tf_op jit(solution)/shard_map/ppermute | solution.py:55
  126.1 19.2 %all-to-all-done.3 = f32[16,256,128]{2,1,0:T(8,128)} async-done(((f32[16,256,128]{2,1,0:T(8,128)}), f32[16,256,128]{2,1,0:T(8,128)}, u32[]{:S(2)}, u32[]{:S(2)}) %all-to-all-start.3) | async-done | bytes 2097184 | tf_op jit(solution)/shard_map/all_to_all | solution.py:63
  145.3 5.4 %all-to-all-start.2 = ((bf16[16,128,128]{2,1,0:T(8,128)(2,1)}), bf16[16,128,128]{2,1,0:T(8,128)(2,1)}, u32[]{:S(2)}, u32[]{:S(2)}) async-start(bf16[16,128,128]{2,1,0:T(8,128)(2,1)} %pack.1), calls=%async_computation.2 | async-start | bytes 1048576 | tf_op jit(solution)/shard_map/all_to_all | solution.py:63
  155.9 3.5 %collective-permute-start.24 = (f32[128,128]{1,0:T(8,128)S(1)}, f32[128,128]{1,0:T(8,128)S(1)}, u32[]{:S(2)}, u32[]{:S(2)}) collective-permute-start(f32[128,128]{1,0:T(8,128)S(1)} %get-tuple-element.47), channel_id=1, source_target_pairs={{0,16},{4,20},{8,24},{12,28},{16,0},{20,4},{24,8},{28,12},{32,48},... | collective-permute-start | bytes 196616 | tf_op jit(solution)/shard_map/ppermute | solution.py:44
  159.6 2.6 %collective-permute-start.16 = (bf16[2048,128]{1,0:T(8,128)(2,1)}, bf16[2048,128]{1,0:T(8,128)(2,1)}, u32[]{:S(2)}, u32[]{:S(2)}) collective-permute-start(bf16[2048,128]{1,0:T(8,128)(2,1)} %bitcast.29.refs_0_), channel_id=1, source_target_pairs={{0,1},{1,2},{2,3},{3,0},{4,5},{5,6},{6,7},{7,4},{8,9},{9,10},{10,1... | collective-permute-start | bytes 1572872 | tf_op jit(solution)/shard_map/ppermute | solution.py:55
  166.0 14.1 %collective-permute-start.29 = (bf16[256,128]{1,0:T(8,128)(2,1)}, bf16[256,128]{1,0:T(8,128)(2,1)}, u32[]{:S(2)}, u32[]{:S(2)}) collective-permute-start(bf16[256,128]{1,0:T(8,128)(2,1)} %fusion.15), channel_id=1, source_target_pairs={{0,1},{1,2},{2,3},{3,0},{4,5},{5,6},{6,7},{7,4},{8,9},{9,10},{10,1... | collective-permute-start | bytes 196616 | tf_op jit(solution)/shard_map/ppermute | solution.py:55
  180.1 2.1 broadcast_in_dim.45
  182.2 8.0 %all-to-all-start.4 = ((bf16[16,256,128]{2,1,0:T(8,128)(2,1)}), bf16[16,256,128]{2,1,0:T(8,128)(2,1)S(1)}, u32[]{:S(2)}, u32[]{:S(2)}) async-start(bf16[16,256,128]{2,1,0:T(8,128)(2,1)} %broadcast_in_dim.45), calls=%async_computation.4 | async-start | bytes 2097152 | tf_op jit(solution)/shard_map/all_to_all | solution.py:63
  191.9 10.1 %collective-permute-done.29 = bf16[256,128]{1,0:T(8,128)(2,1)} collective-permute-done((bf16[256,128]{1,0:T(8,128)(2,1)}, bf16[256,128]{1,0:T(8,128)(2,1)}, u32[]{:S(2)}, u32[]{:S(2)}) %collective-permute-start.29) | collective-permute-done | bytes 65568 | tf_op jit(solution)/shard_map/ppermute | solution.py:55
  203.5 10.9 %collective-permute-done.31 = bf16[256,128]{1,0:T(8,128)(2,1)S(1)} collective-permute-done((bf16[256,128]{1,0:T(8,128)(2,1)}, bf16[256,128]{1,0:T(8,128)(2,1)S(1)}, u32[]{:S(2)}, u32[]{:S(2)}) %collective-permute-start.31) | collective-permute-done | bytes 65568 | tf_op jit(solution)/shard_map/ppermute | solution.py:55
  214.5 3.9 %collective-permute-start.30 = (bf16[256,128]{1,0:T(8,128)(2,1)}, bf16[256,128]{1,0:T(8,128)(2,1)S(1)}, u32[]{:S(2)}, u32[]{:S(2)}) collective-permute-start(bf16[256,128]{1,0:T(8,128)(2,1)} %fusion.15), channel_id=1, source_target_pairs={{0,2},{1,3},{2,0},{3,1},{4,6},{5,7},{6,4},{7,5},{8,10},{9,11},{10,... | collective-permute-start | bytes 196616 | tf_op jit(solution)/shard_map/ppermute | solution.py:55
  232.7 3.7 %owned.1 = (f32[128,128]{1,0:T(8,128)S(1)}, f32[128,128]{1,0:T(8,128)S(1)}, f32[128,128]{1,0:T(8,128)S(1)}, f32[128,128]{1,0:T(8,128)S(1)}) custom-call(s32[3]{0:T(128)S(1)} %pad_add_fusion.place_ref, bf16[2048,128]{1,0:T(8,128)(2,1)} %bitcast.29.refs_0_, bf16[2048,128]{1,0:T(8,128)(2,1)} %collective-permute-done.16.refs_1_, ...), custom_call_target="tpu_custom_call" | custom-call | tf_op jit(solution)/shard_map/owned/pallas_call | solution.py:366
  236.4 2.6 %collective-permute-start.26 = (f32[128,128]{1,0:T(8,128)S(1)}, f32[128,128]{1,0:T(8,128)S(1)}, u32[]{:S(2)}, u32[]{:S(2)}) collective-permute-start(f32[128,128]{1,0:T(8,128)S(1)} %get-tuple-element.44), channel_id=1, source_target_pairs={{0,16},{4,20},{8,24},{12,28},{16,0},{20,4},{24,8},{28,12},{32,48},... | collective-permute-start | bytes 196616 | tf_op jit(solution)/shard_map/ppermute | solution.py:44
  239.1 3.4 %collective-permute-start.28 = (f32[128,128]{1,0:T(8,128)S(1)}, f32[128,128]{1,0:T(8,128)S(1)}, u32[]{:S(2)}, u32[]{:S(2)}) collective-permute-start(f32[128,128]{1,0:T(8,128)S(1)} %get-tuple-element.46), channel_id=1, source_target_pairs={{0,144},{128,16},{4,148},{132,20},{8,152},{136,24},{12,156},{140,2... | collective-permute-start | bytes 196616 | tf_op jit(solution)/shard_map/ppermute | solution.py:51
  242.6 1.8 join.1
  244.9 3.5 %collective-permute-done.28 = f32[128,128]{1,0:T(8,128)S(1)} collective-permute-done((f32[128,128]{1,0:T(8,128)S(1)}, f32[128,128]{1,0:T(8,128)S(1)}, u32[]{:S(2)}, u32[]{:S(2)}) %collective-permute-start.28) | collective-permute-done | bytes 65568 | tf_op jit(solution)/shard_map/ppermute | solution.py:51
  249.1 2.2 finish.1
  (142 shorter events, 49.7 us)
Async XLA Ops:
  1.5 9.7 %collective-permute-start.2 = (bf16[256,128]{1,0:T(8,128)(2,1)S(1)}, bf16[256,128]{1,0:T(8,128)(2,1)S(1)}, u32[]{:S(2)}, u32[]{:S(2)}) collective-permute-start(bf16[256,128]{1,0:T(8,128)(2,1)S(1)} %broadcast_select_fusion.6), channel_id=1, source_target_pairs={{0,16},{1,48},{2,80},{3,112},{4,20},{5,52},{6,84},{7,116},{8,24},{... | collective-permute-start | bytes 196616 | tf_op jit(solution)/shard_map/ppermute | solution.py:466
  13.0 41.8 %all-to-all-start = ((bf16[16,512,128]{2,1,0:T(8,128)(2,1)}), bf16[16,512,128]{2,1,0:T(8,128)(2,1)}, u32[]{:S(2)}, u32[]{:S(2)}) async-start(bf16[16,512,128]{2,1,0:T(8,128)(2,1)} %broadcast_in_dim.16), calls=%async_computation | async-start | bytes 4194304 | tf_op jit(solution)/shard_map/all_to_all | solution.py:63
  58.1 6.2 %collective-permute-start.5 = (f32[128,128]{1,0:T(8,128)S(1)}, f32[128,128]{1,0:T(8,128)S(1)}, u32[]{:S(2)}, u32[]{:S(2)}) collective-permute-start(f32[128,128]{1,0:T(8,128)S(1)} %slice_bitcast_fusion.2), channel_id=1, source_target_pairs={{0,1},{1,2},{2,3},{3,0},{4,5},{5,6},{6,7},{7,4},{8,9},{9,10},{10,1... | collective-permute-start | bytes 196616 | tf_op jit(solution)/shard_map/ppermute | solution.py:55
  58.9 6.6 %collective-permute-start.6 = (f32[128,128]{1,0:T(8,128)S(1)}, f32[128,128]{1,0:T(8,128)S(1)}, u32[]{:S(2)}, u32[]{:S(2)}) collective-permute-start(f32[128,128]{1,0:T(8,128)S(1)} %slice_bitcast_fusion.1), channel_id=1, source_target_pairs={{0,2},{1,3},{2,0},{3,1},{4,6},{5,7},{6,4},{7,5},{8,10},{9,11},{10,... | collective-permute-start | bytes 196616 | tf_op jit(solution)/shard_map/ppermute | solution.py:55
  60.7 4.7 %collective-permute-start.7 = (f32[128,128]{1,0:T(8,128)S(1)}, f32[128,128]{1,0:T(8,128)S(1)}, u32[]{:S(2)}, u32[]{:S(2)}) collective-permute-start(f32[128,128]{1,0:T(8,128)S(1)} %slice_bitcast_fusion), channel_id=1, source_target_pairs={{0,3},{1,0},{2,1},{3,2},{4,7},{5,4},{6,5},{7,6},{8,11},{9,8},{10,9... | collective-permute-start | bytes 196616 | tf_op jit(solution)/shard_map/ppermute | solution.py:55
  65.7 7.9 %collective-permute-start.8 = (bf16[128,128]{1,0:T(8,128)(2,1)S(1)}, bf16[128,128]{1,0:T(8,128)(2,1)S(1)}, u32[]{:S(2)}, u32[]{:S(2)}) collective-permute-start(bf16[128,128]{1,0:T(8,128)(2,1)S(1)} %fusion.21), channel_id=1, source_target_pairs={{0,16},{4,20},{8,24},{12,28},{16,0},{20,4},{24,8},{28,12},{32,48},... | collective-permute-start | bytes 98312 | tf_op jit(solution)/shard_map/ppermute | solution.py:44
  90.4 3.7 %collective-permute-start.9 = (bf16[32,128,128]{2,1,0:T(8,128)(2,1)S(1)}, bf16[32,128,128]{2,1,0:T(8,128)(2,1)S(1)}, u32[]{:S(2)}, u32[]{:S(2)}) collective-permute-start(bf16[32,128,128]{2,1,0:T(8,128)(2,1)S(1)} %bitcast.121), channel_id=1, source_target_pairs={{0,128},{128,0},{1,129},{129,1},{2,130},{130,2},{3,131},{131,3},{4... | collective-permute-start | bytes 3145736 | tf_op jit(solution)/shard_map/ppermute | solution.py:40
  100.2 4.2 %collective-permute-start.23 = (f32[32,128,128]{2,1,0:T(8,128)S(1)}, f32[32,128,128]{2,1,0:T(8,128)S(1)}, u32[]{:S(2)}, u32[]{:S(2)}) collective-permute-start(f32[32,128,128]{2,1,0:T(8,128)S(1)} %get-tuple-element.40), channel_id=1, source_target_pairs={{0,128},{128,0},{1,129},{129,1},{2,130},{130,2},{3,131},{131,3},{4... | collective-permute-start | bytes 6291464 | tf_op jit(solution)/shard_map/ppermute | solution.py:40
  106.1 39.1 %all-to-all-start.3 = ((f32[16,256,128]{2,1,0:T(8,128)}), f32[16,256,128]{2,1,0:T(8,128)}, u32[]{:S(2)}, u32[]{:S(2)}) async-start(f32[16,256,128]{2,1,0:T(8,128)} %bitcast.123), calls=%async_computation.3 | async-start | bytes 4194304 | tf_op jit(solution)/shard_map/all_to_all | solution.py:63
  116.2 8.2 %collective-permute-start.10 = (f32[128,128]{1,0:T(8,128)S(1)}, f32[128,128]{1,0:T(8,128)S(1)}, u32[]{:S(2)}, u32[]{:S(2)}) collective-permute-start(f32[128,128]{1,0:T(8,128)S(1)} %slice.102), channel_id=1, source_target_pairs={{0,1},{1,2},{2,3},{3,0},{4,5},{5,6},{6,7},{7,4},{8,9},{9,10},{10,1... | collective-permute-start | bytes 196616 | tf_op jit(solution)/shard_map/ppermute | solution.py:55
  119.7 6.2 %collective-permute-start.11 = (f32[128,128]{1,0:T(8,128)S(1)}, f32[128,128]{1,0:T(8,128)S(1)}, u32[]{:S(2)}, u32[]{:S(2)}) collective-permute-start(f32[128,128]{1,0:T(8,128)S(1)} %slice.103), channel_id=1, source_target_pairs={{0,2},{1,3},{2,0},{3,1},{4,6},{5,7},{6,4},{7,5},{8,10},{9,11},{10,... | collective-permute-start | bytes 196616 | tf_op jit(solution)/shard_map/ppermute | solution.py:55
  121.2 4.7 %collective-permute-start.12 = (f32[128,128]{1,0:T(8,128)S(1)}, f32[128,128]{1,0:T(8,128)S(1)}, u32[]{:S(2)}, u32[]{:S(2)}) collective-permute-start(f32[128,128]{1,0:T(8,128)S(1)} %slice.104), channel_id=1, source_target_pairs={{0,3},{1,0},{2,1},{3,2},{4,7},{5,4},{6,5},{7,6},{8,11},{9,8},{10,9... | collective-permute-start | bytes 196616 | tf_op jit(solution)/shard_map/ppermute | solution.py:55
  145.3 14.3 %all-to-all-start.2 = ((bf16[16,128,128]{2,1,0:T(8,128)(2,1)}), bf16[16,128,128]{2,1,0:T(8,128)(2,1)}, u32[]{:S(2)}, u32[]{:S(2)}) async-start(bf16[16,128,128]{2,1,0:T(8,128)(2,1)} %pack.1), calls=%async_computation.2 | async-start | bytes 1048576 | tf_op jit(solution)/shard_map/all_to_all | solution.py:63
  154.0 10.6 %collective-permute-start.25 = (f32[128,128]{1,0:T(8,128)S(1)}, f32[128,128]{1,0:T(8,128)S(1)}, u32[]{:S(2)}, u32[]{:S(2)}) collective-permute-start(f32[128,128]{1,0:T(8,128)S(1)} %get-tuple-element.42), channel_id=1, source_target_pairs={{0,128},{128,0},{1,129},{129,1},{2,130},{130,2},{3,131},{131,3},{4... | collective-permute-start | bytes 196616 | tf_op jit(solution)/shard_map/ppermute | solution.py:40
  155.9 8.8 %collective-permute-start.24 = (f32[128,128]{1,0:T(8,128)S(1)}, f32[128,128]{1,0:T(8,128)S(1)}, u32[]{:S(2)}, u32[]{:S(2)}) collective-permute-start(f32[128,128]{1,0:T(8,128)S(1)} %get-tuple-element.47), channel_id=1, source_target_pairs={{0,16},{4,20},{8,24},{12,28},{16,0},{20,4},{24,8},{28,12},{32,48},... | collective-permute-start | bytes 196616 | tf_op jit(solution)/shard_map/ppermute | solution.py:44
  159.6 63.9 %collective-permute-start.16 = (bf16[2048,128]{1,0:T(8,128)(2,1)}, bf16[2048,128]{1,0:T(8,128)(2,1)}, u32[]{:S(2)}, u32[]{:S(2)}) collective-permute-start(bf16[2048,128]{1,0:T(8,128)(2,1)} %bitcast.29.refs_0_), channel_id=1, source_target_pairs={{0,1},{1,2},{2,3},{3,0},{4,5},{5,6},{6,7},{7,4},{8,9},{9,10},{10,1... | collective-permute-start | bytes 1572872 | tf_op jit(solution)/shard_map/ppermute | solution.py:55
  162.2 61.7 %collective-permute-start.17 = (bf16[2048,128]{1,0:T(8,128)(2,1)}, bf16[2048,128]{1,0:T(8,128)(2,1)}, u32[]{:S(2)}, u32[]{:S(2)}) collective-permute-start(bf16[2048,128]{1,0:T(8,128)(2,1)} %bitcast.29.refs_0_), channel_id=1, source_target_pairs={{0,2},{1,3},{2,0},{3,1},{4,6},{5,7},{6,4},{7,5},{8,10},{9,11},{10,... | collective-permute-start | bytes 1572872 | tf_op jit(solution)/shard_map/ppermute | solution.py:55
  163.4 60.6 %collective-permute-start.18 = (bf16[2048,128]{1,0:T(8,128)(2,1)}, bf16[2048,128]{1,0:T(8,128)(2,1)}, u32[]{:S(2)}, u32[]{:S(2)}) collective-permute-start(bf16[2048,128]{1,0:T(8,128)(2,1)} %bitcast.29.refs_0_), channel_id=1, source_target_pairs={{0,3},{1,0},{2,1},{3,2},{4,7},{5,4},{6,5},{7,6},{8,11},{9,8},{10,9... | collective-permute-start | bytes 1572872 | tf_op jit(solution)/shard_map/ppermute | solution.py:55
  164.6 60.5 %collective-permute-start.19 = (bf16[2048,128]{1,0:T(8,128)(2,1)}, bf16[2048,128]{1,0:T(8,128)(2,1)}, u32[]{:S(2)}, u32[]{:S(2)}) collective-permute-start(bf16[2048,128]{1,0:T(8,128)(2,1)} %bitcast.29.refs_0_), channel_id=1, source_target_pairs={{0,128},{128,0},{1,129},{129,1},{2,130},{130,2},{3,131},{131,3},{4... | collective-permute-start | bytes 1572872 | tf_op jit(solution)/shard_map/ppermute | solution.py:40
  166.0 36.0 %collective-permute-start.29 = (bf16[256,128]{1,0:T(8,128)(2,1)}, bf16[256,128]{1,0:T(8,128)(2,1)}, u32[]{:S(2)}, u32[]{:S(2)}) collective-permute-start(bf16[256,128]{1,0:T(8,128)(2,1)} %fusion.15), channel_id=1, source_target_pairs={{0,1},{1,2},{2,3},{3,0},{4,5},{5,6},{6,7},{7,4},{8,9},{9,10},{10,1... | collective-permute-start | bytes 196616 | tf_op jit(solution)/shard_map/ppermute | solution.py:55
  182.2 47.4 %all-to-all-start.4 = ((bf16[16,256,128]{2,1,0:T(8,128)(2,1)}), bf16[16,256,128]{2,1,0:T(8,128)(2,1)S(1)}, u32[]{:S(2)}, u32[]{:S(2)}) async-start(bf16[16,256,128]{2,1,0:T(8,128)(2,1)} %broadcast_in_dim.45), calls=%async_computation.4 | async-start | bytes 2097152 | tf_op jit(solution)/shard_map/all_to_all | solution.py:63
  202.0 12.5 %collective-permute-start.31 = (bf16[256,128]{1,0:T(8,128)(2,1)}, bf16[256,128]{1,0:T(8,128)(2,1)S(1)}, u32[]{:S(2)}, u32[]{:S(2)}) collective-permute-start(bf16[256,128]{1,0:T(8,128)(2,1)} %fusion.15), channel_id=1, source_target_pairs={{0,3},{1,0},{2,1},{3,2},{4,7},{5,4},{6,5},{7,6},{8,11},{9,8},{10,9... | collective-permute-start | bytes 196616 | tf_op jit(solution)/shard_map/ppermute | solution.py:55
  214.5 6.4 %collective-permute-start.30 = (bf16[256,128]{1,0:T(8,128)(2,1)}, bf16[256,128]{1,0:T(8,128)(2,1)S(1)}, u32[]{:S(2)}, u32[]{:S(2)}) collective-permute-start(bf16[256,128]{1,0:T(8,128)(2,1)} %fusion.15), channel_id=1, source_target_pairs={{0,2},{1,3},{2,0},{3,1},{4,6},{5,7},{6,4},{7,5},{8,10},{9,11},{10,... | collective-permute-start | bytes 196616 | tf_op jit(solution)/shard_map/ppermute | solution.py:55
  223.4 25.6 %collective-permute-start.32 = (f32[128,2048]{1,0:T(8,128)}, f32[128,2048]{1,0:T(8,128)}, u32[]{:S(2)}, u32[]{:S(2)}) collective-permute-start(f32[128,2048]{1,0:T(8,128)} %slice.124), channel_id=1, source_target_pairs={{0,128},{128,0},{1,129},{129,1},{2,130},{130,2},{3,131},{131,3},{4... | collective-permute-start | bytes 3145736 | tf_op jit(solution)/shard_map/ppermute | solution.py:40
  223.5 3.6 %collective-permute-start.20 = (bf16[2048,128]{1,0:T(8,128)(2,1)}, bf16[2048,128]{1,0:T(8,128)(2,1)S(1)}, u32[]{:S(2)}, u32[]{:S(2)}) collective-permute-start(bf16[2048,128]{1,0:T(8,128)(2,1)} %collective-permute-done.16.refs_1_), channel_id=1, source_target_pairs={{0,128},{128,0},{1,129},{129,1},{2,130},{130,2},{3,131},{131,3},{4... | collective-permute-start | bytes 1572872 | tf_op jit(solution)/shard_map/ppermute | solution.py:40
  224.0 4.0 %collective-permute-start.21 = (bf16[2048,128]{1,0:T(8,128)(2,1)}, bf16[2048,128]{1,0:T(8,128)(2,1)S(1)}, u32[]{:S(2)}, u32[]{:S(2)}) collective-permute-start(bf16[2048,128]{1,0:T(8,128)(2,1)} %collective-permute-done.17.refs_2_), channel_id=1, source_target_pairs={{0,128},{128,0},{1,129},{129,1},{2,130},{130,2},{3,131},{131,3},{4... | collective-permute-start | bytes 1572872 | tf_op jit(solution)/shard_map/ppermute | solution.py:40
  224.1 4.7 %collective-permute-start.22 = (bf16[2048,128]{1,0:T(8,128)(2,1)}, bf16[2048,128]{1,0:T(8,128)(2,1)S(1)}, u32[]{:S(2)}, u32[]{:S(2)}) collective-permute-start(bf16[2048,128]{1,0:T(8,128)(2,1)} %collective-permute-done.18.refs_3_), channel_id=1, source_target_pairs={{0,128},{128,0},{1,129},{129,1},{2,130},{130,2},{3,131},{131,3},{4... | collective-permute-start | bytes 1572872 | tf_op jit(solution)/shard_map/ppermute | solution.py:40
  225.1 14.0 %collective-permute-start.15 = (bf16[128,512]{1,0:T(8,128)(2,1)}, bf16[128,512]{1,0:T(8,128)(2,1)}, u32[]{:S(2)}, u32[]{:S(2)}) collective-permute-start(bf16[128,512]{1,0:T(8,128)(2,1)} %broadcast_select_fusion.2), channel_id=1, source_target_pairs={{0,128},{128,0},{1,129},{129,1},{2,130},{130,2},{3,131},{131,3},{4... | collective-permute-start | bytes 393224 | tf_op jit(solution)/shard_map/ppermute | solution.py:40
  227.9 14.7 %collective-permute-start.14 = (bf16[128,512]{1,0:T(8,128)(2,1)}, bf16[128,512]{1,0:T(8,128)(2,1)}, u32[]{:S(2)}, u32[]{:S(2)}) collective-permute-start(bf16[128,512]{1,0:T(8,128)(2,1)} %broadcast_select_fusion.3), channel_id=1, source_target_pairs={{0,128},{128,0},{1,129},{129,1},{2,130},{130,2},{3,131},{131,3},{4... | collective-permute-start | bytes 393224 | tf_op jit(solution)/shard_map/ppermute | solution.py:40
  236.4 8.5 %collective-permute-start.26 = (f32[128,128]{1,0:T(8,128)S(1)}, f32[128,128]{1,0:T(8,128)S(1)}, u32[]{:S(2)}, u32[]{:S(2)}) collective-permute-start(f32[128,128]{1,0:T(8,128)S(1)} %get-tuple-element.44), channel_id=1, source_target_pairs={{0,16},{4,20},{8,24},{12,28},{16,0},{20,4},{24,8},{28,12},{32,48},... | collective-permute-start | bytes 196616 | tf_op jit(solution)/shard_map/ppermute | solution.py:44
  239.0 5.9 %collective-permute-start.27 = (f32[128,128]{1,0:T(8,128)S(1)}, f32[128,128]{1,0:T(8,128)S(1)}, u32[]{:S(2)}, u32[]{:S(2)}) collective-permute-start(f32[128,128]{1,0:T(8,128)S(1)} %get-tuple-element.45), channel_id=1, source_target_pairs={{0,128},{128,0},{1,129},{129,1},{2,130},{130,2},{3,131},{131,3},{4... | collective-permute-start | bytes 196616 | tf_op jit(solution)/shard_map/ppermute | solution.py:40
  239.1 9.3 %collective-permute-start.28 = (f32[128,128]{1,0:T(8,128)S(1)}, f32[128,128]{1,0:T(8,128)S(1)}, u32[]{:S(2)}, u32[]{:S(2)}) collective-permute-start(f32[128,128]{1,0:T(8,128)S(1)} %get-tuple-element.46), channel_id=1, source_target_pairs={{0,144},{128,16},{4,148},{132,20},{8,152},{136,24},{12,156},{140,2... | collective-permute-start | bytes 196616 | tf_op jit(solution)/shard_map/ppermute | solution.py:51
  (24 other events, 188.3 us)
